TPU v7x, 32 devices: a whole 2x2x4 slice. The times are simulated.
32 devices in a mesh: grp: 2 (over x), seq: 16 (over z, y, core).
Axes of the slice: x: 2, y: 2, z: 4, core: 2. Of those that a mesh axis runs over, the one named last changes fastest.
Arguments:
- queries: bfloat16 [4, 16384, 128], P(None, ('grp', 'seq')), parts along dimension 1, may hold values from -6 to 6
- key_pairs: bfloat16 [4, 16384, 256], P(None, ('grp', 'seq')), parts along dimension 1, may hold values from -6 to 6
- value_pairs: bfloat16 [4, 16384, 256], P(None, ('grp', 'seq')), parts along dimension 1, may hold values from -6 to 6
- write_rates: float32 [4, 32768], P(None, ('grp', 'seq')), parts along dimension 1, as said below
- conv_query: float32 [4, 4, 128], replicated, may hold values from -3 to 3
- conv_key: float32 [4, 4, 256], replicated, may hold values from -3 to 3
- conv_value: float32 [4, 4, 256], replicated, may hold values from -3 to 3
- out_gain: float32 [4, 128], replicated, may hold values from 0.5 to 1.5
Outputs:
- head_out: float32 [4, 16384, 128], P(None, ('grp', 'seq')), parts along dimension 1
There are 2 independent parts, one for each index of `grp`. A program takes and returns all parts, laid end to end along the dimension named above; an argument that names none is the same for every part. Nothing has to cross between parts.
Inputs may be any that keep to these rules, and one draw needn't show every extreme that they name: `write_rates`: every rate is positive and at most 1.5.
All inputs are finite; a program needn't handle non-finite values.
Results may differ from a plain program's by a relative error of at most 0.0003.
Values may be sent and summed in bfloat16 or wider, within the bound.
No kernel may reach another device: no remote copies, remote signals or barrier semaphores. Data moves between devices by JAX's collectives and lax.ppermute only.
A program may use at most 192 MiB of HBM per device.

v0:
```python
import jax
import jax.numpy as jnp
from jax import lax
from jax.sharding import PartitionSpec as P

BLOCK = 128


exact_prec = lax.Precision.HIGHEST


def shifted(value, axis, steps):
    count = lax.axis_size(axis)
    initial, last = (max(0, -steps), min(count, count - steps))
    return lax.ppermute(value, axis, [(source, source + steps) for source in range(initial, last)])


def prefix(x, axis, combine, identity):
    count, index = (lax.axis_size(axis), lax.axis_index(axis))
    everything = jax.tree.map(lambda part: lax.all_gather(part, axis), x)
    start = jax.tree.map(
        lambda part, zero: jnp.broadcast_to(jnp.asarray(zero, part.dtype), part.shape), x, identity
    )

    def hop(k, before):
        reached = k < index
        new = combine(before, jax.tree.map(lambda part: part[k], everything))
        return jax.tree.map(lambda a, b: jnp.where(reached, a, b), new, before)

    return lax.fori_loop(0, count, hop, start)


def causal_conv(extended, weights, length):
    kernel_len = weights.shape[1]
    summed = jnp.zeros((extended.shape[0], length, extended.shape[2]), jnp.float32)
    for shift_pos in range(kernel_len):
        summed = summed + weights[:, shift_pos][:, None, :] * extended[
            :, shift_pos : shift_pos + length
        ].astype(jnp.float32)
    return jax.nn.silu(summed)


def combine_maps(earlier, latter):
    earlier_map, earlier_state = earlier
    latter_map, latter_state = latter
    new_map = jnp.einsum("hij,hjk->hik", latter_map, earlier_map, precision=exact_prec)
    new_state = (
        jnp.einsum("hij,hjk->hik", latter_map, earlier_state, precision=exact_prec) + latter_state
    )
    return (new_map, new_state)


def identity_maps(head_count, head_dim, val_dim):
    unit_map = jnp.broadcast_to(
        jnp.eye(head_dim, dtype=jnp.float32), (head_count, head_dim, head_dim)
    )
    return (unit_map, jnp.zeros((head_count, head_dim, val_dim), jnp.float32))


def prepare(query_act, key_act, value_act, rates):
    head_count, step_count, head_dim = key_act.shape
    val_dim = value_act.shape[2]
    block_len = BLOCK
    block_count = step_count // block_len
    half_len = block_len // 2
    key_blocks = key_act.reshape(head_count, block_count, block_len, head_dim).transpose(1, 0, 2, 3)
    value_blocks = value_act.reshape(head_count, block_count, block_len, val_dim).transpose(
        1, 0, 2, 3
    )
    rate_blocks = rates.reshape(head_count, block_count, block_len).transpose(1, 0, 2)
    query_blocks = query_act.reshape(head_count, block_count, half_len, head_dim).transpose(
        1, 0, 2, 3
    )
    key_gram = jnp.einsum("nhcd,nhed->nhce", key_blocks, key_blocks, precision=exact_prec)
    strict_lower = jnp.tril(key_gram * rate_blocks[..., None], -1)
    system = strict_lower + jnp.eye(block_len, dtype=jnp.float32)
    right_side = jnp.concatenate(
        [rate_blocks[..., None] * key_blocks, rate_blocks[..., None] * value_blocks], -1
    )
    solved = lax.linalg.triangular_solve(
        system, right_side, left_side=True, lower=True, unit_diagonal=True
    )
    key_weights = solved[..., :head_dim]
    new_values = solved[..., head_dim:]
    causal_mask = (jnp.arange(block_len)[None, :] <= 2 * jnp.arange(half_len)[:, None] + 1).astype(
        jnp.float32
    )
    scores = (
        jnp.einsum("nhtd,nhcd->nhtc", query_blocks, key_blocks, precision=exact_prec) * causal_mask
    )
    pulled_query = query_blocks - jnp.einsum(
        "nhtc,nhcd->nhtd", scores, key_weights, precision=exact_prec
    )
    local_out = jnp.einsum("nhtc,nhce->nhte", scores, new_values, precision=exact_prec)
    transition = jnp.eye(head_dim, dtype=jnp.float32) - jnp.einsum(
        "nhcd,nhce->nhde", key_blocks, key_weights, precision=exact_prec
    )
    written = jnp.einsum("nhcd,nhce->nhde", key_blocks, new_values, precision=exact_prec)
    start_maps = identity_maps(head_count, head_dim, val_dim)

    def fold_only(carried, inputs):
        return (combine_maps(carried, inputs), None)

    totals, _ = lax.scan(fold_only, start_maps, (transition, written))
    return (totals, (pulled_query, local_out, transition, written))


def finish(saved, start_state):

    def read_step(carried, inputs):
        query_b, local_b, transition_b, written_b = inputs
        read_b = jnp.einsum("htd,hde->hte", query_b, carried, precision=exact_prec) + local_b
        carried = (
            jnp.einsum("hij,hjk->hik", transition_b, carried, precision=exact_prec) + written_b
        )
        return (carried, read_b)

    _, result = lax.scan(read_step, start_state, saved)
    block_count, head_count, half_len, val_dim = result.shape
    return jnp.transpose(result, (1, 0, 2, 3)).reshape(head_count, block_count * half_len, val_dim)


def per_device(
    queries, key_pairs, value_pairs, write_rates, conv_query, conv_key, conv_value, out_gain
):
    head_count, tok_count, head_dim = queries.shape
    val_dim = value_pairs.shape[2] // 2
    rim_width = conv_query.shape[1] - 1
    tails = (
        queries[:, tok_count - rim_width :],
        key_pairs[:, tok_count - rim_width :],
        value_pairs[:, tok_count - rim_width :],
    )
    prior_query, prior_key, prior_value = shifted((tails[0], tails[1], tails[2]), "seq", 1)
    query_act = causal_conv(jnp.concatenate([prior_query, queries], 1), conv_query, tok_count)
    key_act = causal_conv(jnp.concatenate([prior_key, key_pairs], 1), conv_key, tok_count).reshape(
        head_count, 2 * tok_count, head_dim
    )
    key_act = key_act * lax.rsqrt(jnp.sum(key_act * key_act, -1, keepdims=True) + 1e-06)
    value_act = causal_conv(
        jnp.concatenate([prior_value, value_pairs], 1), conv_value, tok_count
    ).reshape(head_count, 2 * tok_count, val_dim)
    totals, saved = prepare(query_act, key_act, value_act, write_rates)
    incoming = prefix(totals, "seq", combine_maps, identity_maps(head_count, head_dim, val_dim))
    raw_out = finish(saved, incoming[1])
    squares = jnp.mean(raw_out * raw_out, -1, keepdims=True)
    return raw_out * lax.rsqrt(squares + 1e-06) * out_gain[:, None, :]


def solution(mesh):
    return jax.shard_map(
        per_device,
        mesh=mesh,
        in_specs=(
            P(None, ("grp", "seq"), None),
            P(None, ("grp", "seq"), None),
            P(None, ("grp", "seq"), None),
            P(None, ("grp", "seq")),
            P(),
            P(),
            P(),
            P(),
        ),
        out_specs=P(None, ("grp", "seq"), None),
        check_vma=False,
    )
```

profile of v0, /device:TPU:0, one launch (start us, length us, event | category | flops | bytes accessed | tf_op | source)
XLA Modules:
  0.0 552.4 jit_solution(9902656015343163279)
XLA Ops:
  7.3 2.3 collective-permute-start
  10.9 5.1 collective-permute-start.1
  19.8 4.7 fusion.78
  25.8 2.2 reduce_sum.18
  28.1 1.7 reshape.88
  29.9 3.2 divide_multiply_fusion
  33.1 2.7 reshape_reshape.3
  35.8 3.8 bitcast_multiply_fusion.1
  39.6 6.3 %add_bitcast_fusion = f32[8,4,1,128,128]{4,3,2,1,0:T(8,128)} fusion(f32[4,8,128,128]{3,2,1,0:T(8,128)S(1)} %reshape.88, f32[128,128]{1,0:T(8,128)S(1)} %get-tuple-element.263, f32[8,4,128]{2,1,0:T(4,128)S(1)} %bitcast.124, f32[4,8,128]{2,0,1:T(4,128)S(1)} %rsqrt_bitcast_fusion, f32[128,128]{1,0:T(8,128)S(1)} %fusion.72, pred[128,128]{1,0:T(8,128)(4,1)S(1)} %copy-done.6), kind=kOutput, calls=%fused_computation.48 | convolution fusion | flops 808452096 | bytes 4374528 | tf_op jit(solution)/shard_map/nhcd,nhed->nhce/dot_general | solution.py:74
  45.9 315.8 %custom-call.3 = f32[8,4,1,128,128]{3,4,2,1,0:T(8,128)} custom-call(f32[8,4,1,128,128]{4,3,2,1,0:T(8,128)} %add_bitcast_fusion), custom_call_target="InvertDiagBlocksLowerTriangular" | custom-call | tf_op jit(solution)/shard_map/triangular_solve | solution.py:80
  361.7 6.6 %fusion.27 = f32[8,4,128,256]{3,2,1,0:T(8,128)S(1)} fusion(f32[8,4,128,128]{3,2,1,0:T(8,128)} %get-tuple-element.241, f32[8,4,128,128]{3,2,1,0:T(8,128)} %get-tuple-element.240, f32[8,4,1,128,128]{3,4,2,1,0:T(8,128)} %custom-call.3), kind=kOutput, calls=%fused_computation.31 | convolution fusion | flops 1611661312 | bytes 10485760 | tf_op jit(solution)/shard_map/triangular_solve | solution.py:80
  368.4 5.4 fusion.34
  373.8 5.7 %fusion.48 = f32[8,4,128,128]{3,2,1,0:T(8,128)} fusion(f32[8,4,128,256]{3,2,1,0:T(8,128)S(1)} %fusion.27, f32[4,8,128,128]{3,2,1,0:T(8,128)S(1)} %reshape.88, f32[4,8,128]{2,0,1:T(4,128)S(1)} %rsqrt_bitcast_fusion, f32[128,128]{1,0:T(8,128)S(1)} %fusion.72), kind=kOutput, calls=%fused_computation.56 | convolution fusion | flops 806354944 | bytes 6373376 | tf_op jit(solution)/shard_map/nhcd,nhce->nhde/dot_general | solution.py:95
  379.5 22.9 %while.40 = (s32[]{:T(128)}, f32[4,128,128]{2,1,0:T(8,128)S(1)}, f32[4,128,128]{2,1,0:T(8,128)S(1)}, f32[8,4,128,128]{3,2,1,0:T(8,128)}, f32[8,4,128,128]{3,2,1,0:T(8,128)}, /*index=5*/s32[]{:T(128)}, s32[]{:T(128)}) while((s32[]{:T(128)}, f32[4,128,128]{2,1,0:T(8,128)S(1)}, f32[4,128,128]{2,1,0:T(8,128)S(1)}, ...), condition=%wide.region_2.3_spmd.clone, body=%wide.region_1.2_spmd.clone.sunk | while | flops 201457664 | bytes 2885207 | solution.py:104
  406.7 2.7 divide_multiply_fusion.2
  409.4 4.2 fusion.56
  413.7 2.1 fusion.40
  415.8 2.1 fusion.53
  417.9 35.8 %all-gather.5.cloned.1.call-done = f32[64,128,128]{2,1,0:T(8,128)} async-done(((f32[4,128,128]{2,1,0:T(8,128)}), f32[64,128,128]{2,1,0:T(8,128)}) %all-gather.5.cloned.1.call-update) | async-done | bytes 4194320 | tf_op jit(solution)/shard_map/all_gather | solution.py:20
  453.7 51.2 %all-gather.7.cloned.1.call-done = f32[64,128,128]{2,1,0:T(8,128)} async-done(((f32[4,128,128]{2,1,0:T(8,128)}), f32[64,128,128]{2,1,0:T(8,128)}) %all-gather.7.cloned.1.call-update) | async-done | bytes 4194320 | tf_op jit(solution)/shard_map/all_gather | solution.py:20
  505.0 23.7 %while.41 = (s32[]{:T(128)}, f32[4,128,128]{2,1,0:T(8,128)S(1)}, s32[]{:T(128)}, f32[16,4,128,128]{3,2,1,0:T(8,128)}, f32[16,4,128,128]{3,2,1,0:T(8,128)}, /*index=5*/s32[]{:T(128)}, s32[]{:T(128)}) while((s32[]{:T(128)}, f32[4,128,128]{2,1,0:T(8,128)S(1)}, s32[]{:T(128)}, f32[16,4,128,128]{3,2,1,0:T(8,128)}, ...), condition=%wide.region_4.5_spmd.clone, body=%wide.region_3.4_spmd.clone.sunk | while | flops 100925440 | bytes 1837663 | solution.py:30
  506.5 1.4 fusion.112
  519.8 1.4 fusion.112
  528.7 14.8 %while.39 = (s32[]{:T(128)}, f32[4,128,128]{2,1,0:T(8,128)S(1)}, f32[8,4,64,128]{3,2,1,0:T(8,128)S(1)}, f32[8,4,128,128]{3,2,1,0:T(8,128)}, f32[8,4,128,128]{3,2...) while((s32[]{:T(128)}, f32[4,128,128]{2,1,0:T(8,128)S(1)}, ...), condition=%wide.region_6.7_spmd, body=%wide.region_5.6_spmd.sunk | while | flops 151093248 | bytes 2230357 | solution.py:118
  (138 shorter events, 70.8 us)
Async XLA Ops:
  6.5 447.2 %all-gather.5.cloned.1.call-start = ((), (), s32[]{:S(2)}) async-start(), calls=%async_computation | async-start | bytes 4456448 | tf_op jit(solution)/shard_map/all_gather | solution.py:20
  7.3 12.5 %collective-permute-start = (bf16[4,3,256]{2,1,0:T(4,128)(2,1)S(1)}, bf16[4,3,256]{2,1,0:T(4,128)(2,1)S(1)}, u32[]{:S(2)}, u32[]{:S(2)}) collective-permute-start(bf16[4,3,256]{2,1,0:T(4,128)(2,1)S(1)} %slice.83), channel_id=1, source_target_pairs={{0,1},{1,2},{2,3},{3,4},{4,5},{5,6},{6,7},{7,8},{8,9},{9,10},{10,1... | collective-permute-start | bytes 18440 | tf_op jit(solution)/shard_map/ppermute | solution.py:15
  10.9 18.9 %collective-permute-start.1 = (bf16[4,3,256]{2,1,0:T(4,128)(2,1)}, bf16[4,3,256]{2,1,0:T(4,128)(2,1)}, u32[]{:S(2)}, u32[]{:S(2)}) collective-permute-start(bf16[4,3,256]{2,1,0:T(4,128)(2,1)} %slice.91), channel_id=1, source_target_pairs={{0,1},{1,2},{2,3},{3,4},{4,5},{5,6},{6,7},{7,8},{8,9},{9,10},{10,1... | collective-permute-start | bytes 18440 | tf_op jit(solution)/shard_map/ppermute | solution.py:15
  28.1 1.9 copy-start.4
  33.1 2.7 copy-start.5
  35.8 3.8 copy-start.6
  368.4 5.5 copy-start
  379.5 26.5 %copy-start.7 = (f32[4,4,128]{2,1,0:T(4,128)S(1)}, f32[4,4,128]{2,1,0:T(4,128)}, u32[]{:S(2)}) copy-start(f32[4,4,128]{2,1,0:T(4,128)} %param.18) | copy-start | bytes 24580
  402.4 0.7 copy-start.2
  402.4 0.8 copy-start.3
  403.1 101.8 %all-gather.7.cloned.1.call-start = ((), (), s32[]{:S(2)}) async-start(), calls=%async_computation.1 | async-start | bytes 4456448 | tf_op jit(solution)/shard_map/all_gather | solution.py:20
  404.6 2.1 collective-permute-start.2
  409.4 4.3 copy-start.1
  543.5 0.7 copy-start.8
Sparse Core Ops, SparseCore 0:
  403.2 50.4 all-gather.4
  455.9 49.0 all-gather.6
where the time goes:
time: 554 us; the launch traced here: 552 us
  other arithmetic  335 us (60%)
  matrix products  91.8 us (17%)
  waiting for transfers between devices  88.4 us (16%)
  between operations  13.7 us (2%)
  local copies, waits for them, and re-layouts  13.4 us (2%)
  starting transfers between devices  8.85 us (2%)
    another operation x3, other arithmetic, prepare(): lax.linalg.triangular_solve(system, right_side, left_side=True, lower=Tru...  317 us
    all_gather x2, waiting for transfers between devices, prefix(): everything = jax.tree.map(lambda part: lax.all_gather(part, axis), x)  87.1 us
    dot_general x24, matrix products, combine_maps(): jnp.einsum('hij,hjk->hik', latter_map, earlier_state, precision=exact_prec)  34.3 us
    dot_general x8, matrix products, read_step(): jnp.einsum('hij,hjk->hik', transition_b, carried, precision=exact_prec)  11.4 us
  transfers between devices with their start and end apart: 5, of which 3 were waited for; matrix products, arithmetic and copies ran while one was open for 5% of the time, Pallas kernels for 0%

commit v1 on v0

v1 whole, which is shorter than its diff:
```python
import jax
import jax.numpy as jnp
from jax import lax
from jax.experimental import pallas as pl
from jax.experimental.pallas import tpu as pltpu
from jax.sharding import PartitionSpec as P

BLOCK = 128
GROUP = 16
HALF = BLOCK // 2

f32 = jnp.float32
bf16 = jnp.bfloat16


def split(x):
    high = x.astype(bf16)
    low = (x - high.astype(f32)).astype(bf16)
    return jnp.concatenate([high, low], 1)


def mm(a, b):
    n = b.shape[1] // 2
    p = jnp.dot(a, jnp.concatenate([b, b], 0), preferred_element_type=f32)
    return p[:, :n] + p[:, n:]


def silu(x):
    return x / (1.0 + jnp.exp(-x))


def step_time(r):
    return (r // GROUP) * GROUP + 2 * (r % 8) + (r // 8) % 2


def interleave(a, b):
    parts = []
    for g in range(0, a.shape[0], 8):
        parts += [a[g : g + 8], b[g : g + 8]]
    return jnp.concatenate(parts, 0)


def conv_taps(ref, weights, start, count):
    taps = weights.shape[0]
    total = weights[0:1] * ref[pl.ds(start + 9 - taps, count), :]
    for s in range(1, taps):
        total = total + weights[s : s + 1] * ref[pl.ds(start + 9 - taps + s, count), :]
    return silu(total)


def fill_rows(ref, halo, rows):
    rim = halo.shape[0]
    ref[8 - rim : 8, :] = halo.astype(f32)
    ref[8:, :] = rows.astype(f32)


def maps_kernel(
    key_ref, value_ref, halo_ref, rate_ref, ck_ref, cv_ref,
    kb_ref, w_ref, u_ref, p_ref, s_ref, total_ref,
    k0, k1, v0, v1, kv, nref, dref, cref, xref, brow,
):
    dim = k0.shape[1]
    tokens = key_ref.shape[1]
    blocks = tokens // HALF
    halo = halo_ref[0]
    fill_rows(k0, halo[:, dim : 2 * dim], key_ref[0, :, :dim])
    fill_rows(k1, halo[:, 2 * dim : 3 * dim], key_ref[0, :, dim:])
    fill_rows(v0, halo[:, 3 * dim : 4 * dim], value_ref[0, :, :dim])
    fill_rows(v1, halo[:, 4 * dim :], value_ref[0, :, dim:])
    ck = ck_ref[0]
    cv = cv_ref[0]

    row = lax.broadcasted_iota(jnp.int32, (BLOCK, BLOCK), 0)
    col = lax.broadcasted_iota(jnp.int32, (BLOCK, BLOCK), 1)
    for n in range(blocks):
        brow[n : n + 1, :] = rate_ref[0, :, n * BLOCK : (n + 1) * BLOCK]
    order = (row == step_time(col)).astype(f32)
    rates = jnp.dot(brow[...], order, precision=lax.Precision.HIGHEST, preferred_element_type=f32)

    strict = step_time(col) < step_time(row)
    lane = lax.broadcasted_iota(jnp.int32, (GROUP, BLOCK), 1)
    eye = (row == col).astype(f32)

    for n in range(blocks):
        t0 = n * HALF
        ka = conv_taps(k0, ck[:, :dim], t0, HALF)
        kb = conv_taps(k1, ck[:, dim:], t0, HALF)
        keys = interleave(ka, kb)
        keys = keys * lax.rsqrt(jnp.sum(keys * keys, 1, keepdims=True) + 1e-06)
        va = conv_taps(v0, cv[:, :dim], t0, HALF)
        vb = conv_taps(v1, cv[:, dim:], t0, HALF)
        ks = split(keys)
        kv[n, :, : 2 * dim] = ks
        kv[n, :, 2 * dim :] = split(interleave(va, vb))
        kbs = split(keys.T * rates[n : n + 1, :])
        kb_ref[0, n] = kbs
        lower = jnp.where(strict, mm(ks, kbs), 0.0)
        nref[n] = lower
        diag = jnp.zeros((GROUP, BLOCK), f32)
        for g in range(BLOCK // GROUP):
            diag = jnp.where(lane // GROUP == g, lower[g * GROUP : (g + 1) * GROUP], diag)
        cref[n * GROUP : (n + 1) * GROUP, :] = diag

    lane8 = lax.broadcasted_iota(jnp.int32, (blocks, BLOCK), 1)
    times = [t // 2 + 8 * (t % 2) for t in range(GROUP)]
    coef = [cref[pl.ds(r, blocks, stride=GROUP), :] for r in range(GROUP)]
    sol = [(lane8 % GROUP == r).astype(f32) for r in range(GROUP)]
    for i, s in enumerate(times):
        pick = (lane8 // GROUP) * GROUP + s
        for r in times[i + 1 :]:
            sol[r] = sol[r] - jnp.take_along_axis(coef[r], pick, axis=1) * sol[s]
    for r in range(GROUP):
        xref[pl.ds(r, blocks, stride=GROUP), :] = sol[r]
    for n in range(blocks):
        base = xref[n * GROUP : (n + 1) * GROUP, :]
        dref[n] = split(
            jnp.concatenate(
                [jnp.where(lane // GROUP == g, base, 0.0) for g in range(BLOCK // GROUP)], 0
            )
        )

    lane_h = lax.broadcasted_iota(jnp.int32, (HALF, BLOCK), 1)
    row_h = lax.broadcasted_iota(jnp.int32, (HALF, BLOCK), 0)
    size = GROUP
    while size < BLOCK:
        keep = lane_h // size == 2 * (row_h // size)
        starts = range(size, BLOCK, 2 * size)
        for n in range(blocks):
            inv = dref[n]
            low = jnp.concatenate([nref[n, a : a + size] for a in starts], 0)
            z = split(mm(split(jnp.where(keep, low, 0.0)), inv))
            twice = []
            for i in range(len(starts)):
                twice += [z[i * size : (i + 1) * size]] * 2
            odd = jnp.concatenate([inv[a : a + size] for a in starts], 0)
            new = mm(odd, jnp.concatenate(twice, 0))
            new = split(odd[:, :BLOCK].astype(f32) + odd[:, BLOCK:].astype(f32) - new)
            for i, a in enumerate(starts):
                dref[n, a : a + size] = new[i * size : (i + 1) * size]
        size *= 2

    before_map = split(eye)
    before_state = jnp.zeros((dim, 2 * dim), bf16)
    state = jnp.zeros((dim, dim), f32)
    for n in range(blocks):
        inv = dref[n]
        w = split(mm(inv, kv[n, :, : 2 * dim]))
        u = split(mm(inv, kv[n, :, 2 * dim :]))
        w_ref[0, n] = w
        u_ref[0, n] = u
        p_ref[0, n] = before_map
        s_ref[0, n] = before_state
        kbs = kb_ref[0, n]
        move = split(eye - mm(kbs, w))
        written = mm(kbs, u)
        map_now = mm(move, before_map)
        state = mm(move, before_state) + written
        before_map = split(map_now)
        before_state = split(state)
        if n == blocks - 1:
            total_ref[0, :, :dim] = map_now
            total_ref[0, :, dim:] = state


def reads_kernel(
    query_ref, halo_ref, cq_ref, kb_ref, w_ref, u_ref, p_ref, s_ref, pulled_ref, local_ref, q0
):
    dim = q0.shape[1]
    tokens = query_ref.shape[1]
    blocks = tokens // HALF
    fill_rows(q0, halo_ref[0][:, :dim], query_ref[0])
    cq = cq_ref[0]
    row = lax.broadcasted_iota(jnp.int32, (HALF, BLOCK), 0)
    col = lax.broadcasted_iota(jnp.int32, (HALF, BLOCK), 1)
    causal = step_time(col) <= 2 * row + 1
    for n in range(blocks):
        rows = slice(n * HALF, (n + 1) * HALF)
        query = conv_taps(q0, cq, n * HALF, HALF)
        scores = split(jnp.where(causal, mm(split(query), kb_ref[0, n]), 0.0))
        pulled = query - mm(scores, w_ref[0, n])
        local = mm(scores, u_ref[0, n])
        pulled = split(pulled)
        local_ref[0, rows] = local + mm(pulled, s_ref[0, n])
        pulled_ref[0, rows] = split(mm(pulled, p_ref[0, n]))


def out_kernel(pulled_ref, local_ref, state_ref, gain_ref, out_ref):
    raw = mm(pulled_ref[0], split(state_ref[0])) + local_ref[0]
    mean = jnp.mean(raw * raw, 1, keepdims=True)
    out_ref[0] = raw * lax.rsqrt(mean + 1e-06) * gain_ref[0]


def head_spec(shape):
    rest = tuple(shape[1:])
    return pl.BlockSpec((1,) + rest, lambda h: (h,) + (0,) * len(rest))


def call(kernel, args, outs, scratch=()):
    outs = [jax.ShapeDtypeStruct(s, t) for s, t in outs]
    return pl.pallas_call(
        kernel,
        grid=(args[0].shape[0],),
        in_specs=[head_spec(a.shape) for a in args],
        out_specs=[head_spec(o.shape) for o in outs],
        out_shape=outs,
        scratch_shapes=list(scratch),
        compiler_params=pltpu.CompilerParams(vmem_limit_bytes=56 << 20),
    )(*args)


def compose(later, earlier):
    dim = later.shape[1]
    prod = jnp.einsum(
        "hij,hjk->hik", later[:, :, :dim], earlier, precision=lax.Precision.HIGHEST
    )
    cols = earlier.shape[2]
    return prod + jnp.where(
        jnp.arange(cols)[None, None, :] >= cols - dim, later[:, :, 2 * dim - cols :], 0.0
    )


def swap(x, bit, count):
    return lax.ppermute(x, "seq", [(i, i ^ bit) for i in range(count)])


def start_state(total):
    heads, dim, _ = total.shape
    count = lax.axis_size("seq")
    index = lax.axis_index("seq")
    current = total
    earlier_maps = []
    bit = 1
    while bit < count and current.shape[0] % 2 == 0:
        half = current.shape[0] // 2
        upper = (index & bit) != 0
        mine = jnp.where(upper, current[half:], current[:half])
        got = swap(jnp.where(upper, current[:half], current[half:]), bit, count)
        earlier = jnp.where(upper, got, mine)
        later = jnp.where(upper, mine, got)
        earlier_maps.append((bit, earlier))
        current = compose(later, earlier)
        bit *= 2
    stride = bit
    groups = count // stride
    hop = 1
    while hop < groups - 1:
        got = lax.ppermute(
            current, "seq", [(i, i + hop * stride) for i in range(count - hop * stride)]
        )
        current = compose(current, got)
        hop *= 2
    state = current[:, :, dim:]
    state = lax.ppermute(state, "seq", [(i, i + stride) for i in range(count - stride)])
    for bit, earlier in reversed(earlier_maps):
        upper = (index & bit) != 0
        after = compose(earlier, state)
        got = swap(jnp.where(upper, state, after), bit, count)
        mine = jnp.where(upper, after, state)
        state = jnp.concatenate(
            [jnp.where(upper, got, mine), jnp.where(upper, mine, got)], 0
        )
    return state


def per_device(
    queries, key_pairs, value_pairs, write_rates, conv_query, conv_key, conv_value, out_gain
):
    heads, tokens, dim = queries.shape
    blocks = tokens // HALF
    rim = conv_query.shape[1] - 1
    count = lax.axis_size("seq")
    tails = jnp.concatenate(
        [x[:, tokens - rim :] for x in (queries, key_pairs, value_pairs)], 2
    )
    halo = lax.ppermute(tails, "seq", [(i, i + 1) for i in range(count - 1)])
    rates = write_rates.reshape(heads, 1, 2 * tokens)
    wide = (heads, blocks, BLOCK, 2 * dim)
    rows = pltpu.VMEM((tokens + 8, dim), f32)
    kb, w, u, p, s, total = call(
        maps_kernel,
        (key_pairs, value_pairs, halo, rates, conv_key, conv_value),
        [(wide, bf16)] * 5 + [((heads, dim, 2 * dim), f32)],
        [rows] * 4
        + [
            pltpu.VMEM((blocks, BLOCK, 4 * dim), bf16),
            pltpu.VMEM((blocks, BLOCK, BLOCK), f32),
            pltpu.VMEM((blocks, BLOCK, 2 * BLOCK), bf16),
            pltpu.VMEM((blocks * GROUP, BLOCK), f32),
            pltpu.VMEM((blocks * GROUP, BLOCK), f32),
            pltpu.VMEM((blocks, BLOCK), f32),
        ],
    )
    pulled, local = call(
        reads_kernel,
        (queries, halo, conv_query, kb, w, u, p, s),
        [((heads, tokens, 2 * dim), bf16), ((heads, tokens, dim), f32)],
        [rows],
    )
    state = start_state(total)
    return call(
        out_kernel,
        (pulled, local, state, out_gain.reshape(heads, 1, dim)),
        [((heads, tokens, dim), f32)],
    )[0]


def solution(mesh):
    return jax.shard_map(
        per_device,
        mesh=mesh,
        in_specs=(
            P(None, ("grp", "seq"), None),
            P(None, ("grp", "seq"), None),
            P(None, ("grp", "seq"), None),
            P(None, ("grp", "seq")),
            P(),
            P(),
            P(),
            P(),
        ),
        out_specs=P(None, ("grp", "seq"), None),
        check_vma=False,
    )
```

time: 554 us -> 88 us (0.16)
  other arithmetic: 335 us -> 2.97 us
  matrix products: 91.8 us -> 1.63 us
  waiting for transfers between devices: 88.4 us -> 15.5 us
  Pallas kernels: 0 us -> 39.7 us
  starting transfers between devices: 8.85 us -> 22.7 us
  between operations: 13.7 us -> 0.15 us
  local copies, waits for them, and re-layouts: 13.4 us -> 4.09 us
    another operation x3 -> x0, other arithmetic: 317 us -> none  [prepare(): lax.linalg.triangular_solve(system, right_side, left_side=True, lower=Tru...]
    all_gather x2 -> x0, waiting for transfers between devices: 87.1 us -> none  [prefix(): everything = jax.tree.map(lambda part: lax.all_gather(part, axis), x)]
    dot_general x54 -> x6, matrix products: 85.2 us -> 1.63 us  [compose(): jnp.einsum('hij,hjk->hik', later[:, :, :dim], earlier, precision=lax.Prec...]
    pallas_call x0 -> x3, Pallas kernels: none -> 39.7 us  [call(): pl.pallas_call(kernel, grid=(args[0].shape[0],), in_specs=[head_spec(a.sh...]
    mul x5 -> x0, other arithmetic: 15.7 us -> none  [the longest x2 5.89 us: causal_conv(): return jax.nn.silu(summed)]
    ppermute x3 -> x8, waiting for transfers between devices: 0.68 us -> 15.5 us  [the longest x4 8.6 us: swap(): return lax.ppermute(x, 'seq', [(i, i ^ bit) for i in range(count)])]
    ppermute x3 -> x8, starting transfers between devices: 8.8 us -> 22.7 us  [the longest x2 9.96 us: start_state(): lax.ppermute(current, 'seq', [(i, i + hop * stride) for i in range(count...]
    another operation x1 -> x0, matrix products: 6.61 us -> none  [prepare(): lax.linalg.triangular_solve(system, right_side, left_side=True, lower=Tru...]
  transfers between devices with their start and end apart: 5 -> 8, of which waited for: 3 -> 6; matrix products, arithmetic and copies ran while one was open for 5% -> 2% of each run, Pallas kernels for 0% -> 15%
where the time goes in v1:
time: 88 us; the launch traced here: 86.7 us
  Pallas kernels  39.7 us (45%)
  starting transfers between devices  22.7 us (26%)
  waiting for transfers between devices  15.5 us (18%)
  local copies, waits for them, and re-layouts  4.09 us (5%)
  other arithmetic  2.97 us (3%)
  matrix products  1.63 us (2%)
    pallas_call x3, Pallas kernels, call(): pl.pallas_call(kernel, grid=(args[0].shape[0],), in_specs=[head_spec(a.sh...  39.7 us
    ppermute x2, starting transfers between devices, start_state(): lax.ppermute(current, 'seq', [(i, i + hop * stride) for i in range(count...  9.96 us
    ppermute x4, waiting for transfers between devices, swap(): return lax.ppermute(x, 'seq', [(i, i ^ bit) for i in range(count)])  8.6 us
    ppermute x4, starting transfers between devices, swap(): return lax.ppermute(x, 'seq', [(i, i ^ bit) for i in range(count)])  5.62 us
    ppermute x2, waiting for transfers between devices, start_state(): lax.ppermute(current, 'seq', [(i, i + hop * stride) for i in range(count...  4.98 us
    ppermute x1, starting transfers between devices, start_state(): lax.ppermute(state, 'seq', [(i, i + stride) for i in range(count - stride)])  4.75 us
    ppermute x1, starting transfers between devices, per_device(): halo = lax.ppermute(tails, 'seq', [(i, i + 1) for i in range(count - 1)])  2.36 us
    slice x3, local copies, waits for them, and re-layouts, per_device(): x[:, tokens - rim:]  2.15 us
  transfers between devices with their start and end apart: 8, of which 6 were waited for; matrix products, arithmetic and copies ran while one was open for 2% of the time, Pallas kernels for 15%

profile of v1, /device:TPU:0, one launch (start us, length us, event | category | flops | bytes accessed | tf_op | source)
XLA Modules:
  0.0 86.7 jit_solution(6303281637829254708)
XLA Ops:
  0.0 0.7 slice.53
  0.7 0.7 slice.54
  1.4 0.7 slice.52
  2.2 2.4 %collective-permute-start = (bf16[4,3,640]{2,1,0:T(4,128)(2,1)S(1)}, bf16[4,3,640]{2,1,0:T(4,128)(2,1)S(1)}, u32[]{:S(2)}, u32[]{:S(2)}) collective-permute-start(bf16[4,3,640]{2,1,0:T(4,128)(2,1)S(1)} %pad_maximum_fusion.3), channel_id=1, source_target_pairs={{0,1},{1,2},{2,3},{3,4},{4,5},{5,6},{6,7},{7,8},{8,9},{9,10},{10,1... | collective-permute-start | bytes 46088 | tf_op jit(solution)/shard_map/ppermute | solution.py:275
  4.5 1.3 %reshape.41.rate_ref = f32[4,1,1024]{2,1,0:T(1,128)} reshape(f32[4,1024]{1,0:T(4,128)} %param.11) | data formatting | bytes 32768 | tf_op jit(solution)/shard_map/reshape | solution.py:276
  5.9 0.6 copy-done
  6.5 22.9 %shard_map.82 = (bf16[4,8,128,256]{3,2,1,0:T(8,128)(2,1)}, bf16[4,8,128,256]{3,2,1,0:T(8,128)(2,1)}, bf16[4,8,128,256]{3,2,1,0:T(8,128)(2,1)}, bf16[4,8,128,256]...) custom-call(bf16[4,512,256]{2,1,0:T(8,128)(2,1)} %key_ref.1, ...), custom_call_target="tpu_custom_call" | custom-call | tf_op jit(solution)/shard_map/pallas_call | solution.py:200
  29.3 1.1 %slice_select_fusion = f32[2,128,256]{2,1,0:T(8,128)S(1)} fusion(f32[4,128,256]{2,1,0:T(8,128)} %get-tuple-element.20, pred[]{:T(512)S(6)} %ne.8), kind=kLoop, calls=%fused_computation.10 | loop fusion | flops 65536 | bytes 786433 | tf_op jit(solution)/shard_map/jit(_where)/select_n | solution.py:237
  30.4 2.7 %collective-permute-start.1 = (f32[2,128,256]{2,1,0:T(8,128)S(1)}, f32[2,128,256]{2,1,0:T(8,128)S(1)}, u32[]{:S(2)}, u32[]{:S(2)}) collective-permute-start(f32[2,128,256]{2,1,0:T(8,128)S(1)} %slice_select_fusion), channel_id=1, source_target_pairs={{0,1},{1,0},{2,3},{3,2},{4,5},{5,4},{6,7},{7,6},{8,9},{9,8},{10,11... | collective-permute-start | bytes 786440 | tf_op jit(solution)/shard_map/ppermute | solution.py:223
  33.1 1.2 %collective-permute-done.1 = f32[2,128,256]{2,1,0:T(8,128)S(1)} collective-permute-done((f32[2,128,256]{2,1,0:T(8,128)S(1)}, f32[2,128,256]{2,1,0:T(8,128)S(1)}, u32[]{:S(2)}, u32[]{:S(2)}) %collective-permute-start.1) | collective-permute-done | bytes 262176 | tf_op jit(solution)/shard_map/ppermute | solution.py:223
  34.3 1.1 %broadcast_select_fusion.1 = (f32[2,128,256]{2,1,0:T(8,128)S(1)}, f32[2,128,256]{2,1,0:T(8,128)S(1)}) fusion(f32[2,128,256]{2,1,0:T(8,128)S(1)} %collective-permute-done.1, pred[]{:T(512)S(6)} %ne.8, f32[4,128,256]{2,1,0:T(8,128)} %get-tuple-element.20), kind=kLoop, calls=%fused_computation.19 | loop fusion | flops 196608 | bytes 1310721 | tf_op jit(solution)/shard_map/jit(_where)/select_n | solution.py:239
  35.8 2.2 %collective-permute-start.2 = (f32[1,128,256]{2,1,0:T(8,128)S(1)}, f32[1,128,256]{2,1,0:T(8,128)S(1)}, u32[]{:S(2)}, u32[]{:S(2)}) collective-permute-start(f32[1,128,256]{2,1,0:T(8,128)S(1)} %slice_select_fusion.2), channel_id=1, source_target_pairs={{0,2},{1,3},{2,0},{3,1},{4,6},{5,7},{6,4},{7,5},{8,10},{9,11},{10,... | collective-permute-start | bytes 393224 | tf_op jit(solution)/shard_map/ppermute | solution.py:223
  37.9 3.8 %collective-permute-done.2 = f32[1,128,256]{2,1,0:T(8,128)S(1)} collective-permute-done((f32[1,128,256]{2,1,0:T(8,128)S(1)}, f32[1,128,256]{2,1,0:T(8,128)S(1)}, u32[]{:S(2)}, u32[]{:S(2)}) %collective-permute-start.2) | collective-permute-done | bytes 131104 | tf_op jit(solution)/shard_map/ppermute | solution.py:223
  42.0 4.6 %collective-permute-start.3 = (f32[1,128,256]{2,1,0:T(8,128)S(1)}, f32[1,128,256]{2,1,0:T(8,128)S(1)}, u32[]{:S(2)}, u32[]{:S(2)}) collective-permute-start(f32[1,128,256]{2,1,0:T(8,128)S(1)} %fusion), channel_id=1, source_target_pairs={{0,4},{1,5},{2,6},{3,7},{4,8},{5,9},{6,10},{7,11},{8,12},{9,13},{1... | collective-permute-start | bytes 393224 | tf_op jit(solution)/shard_map/ppermute | solution.py:247
  46.6 2.5 %collective-permute-done.3 = f32[1,128,256]{2,1,0:T(8,128)S(1)} collective-permute-done((f32[1,128,256]{2,1,0:T(8,128)S(1)}, f32[1,128,256]{2,1,0:T(8,128)S(1)}, u32[]{:S(2)}, u32[]{:S(2)}) %collective-permute-start.3) | collective-permute-done | bytes 131104 | tf_op jit(solution)/shard_map/ppermute | solution.py:247
  49.4 5.3 %collective-permute-start.4 = (f32[1,128,256]{2,1,0:T(8,128)S(1)}, f32[1,128,256]{2,1,0:T(8,128)S(1)}, u32[]{:S(2)}, u32[]{:S(2)}) collective-permute-start(f32[1,128,256]{2,1,0:T(8,128)S(1)} %fusion.1), channel_id=1, source_target_pairs={{0,8},{1,9},{2,10},{3,11},{4,12},{5,13},{6,14},{7,15},{16,24},{17,... | collective-permute-start | bytes 393224 | tf_op jit(solution)/shard_map/ppermute | solution.py:247
  54.8 2.5 %collective-permute-done.4 = f32[1,128,256]{2,1,0:T(8,128)S(1)} collective-permute-done((f32[1,128,256]{2,1,0:T(8,128)S(1)}, f32[1,128,256]{2,1,0:T(8,128)S(1)}, u32[]{:S(2)}, u32[]{:S(2)}) %collective-permute-start.4) | collective-permute-done | bytes 131104 | tf_op jit(solution)/shard_map/ppermute | solution.py:247
  57.5 4.7 %collective-permute-start.5 = (f32[1,128,128]{2,1,0:T(8,128)S(1)}, f32[1,128,128]{2,1,0:T(8,128)S(1)}, u32[]{:S(2)}, u32[]{:S(2)}) collective-permute-start(f32[1,128,128]{2,1,0:T(8,128)S(1)} %slice_add_fusion), channel_id=1, source_target_pairs={{0,4},{1,5},{2,6},{3,7},{4,8},{5,9},{6,10},{7,11},{8,12},{9,13},{1... | collective-permute-start | bytes 196616 | tf_op jit(solution)/shard_map/ppermute | solution.py:253
  62.3 1.9 %collective-permute-done.5 = f32[1,128,128]{2,1,0:T(8,128)S(1)} collective-permute-done((f32[1,128,128]{2,1,0:T(8,128)S(1)}, f32[1,128,128]{2,1,0:T(8,128)S(1)}, u32[]{:S(2)}, u32[]{:S(2)}) %collective-permute-start.5) | collective-permute-done | bytes 65568 | tf_op jit(solution)/shard_map/ppermute | solution.py:253
  64.4 0.7 collective-permute-start.6
  65.1 3.6 %collective-permute-done.6 = f32[1,128,128]{2,1,0:T(8,128)S(1)} collective-permute-done((f32[1,128,128]{2,1,0:T(8,128)S(1)}, f32[1,128,128]{2,1,0:T(8,128)S(1)}, u32[]{:S(2)}, u32[]{:S(2)}) %collective-permute-start.6) | collective-permute-done | bytes 65568 | tf_op jit(solution)/shard_map/ppermute | solution.py:223
  69.1 12.7 %shard_map.83 = (bf16[4,512,256]{2,1,0:T(8,128)(2,1)}, f32[4,512,128]{2,1,0:T(8,128)}) custom-call(bf16[4,512,128]{2,1,0:T(8,128)(2,1)} %query_ref.1, bf16[4,3,640]{2,1,0:T(4,128)(2,1)} %copy-done, f32[4,4,128]{2,1,0:T(4,128)} %cq_ref.1, bf16[4,8,128,256]{3,2,1,0:T(8,128)(2,1)} %get-tuple-element.13.kb_ref, ...), custom_call_target="tpu_custom_call" | custom-call | tf_op jit(solution)/shard_map/pallas_call | solution.py:200
  81.8 0.7 pad_maximum_fusion.state_ref
  82.5 4.2 %shard_map.84 = f32[4,512,128]{2,1,0:T(8,128)} custom-call(bf16[4,512,256]{2,1,0:T(8,128)(2,1)} %get-tuple-element.18.pulled_ref, f32[4,512,128]{2,1,0:T(8,128)} %get-tuple-element.19.local_ref, f32[4,128,128]{2,1,0:T(8,128)} %pad_maximum_fusion.state_ref, f32[4,1,128]{2,1,0:T(1,128)} %bitcast.44), custom_call_target="tpu_custom_call" | custom-call | tf_op jit(solution)/shard_map/pallas_call | solution.py:200
  (18 shorter events, 1.8 us)
Async XLA Ops:
  2.2 3.7 %collective-permute-start = (bf16[4,3,640]{2,1,0:T(4,128)(2,1)S(1)}, bf16[4,3,640]{2,1,0:T(4,128)(2,1)S(1)}, u32[]{:S(2)}, u32[]{:S(2)}) collective-permute-start(bf16[4,3,640]{2,1,0:T(4,128)(2,1)S(1)} %pad_maximum_fusion.3), channel_id=1, source_target_pairs={{0,1},{1,2},{2,3},{3,4},{4,5},{5,6},{6,7},{7,8},{8,9},{9,10},{10,1... | collective-permute-start | bytes 46088 | tf_op jit(solution)/shard_map/ppermute | solution.py:275
  5.9 0.6 copy-start
  30.4 3.9 %collective-permute-start.1 = (f32[2,128,256]{2,1,0:T(8,128)S(1)}, f32[2,128,256]{2,1,0:T(8,128)S(1)}, u32[]{:S(2)}, u32[]{:S(2)}) collective-permute-start(f32[2,128,256]{2,1,0:T(8,128)S(1)} %slice_select_fusion), channel_id=1, source_target_pairs={{0,1},{1,0},{2,3},{3,2},{4,5},{5,4},{6,7},{7,6},{8,9},{9,8},{10,11... | collective-permute-start | bytes 786440 | tf_op jit(solution)/shard_map/ppermute | solution.py:223
  35.8 6.0 %collective-permute-start.2 = (f32[1,128,256]{2,1,0:T(8,128)S(1)}, f32[1,128,256]{2,1,0:T(8,128)S(1)}, u32[]{:S(2)}, u32[]{:S(2)}) collective-permute-start(f32[1,128,256]{2,1,0:T(8,128)S(1)} %slice_select_fusion.2), channel_id=1, source_target_pairs={{0,2},{1,3},{2,0},{3,1},{4,6},{5,7},{6,4},{7,5},{8,10},{9,11},{10,... | collective-permute-start | bytes 393224 | tf_op jit(solution)/shard_map/ppermute | solution.py:223
  42.0 7.1 %collective-permute-start.3 = (f32[1,128,256]{2,1,0:T(8,128)S(1)}, f32[1,128,256]{2,1,0:T(8,128)S(1)}, u32[]{:S(2)}, u32[]{:S(2)}) collective-permute-start(f32[1,128,256]{2,1,0:T(8,128)S(1)} %fusion), channel_id=1, source_target_pairs={{0,4},{1,5},{2,6},{3,7},{4,8},{5,9},{6,10},{7,11},{8,12},{9,13},{1... | collective-permute-start | bytes 393224 | tf_op jit(solution)/shard_map/ppermute | solution.py:247
  49.4 7.8 %collective-permute-start.4 = (f32[1,128,256]{2,1,0:T(8,128)S(1)}, f32[1,128,256]{2,1,0:T(8,128)S(1)}, u32[]{:S(2)}, u32[]{:S(2)}) collective-permute-start(f32[1,128,256]{2,1,0:T(8,128)S(1)} %fusion.1), channel_id=1, source_target_pairs={{0,8},{1,9},{2,10},{3,11},{4,12},{5,13},{6,14},{7,15},{16,24},{17,... | collective-permute-start | bytes 393224 | tf_op jit(solution)/shard_map/ppermute | solution.py:247
  57.5 6.6 %collective-permute-start.5 = (f32[1,128,128]{2,1,0:T(8,128)S(1)}, f32[1,128,128]{2,1,0:T(8,128)S(1)}, u32[]{:S(2)}, u32[]{:S(2)}) collective-permute-start(f32[1,128,128]{2,1,0:T(8,128)S(1)} %slice_add_fusion), channel_id=1, source_target_pairs={{0,4},{1,5},{2,6},{3,7},{4,8},{5,9},{6,10},{7,11},{8,12},{9,13},{1... | collective-permute-start | bytes 196616 | tf_op jit(solution)/shard_map/ppermute | solution.py:253
  64.4 4.3 %collective-permute-start.6 = (f32[1,128,128]{2,1,0:T(8,128)S(1)}, f32[1,128,128]{2,1,0:T(8,128)S(1)}, u32[]{:S(2)}, u32[]{:S(2)}) collective-permute-start(f32[1,128,128]{2,1,0:T(8,128)S(1)} %get-tuple-element.29), channel_id=1, source_target_pairs={{0,2},{1,3},{2,0},{3,1},{4,6},{5,7},{6,4},{7,5},{8,10},{9,11},{10,... | collective-permute-start | bytes 196616 | tf_op jit(solution)/shard_map/ppermute | solution.py:223
  69.0 12.8 %collective-permute-start.7 = (f32[2,128,128]{2,1,0:T(8,128)S(1)}, f32[2,128,128]{2,1,0:T(8,128)S(1)}, u32[]{:S(2)}, u32[]{:S(2)}) collective-permute-start(f32[2,128,128]{2,1,0:T(8,128)S(1)} %get-tuple-element.31), channel_id=1, source_target_pairs={{0,1},{1,0},{2,3},{3,2},{4,5},{5,4},{6,7},{7,6},{8,9},{9,8},{10,11... | collective-permute-start | bytes 393224 | tf_op jit(solution)/shard_map/ppermute | solution.py:223

commit v2 on v1

--- a/solution.py
+++ b/solution.py
@@ -25,6 +25,11 @@
     return p[:, :n] + p[:, n:]
 
 
+def pick_row(x, r):
+    row = lax.broadcasted_iota(jnp.int32, x.shape, 0)
+    return jnp.sum(jnp.where(row == r, x, 0.0), 0, keepdims=True)
+
+
 def silu(x):
     return x / (1.0 + jnp.exp(-x))
 
@@ -55,10 +60,11 @@
 
 
 def maps_kernel(
-    key_ref, value_ref, halo_ref, rate_ref, ck_ref, cv_ref,
+    first_ref, key_ref, value_ref, halo_ref, rate_ref, ck_ref, cv_ref,
     kb_ref, w_ref, u_ref, p_ref, s_ref, total_ref,
     k0, k1, v0, v1, kv, nref, dref, cref, xref, brow,
 ):
+    head = first_ref[0] + pl.program_id(0)
     dim = k0.shape[1]
     tokens = key_ref.shape[1]
     blocks = tokens // HALF
@@ -73,7 +79,7 @@
     row = lax.broadcasted_iota(jnp.int32, (BLOCK, BLOCK), 0)
     col = lax.broadcasted_iota(jnp.int32, (BLOCK, BLOCK), 1)
     for n in range(blocks):
-        brow[n : n + 1, :] = rate_ref[0, :, n * BLOCK : (n + 1) * BLOCK]
+        brow[n : n + 1, :] = pick_row(rate_ref[:, n * BLOCK : (n + 1) * BLOCK], head)
     order = (row == step_time(col)).astype(f32)
     rates = jnp.dot(brow[...], order, precision=lax.Precision.HIGHEST, preferred_element_type=f32)
 
@@ -163,8 +169,9 @@
 
 
 def reads_kernel(
-    query_ref, halo_ref, cq_ref, kb_ref, w_ref, u_ref, p_ref, s_ref, pulled_ref, local_ref, q0
+    first_ref, query_ref, halo_ref, cq_ref, kb_ref, w_ref, u_ref, p_ref, s_ref, *rest
 ):
+    pulled_ref, local_ref, q0 = rest[-3:]
     dim = q0.shape[1]
     tokens = query_ref.shape[1]
     blocks = tokens // HALF
@@ -184,82 +191,114 @@
         pulled_ref[0, rows] = split(mm(pulled, p_ref[0, n]))
 
 
-def out_kernel(pulled_ref, local_ref, state_ref, gain_ref, out_ref):
-    raw = mm(pulled_ref[0], split(state_ref[0])) + local_ref[0]
+def out_kernel(first_ref, pulled_ref, local_ref, kept_ref, sent_ref, gain_ref, out_ref):
+    heads = kept_ref.shape[0]
+    h = pl.program_id(0)
+    slot = h % heads
+    state = jnp.where(h // heads == first_ref[0], kept_ref[slot], sent_ref[slot])
+    raw = mm(pulled_ref[0], split(state)) + local_ref[0]
     mean = jnp.mean(raw * raw, 1, keepdims=True)
-    out_ref[0] = raw * lax.rsqrt(mean + 1e-06) * gain_ref[0]
-
-
-def head_spec(shape):
-    rest = tuple(shape[1:])
-    return pl.BlockSpec((1,) + rest, lambda h: (h,) + (0,) * len(rest))
-
-
-def call(kernel, args, outs, scratch=()):
-    outs = [jax.ShapeDtypeStruct(s, t) for s, t in outs]
+    out_ref[0] = raw * lax.rsqrt(mean + 1e-06) * pick_row(gain_ref[...], h)
+
+
+def then(later, earlier):
+    dim = later.shape[0]
+    prod = mm(split(later[:, :dim]), split(earlier))
+    wide = prod.shape[1]
+    if wide == dim:
+        return prod + later[:, dim:]
+    return jnp.concatenate([prod[:, :dim], prod[:, dim:] + later[:, dim:]], 1)
+
+
+def pair_kernel(upper_ref, mine_ref, got_ref, total_ref, earlier_ref):
+    upper = upper_ref[0] != 0
+    for h in range(mine_ref.shape[0]):
+        mine = mine_ref[h]
+        got = got_ref[h]
+        earlier = jnp.where(upper, got, mine)
+        earlier_ref[h] = earlier
+        total_ref[h] = then(jnp.where(upper, mine, got), earlier)
+
+
+def join_kernel(upper_ref, mine_ref, got_ref, before_ref, total_ref, after_ref):
+    upper = upper_ref[0] != 0
+    dim = mine_ref.shape[1]
+    for h in range(mine_ref.shape[0]):
+        mine = mine_ref[h]
+        got = got_ref[h]
+        earlier = jnp.where(upper, got, mine)
+        if total_ref.shape[2] == dim:
+            earlier = earlier[:, dim:]
+        total_ref[h] = then(jnp.where(upper, mine, got), earlier)
+        before = before_ref[h]
+        after_ref[h] = jnp.where(upper, then(before, got), before)
+
+
+def down_kernel(upper_ref, before_ref, got_ref, earlier_ref, mine_ref, other_ref):
+    upper = upper_ref[0] != 0
+    for h in range(before_ref.shape[0]):
+        state = then(before_ref[h], got_ref[h])
+        after = then(earlier_ref[h], state)
+        mine_ref[h] = jnp.where(upper, after, state)
+        other_ref[h] = jnp.where(upper, state, after)
+
+
+def tails_kernel(query_ref, key_ref, value_ref, out_ref):
+    rim = out_ref.shape[1]
+    at = 0
+    for ref in (query_ref, key_ref, value_ref):
+        wide = ref.shape[2]
+        out_ref[:, :, at : at + wide] = ref[:, ref.shape[1] - rim :, :]
+        at += wide
+
+
+def by_head(a):
+    rest = tuple(a.shape[1:])
+    return pl.BlockSpec((1,) + rest, lambda i, first: (first[0] + i,) + (0,) * len(rest))
+
+
+def by_slot(a, slot=0):
+    rest = tuple(a.shape[1:])
+    return pl.BlockSpec((1,) + rest, lambda i, first: (slot + i,) + (0,) * len(rest))
+
+
+def whole(a):
+    return pl.BlockSpec(a.shape, lambda i, first: (0,) * len(a.shape))
+
+
+def shape(dims, dtype):
+    return jax.ShapeDtypeStruct(dims, dtype)
+
+
+def call(kernel, steps, first, args, outs, scratch=(), aliases={}):
     return pl.pallas_call(
         kernel,
-        grid=(args[0].shape[0],),
-        in_specs=[head_spec(a.shape) for a in args],
-        out_specs=[head_spec(o.shape) for o in outs],
+        grid_spec=pltpu.PrefetchScalarGridSpec(
+            num_scalar_prefetch=1,
+            grid=(steps,),
+            in_specs=[spec for _, spec in args],
+            out_specs=[spec for _, spec in outs],
+            scratch_shapes=list(scratch),
+        ),
+        out_shape=[a for a, _ in outs],
+        input_output_aliases=aliases,
+        compiler_params=pltpu.CompilerParams(vmem_limit_bytes=56 << 20),
+    )(first, *[a for a, _ in args])
+
+
+def small(kernel, flag, args, outs):
+    smem = pl.BlockSpec(memory_space=pltpu.SMEM)
+    vmem = pl.BlockSpec(memory_space=pltpu.VMEM)
+    return pl.pallas_call(
+        kernel,
+        in_specs=[smem] + [vmem] * len(args),
+        out_specs=[vmem] * len(outs),
         out_shape=outs,
-        scratch_shapes=list(scratch),
-        compiler_params=pltpu.CompilerParams(vmem_limit_bytes=56 << 20),
-    )(*args)
-
-
-def compose(later, earlier):
-    dim = later.shape[1]
-    prod = jnp.einsum(
-        "hij,hjk->hik", later[:, :, :dim], earlier, precision=lax.Precision.HIGHEST
-    )
-    cols = earlier.shape[2]
-    return prod + jnp.where(
-        jnp.arange(cols)[None, None, :] >= cols - dim, later[:, :, 2 * dim - cols :], 0.0
-    )
+    )(flag, *args)
 
 
 def swap(x, bit, count):
     return lax.ppermute(x, "seq", [(i, i ^ bit) for i in range(count)])
-
-
-def start_state(total):
-    heads, dim, _ = total.shape
-    count = lax.axis_size("seq")
-    index = lax.axis_index("seq")
-    current = total
-    earlier_maps = []
-    bit = 1
-    while bit < count and current.shape[0] % 2 == 0:
-        half = current.shape[0] // 2
-        upper = (index & bit) != 0
-        mine = jnp.where(upper, current[half:], current[:half])
-        got = swap(jnp.where(upper, current[:half], current[half:]), bit, count)
-        earlier = jnp.where(upper, got, mine)
-        later = jnp.where(upper, mine, got)
-        earlier_maps.append((bit, earlier))
-        current = compose(later, earlier)
-        bit *= 2
-    stride = bit
-    groups = count // stride
-    hop = 1
-    while hop < groups - 1:
-        got = lax.ppermute(
-            current, "seq", [(i, i + hop * stride) for i in range(count - hop * stride)]
-        )
-        current = compose(current, got)
-        hop *= 2
-    state = current[:, :, dim:]
-    state = lax.ppermute(state, "seq", [(i, i + stride) for i in range(count - stride)])
-    for bit, earlier in reversed(earlier_maps):
-        upper = (index & bit) != 0
-        after = compose(earlier, state)
-        got = swap(jnp.where(upper, state, after), bit, count)
-        mine = jnp.where(upper, after, state)
-        state = jnp.concatenate(
-            [jnp.where(upper, got, mine), jnp.where(upper, mine, got)], 0
-        )
-    return state
 
 
 def per_device(
@@ -267,40 +306,115 @@
 ):
     heads, tokens, dim = queries.shape
     blocks = tokens // HALF
+    half = heads // 2
     rim = conv_query.shape[1] - 1
     count = lax.axis_size("seq")
-    tails = jnp.concatenate(
-        [x[:, tokens - rim :] for x in (queries, key_pairs, value_pairs)], 2
+    index = lax.axis_index("seq")
+
+    def flag(bit):
+        return ((index & bit) != 0).astype(jnp.int32).reshape(1)
+
+    last = [
+        pl.BlockSpec((heads, 16, x.shape[2]), lambda i: (0, tokens // 16 - 1, 0))
+        for x in (queries, key_pairs, value_pairs)
+    ]
+    tails = pl.pallas_call(
+        tails_kernel,
+        grid=(1,),
+        in_specs=last,
+        out_specs=pl.BlockSpec((heads, rim, 5 * dim), lambda i: (0, 0, 0)),
+        out_shape=shape((heads, rim, 5 * dim), bf16),
+    )(queries, key_pairs, value_pairs)
+    halo = lax.ppermute(tails, "seq", [(i, i + 1) for i in range(count - 1)])
+
+    upper = flag(1)
+    keep_first = upper * half
+    send_first = half - keep_first
+    rows = pltpu.VMEM((tokens + 8, dim), f32)
+    wide = shape((half, blocks, BLOCK, 2 * dim), bf16)
+    total_shape = shape((half, dim, 2 * dim), f32)
+    state_shape = shape((half, dim, dim), f32)
+
+    def maps(first):
+        outs = [wide] * 5 + [total_shape]
+        ins = (key_pairs, value_pairs, halo)
+        return call(
+            maps_kernel,
+            half,
+            first,
+            [(a, by_head(a)) for a in ins]
+            + [(write_rates, whole(write_rates))]
+            + [(a, by_head(a)) for a in (conv_key, conv_value)],
+            [(a, by_slot(a)) for a in outs],
+            [rows] * 4
+            + [
+                pltpu.VMEM((blocks, BLOCK, 4 * dim), bf16),
+                pltpu.VMEM((blocks, BLOCK, BLOCK), f32),
+                pltpu.VMEM((blocks, BLOCK, 2 * BLOCK), bf16),
+                pltpu.VMEM((blocks * GROUP, BLOCK), f32),
+                pltpu.VMEM((blocks * GROUP, BLOCK), f32),
+                pltpu.VMEM((blocks, BLOCK), f32),
+            ],
+        )
+
+    out_arrays = (shape((heads, tokens, 2 * dim), bf16), shape((heads, tokens, dim), f32))
+    any_spec = pl.BlockSpec(memory_space=pl.ANY)
+
+    def reads(first, slot, saved, before):
+        args = [(a, by_head(a)) for a in (queries, halo, conv_query)]
+        args += [(a, by_slot(a, slot)) for a in saved]
+        n = len(args) + 1
+        args += [(a, any_spec) for a in before]
+        aliases = {n + i: i for i in range(len(before))}
+        return call(
+            reads_kernel, 1, first + slot, args, [(a, by_head(a)) for a in out_arrays], [rows], aliases
+        )
+
+    *sent_saved, sent_total = maps(send_first)
+    got = swap(sent_total, 1, count)
+    *kept_saved, kept_total = maps(keep_first)
+    work = [(send_first, i, sent_saved) for i in range(half)]
+    work += [(keep_first, i, kept_saved) for i in range(half)]
+    read = ()
+
+    def beside(x, got, pieces):
+        nonlocal read
+        for _ in range(min(pieces, len(work))):
+            first, slot, saved = work.pop(0)
+            saved, _ = lax.optimization_barrier((saved, x))
+            read = reads(first, slot, saved, read)
+        if pieces:
+            got, read = lax.optimization_barrier((got, tuple(read)))
+        return got
+
+    current, earlier = small(pair_kernel, upper, (kept_total, got), [total_shape] * 2)
+    before = jnp.broadcast_to(
+        jnp.concatenate([jnp.eye(dim, dtype=f32), jnp.zeros((dim, dim), f32)], 1),
+        (half, dim, 2 * dim),
     )
-    halo = lax.ppermute(tails, "seq", [(i, i + 1) for i in range(count - 1)])
-    rates = write_rates.reshape(heads, 1, 2 * tokens)
-    wide = (heads, blocks, BLOCK, 2 * dim)
-    rows = pltpu.VMEM((tokens + 8, dim), f32)
-    kb, w, u, p, s, total = call(
-        maps_kernel,
-        (key_pairs, value_pairs, halo, rates, conv_key, conv_value),
-        [(wide, bf16)] * 5 + [((heads, dim, 2 * dim), f32)],
-        [rows] * 4
-        + [
-            pltpu.VMEM((blocks, BLOCK, 4 * dim), bf16),
-            pltpu.VMEM((blocks, BLOCK, BLOCK), f32),
-            pltpu.VMEM((blocks, BLOCK, 2 * BLOCK), bf16),
-            pltpu.VMEM((blocks * GROUP, BLOCK), f32),
-            pltpu.VMEM((blocks * GROUP, BLOCK), f32),
-            pltpu.VMEM((blocks, BLOCK), f32),
-        ],
-    )
-    pulled, local = call(
-        reads_kernel,
-        (queries, halo, conv_query, kb, w, u, p, s),
-        [((heads, tokens, 2 * dim), bf16), ((heads, tokens, dim), f32)],
-        [rows],
-    )
-    state = start_state(total)
+    bit = 2
+    while bit < count // 2:
+        got = beside(current, swap(current, bit, count), 1 if bit == 2 else 2)
+        final = 2 * bit >= count // 2
+        current, before = small(
+            join_kernel,
+            flag(bit),
+            (current, got, before),
+            [state_shape if final else total_shape, total_shape],
+        )
+        bit *= 2
+    got = lax.ppermute(current, "seq", [(i, i + bit) for i in range(count - bit)])
+    got = beside(current, got, len(work))
+    mine, other = small(down_kernel, upper, (before, got, earlier), [state_shape] * 2)
+    other = swap(other, 1, count)
+    pulled, local = read
     return call(
         out_kernel,
-        (pulled, local, state, out_gain.reshape(heads, 1, dim)),
-        [((heads, tokens, dim), f32)],
+        heads,
+        upper,
+        [(pulled, by_slot(pulled)), (local, by_slot(local))]
+        + [(a, whole(a)) for a in (mine, other, out_gain)],
+        [(out_arrays[1], by_slot(out_arrays[1]))],
     )[0]
 
 

time: 88 us -> 83.5 us (0.949)
  Pallas kernels: 39.7 us -> 59.5 us
  waiting for transfers between devices: 15.5 us -> 4.67 us
  starting transfers between devices: 22.7 us -> 14.5 us
  other arithmetic: 2.97 us -> 0.03 us
  matrix products: 1.63 us -> 0 us
    pallas_call x3 -> x12, Pallas kernels: 39.7 us -> 59.5 us  [the longest x7 49.6 us: call(): pl.pallas_call(kernel, grid_spec=pltpu.PrefetchScalarGridSpec(num_scalar_...]
    ppermute x3 -> x1, starting transfers between devices: 14.7 us -> 4.52 us  [per_device(): lax.ppermute(current, 'seq', [(i, i + bit) for i in range(count - bit)])]
    ppermute x3 -> x1, waiting for transfers between devices: 6.86 us -> 0.01 us  [per_device(): lax.ppermute(current, 'seq', [(i, i + bit) for i in range(count - bit)])]
    ppermute x4, waiting for transfers between devices: 8.6 us -> 3.64 us  [swap(): return lax.ppermute(x, 'seq', [(i, i ^ bit) for i in range(count)])]
    unnamed x2 -> x12, local copies, waits for them, and re-layouts: 0.61 us -> 3.36 us
    select_n x6 -> x0, other arithmetic: 2.23 us -> none  [the longest x2 1.11 us: start_state(): later = jnp.where(upper, mine, got)]
    slice x4 -> x0, local copies, waits for them, and re-layouts: 2.16 us -> none  [the longest x3 2.15 us: per_device(): x[:, tokens - rim:]]
    ppermute x4, starting transfers between devices: 5.62 us -> 7.66 us  [swap(): return lax.ppermute(x, 'seq', [(i, i ^ bit) for i in range(count)])]
  transfers between devices with their start and end apart: 8 -> 6, of which waited for: 6 -> 3; matrix products, arithmetic and copies ran while one was open for 2% -> 0% of each run, Pallas kernels for 15% -> 39%
where the time goes in v2:
time: 83.5 us; the launch traced here: 83 us
  Pallas kernels  59.5 us (71%)
  starting transfers between devices  14.5 us (17%)
  waiting for transfers between devices  4.67 us (6%)
  local copies, waits for them, and re-layouts  4.15 us (5%)
    pallas_call x7, Pallas kernels, call(): pl.pallas_call(kernel, grid_spec=pltpu.PrefetchScalarGridSpec(num_scalar_...  49.6 us
    pallas_call x4, Pallas kernels, small(): pl.pallas_call(kernel, in_specs=[smem] + [vmem] * len(args), out_specs=[v...  8.53 us
    ppermute x4, starting transfers between devices, swap(): return lax.ppermute(x, 'seq', [(i, i ^ bit) for i in range(count)])  7.66 us
    ppermute x1, starting transfers between devices, per_device(): lax.ppermute(current, 'seq', [(i, i + bit) for i in range(count - bit)])  4.52 us
    ppermute x4, waiting for transfers between devices, swap(): return lax.ppermute(x, 'seq', [(i, i ^ bit) for i in range(count)])  3.64 us
    unnamed x12, local copies, waits for them, and re-layouts  3.36 us
    ppermute x1, starting transfers between devices, per_device(): halo = lax.ppermute(tails, 'seq', [(i, i + 1) for i in range(count - 1)])  2.35 us
  transfers between devices with their start and end apart: 6, of which 3 were waited for; matrix products, arithmetic and copies ran while one was open for 0% of the time, Pallas kernels for 39%

profile of v2, /device:TPU:0, one launch (start us, length us, event | category | flops | bytes accessed | tf_op | source)
XLA Modules:
  0.0 83.0 jit_solution(8734911205356478281)
XLA Ops:
  0.0 1.4 %shard_map.82 = bf16[4,3,640]{2,1,0:T(4,128)(2,1)} custom-call(bf16[4,512,128]{2,1,0:T(8,128)(2,1)} %query_ref.9, bf16[4,512,256]{2,1,0:T(8,128)(2,1)} %key_ref.5, bf16[4,512,256]{2,1,0:T(8,128)(2,1)} %value_ref.5), custom_call_target="tpu_custom_call" | custom-call | tf_op jit(solution)/shard_map/pallas_call | solution.py:321
  1.4 2.3 %collective-permute-start = (bf16[4,3,640]{2,1,0:T(4,128)(2,1)}, bf16[4,3,640]{2,1,0:T(4,128)(2,1)S(1)}, u32[]{:S(2)}, u32[]{:S(2)}) collective-permute-start(bf16[4,3,640]{2,1,0:T(4,128)(2,1)} %shard_map.82), channel_id=1, source_target_pairs={{0,1},{1,2},{2,3},{3,4},{4,5},{5,6},{6,7},{7,8},{8,9},{9,10},{10,1... | collective-permute-start | bytes 46088 | tf_op jit(solution)/shard_map/ppermute | solution.py:328
  3.8 1.0 %collective-permute-done.halo_ref = bf16[4,3,640]{2,1,0:T(4,128)(2,1)S(1)} collective-permute-done((bf16[4,3,640]{2,1,0:T(4,128)(2,1)}, bf16[4,3,640]{2,1,0:T(4,128)(2,1)S(1)}, u32[]{:S(2)}, u32[]{:S(2)}) %collective-permute-start) | collective-permute-done | bytes 15392 | tf_op jit(solution)/shard_map/ppermute | solution.py:328
  5.4 12.6 %shard_map.84 = (bf16[2,8,128,256]{3,2,1,0:T(8,128)(2,1)}, bf16[2,8,128,256]{3,2,1,0:T(8,128)(2,1)}, bf16[2,8,128,256]{3,2,1,0:T(8,128)(2,1)}, bf16[2,8,128,256]...) custom-call(s32[1]{0:T(128)S(6)} %sub.3.first_ref, bf16[4,512,256]{2,1,0:T(8,128)(2,1)} %key_ref.5, ...), custom_call_target="tpu_custom_call" | custom-call | tf_op jit(solution)/shard_map/pallas_call | solution.py:274
  18.0 2.7 %collective-permute-start.1 = (f32[2,128,256]{2,1,0:T(8,128)}, f32[2,128,256]{2,1,0:T(8,128)S(1)}, u32[]{:S(2)}, u32[]{:S(2)}) collective-permute-start(f32[2,128,256]{2,1,0:T(8,128)} %get-tuple-element.63), channel_id=1, source_target_pairs={{0,1},{1,0},{2,3},{3,2},{4,5},{5,4},{6,7},{7,6},{8,9},{9,8},{10,11... | collective-permute-start | bytes 786440 | tf_op jit(solution)/shard_map/ppermute | solution.py:301
  20.7 12.6 %shard_map.83 = (bf16[2,8,128,256]{3,2,1,0:T(8,128)(2,1)}, bf16[2,8,128,256]{3,2,1,0:T(8,128)(2,1)}, bf16[2,8,128,256]{3,2,1,0:T(8,128)(2,1)}, bf16[2,8,128,256]...) custom-call(s32[1]{0:T(128)} %bitcast.3.first_ref, bf16[4,512,256]{2,1,0:T(8,128)(2,1)} %key_ref.5, ...), custom_call_target="tpu_custom_call" | custom-call | tf_op jit(solution)/shard_map/pallas_call | solution.py:274
  33.4 0.7 copy-done.1
  34.0 2.0 %shard_map.85 = (f32[2,128,256]{2,1,0:T(8,128)}, f32[2,128,256]{2,1,0:T(8,128)}) custom-call(s32[1]{0:T(128)} %bitcast.upper_ref.first_ref, f32[2,128,256]{2,1,0:T(8,128)} %get-tuple-element.62.mine_ref, f32[2,128,256]{2,1,0:T(8,128)} %copy-done.1), custom_call_target="tpu_custom_call" | custom-call | tf_op jit(solution)/shard_map/pallas_call | solution.py:292
  36.1 2.2 %collective-permute-start.2 = (f32[2,128,256]{2,1,0:T(8,128)}, f32[2,128,256]{2,1,0:T(8,128)S(1)}, u32[]{:S(2)}, u32[]{:S(2)}) collective-permute-start(f32[2,128,256]{2,1,0:T(8,128)} %get-tuple-element.64.mine_ref), channel_id=1, source_target_pairs={{0,2},{1,3},{2,0},{3,1},{4,6},{5,7},{6,4},{7,5},{8,10},{9,11},{10,... | collective-permute-start | bytes 786440 | tf_op jit(solution)/shard_map/ppermute | solution.py:301
  38.3 5.0 %shard_map.86 = (bf16[4,512,256]{2,1,0:T(8,128)(2,1)}, f32[4,512,128]{2,1,0:T(8,128)}) custom-call(s32[1]{0:T(128)S(6)} %sub.3.first_ref, bf16[4,512,128]{2,1,0:T(8,128)(2,1)} %query_ref.9, bf16[4,3,640]{2,1,0:T(4,128)(2,1)} %copy-done, f32[4,4,128]{2,1,0:T(4,128)} %cq_ref.7, bf16[2,8,128,256]{3,2,1,0:T(8,128)(2,1)} %get-tuple-element.89.kb_ref, ...), custom_call_target="tpu_custom_call" | custom-call | tf_op jit(solution)/shard_map/pallas_call | solution.py:274
  43.3 2.1 %collective-permute-done.2.got_ref = f32[2,128,256]{2,1,0:T(8,128)S(1)} collective-permute-done((f32[2,128,256]{2,1,0:T(8,128)}, f32[2,128,256]{2,1,0:T(8,128)S(1)}, u32[]{:S(2)}, u32[]{:S(2)}) %collective-permute-start.2) | collective-permute-done | bytes 262176 | tf_op jit(solution)/shard_map/ppermute | solution.py:301
  45.4 0.8 broadcast_in_dim.4.before_ref
  46.3 2.2 %shard_map.87 = (f32[2,128,256]{2,1,0:T(8,128)}, f32[2,128,256]{2,1,0:T(8,128)}) custom-call(s32[1]{0:T(128)} %bitcast.2.upper_ref, f32[2,128,256]{2,1,0:T(8,128)} %get-tuple-element.64.mine_ref, f32[2,128,256]{2,1,0:T(8,128)} %copy-done.3, f32[2,128,256]{2,1,0:T(8,128)} %broadcast_in_dim.4.before_ref), custom_call_target="tpu_custom_call" | custom-call | tf_op jit(solution)/shard_map/pallas_call | solution.py:292
  48.5 2.7 %collective-permute-start.3 = (f32[2,128,256]{2,1,0:T(8,128)}, f32[2,128,256]{2,1,0:T(8,128)S(1)}, u32[]{:S(2)}, u32[]{:S(2)}) collective-permute-start(f32[2,128,256]{2,1,0:T(8,128)} %get-tuple-element.78.mine_ref), channel_id=1, source_target_pairs={{0,4},{1,5},{2,6},{3,7},{4,0},{5,1},{6,2},{7,3},{8,12},{9,13},{10,... | collective-permute-start | bytes 786440 | tf_op jit(solution)/shard_map/ppermute | solution.py:301
  51.2 5.0 %shard_map.88 = (bf16[4,512,256]{2,1,0:T(8,128)(2,1)}, f32[4,512,128]{2,1,0:T(8,128)}) custom-call(s32[1]{0:T(128)S(6)} %add.7.first_ref, bf16[4,512,128]{2,1,0:T(8,128)(2,1)} %query_ref.9, bf16[4,3,640]{2,1,0:T(4,128)(2,1)} %copy-done, f32[4,4,128]{2,1,0:T(4,128)} %cq_ref.7, ...), custom_call_target="tpu_custom_call", output_to_operand_aliasing={{0}: (9, {}), {1}: (10, {})} | custom-call | tf_op jit(solution)/shard_map/pallas_call | solution.py:274
  56.2 5.0 %shard_map.89 = (bf16[4,512,256]{2,1,0:T(8,128)(2,1)}, f32[4,512,128]{2,1,0:T(8,128)}) custom-call(s32[1]{0:T(128)} %bitcast.3.first_ref, bf16[4,512,128]{2,1,0:T(8,128)(2,1)} %query_ref.9, bf16[4,3,640]{2,1,0:T(4,128)(2,1)} %copy-done, f32[4,4,128]{2,1,0:T(4,128)} %cq_ref.7, ...), custom_call_target="tpu_custom_call", output_to_operand_aliasing={{0}: (9, {}), {1}: (10, {})} | custom-call | tf_op jit(solution)/shard_map/pallas_call | solution.py:274
  61.3 0.7 copy-done.2
  62.0 2.1 %shard_map.90 = (f32[2,128,128]{2,1,0:T(8,128)}, f32[2,128,256]{2,1,0:T(8,128)}) custom-call(s32[1]{0:T(128)} %bitcast.1.upper_ref, f32[2,128,256]{2,1,0:T(8,128)} %get-tuple-element.78.mine_ref, f32[2,128,256]{2,1,0:T(8,128)} %copy-done.2, f32[2,128,256]{2,1,0:T(8,128)} %get-tuple-element.101.before_ref), custom_call_target="tpu_custom_call" | custom-call | tf_op jit(solution)/shard_map/pallas_call | solution.py:292
  64.1 4.5 %collective-permute-start.4 = (f32[2,128,128]{2,1,0:T(8,128)}, f32[2,128,128]{2,1,0:T(8,128)S(1)}, u32[]{:S(2)}, u32[]{:S(2)}) collective-permute-start(f32[2,128,128]{2,1,0:T(8,128)} %get-tuple-element.102), channel_id=1, source_target_pairs={{0,8},{1,9},{2,10},{3,11},{4,12},{5,13},{6,14},{7,15},{16,24},{17,... | collective-permute-start | bytes 393224 | tf_op jit(solution)/shard_map/ppermute | solution.py:406
  68.6 5.1 %shard_map.91 = (bf16[4,512,256]{2,1,0:T(8,128)(2,1)}, f32[4,512,128]{2,1,0:T(8,128)}) custom-call(s32[1]{0:T(128)S(6)} %add.8.first_ref, bf16[4,512,128]{2,1,0:T(8,128)(2,1)} %query_ref.9, bf16[4,3,640]{2,1,0:T(4,128)(2,1)} %copy-done, f32[4,4,128]{2,1,0:T(4,128)} %cq_ref.7, ...), custom_call_target="tpu_custom_call", output_to_operand_aliasing={{0}: (9, {}), {1}: (10, {})} | custom-call | tf_op jit(solution)/shard_map/pallas_call | solution.py:274
  73.7 0.6 copy-done.5
  74.3 2.2 %shard_map.92 = (f32[2,128,128]{2,1,0:T(8,128)}, f32[2,128,128]{2,1,0:T(8,128)}) custom-call(s32[1]{0:T(128)} %bitcast.upper_ref.first_ref, f32[2,128,256]{2,1,0:T(8,128)} %get-tuple-element.114.before_ref, f32[2,128,128]{2,1,0:T(8,128)} %copy-done.5, f32[2,128,256]{2,1,0:T(8,128)} %get-tuple-element.116.earlier_ref), custom_call_target="tpu_custom_call" | custom-call | tf_op jit(solution)/shard_map/pallas_call | solution.py:292
  76.5 1.6 %collective-permute-done.5.sent_ref = f32[2,128,128]{2,1,0:T(8,128)S(1)} collective-permute-done((f32[2,128,128]{2,1,0:T(8,128)}, f32[2,128,128]{2,1,0:T(8,128)S(1)}, u32[]{:S(2)}, u32[]{:S(2)}) %collective-permute-start.5) | collective-permute-done | bytes 131104 | tf_op jit(solution)/shard_map/ppermute | solution.py:301
  78.7 4.2 %shard_map.93 = f32[4,512,128]{2,1,0:T(8,128)} custom-call(s32[1]{0:T(128)} %bitcast.upper_ref.first_ref, bf16[4,512,256]{2,1,0:T(8,128)(2,1)} %get-tuple-element.112.pulled_ref, f32[4,512,128]{2,1,0:T(8,128)} %get-tuple-element.113.local_ref, f32[2,128,128]{2,1,0:T(8,128)} %get-tuple-element.117.kept_ref, f32[2,128,128]{2,1,0:T(8,128)} %copy-done.4, ...), custom_call_target="tpu_custom_call" | custom-call | tf_op jit(solution)/shard_map/pallas_call | solution.py:274
  (15 shorter events, 1.3 us)
Async XLA Ops:
  1.4 3.4 %collective-permute-start = (bf16[4,3,640]{2,1,0:T(4,128)(2,1)}, bf16[4,3,640]{2,1,0:T(4,128)(2,1)S(1)}, u32[]{:S(2)}, u32[]{:S(2)}) collective-permute-start(bf16[4,3,640]{2,1,0:T(4,128)(2,1)} %shard_map.82), channel_id=1, source_target_pairs={{0,1},{1,2},{2,3},{3,4},{4,5},{5,6},{6,7},{7,8},{8,9},{9,10},{10,1... | collective-permute-start | bytes 46088 | tf_op jit(solution)/shard_map/ppermute | solution.py:328
  4.8 0.6 copy-start
  18.0 15.3 %collective-permute-start.1 = (f32[2,128,256]{2,1,0:T(8,128)}, f32[2,128,256]{2,1,0:T(8,128)S(1)}, u32[]{:S(2)}, u32[]{:S(2)}) collective-permute-start(f32[2,128,256]{2,1,0:T(8,128)} %get-tuple-element.63), channel_id=1, source_target_pairs={{0,1},{1,0},{2,3},{3,2},{4,5},{5,4},{6,7},{7,6},{8,9},{9,8},{10,11... | collective-permute-start | bytes 786440 | tf_op jit(solution)/shard_map/ppermute | solution.py:301
  33.3 0.7 copy-start.1
  36.1 9.4 %collective-permute-start.2 = (f32[2,128,256]{2,1,0:T(8,128)}, f32[2,128,256]{2,1,0:T(8,128)S(1)}, u32[]{:S(2)}, u32[]{:S(2)}) collective-permute-start(f32[2,128,256]{2,1,0:T(8,128)} %get-tuple-element.64.mine_ref), channel_id=1, source_target_pairs={{0,2},{1,3},{2,0},{3,1},{4,6},{5,7},{6,4},{7,5},{8,10},{9,11},{10,... | collective-permute-start | bytes 786440 | tf_op jit(solution)/shard_map/ppermute | solution.py:301
  45.4 0.8 %copy-start.3 = (f32[2,128,256]{2,1,0:T(8,128)}, f32[2,128,256]{2,1,0:T(8,128)S(1)}, u32[]{:S(2)}) copy-start(f32[2,128,256]{2,1,0:T(8,128)S(1)} %collective-permute-done.2.got_ref) | copy-start | bytes 786436
  48.5 12.8 %collective-permute-start.3 = (f32[2,128,256]{2,1,0:T(8,128)}, f32[2,128,256]{2,1,0:T(8,128)S(1)}, u32[]{:S(2)}, u32[]{:S(2)}) collective-permute-start(f32[2,128,256]{2,1,0:T(8,128)} %get-tuple-element.78.mine_ref), channel_id=1, source_target_pairs={{0,4},{1,5},{2,6},{3,7},{4,0},{5,1},{6,2},{7,3},{8,12},{9,13},{10,... | collective-permute-start | bytes 786440 | tf_op jit(solution)/shard_map/ppermute | solution.py:301
  61.3 0.7 copy-start.2
  64.1 9.6 %collective-permute-start.4 = (f32[2,128,128]{2,1,0:T(8,128)}, f32[2,128,128]{2,1,0:T(8,128)S(1)}, u32[]{:S(2)}, u32[]{:S(2)}) collective-permute-start(f32[2,128,128]{2,1,0:T(8,128)} %get-tuple-element.102), channel_id=1, source_target_pairs={{0,8},{1,9},{2,10},{3,11},{4,12},{5,13},{6,14},{7,15},{16,24},{17,... | collective-permute-start | bytes 393224 | tf_op jit(solution)/shard_map/ppermute | solution.py:406
  73.7 0.7 copy-start.5
  76.5 1.6 %collective-permute-start.5 = (f32[2,128,128]{2,1,0:T(8,128)}, f32[2,128,128]{2,1,0:T(8,128)S(1)}, u32[]{:S(2)}, u32[]{:S(2)}) collective-permute-start(f32[2,128,128]{2,1,0:T(8,128)} %get-tuple-element.118), channel_id=1, source_target_pairs={{0,1},{1,0},{2,3},{3,2},{4,5},{5,4},{6,7},{7,6},{8,9},{9,8},{10,11... | collective-permute-start | bytes 393224 | tf_op jit(solution)/shard_map/ppermute | solution.py:301
  78.1 0.7 copy-start.4

commit v3 on v2

v3 whole, which is shorter than its diff:
```python
import functools

import jax
import jax.numpy as jnp
from jax import lax
from jax.experimental import pallas as pl
from jax.experimental.pallas import tpu as pltpu
from jax.sharding import PartitionSpec as P

BLOCK = 128
GROUP = 16
HALF = BLOCK // 2
LIMIT = 12 << 20

f32 = jnp.float32
bf16 = jnp.bfloat16


def split(x):
    high = x.astype(bf16)
    low = (x - high.astype(f32)).astype(bf16)
    return jnp.concatenate([high, low], 1)


def mm(a, b):
    n = b.shape[1] // 2
    p = jnp.dot(a, jnp.concatenate([b, b], 0), preferred_element_type=f32)
    return p[:, :n] + p[:, n:]


def pick_row(x, r):
    row = lax.broadcasted_iota(jnp.int32, x.shape, 0)
    return jnp.sum(jnp.where(row == r, x, 0.0), 0, keepdims=True)


def silu(x):
    return x / (1.0 + jnp.exp(-x))


def step_time(r):
    return (r // GROUP) * GROUP + 2 * (r % 8) + (r // 8) % 2


def interleave(a, b):
    parts = []
    for g in range(0, a.shape[0], 8):
        parts += [a[g : g + 8], b[g : g + 8]]
    return jnp.concatenate(parts, 0)


def conv_taps(ref, weights, start, count):
    taps = weights.shape[0]
    total = weights[0:1] * ref[pl.ds(start + 9 - taps, count), :]
    for s in range(1, taps):
        total = total + weights[s : s + 1] * ref[pl.ds(start + 9 - taps + s, count), :]
    return silu(total)


def fill_rows(ref, halo, rows):
    rim = halo.shape[0]
    ref[8 - rim : 8, :] = halo.astype(f32)
    ref[8:, :] = rows.astype(f32)


def first_head(index_ref, kept, half):
    upper = index_ref[0] & 1
    return (upper if kept else 1 - upper) * half


def maps_kernel(
    kept, index_ref, key_ref, value_ref, halo_ref, rate_ref, ck_ref, cv_ref,
    kb_ref, w_ref, u_ref, p_ref, s_ref, total_ref,
    k0, k1, v0, v1, kv, nref, dref, cref, xref, brow,
):
    first = first_head(index_ref, kept, total_ref.shape[0])

    def one(slot, carry):
        one_head_maps(
            slot, first + slot, key_ref, value_ref, halo_ref, rate_ref, ck_ref, cv_ref,
            kb_ref, w_ref, u_ref, p_ref, s_ref, total_ref,
            k0, k1, v0, v1, kv, nref, dref, cref, xref, brow,
        )
        return carry

    lax.fori_loop(0, total_ref.shape[0], one, 0)


def one_head_maps(
    slot, head, key_ref, value_ref, halo_ref, rate_ref, ck_ref, cv_ref,
    kb_ref, w_ref, u_ref, p_ref, s_ref, total_ref,
    k0, k1, v0, v1, kv, nref, dref, cref, xref, brow,
):
    dim = k0.shape[1]
    tokens = key_ref.shape[1]
    blocks = tokens // HALF
    halo = halo_ref[head]
    fill_rows(k0, halo[:, dim : 2 * dim], key_ref[head, :, :dim])
    fill_rows(k1, halo[:, 2 * dim : 3 * dim], key_ref[head, :, dim:])
    fill_rows(v0, halo[:, 3 * dim : 4 * dim], value_ref[head, :, :dim])
    fill_rows(v1, halo[:, 4 * dim :], value_ref[head, :, dim:])
    ck = ck_ref[head]
    cv = cv_ref[head]

    row = lax.broadcasted_iota(jnp.int32, (BLOCK, BLOCK), 0)
    col = lax.broadcasted_iota(jnp.int32, (BLOCK, BLOCK), 1)
    for n in range(blocks):
        brow[n : n + 1, :] = pick_row(rate_ref[:, n * BLOCK : (n + 1) * BLOCK], head)
    order = (row == step_time(col)).astype(f32)
    rates = jnp.dot(brow[...], order, precision=lax.Precision.HIGHEST, preferred_element_type=f32)

    strict = step_time(col) < step_time(row)
    lane = lax.broadcasted_iota(jnp.int32, (GROUP, BLOCK), 1)
    eye = (row == col).astype(f32)

    for n in range(blocks):
        t0 = n * HALF
        ka = conv_taps(k0, ck[:, :dim], t0, HALF)
        kb = conv_taps(k1, ck[:, dim:], t0, HALF)
        keys = interleave(ka, kb)
        keys = keys * lax.rsqrt(jnp.sum(keys * keys, 1, keepdims=True) + 1e-06)
        va = conv_taps(v0, cv[:, :dim], t0, HALF)
        vb = conv_taps(v1, cv[:, dim:], t0, HALF)
        ks = split(keys)
        kv[n, :, : 2 * dim] = ks
        kv[n, :, 2 * dim :] = split(interleave(va, vb))
        kbs = split(keys.T * rates[n : n + 1, :])
        kb_ref[slot, n] = kbs
        lower = jnp.where(strict, mm(ks, kbs), 0.0)
        nref[n] = lower
        diag = jnp.zeros((GROUP, BLOCK), f32)
        for g in range(BLOCK // GROUP):
            diag = jnp.where(lane // GROUP == g, lower[g * GROUP : (g + 1) * GROUP], diag)
        cref[n * GROUP : (n + 1) * GROUP, :] = diag

    lane8 = lax.broadcasted_iota(jnp.int32, (blocks, BLOCK), 1)
    times = [t // 2 + 8 * (t % 2) for t in range(GROUP)]
    coef = [cref[pl.ds(r, blocks, stride=GROUP), :] for r in range(GROUP)]
    sol = [(lane8 % GROUP == r).astype(f32) for r in range(GROUP)]
    for i, s in enumerate(times):
        pick = (lane8 // GROUP) * GROUP + s
        for r in times[i + 1 :]:
            sol[r] = sol[r] - jnp.take_along_axis(coef[r], pick, axis=1) * sol[s]
    for r in range(GROUP):
        xref[pl.ds(r, blocks, stride=GROUP), :] = sol[r]
    for n in range(blocks):
        base = xref[n * GROUP : (n + 1) * GROUP, :]
        dref[n] = split(
            jnp.concatenate(
                [jnp.where(lane // GROUP == g, base, 0.0) for g in range(BLOCK // GROUP)], 0
            )
        )

    lane_h = lax.broadcasted_iota(jnp.int32, (HALF, BLOCK), 1)
    row_h = lax.broadcasted_iota(jnp.int32, (HALF, BLOCK), 0)
    size = GROUP
    while size < BLOCK:
        keep = lane_h // size == 2 * (row_h // size)
        starts = range(size, BLOCK, 2 * size)
        for n in range(blocks):
            inv = dref[n]
            low = jnp.concatenate([nref[n, a : a + size] for a in starts], 0)
            z = split(mm(split(jnp.where(keep, low, 0.0)), inv))
            twice = []
            for i in range(len(starts)):
                twice += [z[i * size : (i + 1) * size]] * 2
            odd = jnp.concatenate([inv[a : a + size] for a in starts], 0)
            new = mm(odd, jnp.concatenate(twice, 0))
            new = split(odd[:, :BLOCK].astype(f32) + odd[:, BLOCK:].astype(f32) - new)
            for i, a in enumerate(starts):
                dref[n, a : a + size] = new[i * size : (i + 1) * size]
        size *= 2

    before_map = split(eye)
    before_state = jnp.zeros((dim, 2 * dim), bf16)
    state = jnp.zeros((dim, dim), f32)
    for n in range(blocks):
        inv = dref[n]
        w = split(mm(inv, kv[n, :, : 2 * dim]))
        u = split(mm(inv, kv[n, :, 2 * dim :]))
        w_ref[slot, n] = w
        u_ref[slot, n] = u
        p_ref[slot, n] = before_map
        s_ref[slot, n] = before_state
        kbs = kb_ref[slot, n]
        move = split(eye - mm(kbs, w))
        written = mm(kbs, u)
        map_now = mm(move, before_map)
        state = mm(move, before_state) + written
        before_map = split(map_now)
        before_state = split(state)
        if n == blocks - 1:
            total_ref[slot, :, :dim] = map_now
            total_ref[slot, :, dim:] = state


def reads_kernel(
    kept, slot, index_ref, query_ref, halo_ref, cq_ref, kb_ref, w_ref, u_ref, p_ref, s_ref,
    pulled_ref, local_ref, q0,
):
    head = first_head(index_ref, kept, w_ref.shape[0]) + slot
    dim = q0.shape[1]
    tokens = query_ref.shape[1]
    blocks = tokens // HALF
    fill_rows(q0, halo_ref[head][:, :dim], query_ref[head])
    cq = cq_ref[head]
    row = lax.broadcasted_iota(jnp.int32, (HALF, BLOCK), 0)
    col = lax.broadcasted_iota(jnp.int32, (HALF, BLOCK), 1)
    causal = step_time(col) <= 2 * row + 1
    for n in range(blocks):
        rows = slice(n * HALF, (n + 1) * HALF)
        query = conv_taps(q0, cq, n * HALF, HALF)
        scores = split(jnp.where(causal, mm(split(query), kb_ref[slot, n]), 0.0))
        pulled = query - mm(scores, w_ref[slot, n])
        local = mm(scores, u_ref[slot, n])
        pulled = split(pulled)
        local_ref[rows] = local + mm(pulled, s_ref[slot, n])
        pulled_ref[rows] = split(mm(pulled, p_ref[slot, n]))


def out_kernel(index_ref, mine_ref, other_ref, gain_ref, *rest):
    out_ref = rest[-1]
    half = mine_ref.shape[0]
    for i in range(2 * half):

        @pl.when(pl.program_id(0) == i)
        def _():
            kept = i < half
            slot = i % half
            h = first_head(index_ref, kept, half) + slot
            state = mine_ref[slot] if kept else other_ref[slot]
            raw = mm(rest[2 * i][...], split(state)) + rest[2 * i + 1][...]
            mean = jnp.mean(raw * raw, 1, keepdims=True)
            out_ref[0] = raw * lax.rsqrt(mean + 1e-06) * pick_row(gain_ref[...], h)


def then(later, earlier):
    dim = later.shape[0]
    prod = mm(split(later[:, :dim]), split(earlier))
    wide = prod.shape[1]
    if wide == dim:
        return prod + later[:, dim:]
    return jnp.concatenate([prod[:, :dim], prod[:, dim:] + later[:, dim:]], 1)


def pair_kernel(index_ref, mine_ref, got_ref, total_ref, earlier_ref):
    upper = (index_ref[0] & 1) != 0
    for h in range(mine_ref.shape[0]):
        mine = mine_ref[h]
        got = got_ref[h]
        earlier = jnp.where(upper, got, mine)
        earlier_ref[h] = earlier
        total_ref[h] = then(jnp.where(upper, mine, got), earlier)


def join_kernel(bit, index_ref, mine_ref, got_ref, *rest):
    *before_ref, total_ref, after_ref = rest
    upper = (index_ref[0] & bit) != 0
    dim = mine_ref.shape[1]
    row = lax.broadcasted_iota(jnp.int32, (dim, 2 * dim), 0)
    col = lax.broadcasted_iota(jnp.int32, (dim, 2 * dim), 1)
    for h in range(mine_ref.shape[0]):
        mine = mine_ref[h]
        got = got_ref[h]
        earlier = jnp.where(upper, got, mine)
        if total_ref.shape[2] == dim:
            earlier = earlier[:, dim:]
        total_ref[h] = then(jnp.where(upper, mine, got), earlier)
        if before_ref:
            before = before_ref[0][h]
            after_ref[h] = jnp.where(upper, then(before, got), before)
        else:
            after_ref[h] = jnp.where(upper, got, (row == col).astype(f32))


def down_kernel(index_ref, before_ref, got_ref, earlier_ref, mine_ref, other_ref):
    upper = (index_ref[0] & 1) != 0
    for h in range(before_ref.shape[0]):
        state = then(before_ref[h], got_ref[h])
        after = then(earlier_ref[h], state)
        mine_ref[h] = jnp.where(upper, after, state)
        other_ref[h] = jnp.where(upper, state, after)


def tails_kernel(index_ref, query_ref, key_ref, value_ref, out_ref):
    rim = out_ref.shape[1]
    at = 0
    for ref in (query_ref, key_ref, value_ref):
        wide = ref.shape[2]
        out_ref[:, :, at : at + wide] = ref[:, ref.shape[1] - rim :, :]
        at += wide


def shape(dims, dtype):
    return jax.ShapeDtypeStruct(dims, dtype)


def resident(kernel, index, args, outs, scratch=(), limit=4 << 20):
    smem = pl.BlockSpec(memory_space=pltpu.SMEM)
    vmem = pl.BlockSpec(memory_space=pltpu.VMEM)
    return pl.pallas_call(
        kernel,
        in_specs=[smem] + [vmem] * len(args),
        out_specs=[vmem] * len(outs),
        out_shape=[pltpu.VMEM(o.shape, o.dtype) for o in outs],
        scratch_shapes=list(scratch),
        compiler_params=pltpu.CompilerParams(vmem_limit_bytes=limit),
    )(index, *[pltpu.with_memory_space_constraint(a, pltpu.VMEM) for a in args])


def swap(x, bit, count):
    return lax.ppermute(x, "seq", [(i, i ^ bit) for i in range(count)])


def per_device(
    queries, key_pairs, value_pairs, write_rates, conv_query, conv_key, conv_value, out_gain
):
    heads, tokens, dim = queries.shape
    blocks = tokens // HALF
    half = heads // 2
    rim = conv_query.shape[1] - 1
    count = lax.axis_size("seq")
    index = lax.axis_index("seq").reshape(1)

    parts = (queries, key_pairs, value_pairs)
    last = [
        pl.BlockSpec((heads, 16, x.shape[2]), lambda i, index_ref: (0, tokens // 16 - 1, 0))
        for x in parts
    ]
    tails = pl.pallas_call(
        tails_kernel,
        grid_spec=pltpu.PrefetchScalarGridSpec(
            num_scalar_prefetch=1,
            grid=(1,),
            in_specs=last,
            out_specs=pl.BlockSpec((heads, rim, 5 * dim), lambda i, index_ref: (0, 0, 0)),
        ),
        out_shape=shape((heads, rim, 5 * dim), bf16),
        compiler_params=pltpu.CompilerParams(vmem_limit_bytes=4 << 20),
    )(index, *[pltpu.with_memory_space_constraint(x, pltpu.HBM) for x in parts])
    halo = lax.ppermute(tails, "seq", [(i, i + 1) for i in range(count - 1)])

    rows = pltpu.VMEM((tokens + 8, dim), f32)
    wide = shape((half, blocks, BLOCK, 2 * dim), bf16)
    total_shape = shape((half, dim, 2 * dim), f32)
    state_shape = shape((half, dim, dim), f32)

    def maps(kept):
        return resident(
            functools.partial(maps_kernel, kept),
            index,
            (key_pairs, value_pairs, halo, write_rates, conv_key, conv_value),
            [wide] * 5 + [total_shape],
            [rows] * 4
            + [
                pltpu.VMEM((blocks, BLOCK, 4 * dim), bf16),
                pltpu.VMEM((blocks, BLOCK, BLOCK), f32),
                pltpu.VMEM((blocks, BLOCK, 2 * BLOCK), bf16),
                pltpu.VMEM((blocks * GROUP, BLOCK), f32),
                pltpu.VMEM((blocks * GROUP, BLOCK), f32),
                pltpu.VMEM((blocks, BLOCK), f32),
            ],
            LIMIT,
        )

    def reads(kept, slot, saved, after):
        at, _ = lax.optimization_barrier((index, after))
        return resident(
            functools.partial(reads_kernel, kept, slot),
            at,
            (queries, halo, conv_query, *saved),
            [shape((tokens, 2 * dim), bf16), shape((tokens, dim), f32)],
            [rows],
            LIMIT,
        )

    *sent_saved, sent_total = maps(False)
    got = swap(sent_total, 1, count)
    *kept_saved, kept_total = maps(True)
    work = [(False, i, sent_saved) for i in range(half)]
    work += [(True, i, kept_saved) for i in range(half)]
    read = {}

    def beside(x, got, pieces):
        for _ in range(min(pieces, len(work))):
            kept, slot, saved = work.pop(0)
            one = reads(kept, slot, saved, x)
            got, read[kept, slot] = lax.optimization_barrier((got, one))
        return got

    current, earlier = resident(pair_kernel, index, (kept_total, got), [total_shape] * 2)
    before = ()
    bit = 2
    while bit < count // 2:
        got = beside(current, swap(current, bit, count), 1 if bit == 2 else 2)
        final = 2 * bit >= count // 2
        current, before = resident(
            functools.partial(join_kernel, bit),
            index,
            (current, got) + ((before,) if bit > 2 else ()),
            [state_shape if final else total_shape, total_shape],
        )
        bit *= 2
    got = lax.ppermute(current, "seq", [(i, i + bit) for i in range(count - bit)])
    got = beside(current, got, len(work))
    mine, other = resident(down_kernel, index, (before, got, earlier), [state_shape] * 2)
    other = swap(other, 1, count)
    pieces = [a for kept in (True, False) for i in range(half) for a in read[kept, i]]
    vmem = pl.BlockSpec(memory_space=pltpu.VMEM)

    def out_block(i, index_ref):
        upper = index_ref[0] & 1
        side = jnp.where(i < half, upper, 1 - upper)
        return (side * half + i % half, 0, 0)

    args = [mine, other, out_gain, *pieces]
    return pl.pallas_call(
        out_kernel,
        grid_spec=pltpu.PrefetchScalarGridSpec(
            num_scalar_prefetch=1,
            grid=(heads,),
            in_specs=[vmem] * len(args),
            out_specs=pl.BlockSpec((1, tokens, dim), out_block),
        ),
        out_shape=shape((heads, tokens, dim), f32),
        compiler_params=pltpu.CompilerParams(vmem_limit_bytes=LIMIT),
    )(index, *[pltpu.with_memory_space_constraint(a, pltpu.VMEM) for a in args])


def solution(mesh):
    return jax.shard_map(
        per_device,
        mesh=mesh,
        in_specs=(
            P(None, ("grp", "seq"), None),
            P(None, ("grp", "seq"), None),
            P(None, ("grp", "seq"), None),
            P(None, ("grp", "seq")),
            P(),
            P(),
            P(),
            P(),
        ),
        out_specs=P(None, ("grp", "seq"), None),
        check_vma=False,
    )
```

time: 83.5 us -> 59.8 us (0.72)
  the two profiles are of different devices: /device:TPU:0 before, /device:TPU:25 now
where the time goes in v3:
time: 59.8 us; the launch traced here: 59.6 us
  Pallas kernels  35.2 us (59%)
  waiting for transfers between devices  14.8 us (25%)
  starting transfers between devices  9.15 us (15%)
    pallas_call x10, Pallas kernels, resident(): pl.pallas_call(kernel, in_specs=[smem] + [vmem] * len(args), out_specs=[v...  31.8 us
    ppermute x4, waiting for transfers between devices, swap(): return lax.ppermute(x, 'seq', [(i, i ^ bit) for i in range(count)])  7.6 us
    ppermute x1, waiting for transfers between devices, per_device(): lax.ppermute(current, 'seq', [(i, i + bit) for i in range(count - bit)])  6.29 us
    ppermute x4, starting transfers between devices, swap(): return lax.ppermute(x, 'seq', [(i, i ^ bit) for i in range(count)])  4.15 us
    ppermute x1, starting transfers between devices, per_device(): halo = lax.ppermute(tails, 'seq', [(i, i + 1) for i in range(count - 1)])  3.71 us
    pallas_call x1, Pallas kernels, per_device(): pl.pallas_call(out_kernel, grid_spec=pltpu.PrefetchScalarGridSpec(num_sca...  2.45 us
    ppermute x1, starting transfers between devices, per_device(): lax.ppermute(current, 'seq', [(i, i + bit) for i in range(count - bit)])  1.29 us
  transfers between devices with their start and end apart: 6, of which 5 were waited for; matrix products, arithmetic and copies ran while one was open for 0% of the time, Pallas kernels for 34%

profile of v3, /device:TPU:25, one launch (start us, length us, event | category | flops | bytes accessed | tf_op | source)
XLA Modules:
  0.0 59.6 jit_solution(16935561890933711963)
XLA Ops:
  0.0 1.0 %shard_map.82 = bf16[4,3,640]{2,1,0:T(4,128)(2,1)S(1)} custom-call(s32[1]{0:T(128)} %bitcast.index_ref, bf16[4,512,128]{2,1,0:T(8,128)(2,1)} %query_ref.9, bf16[4,512,256]{2,1,0:T(8,128)(2,1)} %key_ref.5, bf16[4,512,256]{2,1,0:T(8,128)(2,1)} %value_ref.5), custom_call_target="tpu_custom_call" | custom-call | tf_op jit(solution)/shard_map/pallas_call | solution.py:329
  1.0 3.7 %collective-permute-start = (bf16[4,3,640]{2,1,0:T(4,128)(2,1)S(1)}, bf16[4,3,640]{2,1,0:T(4,128)(2,1)S(1)}, u32[]{:S(2)}, u32[]{:S(2)}) collective-permute-start(bf16[4,3,640]{2,1,0:T(4,128)(2,1)S(1)} %shard_map.82), channel_id=1, source_target_pairs={{0,1},{1,2},{2,3},{3,4},{4,5},{5,6},{6,7},{7,8},{8,9},{9,10},{10,1... | collective-permute-start | bytes 46088 | tf_op jit(solution)/shard_map/ppermute | solution.py:340
  4.7 0.9 %collective-permute-done.halo_ref = bf16[4,3,640]{2,1,0:T(4,128)(2,1)S(1)} collective-permute-done((bf16[4,3,640]{2,1,0:T(4,128)(2,1)S(1)}, bf16[4,3,640]{2,1,0:T(4,128)(2,1)S(1)}, u32[]{:S(2)}, u32[]{:S(2)}) %collective-permute-start) | collective-permute-done | bytes 15392 | tf_op jit(solution)/shard_map/ppermute | solution.py:340
  5.6 10.3 %shard_map.84 = (bf16[2,8,128,256]{3,2,1,0:T(8,128)(2,1)S(1)}, bf16[2,8,128,256]{3,2,1,0:T(8,128)(2,1)S(1)}, bf16[2,8,128,256]{3,2,1,0:T(8,128)(2,1)S(1)}, bf16[...) custom-call(s32[1]{0:T(128)} %bitcast.index_ref, ...), custom_call_target="tpu_custom_call" | custom-call | tf_op jit(solution)/shard_map/pallas_call | solution.py:300
  15.9 2.1 %collective-permute-start.1 = (f32[2,128,256]{2,1,0:T(8,128)S(1)}, f32[2,128,256]{2,1,0:T(8,128)S(1)}, u32[]{:S(2)}, u32[]{:S(2)}) collective-permute-start(f32[2,128,256]{2,1,0:T(8,128)S(1)} %get-tuple-element.49), channel_id=1, source_target_pairs={{0,1},{1,0},{2,3},{3,2},{4,5},{5,4},{6,7},{7,6},{8,9},{9,8},{10,11... | collective-permute-start | bytes 786440 | tf_op jit(solution)/shard_map/ppermute | solution.py:311
  18.1 10.3 %shard_map.83 = (bf16[2,8,128,256]{3,2,1,0:T(8,128)(2,1)S(1)}, bf16[2,8,128,256]{3,2,1,0:T(8,128)(2,1)S(1)}, bf16[2,8,128,256]{3,2,1,0:T(8,128)(2,1)S(1)}, bf16[...) custom-call(s32[1]{0:T(128)} %bitcast.index_ref, ...), custom_call_target="tpu_custom_call" | custom-call | tf_op jit(solution)/shard_map/pallas_call | solution.py:300
  28.4 0.3 shard_map.85
  28.7 0.4 collective-permute-start.2
  29.1 0.3 copy-done
  29.4 2.5 %shard_map.86 = (bf16[512,256]{1,0:T(8,128)(2,1)S(1)}, f32[512,128]{1,0:T(8,128)S(1)}) custom-call(s32[1]{0:T(128)} %bitcast.index_ref, bf16[4,512,128]{2,1,0:T(8,128)(2,1)S(1)} %copy-done, bf16[4,3,640]{2,1,0:T(4,128)(2,1)S(1)} %collective-permute-done.halo_ref, f32[4,4,128]{2,1,0:T(4,128)S(1)} %copy-done.3, ...), custom_call_target="tpu_custom_call" | custom-call | tf_op jit(solution)/shard_map/pallas_call | solution.py:300
  31.9 4.7 %collective-permute-done.2.got_ref = f32[2,128,256]{2,1,0:T(8,128)S(1)} collective-permute-done((f32[2,128,256]{2,1,0:T(8,128)S(1)}, f32[2,128,256]{2,1,0:T(8,128)S(1)}, u32[]{:S(2)}, u32[]{:S(2)}) %collective-permute-start.2) | collective-permute-done | bytes 262176 | tf_op jit(solution)/shard_map/ppermute | solution.py:311
  36.7 0.3 shard_map.87
  36.9 0.2 collective-permute-start.3
  37.2 2.5 %shard_map.88 = (bf16[512,256]{1,0:T(8,128)(2,1)S(1)}, f32[512,128]{1,0:T(8,128)S(1)}) custom-call(s32[1]{0:T(128)} %bitcast.index_ref, bf16[4,512,128]{2,1,0:T(8,128)(2,1)S(1)} %copy-done, bf16[4,3,640]{2,1,0:T(4,128)(2,1)S(1)} %collective-permute-done.halo_ref, f32[4,4,128]{2,1,0:T(4,128)S(1)} %copy-done.3, ...), custom_call_target="tpu_custom_call" | custom-call | tf_op jit(solution)/shard_map/pallas_call | solution.py:300
  39.7 2.5 %shard_map.89 = (bf16[512,256]{1,0:T(8,128)(2,1)S(1)}, f32[512,128]{1,0:T(8,128)S(1)}) custom-call(s32[1]{0:T(128)} %bitcast.index_ref, bf16[4,512,128]{2,1,0:T(8,128)(2,1)S(1)} %copy-done, bf16[4,3,640]{2,1,0:T(4,128)(2,1)S(1)} %collective-permute-done.halo_ref, f32[4,4,128]{2,1,0:T(4,128)S(1)} %copy-done.3, ...), custom_call_target="tpu_custom_call" | custom-call | tf_op jit(solution)/shard_map/pallas_call | solution.py:300
  42.2 1.9 %collective-permute-done.3.got_ref = f32[2,128,256]{2,1,0:T(8,128)S(1)} collective-permute-done((f32[2,128,256]{2,1,0:T(8,128)S(1)}, f32[2,128,256]{2,1,0:T(8,128)S(1)}, u32[]{:S(2)}, u32[]{:S(2)}) %collective-permute-start.3) | collective-permute-done | bytes 262176 | tf_op jit(solution)/shard_map/ppermute | solution.py:311
  44.0 0.3 shard_map.90
  44.3 1.3 %collective-permute-start.4 = (f32[2,128,128]{2,1,0:T(8,128)S(1)}, f32[2,128,128]{2,1,0:T(8,128)S(1)}, u32[]{:S(2)}, u32[]{:S(2)}) collective-permute-start(f32[2,128,128]{2,1,0:T(8,128)S(1)} %get-tuple-element.75), channel_id=1, source_target_pairs={{0,8},{1,9},{2,10},{3,11},{4,12},{5,13},{6,14},{7,15},{16,24},{17,... | collective-permute-start | bytes 393224 | tf_op jit(solution)/shard_map/ppermute | solution.py:403
  45.6 2.5 %shard_map.91 = (bf16[512,256]{1,0:T(8,128)(2,1)S(1)}, f32[512,128]{1,0:T(8,128)S(1)}) custom-call(s32[1]{0:T(128)} %bitcast.index_ref, bf16[4,512,128]{2,1,0:T(8,128)(2,1)S(1)} %copy-done, bf16[4,3,640]{2,1,0:T(4,128)(2,1)S(1)} %collective-permute-done.halo_ref, f32[4,4,128]{2,1,0:T(4,128)S(1)} %copy-done.3, ...), custom_call_target="tpu_custom_call" | custom-call | tf_op jit(solution)/shard_map/pallas_call | solution.py:300
  48.1 6.3 %collective-permute-done.4.got_ref = f32[2,128,128]{2,1,0:T(8,128)S(1)} collective-permute-done((f32[2,128,128]{2,1,0:T(8,128)S(1)}, f32[2,128,128]{2,1,0:T(8,128)S(1)}, u32[]{:S(2)}, u32[]{:S(2)}) %collective-permute-start.4) | collective-permute-done | bytes 131104 | tf_op jit(solution)/shard_map/ppermute | solution.py:403
  54.4 0.4 shard_map.92
  54.8 1.4 %collective-permute-start.5 = (f32[2,128,128]{2,1,0:T(8,128)S(1)}, f32[2,128,128]{2,1,0:T(8,128)S(1)}, u32[]{:S(2)}, u32[]{:S(2)}) collective-permute-start(f32[2,128,128]{2,1,0:T(8,128)S(1)} %get-tuple-element.82), channel_id=1, source_target_pairs={{0,1},{1,0},{2,3},{3,2},{4,5},{5,4},{6,7},{7,6},{8,9},{9,8},{10,11... | collective-permute-start | bytes 393224 | tf_op jit(solution)/shard_map/ppermute | solution.py:311
  56.2 1.0 %collective-permute-done.5.other_ref = f32[2,128,128]{2,1,0:T(8,128)S(1)} collective-permute-done((f32[2,128,128]{2,1,0:T(8,128)S(1)}, f32[2,128,128]{2,1,0:T(8,128)S(1)}, u32[]{:S(2)}, u32[]{:S(2)}) %collective-permute-start.5) | collective-permute-done | bytes 131104 | tf_op jit(solution)/shard_map/ppermute | solution.py:311
  57.2 2.4 %shard_map.93 = f32[4,512,128]{2,1,0:T(8,128)} custom-call(s32[1]{0:T(128)} %bitcast.index_ref, f32[2,128,128]{2,1,0:T(8,128)S(1)} %get-tuple-element.81.mine_ref, f32[2,128,128]{2,1,0:T(8,128)S(1)} %collective-permute-done.5.other_ref, f32[4,128]{1,0:T(4,128)S(1)} %copy-done.7, bf16[512,256]{1,0:T(8,128)(2,1)S(1)} %get-tuple-element.83.rest_0_, ...), custom_call_target="tpu_custom_call" | custom-call | tf_op jit(solution)/shard_map/pallas_call | solution.py:416
  (16 shorter events, 0.0 us)
Async XLA Ops:
  0.0 5.6 %copy-start.1 = (bf16[4,512,256]{2,1,0:T(8,128)(2,1)S(1)}, bf16[4,512,256]{2,1,0:T(8,128)(2,1)}, u32[]{:S(2)}) copy-start(bf16[4,512,256]{2,1,0:T(8,128)(2,1)} %key_ref.5) | copy-start | bytes 3145732
  0.0 5.6 %copy-start.2 = (bf16[4,512,256]{2,1,0:T(8,128)(2,1)S(1)}, bf16[4,512,256]{2,1,0:T(8,128)(2,1)}, u32[]{:S(2)}) copy-start(bf16[4,512,256]{2,1,0:T(8,128)(2,1)} %value_ref.5) | copy-start | bytes 3145732
  0.0 5.6 %copy-start.4 = (f32[4,1024]{1,0:T(4,128)S(1)}, f32[4,1024]{1,0:T(4,128)}, u32[]{:S(2)}) copy-start(f32[4,1024]{1,0:T(4,128)} %rate_ref.3) | copy-start | bytes 49156
  0.0 5.6 %copy-start.5 = (f32[4,4,256]{2,1,0:T(4,128)S(1)}, f32[4,4,256]{2,1,0:T(4,128)}, u32[]{:S(2)}) copy-start(f32[4,4,256]{2,1,0:T(4,128)} %ck_ref.3) | copy-start | bytes 49156
  0.0 5.6 %copy-start.6 = (f32[4,4,256]{2,1,0:T(4,128)S(1)}, f32[4,4,256]{2,1,0:T(4,128)}, u32[]{:S(2)}) copy-start(f32[4,4,256]{2,1,0:T(4,128)} %cv_ref.3) | copy-start | bytes 49156
  1.0 4.6 %collective-permute-start = (bf16[4,3,640]{2,1,0:T(4,128)(2,1)S(1)}, bf16[4,3,640]{2,1,0:T(4,128)(2,1)S(1)}, u32[]{:S(2)}, u32[]{:S(2)}) collective-permute-start(bf16[4,3,640]{2,1,0:T(4,128)(2,1)S(1)} %shard_map.82), channel_id=1, source_target_pairs={{0,1},{1,2},{2,3},{3,4},{4,5},{5,6},{6,7},{7,8},{8,9},{9,10},{10,1... | collective-permute-start | bytes 46088 | tf_op jit(solution)/shard_map/ppermute | solution.py:340
  15.9 12.5 %collective-permute-start.1 = (f32[2,128,256]{2,1,0:T(8,128)S(1)}, f32[2,128,256]{2,1,0:T(8,128)S(1)}, u32[]{:S(2)}, u32[]{:S(2)}) collective-permute-start(f32[2,128,256]{2,1,0:T(8,128)S(1)} %get-tuple-element.49), channel_id=1, source_target_pairs={{0,1},{1,0},{2,3},{3,2},{4,5},{5,4},{6,7},{7,6},{8,9},{9,8},{10,11... | collective-permute-start | bytes 786440 | tf_op jit(solution)/shard_map/ppermute | solution.py:311
  28.4 1.0 %copy-start = (bf16[4,512,128]{2,1,0:T(8,128)(2,1)S(1)}, bf16[4,512,128]{2,1,0:T(8,128)(2,1)}, u32[]{:S(2)}) copy-start(bf16[4,512,128]{2,1,0:T(8,128)(2,1)} %query_ref.9) | copy-start | bytes 1572868
  28.7 0.7 %copy-start.3 = (f32[4,4,128]{2,1,0:T(4,128)S(1)}, f32[4,4,128]{2,1,0:T(4,128)}, u32[]{:S(2)}) copy-start(f32[4,4,128]{2,1,0:T(4,128)} %cq_ref.7) | copy-start | bytes 24580
  28.7 8.0 %collective-permute-start.2 = (f32[2,128,256]{2,1,0:T(8,128)S(1)}, f32[2,128,256]{2,1,0:T(8,128)S(1)}, u32[]{:S(2)}, u32[]{:S(2)}) collective-permute-start(f32[2,128,256]{2,1,0:T(8,128)S(1)} %get-tuple-element.50.mine_ref), channel_id=1, source_target_pairs={{0,2},{1,3},{2,0},{3,1},{4,6},{5,7},{6,4},{7,5},{8,10},{9,11},{10,... | collective-permute-start | bytes 786440 | tf_op jit(solution)/shard_map/ppermute | solution.py:311
  36.9 7.1 %collective-permute-start.3 = (f32[2,128,256]{2,1,0:T(8,128)S(1)}, f32[2,128,256]{2,1,0:T(8,128)S(1)}, u32[]{:S(2)}, u32[]{:S(2)}) collective-permute-start(f32[2,128,256]{2,1,0:T(8,128)S(1)} %get-tuple-element.60.mine_ref), channel_id=1, source_target_pairs={{0,4},{1,5},{2,6},{3,7},{4,0},{5,1},{6,2},{7,3},{8,12},{9,13},{10,... | collective-permute-start | bytes 786440 | tf_op jit(solution)/shard_map/ppermute | solution.py:311
  44.3 10.1 %collective-permute-start.4 = (f32[2,128,128]{2,1,0:T(8,128)S(1)}, f32[2,128,128]{2,1,0:T(8,128)S(1)}, u32[]{:S(2)}, u32[]{:S(2)}) collective-permute-start(f32[2,128,128]{2,1,0:T(8,128)S(1)} %get-tuple-element.75), channel_id=1, source_target_pairs={{0,8},{1,9},{2,10},{3,11},{4,12},{5,13},{6,14},{7,15},{16,24},{17,... | collective-permute-start | bytes 393224 | tf_op jit(solution)/shard_map/ppermute | solution.py:403
  54.8 2.4 %copy-start.7 = (f32[4,128]{1,0:T(4,128)S(1)}, f32[4,128]{1,0:T(4,128)}, u32[]{:S(2)}) copy-start(f32[4,128]{1,0:T(4,128)} %gain_ref.1) | copy-start | bytes 6148
  54.8 2.4 %collective-permute-start.5 = (f32[2,128,128]{2,1,0:T(8,128)S(1)}, f32[2,128,128]{2,1,0:T(8,128)S(1)}, u32[]{:S(2)}, u32[]{:S(2)}) collective-permute-start(f32[2,128,128]{2,1,0:T(8,128)S(1)} %get-tuple-element.82), channel_id=1, source_target_pairs={{0,1},{1,0},{2,3},{3,2},{4,5},{5,4},{6,7},{7,6},{8,9},{9,8},{10,11... | collective-permute-start | bytes 393224 | tf_op jit(solution)/shard_map/ppermute | solution.py:311

commit v4 on v3

--- a/solution.py
+++ b/solution.py
@@ -10,7 +10,7 @@
 BLOCK = 128
 GROUP = 16
 HALF = BLOCK // 2
-LIMIT = 12 << 20
+LIMIT = 16 << 20
 
 f32 = jnp.float32
 bf16 = jnp.bfloat16
@@ -70,85 +70,89 @@
 def maps_kernel(
     kept, index_ref, key_ref, value_ref, halo_ref, rate_ref, ck_ref, cv_ref,
     kb_ref, w_ref, u_ref, p_ref, s_ref, total_ref,
-    k0, k1, v0, v1, kv, nref, dref, cref, xref, brow,
+    rows, kv, nref, dref, cref, xref, brow, move, written,
 ):
-    first = first_head(index_ref, kept, total_ref.shape[0])
-
-    def one(slot, carry):
-        one_head_maps(
-            slot, first + slot, key_ref, value_ref, halo_ref, rate_ref, ck_ref, cv_ref,
+    half, blocks = kb_ref.shape[:2]
+    dim = rows.shape[3]
+    first = first_head(index_ref, kept, half)
+    for slots in (tuple(range(half)),):
+        heads_maps(
+            slots, first, blocks, dim, key_ref, value_ref, halo_ref, rate_ref, ck_ref, cv_ref,
             kb_ref, w_ref, u_ref, p_ref, s_ref, total_ref,
-            k0, k1, v0, v1, kv, nref, dref, cref, xref, brow,
+            rows, kv, nref, dref, cref, xref, brow, move, written,
         )
-        return carry
-
-    lax.fori_loop(0, total_ref.shape[0], one, 0)
-
-
-def one_head_maps(
-    slot, head, key_ref, value_ref, halo_ref, rate_ref, ck_ref, cv_ref,
+
+
+def heads_maps(
+    slots, first, blocks, dim, key_ref, value_ref, halo_ref, rate_ref, ck_ref, cv_ref,
     kb_ref, w_ref, u_ref, p_ref, s_ref, total_ref,
-    k0, k1, v0, v1, kv, nref, dref, cref, xref, brow,
+    rows, kv, nref, dref, cref, xref, brow, move, written,
 ):
-    dim = k0.shape[1]
-    tokens = key_ref.shape[1]
-    blocks = tokens // HALF
-    halo = halo_ref[head]
-    fill_rows(k0, halo[:, dim : 2 * dim], key_ref[head, :, :dim])
-    fill_rows(k1, halo[:, 2 * dim : 3 * dim], key_ref[head, :, dim:])
-    fill_rows(v0, halo[:, 3 * dim : 4 * dim], value_ref[head, :, :dim])
-    fill_rows(v1, halo[:, 4 * dim :], value_ref[head, :, dim:])
-    ck = ck_ref[head]
-    cv = cv_ref[head]
-
     row = lax.broadcasted_iota(jnp.int32, (BLOCK, BLOCK), 0)
     col = lax.broadcasted_iota(jnp.int32, (BLOCK, BLOCK), 1)
-    for n in range(blocks):
-        brow[n : n + 1, :] = pick_row(rate_ref[:, n * BLOCK : (n + 1) * BLOCK], head)
-    order = (row == step_time(col)).astype(f32)
-    rates = jnp.dot(brow[...], order, precision=lax.Precision.HIGHEST, preferred_element_type=f32)
-
     strict = step_time(col) < step_time(row)
     lane = lax.broadcasted_iota(jnp.int32, (GROUP, BLOCK), 1)
     eye = (row == col).astype(f32)
-
-    for n in range(blocks):
-        t0 = n * HALF
-        ka = conv_taps(k0, ck[:, :dim], t0, HALF)
-        kb = conv_taps(k1, ck[:, dim:], t0, HALF)
-        keys = interleave(ka, kb)
-        keys = keys * lax.rsqrt(jnp.sum(keys * keys, 1, keepdims=True) + 1e-06)
-        va = conv_taps(v0, cv[:, :dim], t0, HALF)
-        vb = conv_taps(v1, cv[:, dim:], t0, HALF)
-        ks = split(keys)
-        kv[n, :, : 2 * dim] = ks
-        kv[n, :, 2 * dim :] = split(interleave(va, vb))
-        kbs = split(keys.T * rates[n : n + 1, :])
-        kb_ref[slot, n] = kbs
-        lower = jnp.where(strict, mm(ks, kbs), 0.0)
-        nref[n] = lower
-        diag = jnp.zeros((GROUP, BLOCK), f32)
-        for g in range(BLOCK // GROUP):
-            diag = jnp.where(lane // GROUP == g, lower[g * GROUP : (g + 1) * GROUP], diag)
-        cref[n * GROUP : (n + 1) * GROUP, :] = diag
+    order = (row == step_time(col)).astype(f32)
+
+    rates = {}
+    for h in slots:
+        head = first + h
+        halo = halo_ref[head]
+        for i, ref in enumerate((key_ref, value_ref)):
+            for j in range(2):
+                at = (1 + 2 * i + j) * dim
+                fill_rows(
+                    rows.at[h, 2 * i + j], halo[:, at : at + dim], ref[head, :, j * dim : (j + 1) * dim]
+                )
+        for n in range(blocks):
+            brow[h, n : n + 1, :] = pick_row(rate_ref[:, n * BLOCK : (n + 1) * BLOCK], head)
+        rates[h] = jnp.dot(
+            brow[h], order, precision=lax.Precision.HIGHEST, preferred_element_type=f32
+        )
+
+    for h in slots:
+        ck = ck_ref[first + h]
+        cv = cv_ref[first + h]
+        for n in range(blocks):
+            t0 = n * HALF
+            ka = conv_taps(rows.at[h, 0], ck[:, :dim], t0, HALF)
+            kb = conv_taps(rows.at[h, 1], ck[:, dim:], t0, HALF)
+            keys = interleave(ka, kb)
+            keys = keys * lax.rsqrt(jnp.sum(keys * keys, 1, keepdims=True) + 1e-06)
+            va = conv_taps(rows.at[h, 2], cv[:, :dim], t0, HALF)
+            vb = conv_taps(rows.at[h, 3], cv[:, dim:], t0, HALF)
+            ks = split(keys)
+            kv[h, n, :, : 2 * dim] = ks
+            kv[h, n, :, 2 * dim :] = split(interleave(va, vb))
+            kbs = split(keys.T * rates[h][n : n + 1, :])
+            kb_ref[h, n] = kbs
+            lower = jnp.where(strict, mm(ks, kbs), 0.0)
+            nref[h, n] = lower
+            diag = jnp.zeros((GROUP, BLOCK), f32)
+            for g in range(BLOCK // GROUP):
+                diag = jnp.where(lane // GROUP == g, lower[g * GROUP : (g + 1) * GROUP], diag)
+            cref[h, n * GROUP : (n + 1) * GROUP, :] = diag
 
     lane8 = lax.broadcasted_iota(jnp.int32, (blocks, BLOCK), 1)
     times = [t // 2 + 8 * (t % 2) for t in range(GROUP)]
-    coef = [cref[pl.ds(r, blocks, stride=GROUP), :] for r in range(GROUP)]
-    sol = [(lane8 % GROUP == r).astype(f32) for r in range(GROUP)]
-    for i, s in enumerate(times):
-        pick = (lane8 // GROUP) * GROUP + s
-        for r in times[i + 1 :]:
-            sol[r] = sol[r] - jnp.take_along_axis(coef[r], pick, axis=1) * sol[s]
-    for r in range(GROUP):
-        xref[pl.ds(r, blocks, stride=GROUP), :] = sol[r]
-    for n in range(blocks):
-        base = xref[n * GROUP : (n + 1) * GROUP, :]
-        dref[n] = split(
-            jnp.concatenate(
-                [jnp.where(lane // GROUP == g, base, 0.0) for g in range(BLOCK // GROUP)], 0
+    for h in slots:
+        coef = [cref[h, pl.ds(r, blocks, stride=GROUP), :] for r in range(GROUP)]
+        sol = [(lane8 % GROUP == r).astype(f32) for r in range(GROUP)]
+        for i, s in enumerate(times):
+            pick = (lane8 // GROUP) * GROUP + s
+            for r in times[i + 1 :]:
+                sol[r] = sol[r] - jnp.take_along_axis(coef[r], pick, axis=1) * sol[s]
+        for r in range(GROUP):
+            xref[h, pl.ds(r, blocks, stride=GROUP), :] = sol[r]
+    for h in slots:
+        for n in range(blocks):
+            base = xref[h, n * GROUP : (n + 1) * GROUP, :]
+            dref[h, n] = split(
+                jnp.concatenate(
+                    [jnp.where(lane // GROUP == g, base, 0.0) for g in range(BLOCK // GROUP)], 0
+                )
             )
-        )
 
     lane_h = lax.broadcasted_iota(jnp.int32, (HALF, BLOCK), 1)
     row_h = lax.broadcasted_iota(jnp.int32, (HALF, BLOCK), 0)
@@ -156,65 +160,69 @@
     while size < BLOCK:
         keep = lane_h // size == 2 * (row_h // size)
         starts = range(size, BLOCK, 2 * size)
+        for h in slots:
+            for n in range(blocks):
+                inv = dref[h, n]
+                low = jnp.concatenate([nref[h, n, a : a + size] for a in starts], 0)
+                z = split(mm(split(jnp.where(keep, low, 0.0)), inv))
+                twice = []
+                for i in range(len(starts)):
+                    twice += [z[i * size : (i + 1) * size]] * 2
+                odd = jnp.concatenate([inv[a : a + size] for a in starts], 0)
+                new = mm(odd, jnp.concatenate(twice, 0))
+                new = split(odd[:, :BLOCK].astype(f32) + odd[:, BLOCK:].astype(f32) - new)
+                for i, a in enumerate(starts):
+                    dref[h, n, a : a + size] = new[i * size : (i + 1) * size]
+        size *= 2
+
+    for h in slots:
         for n in range(blocks):
-            inv = dref[n]
-            low = jnp.concatenate([nref[n, a : a + size] for a in starts], 0)
-            z = split(mm(split(jnp.where(keep, low, 0.0)), inv))
-            twice = []
-            for i in range(len(starts)):
-                twice += [z[i * size : (i + 1) * size]] * 2
-            odd = jnp.concatenate([inv[a : a + size] for a in starts], 0)
-            new = mm(odd, jnp.concatenate(twice, 0))
-            new = split(odd[:, :BLOCK].astype(f32) + odd[:, BLOCK:].astype(f32) - new)
-            for i, a in enumerate(starts):
-                dref[n, a : a + size] = new[i * size : (i + 1) * size]
-        size *= 2
-
-    before_map = split(eye)
-    before_state = jnp.zeros((dim, 2 * dim), bf16)
-    state = jnp.zeros((dim, dim), f32)
+            inv = dref[h, n]
+            w_ref[h, n] = split(mm(inv, kv[h, n, :, : 2 * dim]))
+            u_ref[h, n] = split(mm(inv, kv[h, n, :, 2 * dim :]))
+    for h in slots:
+        for n in range(blocks):
+            kbs = kb_ref[h, n]
+            move[h, n] = split(eye - mm(kbs, w_ref[h, n]))
+            written[h, n] = mm(kbs, u_ref[h, n])
+    before_map = {h: split(eye) for h in slots}
+    before_state = {h: jnp.zeros((dim, 2 * dim), bf16) for h in slots}
     for n in range(blocks):
-        inv = dref[n]
-        w = split(mm(inv, kv[n, :, : 2 * dim]))
-        u = split(mm(inv, kv[n, :, 2 * dim :]))
-        w_ref[slot, n] = w
-        u_ref[slot, n] = u
-        p_ref[slot, n] = before_map
-        s_ref[slot, n] = before_state
-        kbs = kb_ref[slot, n]
-        move = split(eye - mm(kbs, w))
-        written = mm(kbs, u)
-        map_now = mm(move, before_map)
-        state = mm(move, before_state) + written
-        before_map = split(map_now)
-        before_state = split(state)
-        if n == blocks - 1:
-            total_ref[slot, :, :dim] = map_now
-            total_ref[slot, :, dim:] = state
+        for h in slots:
+            p_ref[h, n] = before_map[h]
+            s_ref[h, n] = before_state[h]
+            map_now = mm(move[h, n], before_map[h])
+            state = mm(move[h, n], before_state[h]) + written[h, n]
+            before_map[h] = split(map_now)
+            before_state[h] = split(state)
+            if n == blocks - 1:
+                total_ref[h, :, :dim] = map_now
+                total_ref[h, :, dim:] = state
 
 
 def reads_kernel(
     kept, slot, index_ref, query_ref, halo_ref, cq_ref, kb_ref, w_ref, u_ref, p_ref, s_ref,
-    pulled_ref, local_ref, q0,
+    pulled_ref, local_ref, q0, query, scores, pulled,
 ):
     head = first_head(index_ref, kept, w_ref.shape[0]) + slot
     dim = q0.shape[1]
-    tokens = query_ref.shape[1]
-    blocks = tokens // HALF
+    blocks = w_ref.shape[1]
     fill_rows(q0, halo_ref[head][:, :dim], query_ref[head])
     cq = cq_ref[head]
     row = lax.broadcasted_iota(jnp.int32, (HALF, BLOCK), 0)
     col = lax.broadcasted_iota(jnp.int32, (HALF, BLOCK), 1)
     causal = step_time(col) <= 2 * row + 1
+    rows = [slice(n * HALF, (n + 1) * HALF) for n in range(blocks)]
     for n in range(blocks):
-        rows = slice(n * HALF, (n + 1) * HALF)
-        query = conv_taps(q0, cq, n * HALF, HALF)
-        scores = split(jnp.where(causal, mm(split(query), kb_ref[slot, n]), 0.0))
-        pulled = query - mm(scores, w_ref[slot, n])
-        local = mm(scores, u_ref[slot, n])
-        pulled = split(pulled)
-        local_ref[rows] = local + mm(pulled, s_ref[slot, n])
-        pulled_ref[rows] = split(mm(pulled, p_ref[slot, n]))
+        q = conv_taps(q0, cq, n * HALF, HALF)
+        query[rows[n]] = q
+        scores[rows[n]] = split(jnp.where(causal, mm(split(q), kb_ref[slot, n]), 0.0))
+    for n in range(blocks):
+        pulled[rows[n]] = split(query[rows[n]] - mm(scores[rows[n]], w_ref[slot, n]))
+        local_ref[rows[n]] = mm(scores[rows[n]], u_ref[slot, n])
+    for n in range(blocks):
+        local_ref[rows[n]] += mm(pulled[rows[n]], s_ref[slot, n])
+        pulled_ref[rows[n]] = split(mm(pulled[rows[n]], p_ref[slot, n]))
 
 
 def out_kernel(index_ref, mine_ref, other_ref, gain_ref, *rest):
@@ -307,6 +315,32 @@
     )(index, *[pltpu.with_memory_space_constraint(a, pltpu.VMEM) for a in args])
 
 
+def maps_call(index, kept, key_pairs, value_pairs, halo, write_rates, conv_key, conv_value):
+    heads, tokens, _ = key_pairs.shape
+    dim = key_pairs.shape[2] // 2
+    half = heads // 2
+    blocks = tokens // HALF
+    wide = shape((half, blocks, BLOCK, 2 * dim), bf16)
+    return resident(
+        functools.partial(maps_kernel, kept),
+        index,
+        (key_pairs, value_pairs, halo, write_rates, conv_key, conv_value),
+        [wide] * 5 + [shape((half, dim, 2 * dim), f32)],
+        [
+            pltpu.VMEM((half, 4, tokens + 8, dim), f32),
+            pltpu.VMEM((half, blocks, BLOCK, 4 * dim), bf16),
+            pltpu.VMEM((half, blocks, BLOCK, BLOCK), f32),
+            pltpu.VMEM((half, blocks, BLOCK, 2 * BLOCK), bf16),
+            pltpu.VMEM((half, blocks * GROUP, BLOCK), f32),
+            pltpu.VMEM((half, blocks * GROUP, BLOCK), f32),
+            pltpu.VMEM((half, blocks, BLOCK), f32),
+            pltpu.VMEM((half, blocks, dim, 2 * dim), bf16),
+            pltpu.VMEM((half, blocks, dim, dim), f32),
+        ],
+        LIMIT,
+    )
+
+
 def swap(x, bit, count):
     return lax.ppermute(x, "seq", [(i, i ^ bit) for i in range(count)])
 
@@ -339,28 +373,11 @@
     )(index, *[pltpu.with_memory_space_constraint(x, pltpu.HBM) for x in parts])
     halo = lax.ppermute(tails, "seq", [(i, i + 1) for i in range(count - 1)])
 
-    rows = pltpu.VMEM((tokens + 8, dim), f32)
-    wide = shape((half, blocks, BLOCK, 2 * dim), bf16)
     total_shape = shape((half, dim, 2 * dim), f32)
     state_shape = shape((half, dim, dim), f32)
 
     def maps(kept):
-        return resident(
-            functools.partial(maps_kernel, kept),
-            index,
-            (key_pairs, value_pairs, halo, write_rates, conv_key, conv_value),
-            [wide] * 5 + [total_shape],
-            [rows] * 4
-            + [
-                pltpu.VMEM((blocks, BLOCK, 4 * dim), bf16),
-                pltpu.VMEM((blocks, BLOCK, BLOCK), f32),
-                pltpu.VMEM((blocks, BLOCK, 2 * BLOCK), bf16),
-                pltpu.VMEM((blocks * GROUP, BLOCK), f32),
-                pltpu.VMEM((blocks * GROUP, BLOCK), f32),
-                pltpu.VMEM((blocks, BLOCK), f32),
-            ],
-            LIMIT,
-        )
+        return maps_call(index, kept, key_pairs, value_pairs, halo, write_rates, conv_key, conv_value)
 
     def reads(kept, slot, saved, after):
         at, _ = lax.optimization_barrier((index, after))
@@ -369,7 +386,12 @@
             at,
             (queries, halo, conv_query, *saved),
             [shape((tokens, 2 * dim), bf16), shape((tokens, dim), f32)],
-            [rows],
+            [
+                pltpu.VMEM((tokens + 8, dim), f32),
+                pltpu.VMEM((tokens, dim), f32),
+                pltpu.VMEM((tokens, 2 * dim), bf16),
+                pltpu.VMEM((tokens, 2 * dim), bf16),
+            ],
             LIMIT,
         )
 

time: 59.8 us -> 53.7 us (0.90)
  Pallas kernels: 35.2 us -> 23.4 us
  waiting for transfers between devices: 14.8 us -> 20.6 us
    pallas_call x10, Pallas kernels: 31.8 us -> 20 us  [resident(): pl.pallas_call(kernel, in_specs=[smem] + [vmem] * len(args), out_specs=[v...]
    ppermute x4, waiting for transfers between devices: 7.6 us -> 11.9 us  [swap(): return lax.ppermute(x, 'seq', [(i, i ^ bit) for i in range(count)])]
    ppermute x1, waiting for transfers between devices: 6.29 us -> 7.74 us  [per_device(): lax.ppermute(current, 'seq', [(i, i + bit) for i in range(count - bit)])]
  transfers between devices with their start and end apart: 6 -> 6, of which waited for: 5 -> 5; matrix products, arithmetic and copies ran while one was open for 0% -> 0% of each run, Pallas kernels for 34% -> 22%
where the time goes in v4:
time: 53.7 us; the launch traced here: 53.6 us
  Pallas kernels  23.4 us (44%)
  waiting for transfers between devices  20.6 us (38%)
  starting transfers between devices  9.16 us (17%)
    pallas_call x10, Pallas kernels, resident(): pl.pallas_call(kernel, in_specs=[smem] + [vmem] * len(args), out_specs=[v...  20 us
    ppermute x4, waiting for transfers between devices, swap(): return lax.ppermute(x, 'seq', [(i, i ^ bit) for i in range(count)])  11.9 us
    ppermute x1, waiting for transfers between devices, per_device(): lax.ppermute(current, 'seq', [(i, i + bit) for i in range(count - bit)])  7.74 us
    ppermute x4, starting transfers between devices, swap(): return lax.ppermute(x, 'seq', [(i, i ^ bit) for i in range(count)])  4.16 us
    ppermute x1, starting transfers between devices, per_device(): halo = lax.ppermute(tails, 'seq', [(i, i + 1) for i in range(count - 1)])  3.71 us
    pallas_call x1, Pallas kernels, per_device(): pl.pallas_call(out_kernel, grid_spec=pltpu.PrefetchScalarGridSpec(num_sca...  2.44 us
    ppermute x1, starting transfers between devices, per_device(): lax.ppermute(current, 'seq', [(i, i + bit) for i in range(count - bit)])  1.29 us
  transfers between devices with their start and end apart: 6, of which 5 were waited for; matrix products, arithmetic and copies ran while one was open for 0% of the time, Pallas kernels for 22%

profile of v4, /device:TPU:25, one launch (start us, length us, event | category | flops | bytes accessed | tf_op | source)
XLA Modules:
  0.0 53.6 jit_solution(4618756526724684640)
XLA Ops:
  0.0 1.0 %shard_map.82 = bf16[4,3,640]{2,1,0:T(4,128)(2,1)S(1)} custom-call(s32[1]{0:T(128)} %bitcast.index_ref, bf16[4,512,128]{2,1,0:T(8,128)(2,1)} %query_ref.9, bf16[4,512,256]{2,1,0:T(8,128)(2,1)} %key_ref.5, bf16[4,512,256]{2,1,0:T(8,128)(2,1)} %value_ref.5), custom_call_target="tpu_custom_call" | custom-call | tf_op jit(solution)/shard_map/pallas_call | solution.py:363
  1.0 3.7 %collective-permute-start = (bf16[4,3,640]{2,1,0:T(4,128)(2,1)S(1)}, bf16[4,3,640]{2,1,0:T(4,128)(2,1)S(1)}, u32[]{:S(2)}, u32[]{:S(2)}) collective-permute-start(bf16[4,3,640]{2,1,0:T(4,128)(2,1)S(1)} %shard_map.82), channel_id=1, source_target_pairs={{0,1},{1,2},{2,3},{3,4},{4,5},{5,6},{6,7},{7,8},{8,9},{9,10},{10,1... | collective-permute-start | bytes 46088 | tf_op jit(solution)/shard_map/ppermute | solution.py:374
  4.7 0.9 %collective-permute-done.halo_ref = bf16[4,3,640]{2,1,0:T(4,128)(2,1)S(1)} collective-permute-done((bf16[4,3,640]{2,1,0:T(4,128)(2,1)S(1)}, bf16[4,3,640]{2,1,0:T(4,128)(2,1)S(1)}, u32[]{:S(2)}, u32[]{:S(2)}) %collective-permute-start) | collective-permute-done | bytes 15392 | tf_op jit(solution)/shard_map/ppermute | solution.py:374
  5.6 7.2 %shard_map.84 = (bf16[2,8,128,256]{3,2,1,0:T(8,128)(2,1)S(1)}, bf16[2,8,128,256]{3,2,1,0:T(8,128)(2,1)S(1)}, bf16[2,8,128,256]{3,2,1,0:T(8,128)(2,1)S(1)}, bf16[...) custom-call(s32[1]{0:T(128)} %bitcast.index_ref, ...), custom_call_target="tpu_custom_call" | custom-call | tf_op jit(solution)/shard_map/pallas_call | solution.py:308
  12.8 2.1 %collective-permute-start.1 = (f32[2,128,256]{2,1,0:T(8,128)S(1)}, f32[2,128,256]{2,1,0:T(8,128)S(1)}, u32[]{:S(2)}, u32[]{:S(2)}) collective-permute-start(f32[2,128,256]{2,1,0:T(8,128)S(1)} %get-tuple-element.49), channel_id=1, source_target_pairs={{0,1},{1,0},{2,3},{3,2},{4,5},{5,4},{6,7},{7,6},{8,9},{9,8},{10,11... | collective-permute-start | bytes 786440 | tf_op jit(solution)/shard_map/ppermute | solution.py:345
  15.0 7.3 %shard_map.83 = (bf16[2,8,128,256]{3,2,1,0:T(8,128)(2,1)S(1)}, bf16[2,8,128,256]{3,2,1,0:T(8,128)(2,1)S(1)}, bf16[2,8,128,256]{3,2,1,0:T(8,128)(2,1)S(1)}, bf16[...) custom-call(s32[1]{0:T(128)} %bitcast.index_ref, ...), custom_call_target="tpu_custom_call" | custom-call | tf_op jit(solution)/shard_map/pallas_call | solution.py:308
  22.3 0.3 shard_map.85
  22.6 0.4 collective-permute-start.2
  23.0 0.3 copy-done
  23.3 1.1 %shard_map.86 = (bf16[512,256]{1,0:T(8,128)(2,1)S(1)}, f32[512,128]{1,0:T(8,128)S(1)}) custom-call(s32[1]{0:T(128)} %bitcast.index_ref, bf16[4,512,128]{2,1,0:T(8,128)(2,1)S(1)} %copy-done, bf16[4,3,640]{2,1,0:T(4,128)(2,1)S(1)} %collective-permute-done.halo_ref, f32[4,4,128]{2,1,0:T(4,128)S(1)} %copy-done.3, ...), custom_call_target="tpu_custom_call" | custom-call | tf_op jit(solution)/shard_map/pallas_call | solution.py:308
  24.4 6.2 %collective-permute-done.2.got_ref = f32[2,128,256]{2,1,0:T(8,128)S(1)} collective-permute-done((f32[2,128,256]{2,1,0:T(8,128)S(1)}, f32[2,128,256]{2,1,0:T(8,128)S(1)}, u32[]{:S(2)}, u32[]{:S(2)}) %collective-permute-start.2) | collective-permute-done | bytes 262176 | tf_op jit(solution)/shard_map/ppermute | solution.py:345
  30.6 0.3 shard_map.87
  30.9 0.2 collective-permute-start.3
  31.1 1.1 %shard_map.88 = (bf16[512,256]{1,0:T(8,128)(2,1)S(1)}, f32[512,128]{1,0:T(8,128)S(1)}) custom-call(s32[1]{0:T(128)} %bitcast.index_ref, bf16[4,512,128]{2,1,0:T(8,128)(2,1)S(1)} %copy-done, bf16[4,3,640]{2,1,0:T(4,128)(2,1)S(1)} %collective-permute-done.halo_ref, f32[4,4,128]{2,1,0:T(4,128)S(1)} %copy-done.3, ...), custom_call_target="tpu_custom_call" | custom-call | tf_op jit(solution)/shard_map/pallas_call | solution.py:308
  32.1 1.1 %shard_map.89 = (bf16[512,256]{1,0:T(8,128)(2,1)S(1)}, f32[512,128]{1,0:T(8,128)S(1)}) custom-call(s32[1]{0:T(128)} %bitcast.index_ref, bf16[4,512,128]{2,1,0:T(8,128)(2,1)S(1)} %copy-done, bf16[4,3,640]{2,1,0:T(4,128)(2,1)S(1)} %collective-permute-done.halo_ref, f32[4,4,128]{2,1,0:T(4,128)S(1)} %copy-done.3, ...), custom_call_target="tpu_custom_call" | custom-call | tf_op jit(solution)/shard_map/pallas_call | solution.py:308
  33.2 4.7 %collective-permute-done.3.got_ref = f32[2,128,256]{2,1,0:T(8,128)S(1)} collective-permute-done((f32[2,128,256]{2,1,0:T(8,128)S(1)}, f32[2,128,256]{2,1,0:T(8,128)S(1)}, u32[]{:S(2)}, u32[]{:S(2)}) %collective-permute-start.3) | collective-permute-done | bytes 262176 | tf_op jit(solution)/shard_map/ppermute | solution.py:345
  38.0 0.3 shard_map.90
  38.3 1.3 %collective-permute-start.4 = (f32[2,128,128]{2,1,0:T(8,128)S(1)}, f32[2,128,128]{2,1,0:T(8,128)S(1)}, u32[]{:S(2)}, u32[]{:S(2)}) collective-permute-start(f32[2,128,128]{2,1,0:T(8,128)S(1)} %get-tuple-element.75), channel_id=1, source_target_pairs={{0,8},{1,9},{2,10},{3,11},{4,12},{5,13},{6,14},{7,15},{16,24},{17,... | collective-permute-start | bytes 393224 | tf_op jit(solution)/shard_map/ppermute | solution.py:425
  39.6 1.1 %shard_map.91 = (bf16[512,256]{1,0:T(8,128)(2,1)S(1)}, f32[512,128]{1,0:T(8,128)S(1)}) custom-call(s32[1]{0:T(128)} %bitcast.index_ref, bf16[4,512,128]{2,1,0:T(8,128)(2,1)S(1)} %copy-done, bf16[4,3,640]{2,1,0:T(4,128)(2,1)S(1)} %collective-permute-done.halo_ref, f32[4,4,128]{2,1,0:T(4,128)S(1)} %copy-done.3, ...), custom_call_target="tpu_custom_call" | custom-call | tf_op jit(solution)/shard_map/pallas_call | solution.py:308
  40.6 7.7 %collective-permute-done.4.got_ref = f32[2,128,128]{2,1,0:T(8,128)S(1)} collective-permute-done((f32[2,128,128]{2,1,0:T(8,128)S(1)}, f32[2,128,128]{2,1,0:T(8,128)S(1)}, u32[]{:S(2)}, u32[]{:S(2)}) %collective-permute-start.4) | collective-permute-done | bytes 131104 | tf_op jit(solution)/shard_map/ppermute | solution.py:425
  48.4 0.4 shard_map.92
  48.8 1.4 %collective-permute-start.5 = (f32[2,128,128]{2,1,0:T(8,128)S(1)}, f32[2,128,128]{2,1,0:T(8,128)S(1)}, u32[]{:S(2)}, u32[]{:S(2)}) collective-permute-start(f32[2,128,128]{2,1,0:T(8,128)S(1)} %get-tuple-element.82), channel_id=1, source_target_pairs={{0,1},{1,0},{2,3},{3,2},{4,5},{5,4},{6,7},{7,6},{8,9},{9,8},{10,11... | collective-permute-start | bytes 393224 | tf_op jit(solution)/shard_map/ppermute | solution.py:345
  50.1 1.0 %collective-permute-done.5.other_ref = f32[2,128,128]{2,1,0:T(8,128)S(1)} collective-permute-done((f32[2,128,128]{2,1,0:T(8,128)S(1)}, f32[2,128,128]{2,1,0:T(8,128)S(1)}, u32[]{:S(2)}, u32[]{:S(2)}) %collective-permute-start.5) | collective-permute-done | bytes 131104 | tf_op jit(solution)/shard_map/ppermute | solution.py:345
  51.1 2.4 %shard_map.93 = f32[4,512,128]{2,1,0:T(8,128)} custom-call(s32[1]{0:T(128)} %bitcast.index_ref, f32[2,128,128]{2,1,0:T(8,128)S(1)} %get-tuple-element.81.mine_ref, f32[2,128,128]{2,1,0:T(8,128)S(1)} %collective-permute-done.5.other_ref, f32[4,128]{1,0:T(4,128)S(1)} %copy-done.7, bf16[512,256]{1,0:T(8,128)(2,1)S(1)} %get-tuple-element.83.rest_0_, ...), custom_call_target="tpu_custom_call" | custom-call | tf_op jit(solution)/shard_map/pallas_call | solution.py:438
  (16 shorter events, 0.0 us)
Async XLA Ops:
  0.0 5.6 %copy-start.1 = (bf16[4,512,256]{2,1,0:T(8,128)(2,1)S(1)}, bf16[4,512,256]{2,1,0:T(8,128)(2,1)}, u32[]{:S(2)}) copy-start(bf16[4,512,256]{2,1,0:T(8,128)(2,1)} %key_ref.5) | copy-start | bytes 3145732
  0.0 5.6 %copy-start.2 = (bf16[4,512,256]{2,1,0:T(8,128)(2,1)S(1)}, bf16[4,512,256]{2,1,0:T(8,128)(2,1)}, u32[]{:S(2)}) copy-start(bf16[4,512,256]{2,1,0:T(8,128)(2,1)} %value_ref.5) | copy-start | bytes 3145732
  0.0 5.6 %copy-start.4 = (f32[4,1024]{1,0:T(4,128)S(1)}, f32[4,1024]{1,0:T(4,128)}, u32[]{:S(2)}) copy-start(f32[4,1024]{1,0:T(4,128)} %rate_ref.3) | copy-start | bytes 49156
  0.0 5.6 %copy-start.5 = (f32[4,4,256]{2,1,0:T(4,128)S(1)}, f32[4,4,256]{2,1,0:T(4,128)}, u32[]{:S(2)}) copy-start(f32[4,4,256]{2,1,0:T(4,128)} %ck_ref.3) | copy-start | bytes 49156
  0.0 5.6 %copy-start.6 = (f32[4,4,256]{2,1,0:T(4,128)S(1)}, f32[4,4,256]{2,1,0:T(4,128)}, u32[]{:S(2)}) copy-start(f32[4,4,256]{2,1,0:T(4,128)} %cv_ref.3) | copy-start | bytes 49156
  1.0 4.6 %collective-permute-start = (bf16[4,3,640]{2,1,0:T(4,128)(2,1)S(1)}, bf16[4,3,640]{2,1,0:T(4,128)(2,1)S(1)}, u32[]{:S(2)}, u32[]{:S(2)}) collective-permute-start(bf16[4,3,640]{2,1,0:T(4,128)(2,1)S(1)} %shard_map.82), channel_id=1, source_target_pairs={{0,1},{1,2},{2,3},{3,4},{4,5},{5,6},{6,7},{7,8},{8,9},{9,10},{10,1... | collective-permute-start | bytes 46088 | tf_op jit(solution)/shard_map/ppermute | solution.py:374
  12.8 9.5 %collective-permute-start.1 = (f32[2,128,256]{2,1,0:T(8,128)S(1)}, f32[2,128,256]{2,1,0:T(8,128)S(1)}, u32[]{:S(2)}, u32[]{:S(2)}) collective-permute-start(f32[2,128,256]{2,1,0:T(8,128)S(1)} %get-tuple-element.49), channel_id=1, source_target_pairs={{0,1},{1,0},{2,3},{3,2},{4,5},{5,4},{6,7},{7,6},{8,9},{9,8},{10,11... | collective-permute-start | bytes 786440 | tf_op jit(solution)/shard_map/ppermute | solution.py:345
  22.3 1.0 %copy-start = (bf16[4,512,128]{2,1,0:T(8,128)(2,1)S(1)}, bf16[4,512,128]{2,1,0:T(8,128)(2,1)}, u32[]{:S(2)}) copy-start(bf16[4,512,128]{2,1,0:T(8,128)(2,1)} %query_ref.9) | copy-start | bytes 1572868
  22.6 0.7 %copy-start.3 = (f32[4,4,128]{2,1,0:T(4,128)S(1)}, f32[4,4,128]{2,1,0:T(4,128)}, u32[]{:S(2)}) copy-start(f32[4,4,128]{2,1,0:T(4,128)} %cq_ref.7) | copy-start | bytes 24580
  22.6 8.0 %collective-permute-start.2 = (f32[2,128,256]{2,1,0:T(8,128)S(1)}, f32[2,128,256]{2,1,0:T(8,128)S(1)}, u32[]{:S(2)}, u32[]{:S(2)}) collective-permute-start(f32[2,128,256]{2,1,0:T(8,128)S(1)} %get-tuple-element.50.mine_ref), channel_id=1, source_target_pairs={{0,2},{1,3},{2,0},{3,1},{4,6},{5,7},{6,4},{7,5},{8,10},{9,11},{10,... | collective-permute-start | bytes 786440 | tf_op jit(solution)/shard_map/ppermute | solution.py:345
  30.9 7.1 %collective-permute-start.3 = (f32[2,128,256]{2,1,0:T(8,128)S(1)}, f32[2,128,256]{2,1,0:T(8,128)S(1)}, u32[]{:S(2)}, u32[]{:S(2)}) collective-permute-start(f32[2,128,256]{2,1,0:T(8,128)S(1)} %get-tuple-element.60.mine_ref), channel_id=1, source_target_pairs={{0,4},{1,5},{2,6},{3,7},{4,0},{5,1},{6,2},{7,3},{8,12},{9,13},{10,... | collective-permute-start | bytes 786440 | tf_op jit(solution)/shard_map/ppermute | solution.py:345
  38.3 10.1 %collective-permute-start.4 = (f32[2,128,128]{2,1,0:T(8,128)S(1)}, f32[2,128,128]{2,1,0:T(8,128)S(1)}, u32[]{:S(2)}, u32[]{:S(2)}) collective-permute-start(f32[2,128,128]{2,1,0:T(8,128)S(1)} %get-tuple-element.75), channel_id=1, source_target_pairs={{0,8},{1,9},{2,10},{3,11},{4,12},{5,13},{6,14},{7,15},{16,24},{17,... | collective-permute-start | bytes 393224 | tf_op jit(solution)/shard_map/ppermute | solution.py:425
  48.8 2.4 %copy-start.7 = (f32[4,128]{1,0:T(4,128)S(1)}, f32[4,128]{1,0:T(4,128)}, u32[]{:S(2)}) copy-start(f32[4,128]{1,0:T(4,128)} %gain_ref.1) | copy-start | bytes 6148
  48.8 2.4 %collective-permute-start.5 = (f32[2,128,128]{2,1,0:T(8,128)S(1)}, f32[2,128,128]{2,1,0:T(8,128)S(1)}, u32[]{:S(2)}, u32[]{:S(2)}) collective-permute-start(f32[2,128,128]{2,1,0:T(8,128)S(1)} %get-tuple-element.82), channel_id=1, source_target_pairs={{0,1},{1,0},{2,3},{3,2},{4,5},{5,4},{6,7},{7,6},{8,9},{9,8},{10,11... | collective-permute-start | bytes 393224 | tf_op jit(solution)/shard_map/ppermute | solution.py:345

commit v5 on v4

v5 whole, which is shorter than its diff:
```python
import functools

import jax
import jax.numpy as jnp
from jax import lax
from jax.experimental import pallas as pl
from jax.experimental.pallas import tpu as pltpu
from jax.sharding import PartitionSpec as P

BLOCK = 128
GROUP = 16
HALF = BLOCK // 2
LIMIT = 20 << 20

f32 = jnp.float32
bf16 = jnp.bfloat16


def split(x):
    high = x.astype(bf16)
    low = (x - high.astype(f32)).astype(bf16)
    return jnp.concatenate([high, low], 1)


def mm(a, b):
    n = b.shape[1] // 2
    p = jnp.dot(a, jnp.concatenate([b, b], 0), preferred_element_type=f32)
    return p[:, :n] + p[:, n:]


def pick_row(x, r):
    row = lax.broadcasted_iota(jnp.int32, x.shape, 0)
    return jnp.sum(jnp.where(row == r, x, 0.0), 0, keepdims=True)


def silu(x):
    return x / (1.0 + jnp.exp(-x))


def step_time(r):
    return (r // GROUP) * GROUP + 2 * (r % 8) + (r // 8) % 2


def interleave(a, b):
    parts = []
    for g in range(0, a.shape[0], 8):
        parts += [a[g : g + 8], b[g : g + 8]]
    return jnp.concatenate(parts, 0)


def conv_taps(ref, weights, start, count):
    taps = weights.shape[0]
    total = weights[0:1] * ref[pl.ds(start + 9 - taps, count), :]
    for s in range(1, taps):
        total = total + weights[s : s + 1] * ref[pl.ds(start + 9 - taps + s, count), :]
    return silu(total)


def fill_rows(ref, halo, rows):
    rim = halo.shape[0]
    ref[8 - rim : 8, :] = halo.astype(f32)
    ref[8:, :] = rows.astype(f32)


def first_head(index_ref, kept, half):
    upper = index_ref[0] & 1
    return (upper if kept else 1 - upper) * half


def block_masks():
    row = lax.broadcasted_iota(jnp.int32, (BLOCK, BLOCK), 0)
    col = lax.broadcasted_iota(jnp.int32, (BLOCK, BLOCK), 1)
    lane = lax.broadcasted_iota(jnp.int32, (GROUP, BLOCK), 1)
    return row, col, lane


def block_inputs(key_rows, value_rows, ck, cv, t0, rates):
    row, col, lane = block_masks()
    dim = key_rows[0].shape[1]
    ka, kb = [conv_taps(r, ck[:, j * dim : (j + 1) * dim], t0, HALF) for j, r in enumerate(key_rows)]
    keys = interleave(ka, kb)
    keys = keys * lax.rsqrt(jnp.sum(keys * keys, 1, keepdims=True) + 1e-06)
    va, vb = [conv_taps(r, cv[:, j * dim : (j + 1) * dim], t0, HALF) for j, r in enumerate(value_rows)]
    ks = split(keys)
    kv = jnp.concatenate([ks, split(interleave(va, vb))], 1)
    kbs = split(keys.T * rates)
    lower = jnp.where(step_time(col) < step_time(row), mm(ks, kbs), 0.0)
    diag = jnp.zeros((GROUP, BLOCK), f32)
    for g in range(BLOCK // GROUP):
        diag = jnp.where(lane // GROUP == g, lower[g * GROUP : (g + 1) * GROUP], diag)
    return kv, kbs, lower, diag


def front_kernel(
    index_ref, key_ref, value_ref, rate_ref, ck_ref, cv_ref,
    kv_ref, kb_ref, low_ref, diag_ref, rates_ref, rows, brow,
):
    dim = rows.shape[2]
    blocks = rates_ref.shape[1]
    row, col, _ = block_masks()
    order = (row == step_time(col)).astype(f32)

    def one(h, carry):
        for i, ref in enumerate((key_ref, value_ref)):
            for j in range(2):
                rows[2 * i + j, 8:, :] = ref[h, :, j * dim : (j + 1) * dim].astype(f32)
        for n in range(blocks):
            brow[n : n + 1, :] = pick_row(rate_ref[:, n * BLOCK : (n + 1) * BLOCK], h)
        rates = jnp.dot(
            brow[...], order, precision=lax.Precision.HIGHEST, preferred_element_type=f32
        )
        rates_ref[h] = rates
        for n in range(1, blocks):
            kv_ref[h, n - 1], kb_ref[h, n - 1], low_ref[h, n - 1], diag_ref[h, n - 1] = block_inputs(
                [rows.at[0], rows.at[1]], [rows.at[2], rows.at[3]],
                ck_ref[h], cv_ref[h], n * HALF, rates[n : n + 1],
            )
        return carry

    lax.fori_loop(0, key_ref.shape[0], one, 0)


def own_halo(index_ref, halo):
    return jnp.where(index_ref[0] == 0, 0.0, halo.astype(f32))


def maps_kernel(
    kept, start, half, index_ref, key_ref, value_ref, halo_ref, ck_ref, cv_ref,
    kv_ref, kb_ref, low_ref, diag_ref, rates_ref,
    kb0_ref, w_ref, u_ref, p_ref, s_ref, total_ref,
    rows, kv0, low0, dref, cref, xref, move, written,
):
    count, blocks = w_ref.shape[:2]
    dim = rows.shape[2]
    slots = range(count)
    first = first_head(index_ref, kept, half) + start
    row, col, lane = block_masks()
    eye = (row == col).astype(f32)

    for h in slots:
        head = first + h
        halo = own_halo(index_ref, halo_ref[head])
        for i, ref in enumerate((key_ref, value_ref)):
            for j in range(2):
                at = (1 + 2 * i + j) * dim
                fill_rows(
                    rows.at[2 * i + j],
                    halo[:, at : at + dim],
                    ref[head, :HALF, j * dim : (j + 1) * dim],
                )
        kv0[h], kb0_ref[h], low0[h], diag = block_inputs(
            [rows.at[0], rows.at[1]], [rows.at[2], rows.at[3]],
            ck_ref[head], cv_ref[head], 0, rates_ref[head][0:1],
        )
        cref[h, 0:GROUP, :] = diag
        for n in range(1, blocks):
            cref[h, n * GROUP : (n + 1) * GROUP, :] = diag_ref[head, n - 1]

    def keys_values(h, n):
        return kv0[h] if n == 0 else kv_ref[first + h, n - 1]

    def key_columns(h, n):
        return kb0_ref[h] if n == 0 else kb_ref[first + h, n - 1]

    def lower_rows(h, n, a, size):
        return low0[h, a : a + size] if n == 0 else low_ref[first + h, n - 1, a : a + size]

    lane8 = lax.broadcasted_iota(jnp.int32, (blocks, BLOCK), 1)
    times = [t // 2 + 8 * (t % 2) for t in range(GROUP)]
    for h in slots:
        coef = [cref[h, pl.ds(r, blocks, stride=GROUP), :] for r in range(GROUP)]
        sol = [(lane8 % GROUP == r).astype(f32) for r in range(GROUP)]
        for i, s in enumerate(times):
            pick = (lane8 // GROUP) * GROUP + s
            for r in times[i + 1 :]:
                sol[r] = sol[r] - jnp.take_along_axis(coef[r], pick, axis=1) * sol[s]
        for r in range(GROUP):
            xref[h, pl.ds(r, blocks, stride=GROUP), :] = sol[r]
    for h in slots:
        for n in range(blocks):
            base = xref[h, n * GROUP : (n + 1) * GROUP, :]
            dref[h, n] = split(
                jnp.concatenate(
                    [jnp.where(lane // GROUP == g, base, 0.0) for g in range(BLOCK // GROUP)], 0
                )
            )

    lane_h = lax.broadcasted_iota(jnp.int32, (HALF, BLOCK), 1)
    row_h = lax.broadcasted_iota(jnp.int32, (HALF, BLOCK), 0)
    size = GROUP
    while size < BLOCK:
        keep = lane_h // size == 2 * (row_h // size)
        starts = range(size, BLOCK, 2 * size)
        for h in slots:
            for n in range(blocks):
                inv = dref[h, n]
                low = jnp.concatenate([lower_rows(h, n, a, size) for a in starts], 0)
                z = split(mm(split(jnp.where(keep, low, 0.0)), inv))
                twice = []
                for i in range(len(starts)):
                    twice += [z[i * size : (i + 1) * size]] * 2
                odd = jnp.concatenate([inv[a : a + size] for a in starts], 0)
                new = mm(odd, jnp.concatenate(twice, 0))
                new = split(odd[:, :BLOCK].astype(f32) + odd[:, BLOCK:].astype(f32) - new)
                for i, a in enumerate(starts):
                    dref[h, n, a : a + size] = new[i * size : (i + 1) * size]
        size *= 2

    for h in slots:
        for n in range(blocks):
            inv = dref[h, n]
            both = keys_values(h, n)
            w_ref[h, n] = split(mm(inv, both[:, : 2 * dim]))
            u_ref[h, n] = split(mm(inv, both[:, 2 * dim :]))
    for h in slots:
        for n in range(blocks):
            kbs = key_columns(h, n)
            move[h, n] = split(eye - mm(kbs, w_ref[h, n]))
            written[h, n] = mm(kbs, u_ref[h, n])
    before_map = {h: split(eye) for h in slots}
    before_state = {h: jnp.zeros((dim, 2 * dim), bf16) for h in slots}
    for n in range(blocks):
        for h in slots:
            p_ref[h, n] = before_map[h]
            s_ref[h, n] = before_state[h]
            map_now = mm(move[h, n], before_map[h])
            state = mm(move[h, n], before_state[h]) + written[h, n]
            before_map[h] = split(map_now)
            before_state[h] = split(state)
            if n == blocks - 1:
                total_ref[h, :, :dim] = map_now
                total_ref[h, :, dim:] = state


def reads_kernel(
    kept, slot, at, half, index_ref, query_ref, halo_ref, cq_ref, kb_ref, kb0_ref, w_ref, u_ref, p_ref, s_ref,
    pulled_ref, local_ref, q0, query, scores, pulled,
):
    head = first_head(index_ref, kept, half) + at
    dim = q0.shape[1]
    blocks = w_ref.shape[1]
    fill_rows(q0, own_halo(index_ref, halo_ref[head])[:, :dim], query_ref[head])
    cq = cq_ref[head]
    row = lax.broadcasted_iota(jnp.int32, (HALF, BLOCK), 0)
    col = lax.broadcasted_iota(jnp.int32, (HALF, BLOCK), 1)
    causal = step_time(col) <= 2 * row + 1
    rows = [slice(n * HALF, (n + 1) * HALF) for n in range(blocks)]
    for n in range(blocks):
        q = conv_taps(q0, cq, n * HALF, HALF)
        query[rows[n]] = q
        kbs = kb0_ref[slot] if n == 0 else kb_ref[head, n - 1]
        scores[rows[n]] = split(jnp.where(causal, mm(split(q), kbs), 0.0))
    for n in range(blocks):
        pulled[rows[n]] = split(query[rows[n]] - mm(scores[rows[n]], w_ref[slot, n]))
        local_ref[rows[n]] = mm(scores[rows[n]], u_ref[slot, n])
    for n in range(blocks):
        local_ref[rows[n]] += mm(pulled[rows[n]], s_ref[slot, n])
        pulled_ref[rows[n]] = split(mm(pulled[rows[n]], p_ref[slot, n]))


def out_kernel(slot, half, index_ref, mine_ref, other_ref, gain_ref, *rest):
    out_ref = rest[-1]
    for i in range(2):

        @pl.when(pl.program_id(0) == i)
        def _():
            h = first_head(index_ref, i == 0, half) + slot
            state = mine_ref[0] if i == 0 else other_ref[0]
            raw = mm(rest[2 * i][...], split(state)) + rest[2 * i + 1][...]
            mean = jnp.mean(raw * raw, 1, keepdims=True)
            out_ref[0] = raw * lax.rsqrt(mean + 1e-06) * pick_row(gain_ref[...], h)


def then(later, earlier):
    dim = later.shape[0]
    prod = mm(split(later[:, :dim]), split(earlier))
    wide = prod.shape[1]
    if wide == dim:
        return prod + later[:, dim:]
    return jnp.concatenate([prod[:, :dim], prod[:, dim:] + later[:, dim:]], 1)


def pair_kernel(slot, index_ref, mine_ref, got_ref, total_ref, earlier_ref):
    upper = (index_ref[0] & 1) != 0
    for h in range(mine_ref.shape[0]):
        mine = mine_ref[h]
        got = got_ref[slot + h]
        earlier = jnp.where(upper, got, mine)
        earlier_ref[h] = earlier
        total_ref[h] = then(jnp.where(upper, mine, got), earlier)


def join_kernel(bit, index_ref, mine_ref, got_ref, *rest):
    *before_ref, total_ref, after_ref = rest
    upper = (index_ref[0] & bit) != 0
    dim = mine_ref.shape[1]
    row = lax.broadcasted_iota(jnp.int32, (dim, 2 * dim), 0)
    col = lax.broadcasted_iota(jnp.int32, (dim, 2 * dim), 1)
    for h in range(mine_ref.shape[0]):
        mine = mine_ref[h]
        got = got_ref[h]
        earlier = jnp.where(upper, got, mine)
        if total_ref.shape[2] == dim:
            earlier = earlier[:, dim:]
        total_ref[h] = then(jnp.where(upper, mine, got), earlier)
        if before_ref:
            before = before_ref[0][h]
            after_ref[h] = jnp.where(upper, then(before, got), before)
        else:
            after_ref[h] = jnp.where(upper, got, (row == col).astype(f32))


def down_kernel(bit, index_ref, before_ref, got_ref, earlier_ref, mine_ref, other_ref):
    upper = (index_ref[0] & 1) != 0
    for h in range(before_ref.shape[0]):
        got = jnp.where((index_ref[0] & bit) != 0, got_ref[h], 0.0)
        state = then(before_ref[h], got)
        after = then(earlier_ref[h], state)
        mine_ref[h] = jnp.where(upper, after, state)
        other_ref[h] = jnp.where(upper, state, after)


def tails_kernel(index_ref, query_ref, key_ref, value_ref, out_ref):
    rim = out_ref.shape[1]
    at = 0
    for ref in (query_ref, key_ref, value_ref):
        wide = ref.shape[2]
        out_ref[:, :, at : at + wide] = ref[:, ref.shape[1] - rim :, :]
        at += wide


def shape(dims, dtype):
    return jax.ShapeDtypeStruct(dims, dtype)


def resident(kernel, index, args, outs, scratch=(), limit=4 << 20):
    smem = pl.BlockSpec(memory_space=pltpu.SMEM)
    vmem = pl.BlockSpec(memory_space=pltpu.VMEM)
    return pl.pallas_call(
        kernel,
        in_specs=[smem] + [vmem] * len(args),
        out_specs=[vmem] * len(outs),
        out_shape=[pltpu.VMEM(o.shape, o.dtype) for o in outs],
        scratch_shapes=list(scratch),
        compiler_params=pltpu.CompilerParams(vmem_limit_bytes=limit),
    )(index, *[pltpu.with_memory_space_constraint(a, pltpu.VMEM) for a in args])


def swap(x, bit, count):
    return lax.ppermute(x, "seq", [(i, i ^ bit) for i in range(count)])


def per_device(
    queries, key_pairs, value_pairs, write_rates, conv_query, conv_key, conv_value, out_gain
):
    heads, tokens, dim = queries.shape
    blocks = tokens // HALF
    half = heads // 2
    rim = conv_query.shape[1] - 1
    count = lax.axis_size("seq")
    index = lax.axis_index("seq").reshape(1)

    parts = (queries, key_pairs, value_pairs)
    last = [
        pl.BlockSpec((heads, 16, x.shape[2]), lambda i, index_ref: (0, tokens // 16 - 1, 0))
        for x in parts
    ]
    tails = pl.pallas_call(
        tails_kernel,
        grid_spec=pltpu.PrefetchScalarGridSpec(
            num_scalar_prefetch=1,
            grid=(1,),
            in_specs=last,
            out_specs=pl.BlockSpec((heads, rim, 5 * dim), lambda i, index_ref: (0, 0, 0)),
        ),
        out_shape=shape((heads, rim, 5 * dim), bf16),
        compiler_params=pltpu.CompilerParams(vmem_limit_bytes=4 << 20),
    )(index, *[pltpu.with_memory_space_constraint(x, pltpu.HBM) for x in parts])
    halo = lax.ppermute(tails, "seq", [(i, (i + 1) % count) for i in range(count)])

    def in_order(*after):
        return lax.optimization_barrier((index, after))[0]

    inner = (heads, blocks - 1, BLOCK)
    front = resident(
        front_kernel,
        in_order(tails),
        (key_pairs, value_pairs, write_rates, conv_key, conv_value),
        [
            shape(inner + (4 * dim,), bf16),
            shape(inner + (2 * dim,), bf16),
            shape(inner + (BLOCK,), f32),
            shape((heads, blocks - 1, GROUP, BLOCK), f32),
            shape((heads, blocks, BLOCK), f32),
        ],
        [pltpu.VMEM((4, tokens + 8, dim), f32), pltpu.VMEM((blocks, BLOCK), f32)],
        LIMIT,
    )
    halo = lax.optimization_barrier((halo, front[-1]))[0]

    def maps(kept, start, size, *after):
        wide = shape((size, blocks, BLOCK, 2 * dim), bf16)
        return resident(
            functools.partial(maps_kernel, kept, start, half),
            in_order(*after),
            (key_pairs, value_pairs, halo, conv_key, conv_value, *front),
            [shape((size, BLOCK, 2 * dim), bf16)] + [wide] * 4 + [shape((size, dim, 2 * dim), f32)],
            [
                pltpu.VMEM((4, HALF + 8, dim), f32),
                pltpu.VMEM((size, BLOCK, 4 * dim), bf16),
                pltpu.VMEM((size, BLOCK, BLOCK), f32),
                pltpu.VMEM((size, blocks, BLOCK, 2 * BLOCK), bf16),
                pltpu.VMEM((size, blocks * GROUP, BLOCK), f32),
                pltpu.VMEM((size, blocks * GROUP, BLOCK), f32),
                pltpu.VMEM((size, blocks, dim, 2 * dim), bf16),
                pltpu.VMEM((size, blocks, dim, dim), f32),
            ],
            LIMIT,
        )

    def reads(kept, at, *after):
        slot, saved = (0, kept_saved[at]) if kept else (at, sent_saved)
        return resident(
            functools.partial(reads_kernel, kept, slot, at, half),
            in_order(*after),
            (queries, halo, conv_query, front[1], *saved),
            [shape((tokens, 2 * dim), bf16), shape((tokens, dim), f32)],
            [
                pltpu.VMEM((tokens + 8, dim), f32),
                pltpu.VMEM((tokens, dim), f32),
                pltpu.VMEM((tokens, 2 * dim), bf16),
                pltpu.VMEM((tokens, 2 * dim), bf16),
            ],
            LIMIT,
        )

    total_shape = shape((1, dim, 2 * dim), f32)
    state_shape = shape((1, dim, dim), f32)
    bits = []
    while 2 << len(bits) < count:
        bits.append(2 << len(bits))
    chains = {}

    def begin(at, got):
        total, earlier = resident(
            functools.partial(pair_kernel, at), index, (kept_total[at], got), [total_shape] * 2
        )
        chains[at] = dict(current=total, earlier=earlier, before=None, left=list(bits))
        send(at)
        return total

    def send(at):
        chain = chains[at]
        chain["got"] = swap(chain["current"], chain["left"][0], count)

    def join(at, *after):
        chain = chains[at]
        bit = chain["left"].pop(0)
        got = lax.optimization_barrier((chain["got"], after))[0]
        before = () if chain["before"] is None else (chain["before"],)
        last = len(chain["left"]) == 1
        chain["current"], chain["before"] = resident(
            functools.partial(join_kernel, bit),
            index,
            (chain["current"], got) + before,
            [state_shape if last else total_shape, total_shape],
        )
        send(at)
        return chain["current"]

    def down(at, *after):
        chain = chains[at]
        got = lax.optimization_barrier((chain["got"], after))[0]
        mine, other = resident(
            functools.partial(down_kernel, bits[-1]), index, (chain["before"], got, chain["earlier"]), [state_shape] * 2
        )
        return mine, swap(other, 1, count)

    out_shape = shape((heads, tokens, dim), f32)

    def finish(at, mine, other, done, *after):
        vmem = pl.BlockSpec(memory_space=pltpu.VMEM)

        def out_block(i, index_ref):
            upper = index_ref[0] & 1
            return (jnp.where(i == 0, upper, 1 - upper) * half + at, 0, 0)

        args = [mine, other, out_gain, *read[True, at], *read[False, at]]
        args = [pltpu.with_memory_space_constraint(a, pltpu.VMEM) for a in args]
        return pl.pallas_call(
            functools.partial(out_kernel, at, half),
            grid_spec=pltpu.PrefetchScalarGridSpec(
                num_scalar_prefetch=1,
                grid=(2,),
                in_specs=[vmem] * len(args) + [pl.BlockSpec(memory_space=pl.ANY)] * len(done),
                out_specs=pl.BlockSpec((1, tokens, dim), out_block),
            ),
            out_shape=out_shape,
            input_output_aliases={len(args) + 1: 0} if done else {},
            compiler_params=pltpu.CompilerParams(vmem_limit_bytes=LIMIT),
        )(in_order(*after), *args, *done)

    kept_saved, kept_total, read = {}, {}, {}

    def keep(at, *after):
        *kept_saved[at], kept_total[at] = maps(True, at, 1, *after)

    *sent_saved, sent_total = maps(False, 0, half)
    got = swap(sent_total, 1, count)
    keep(0, sent_total)
    step = begin(0, got)
    for at in range(1, half):
        keep(at, step)
        for other in range(at):
            if len(chains[other]["left"]) > 1:
                step = join(other, kept_total[at])
        step = begin(at, got)
    todo = [(kept, at) for at in range(half) for kept in (False, True)]

    def read_one(after):
        if todo:
            kept, at = todo.pop(0)
            read[kept, at] = reads(kept, at, after)
            return read[kept, at][1]
        return after

    step = read_one(read_one(step))
    while any(len(chain["left"]) > 1 for chain in chains.values()):
        for at in range(half):
            if len(chains[at]["left"]) > 1:
                step = read_one(join(at, step))
    while todo:
        step = read_one(step)
    done = ()
    states = [down(0, step)]
    for at in range(half):
        out = finish(at, *states[at], done)
        if at + 1 < half:
            states.append(down(at + 1, out))
        done = (out,)
    return done[0]


def solution(mesh):
    return jax.shard_map(
        per_device,
        mesh=mesh,
        in_specs=(
            P(None, ("grp", "seq"), None),
            P(None, ("grp", "seq"), None),
            P(None, ("grp", "seq"), None),
            P(None, ("grp", "seq")),
            P(),
            P(),
            P(),
            P(),
        ),
        out_specs=P(None, ("grp", "seq"), None),
        check_vma=False,
    )
```

time: 53.7 us -> 48.1 us (0.90)
  the two profiles are of different devices: /device:TPU:25 before, /device:TPU:0 now
where the time goes in v5:
time: 48.1 us; the launch traced here: 47.9 us
  Pallas kernels  27.8 us (58%)
  starting transfers between devices  11.6 us (24%)
  waiting for transfers between devices  8.18 us (17%)
    pallas_call x16, Pallas kernels, resident(): pl.pallas_call(kernel, in_specs=[smem] + [vmem] * len(args), out_specs=[v...  24.1 us
    ppermute x9, starting transfers between devices, swap(): return lax.ppermute(x, 'seq', [(i, i ^ bit) for i in range(count)])  11.1 us
    ppermute x9, waiting for transfers between devices, swap(): return lax.ppermute(x, 'seq', [(i, i ^ bit) for i in range(count)])  5.88 us
    pallas_call x2, Pallas kernels, finish(): pl.pallas_call(functools.partial(out_kernel, at, half), grid_spec=pltpu.P...  2.76 us
    ppermute x1, waiting for transfers between devices, per_device(): lax.ppermute(tails, 'seq', [(i, (i + 1) % count) for i in range(count)])  2.3 us
  transfers between devices with their start and end apart: 10, of which 6 were waited for; matrix products, arithmetic and copies ran while one was open for 0% of the time, Pallas kernels for 38%

profile of v5, /device:TPU:0, one launch (start us, length us, event | category | flops | bytes accessed | tf_op | source)
XLA Modules:
  0.0 47.9 jit_solution(17742601466570740770)
XLA Ops:
  0.0 1.0 %shard_map.82 = bf16[4,3,640]{2,1,0:T(4,128)(2,1)S(1)} custom-call(s32[1]{0:T(128)} %bitcast.index_ref, bf16[4,512,128]{2,1,0:T(8,128)(2,1)} %query_ref.9, bf16[4,512,256]{2,1,0:T(8,128)(2,1)} %key_ref.9, bf16[4,512,256]{2,1,0:T(8,128)(2,1)} %value_ref.9), custom_call_target="tpu_custom_call" | custom-call | tf_op jit(solution)/shard_map/pallas_call | solution.py:368
  1.0 0.5 %collective-permute-start = (bf16[4,3,640]{2,1,0:T(4,128)(2,1)S(1)}, bf16[4,3,640]{2,1,0:T(4,128)(2,1)S(1)}, u32[]{:S(2)}, u32[]{:S(2)}) collective-permute-start(bf16[4,3,640]{2,1,0:T(4,128)(2,1)S(1)} %shard_map.82), channel_id=1, source_target_pairs={{0,1},{1,2},{2,3},{3,4},{4,5},{5,6},{6,7},{7,8},{8,9},{9,10},{10,1... | collective-permute-start | bytes 46088 | tf_op jit(solution)/shard_map/ppermute | solution.py:379
  1.6 4.1 %shard_map.83 = (bf16[4,7,128,512]{3,2,1,0:T(8,128)(2,1)S(1)}, bf16[4,7,128,256]{3,2,1,0:T(8,128)(2,1)S(1)}, f32[4,7,128,128]{3,2,1,0:T(8,128)S(1)}, f32[4,7,16,128]{3,2,1,0:T(8,128)S(1)}, f32[4,8,128]{2,1,0:T(8,128)S(1)}) custom-call(s32[1]{0:T(128)} %bitcast.index_ref, bf16[4,512,256]{2,1,0:T(8,128)(2,1)S(1)} %copy-done, ...), custom_call_target="tpu_custom_call" | custom-call | tf_op jit(solution)/shard_map/pallas_call | solution.py:339
  5.7 2.3 %collective-permute-done.halo_ref = bf16[4,3,640]{2,1,0:T(4,128)(2,1)S(1)} collective-permute-done((bf16[4,3,640]{2,1,0:T(4,128)(2,1)S(1)}, bf16[4,3,640]{2,1,0:T(4,128)(2,1)S(1)}, u32[]{:S(2)}, u32[]{:S(2)}) %collective-permute-start) | collective-permute-done | bytes 15392 | tf_op jit(solution)/shard_map/ppermute | solution.py:379
  8.0 5.7 %shard_map.84 = (bf16[2,128,256]{2,1,0:T(8,128)(2,1)S(1)}, bf16[2,8,128,256]{3,2,1,0:T(8,128)(2,1)S(1)}, bf16[2,8,128,256]{3,2,1,0:T(8,128)(2,1)S(1)}, bf16[2,8,...) custom-call(s32[1]{0:T(128)} %bitcast.index_ref, ...), custom_call_target="tpu_custom_call" | custom-call | tf_op jit(solution)/shard_map/pallas_call | solution.py:339
  14.0 4.0 %shard_map.85 = (bf16[1,128,256]{2,1,0:T(8,128)(2,1)S(1)}, bf16[1,8,128,256]{3,2,1,0:T(8,128)(2,1)S(1)}, bf16[1,8,128,256]{3,2,1,0:T(8,128)(2,1)S(1)}, bf16[1,8,...) custom-call(s32[1]{0:T(128)} %bitcast.index_ref, ...), custom_call_target="tpu_custom_call" | custom-call | tf_op jit(solution)/shard_map/pallas_call | solution.py:339
  18.3 1.6 %collective-permute-start.3 = (f32[1,128,256]{2,1,0:T(8,128)S(1)}, f32[1,128,256]{2,1,0:T(8,128)S(1)}, u32[]{:S(2)}, u32[]{:S(2)}) collective-permute-start(f32[1,128,256]{2,1,0:T(8,128)S(1)} %get-tuple-element.76.mine_ref), channel_id=1, source_target_pairs={{0,2},{1,3},{2,0},{3,1},{4,6},{5,7},{6,4},{7,5},{8,10},{9,11},{10,... | collective-permute-start | bytes 393224 | tf_op jit(solution)/shard_map/ppermute | solution.py:350
  19.8 4.0 %shard_map.87 = (bf16[1,128,256]{2,1,0:T(8,128)(2,1)S(1)}, bf16[1,8,128,256]{3,2,1,0:T(8,128)(2,1)S(1)}, bf16[1,8,128,256]{3,2,1,0:T(8,128)(2,1)S(1)}, bf16[1,8,...) custom-call(s32[1]{0:T(128)} %bitcast.index_ref, ...), custom_call_target="tpu_custom_call" | custom-call | tf_op jit(solution)/shard_map/pallas_call | solution.py:339
  24.2 1.5 %collective-permute-start.4 = (f32[1,128,256]{2,1,0:T(8,128)S(1)}, f32[1,128,256]{2,1,0:T(8,128)S(1)}, u32[]{:S(2)}, u32[]{:S(2)}) collective-permute-start(f32[1,128,256]{2,1,0:T(8,128)S(1)} %get-tuple-element.81.mine_ref), channel_id=1, source_target_pairs={{0,4},{1,5},{2,6},{3,7},{4,0},{5,1},{6,2},{7,3},{8,12},{9,13},{10,... | collective-permute-start | bytes 393224 | tf_op jit(solution)/shard_map/ppermute | solution.py:350
  25.9 1.5 %collective-permute-start.2 = (f32[1,128,256]{2,1,0:T(8,128)S(1)}, f32[1,128,256]{2,1,0:T(8,128)S(1)}, u32[]{:S(2)}, u32[]{:S(2)}) collective-permute-start(f32[1,128,256]{2,1,0:T(8,128)S(1)} %get-tuple-element.79.mine_ref), channel_id=1, source_target_pairs={{0,2},{1,3},{2,0},{3,1},{4,6},{5,7},{6,4},{7,5},{8,10},{9,11},{10,... | collective-permute-start | bytes 393224 | tf_op jit(solution)/shard_map/ppermute | solution.py:350
  27.4 1.1 %shard_map.90 = (bf16[512,256]{1,0:T(8,128)(2,1)S(1)}, f32[512,128]{1,0:T(8,128)S(1)}) custom-call(s32[1]{0:T(128)} %bitcast.index_ref, bf16[4,512,128]{2,1,0:T(8,128)(2,1)S(1)} %copy-done.2, bf16[4,3,640]{2,1,0:T(4,128)(2,1)S(1)} %collective-permute-done.halo_ref, f32[4,4,128]{2,1,0:T(4,128)S(1)} %copy-done.5, ...), custom_call_target="tpu_custom_call" | custom-call | tf_op jit(solution)/shard_map/pallas_call | solution.py:339
  28.5 1.2 %shard_map.91 = (bf16[512,256]{1,0:T(8,128)(2,1)S(1)}, f32[512,128]{1,0:T(8,128)S(1)}) custom-call(s32[1]{0:T(128)} %bitcast.index_ref, bf16[4,512,128]{2,1,0:T(8,128)(2,1)S(1)} %copy-done.2, bf16[4,3,640]{2,1,0:T(4,128)(2,1)S(1)} %collective-permute-done.halo_ref, f32[4,4,128]{2,1,0:T(4,128)S(1)} %copy-done.5, ...), custom_call_target="tpu_custom_call" | custom-call | tf_op jit(solution)/shard_map/pallas_call | solution.py:339
  29.9 1.1 %shard_map.93 = (bf16[512,256]{1,0:T(8,128)(2,1)S(1)}, f32[512,128]{1,0:T(8,128)S(1)}) custom-call(s32[1]{0:T(128)} %bitcast.index_ref, bf16[4,512,128]{2,1,0:T(8,128)(2,1)S(1)} %copy-done.2, bf16[4,3,640]{2,1,0:T(4,128)(2,1)S(1)} %collective-permute-done.halo_ref, f32[4,4,128]{2,1,0:T(4,128)S(1)} %copy-done.5, ...), custom_call_target="tpu_custom_call" | custom-call | tf_op jit(solution)/shard_map/pallas_call | solution.py:339
  31.2 1.2 %collective-permute-start.5 = (f32[1,128,256]{2,1,0:T(8,128)S(1)}, f32[1,128,256]{2,1,0:T(8,128)S(1)}, u32[]{:S(2)}, u32[]{:S(2)}) collective-permute-start(f32[1,128,256]{2,1,0:T(8,128)S(1)} %get-tuple-element.102.mine_ref), channel_id=1, source_target_pairs={{0,4},{1,5},{2,6},{3,7},{4,0},{5,1},{6,2},{7,3},{8,12},{9,13},{10,... | collective-permute-start | bytes 393224 | tf_op jit(solution)/shard_map/ppermute | solution.py:350
  32.4 2.3 %collective-permute-start.7 = (f32[1,128,128]{2,1,0:T(8,128)S(1)}, f32[1,128,128]{2,1,0:T(8,128)S(1)}, u32[]{:S(2)}, u32[]{:S(2)}) collective-permute-start(f32[1,128,128]{2,1,0:T(8,128)S(1)} %get-tuple-element.98), channel_id=1, source_target_pairs={{0,8},{1,9},{2,10},{3,11},{4,12},{5,13},{6,14},{7,15},{8,0},{9,1},... | collective-permute-start | bytes 196616 | tf_op jit(solution)/shard_map/ppermute | solution.py:350
  34.8 1.1 %shard_map.95 = (bf16[512,256]{1,0:T(8,128)(2,1)S(1)}, f32[512,128]{1,0:T(8,128)S(1)}) custom-call(s32[1]{0:T(128)} %bitcast.index_ref, bf16[4,512,128]{2,1,0:T(8,128)(2,1)S(1)} %copy-done.2, bf16[4,3,640]{2,1,0:T(4,128)(2,1)S(1)} %collective-permute-done.halo_ref, f32[4,4,128]{2,1,0:T(4,128)S(1)} %copy-done.5, ...), custom_call_target="tpu_custom_call" | custom-call | tf_op jit(solution)/shard_map/pallas_call | solution.py:339
  35.8 0.8 %collective-permute-done.5.got_ref = f32[1,128,256]{2,1,0:T(8,128)S(1)} collective-permute-done((f32[1,128,256]{2,1,0:T(8,128)S(1)}, f32[1,128,256]{2,1,0:T(8,128)S(1)}, u32[]{:S(2)}, u32[]{:S(2)}) %collective-permute-start.5) | collective-permute-done | bytes 131104 | tf_op jit(solution)/shard_map/ppermute | solution.py:350
  36.9 0.7 %collective-permute-done.7.got_ref = f32[1,128,128]{2,1,0:T(8,128)S(1)} collective-permute-done((f32[1,128,128]{2,1,0:T(8,128)S(1)}, f32[1,128,128]{2,1,0:T(8,128)S(1)}, u32[]{:S(2)}, u32[]{:S(2)}) %collective-permute-start.7) | collective-permute-done | bytes 65568 | tf_op jit(solution)/shard_map/ppermute | solution.py:350
  37.6 0.4 shard_map.97
  38.1 2.5 %collective-permute-start.6 = (f32[1,128,128]{2,1,0:T(8,128)S(1)}, f32[1,128,128]{2,1,0:T(8,128)S(1)}, u32[]{:S(2)}, u32[]{:S(2)}) collective-permute-start(f32[1,128,128]{2,1,0:T(8,128)S(1)} %get-tuple-element.113), channel_id=1, source_target_pairs={{0,8},{1,9},{2,10},{3,11},{4,12},{5,13},{6,14},{7,15},{8,0},{9,1},... | collective-permute-start | bytes 196616 | tf_op jit(solution)/shard_map/ppermute | solution.py:350
  40.5 1.4 %shard_map.98.rest_4_ = f32[4,512,128]{2,1,0:T(8,128)} custom-call(s32[1]{0:T(128)} %bitcast.index_ref, f32[1,128,128]{2,1,0:T(8,128)S(1)} %get-tuple-element.117.mine_ref, f32[1,128,128]{2,1,0:T(8,128)S(1)} %collective-permute-done.8.other_ref, f32[4,128]{1,0:T(4,128)S(1)} %copy-done.7, bf16[512,256]{1,0:T(8,128)(2,1)S(1)} %get-tuple-element.119.rest_0_, ...), custom_call_target="tpu_custom_call" | custom-call | tf_op jit(solution)/shard_map/pallas_call | solution.py:490
  41.9 2.9 %collective-permute-done.6.got_ref = f32[1,128,128]{2,1,0:T(8,128)S(1)} collective-permute-done((f32[1,128,128]{2,1,0:T(8,128)S(1)}, f32[1,128,128]{2,1,0:T(8,128)S(1)}, u32[]{:S(2)}, u32[]{:S(2)}) %collective-permute-start.6) | collective-permute-done | bytes 65568 | tf_op jit(solution)/shard_map/ppermute | solution.py:350
  45.3 1.2 %collective-permute-done.9.other_ref = f32[1,128,128]{2,1,0:T(8,128)S(1)} collective-permute-done((f32[1,128,128]{2,1,0:T(8,128)S(1)}, f32[1,128,128]{2,1,0:T(8,128)S(1)}, u32[]{:S(2)}, u32[]{:S(2)}) %collective-permute-start.9) | collective-permute-done | bytes 65568 | tf_op jit(solution)/shard_map/ppermute | solution.py:350
  46.6 1.4 %shard_map.100 = f32[4,512,128]{2,1,0:T(8,128)} custom-call(s32[1]{0:T(128)} %bitcast.index_ref, f32[1,128,128]{2,1,0:T(8,128)S(1)} %get-tuple-element.123.mine_ref, f32[1,128,128]{2,1,0:T(8,128)S(1)} %collective-permute-done.9.other_ref, f32[4,128]{1,0:T(4,128)S(1)} %copy-done.7, ...), custom_call_target="tpu_custom_call", output_to_operand_aliasing={{}: (8, {})} | custom-call | tf_op jit(solution)/shard_map/pallas_call | solution.py:490
  (31 shorter events, 2.4 us)
Async XLA Ops:
  0.0 1.5 %copy-start.1 = (bf16[4,512,256]{2,1,0:T(8,128)(2,1)S(1)}, bf16[4,512,256]{2,1,0:T(8,128)(2,1)}, u32[]{:S(2)}) copy-start(bf16[4,512,256]{2,1,0:T(8,128)(2,1)} %value_ref.9) | copy-start | bytes 3145732
  0.0 1.6 %copy-start = (bf16[4,512,256]{2,1,0:T(8,128)(2,1)S(1)}, bf16[4,512,256]{2,1,0:T(8,128)(2,1)}, u32[]{:S(2)}) copy-start(bf16[4,512,256]{2,1,0:T(8,128)(2,1)} %key_ref.9) | copy-start | bytes 3145732
  0.0 1.6 %copy-start.4 = (f32[4,4,256]{2,1,0:T(4,128)S(1)}, f32[4,4,256]{2,1,0:T(4,128)}, u32[]{:S(2)}) copy-start(f32[4,4,256]{2,1,0:T(4,128)} %cv_ref.7) | copy-start | bytes 49156
  0.0 1.6 %copy-start.3 = (f32[4,4,256]{2,1,0:T(4,128)S(1)}, f32[4,4,256]{2,1,0:T(4,128)}, u32[]{:S(2)}) copy-start(f32[4,4,256]{2,1,0:T(4,128)} %ck_ref.7) | copy-start | bytes 49156
  0.0 1.6 %copy-start.6 = (f32[4,1024]{1,0:T(4,128)S(1)}, f32[4,1024]{1,0:T(4,128)}, u32[]{:S(2)}) copy-start(f32[4,1024]{1,0:T(4,128)} %rate_ref.1) | copy-start | bytes 49156
  1.0 7.0 %collective-permute-start = (bf16[4,3,640]{2,1,0:T(4,128)(2,1)S(1)}, bf16[4,3,640]{2,1,0:T(4,128)(2,1)S(1)}, u32[]{:S(2)}, u32[]{:S(2)}) collective-permute-start(bf16[4,3,640]{2,1,0:T(4,128)(2,1)S(1)} %shard_map.82), channel_id=1, source_target_pairs={{0,1},{1,2},{2,3},{3,4},{4,5},{5,6},{6,7},{7,8},{8,9},{9,10},{10,1... | collective-permute-start | bytes 46088 | tf_op jit(solution)/shard_map/ppermute | solution.py:379
  13.7 4.3 %collective-permute-start.1 = (f32[2,128,256]{2,1,0:T(8,128)S(1)}, f32[2,128,256]{2,1,0:T(8,128)S(1)}, u32[]{:S(2)}, u32[]{:S(2)}) collective-permute-start(f32[2,128,256]{2,1,0:T(8,128)S(1)} %get-tuple-element.73), channel_id=1, source_target_pairs={{0,1},{1,0},{2,3},{3,2},{4,5},{5,4},{6,7},{7,6},{8,9},{9,8},{10,11... | collective-permute-start | bytes 786440 | tf_op jit(solution)/shard_map/ppermute | solution.py:350
  18.2 9.2 %copy-start.2 = (bf16[4,512,128]{2,1,0:T(8,128)(2,1)S(1)}, bf16[4,512,128]{2,1,0:T(8,128)(2,1)}, u32[]{:S(2)}) copy-start(bf16[4,512,128]{2,1,0:T(8,128)(2,1)} %query_ref.9) | copy-start | bytes 1572868
  18.2 9.2 %copy-start.5 = (f32[4,4,128]{2,1,0:T(4,128)S(1)}, f32[4,4,128]{2,1,0:T(4,128)}, u32[]{:S(2)}) copy-start(f32[4,4,128]{2,1,0:T(4,128)} %cq_ref.7) | copy-start | bytes 24580
  18.3 5.7 %collective-permute-start.3 = (f32[1,128,256]{2,1,0:T(8,128)S(1)}, f32[1,128,256]{2,1,0:T(8,128)S(1)}, u32[]{:S(2)}, u32[]{:S(2)}) collective-permute-start(f32[1,128,256]{2,1,0:T(8,128)S(1)} %get-tuple-element.76.mine_ref), channel_id=1, source_target_pairs={{0,2},{1,3},{2,0},{3,1},{4,6},{5,7},{6,4},{7,5},{8,10},{9,11},{10,... | collective-permute-start | bytes 393224 | tf_op jit(solution)/shard_map/ppermute | solution.py:350
  24.2 5.5 %collective-permute-start.4 = (f32[1,128,256]{2,1,0:T(8,128)S(1)}, f32[1,128,256]{2,1,0:T(8,128)S(1)}, u32[]{:S(2)}, u32[]{:S(2)}) collective-permute-start(f32[1,128,256]{2,1,0:T(8,128)S(1)} %get-tuple-element.81.mine_ref), channel_id=1, source_target_pairs={{0,4},{1,5},{2,6},{3,7},{4,0},{5,1},{6,2},{7,3},{8,12},{9,13},{10,... | collective-permute-start | bytes 393224 | tf_op jit(solution)/shard_map/ppermute | solution.py:350
  25.9 5.1 %collective-permute-start.2 = (f32[1,128,256]{2,1,0:T(8,128)S(1)}, f32[1,128,256]{2,1,0:T(8,128)S(1)}, u32[]{:S(2)}, u32[]{:S(2)}) collective-permute-start(f32[1,128,256]{2,1,0:T(8,128)S(1)} %get-tuple-element.79.mine_ref), channel_id=1, source_target_pairs={{0,2},{1,3},{2,0},{3,1},{4,6},{5,7},{6,4},{7,5},{8,10},{9,11},{10,... | collective-permute-start | bytes 393224 | tf_op jit(solution)/shard_map/ppermute | solution.py:350
  31.2 5.4 %collective-permute-start.5 = (f32[1,128,256]{2,1,0:T(8,128)S(1)}, f32[1,128,256]{2,1,0:T(8,128)S(1)}, u32[]{:S(2)}, u32[]{:S(2)}) collective-permute-start(f32[1,128,256]{2,1,0:T(8,128)S(1)} %get-tuple-element.102.mine_ref), channel_id=1, source_target_pairs={{0,4},{1,5},{2,6},{3,7},{4,0},{5,1},{6,2},{7,3},{8,12},{9,13},{10,... | collective-permute-start | bytes 393224 | tf_op jit(solution)/shard_map/ppermute | solution.py:350
  32.4 5.2 %collective-permute-start.7 = (f32[1,128,128]{2,1,0:T(8,128)S(1)}, f32[1,128,128]{2,1,0:T(8,128)S(1)}, u32[]{:S(2)}, u32[]{:S(2)}) collective-permute-start(f32[1,128,128]{2,1,0:T(8,128)S(1)} %get-tuple-element.98), channel_id=1, source_target_pairs={{0,8},{1,9},{2,10},{3,11},{4,12},{5,13},{6,14},{7,15},{8,0},{9,1},... | collective-permute-start | bytes 196616 | tf_op jit(solution)/shard_map/ppermute | solution.py:350
  34.8 5.8 %copy-start.7 = (f32[4,128]{1,0:T(4,128)S(1)}, f32[4,128]{1,0:T(4,128)}, u32[]{:S(2)}) copy-start(f32[4,128]{1,0:T(4,128)} %gain_ref.3) | copy-start | bytes 6148
  38.0 2.6 %collective-permute-start.8 = (f32[1,128,128]{2,1,0:T(8,128)S(1)}, f32[1,128,128]{2,1,0:T(8,128)S(1)}, u32[]{:S(2)}, u32[]{:S(2)}) collective-permute-start(f32[1,128,128]{2,1,0:T(8,128)S(1)} %get-tuple-element.118), channel_id=1, source_target_pairs={{0,1},{1,0},{2,3},{3,2},{4,5},{5,4},{6,7},{7,6},{8,9},{9,8},{10,11... | collective-permute-start | bytes 196616 | tf_op jit(solution)/shard_map/ppermute | solution.py:350
  38.1 6.8 %collective-permute-start.6 = (f32[1,128,128]{2,1,0:T(8,128)S(1)}, f32[1,128,128]{2,1,0:T(8,128)S(1)}, u32[]{:S(2)}, u32[]{:S(2)}) collective-permute-start(f32[1,128,128]{2,1,0:T(8,128)S(1)} %get-tuple-element.113), channel_id=1, source_target_pairs={{0,8},{1,9},{2,10},{3,11},{4,12},{5,13},{6,14},{7,15},{8,0},{9,1},... | collective-permute-start | bytes 196616 | tf_op jit(solution)/shard_map/ppermute | solution.py:350
  45.2 1.3 %collective-permute-start.9 = (f32[1,128,128]{2,1,0:T(8,128)S(1)}, f32[1,128,128]{2,1,0:T(8,128)S(1)}, u32[]{:S(2)}, u32[]{:S(2)}) collective-permute-start(f32[1,128,128]{2,1,0:T(8,128)S(1)} %get-tuple-element.124), channel_id=1, source_target_pairs={{0,1},{1,0},{2,3},{3,2},{4,5},{5,4},{6,7},{7,6},{8,9},{9,8},{10,11... | collective-permute-start | bytes 196616 | tf_op jit(solution)/shard_map/ppermute | solution.py:350

commit v6 on v5

--- a/solution.py
+++ b/solution.py
@@ -91,9 +91,22 @@
     return kv, kbs, lower, diag
 
 
+def invert_groups(diag, out, blocks):
+    lane = lax.broadcasted_iota(jnp.int32, (blocks, BLOCK), 1)
+    times = [t // 2 + 8 * (t % 2) for t in range(GROUP)]
+    coef = [diag[pl.ds(r, blocks, stride=GROUP), :] for r in range(GROUP)]
+    sol = [(lane % GROUP == r).astype(f32) for r in range(GROUP)]
+    for i, s in enumerate(times):
+        pick = (lane // GROUP) * GROUP + s
+        for r in times[i + 1 :]:
+            sol[r] = sol[r] - jnp.take_along_axis(coef[r], pick, axis=1) * sol[s]
+    for r in range(GROUP):
+        out[pl.ds(r, blocks, stride=GROUP), :] = sol[r]
+
+
 def front_kernel(
     index_ref, key_ref, value_ref, rate_ref, ck_ref, cv_ref,
-    kv_ref, kb_ref, low_ref, diag_ref, rates_ref, rows, brow,
+    kv_ref, kb_ref, low_ref, sol_ref, rates_ref, rows, brow, diag,
 ):
     dim = rows.shape[2]
     blocks = rates_ref.shape[1]
@@ -111,13 +124,42 @@
         )
         rates_ref[h] = rates
         for n in range(1, blocks):
-            kv_ref[h, n - 1], kb_ref[h, n - 1], low_ref[h, n - 1], diag_ref[h, n - 1] = block_inputs(
+            kv_ref[h, n - 1], kb_ref[h, n - 1], low_ref[h, n - 1], groups = block_inputs(
                 [rows.at[0], rows.at[1]], [rows.at[2], rows.at[3]],
                 ck_ref[h], cv_ref[h], n * HALF, rates[n : n + 1],
             )
+            diag[h, n * GROUP : (n + 1) * GROUP] = groups
+        diag[h, 0:GROUP] = jnp.zeros((GROUP, BLOCK), f32)
         return carry
 
     lax.fori_loop(0, key_ref.shape[0], one, 0)
+    for h in range(key_ref.shape[0]):
+        invert_groups(diag.at[h], sol_ref.at[h], blocks)
+
+
+def first_kernel(
+    index_ref, key_ref, value_ref, halo_ref, ck_ref, cv_ref, rates_ref,
+    kv_ref, kb_ref, low_ref, sol_ref, rows, diag,
+):
+    heads = key_ref.shape[0]
+    dim = rows.shape[3]
+    for h in range(heads):
+        halo = own_halo(index_ref, halo_ref[h])
+        for i, ref in enumerate((key_ref, value_ref)):
+            for j in range(2):
+                at = (1 + 2 * i + j) * dim
+                fill_rows(
+                    rows.at[h, 2 * i + j],
+                    halo[:, at : at + dim],
+                    ref[h, :HALF, j * dim : (j + 1) * dim],
+                )
+    for h in range(heads):
+        kv_ref[h], kb_ref[h], low_ref[h], groups = block_inputs(
+            [rows.at[h, 0], rows.at[h, 1]], [rows.at[h, 2], rows.at[h, 3]],
+            ck_ref[h], cv_ref[h], 0, rates_ref[h][0:1],
+        )
+        diag[h * GROUP : (h + 1) * GROUP] = groups
+    invert_groups(diag, sol_ref, heads)
 
 
 def own_halo(index_ref, halo):
@@ -125,60 +167,27 @@
 
 
 def maps_kernel(
-    kept, start, half, index_ref, key_ref, value_ref, halo_ref, ck_ref, cv_ref,
-    kv_ref, kb_ref, low_ref, diag_ref, rates_ref,
-    kb0_ref, w_ref, u_ref, p_ref, s_ref, total_ref,
-    rows, kv0, low0, dref, cref, xref, move, written,
+    kept, start, half, index_ref, kv_ref, kb_ref, low_ref, sol_ref,
+    kv0_ref, kb0_ref, low0_ref, sol0_ref,
+    w_ref, u_ref, p_ref, s_ref, total_ref,
+    dref, move, written,
 ):
     count, blocks = w_ref.shape[:2]
-    dim = rows.shape[2]
+    dim = total_ref.shape[1]
     slots = range(count)
     first = first_head(index_ref, kept, half) + start
     row, col, lane = block_masks()
     eye = (row == col).astype(f32)
 
-    for h in slots:
-        head = first + h
-        halo = own_halo(index_ref, halo_ref[head])
-        for i, ref in enumerate((key_ref, value_ref)):
-            for j in range(2):
-                at = (1 + 2 * i + j) * dim
-                fill_rows(
-                    rows.at[2 * i + j],
-                    halo[:, at : at + dim],
-                    ref[head, :HALF, j * dim : (j + 1) * dim],
-                )
-        kv0[h], kb0_ref[h], low0[h], diag = block_inputs(
-            [rows.at[0], rows.at[1]], [rows.at[2], rows.at[3]],
-            ck_ref[head], cv_ref[head], 0, rates_ref[head][0:1],
-        )
-        cref[h, 0:GROUP, :] = diag
-        for n in range(1, blocks):
-            cref[h, n * GROUP : (n + 1) * GROUP, :] = diag_ref[head, n - 1]
-
-    def keys_values(h, n):
-        return kv0[h] if n == 0 else kv_ref[first + h, n - 1]
-
-    def key_columns(h, n):
-        return kb0_ref[h] if n == 0 else kb_ref[first + h, n - 1]
-
-    def lower_rows(h, n, a, size):
-        return low0[h, a : a + size] if n == 0 else low_ref[first + h, n - 1, a : a + size]
-
-    lane8 = lax.broadcasted_iota(jnp.int32, (blocks, BLOCK), 1)
-    times = [t // 2 + 8 * (t % 2) for t in range(GROUP)]
-    for h in slots:
-        coef = [cref[h, pl.ds(r, blocks, stride=GROUP), :] for r in range(GROUP)]
-        sol = [(lane8 % GROUP == r).astype(f32) for r in range(GROUP)]
-        for i, s in enumerate(times):
-            pick = (lane8 // GROUP) * GROUP + s
-            for r in times[i + 1 :]:
-                sol[r] = sol[r] - jnp.take_along_axis(coef[r], pick, axis=1) * sol[s]
-        for r in range(GROUP):
-            xref[h, pl.ds(r, blocks, stride=GROUP), :] = sol[r]
+    def at(inner, first_one, h, n):
+        return first_one[first + h] if n == 0 else inner[first + h, n - 1]
+
     for h in slots:
         for n in range(blocks):
-            base = xref[h, n * GROUP : (n + 1) * GROUP, :]
+            if n == 0:
+                base = sol0_ref[pl.ds((first + h) * GROUP, GROUP), :]
+            else:
+                base = sol_ref[first + h, n * GROUP : (n + 1) * GROUP, :]
             dref[h, n] = split(
                 jnp.concatenate(
                     [jnp.where(lane // GROUP == g, base, 0.0) for g in range(BLOCK // GROUP)], 0
@@ -194,7 +203,8 @@
         for h in slots:
             for n in range(blocks):
                 inv = dref[h, n]
-                low = jnp.concatenate([lower_rows(h, n, a, size) for a in starts], 0)
+                lower = at(low_ref, low0_ref, h, n)
+                low = jnp.concatenate([lower[a : a + size] for a in starts], 0)
                 z = split(mm(split(jnp.where(keep, low, 0.0)), inv))
                 twice = []
                 for i in range(len(starts)):
@@ -209,27 +219,42 @@
     for h in slots:
         for n in range(blocks):
             inv = dref[h, n]
-            both = keys_values(h, n)
+            both = at(kv_ref, kv0_ref, h, n)
             w_ref[h, n] = split(mm(inv, both[:, : 2 * dim]))
             u_ref[h, n] = split(mm(inv, both[:, 2 * dim :]))
     for h in slots:
         for n in range(blocks):
-            kbs = key_columns(h, n)
+            kbs = at(kb_ref, kb0_ref, h, n)
             move[h, n] = split(eye - mm(kbs, w_ref[h, n]))
             written[h, n] = mm(kbs, u_ref[h, n])
-    before_map = {h: split(eye) for h in slots}
-    before_state = {h: jnp.zeros((dim, 2 * dim), bf16) for h in slots}
-    for n in range(blocks):
+
+    span = {(h, n, n + 1): (move[h, n], split(written[h, n])) for h in slots for n in range(blocks)}
+
+    def run(h, i, mid, j):
+        later, earlier = span[h, mid, j], span[h, i, mid]
+        state = later[1]
+        added = state[:, :dim].astype(f32) + state[:, dim:].astype(f32)
+        full = (mm(later[0], earlier[0]), mm(later[0], earlier[1]) + added)
+        if (i, j) == (0, blocks):
+            total_ref[h, :, :dim], total_ref[h, :, dim:] = full
+        span[h, i, j] = tuple(split(x) for x in full)
+
+    size = 2
+    while size <= blocks:
         for h in slots:
-            p_ref[h, n] = before_map[h]
-            s_ref[h, n] = before_state[h]
-            map_now = mm(move[h, n], before_map[h])
-            state = mm(move[h, n], before_state[h]) + written[h, n]
-            before_map[h] = split(map_now)
-            before_state[h] = split(state)
-            if n == blocks - 1:
-                total_ref[h, :, :dim] = map_now
-                total_ref[h, :, dim:] = state
+            for i in range(0, blocks, size):
+                run(h, i, i + size // 2, i + size)
+        for j in range(size // 2 + 1, size):
+            low_bit = j & -j
+            if low_bit < size // 2:
+                for h in slots:
+                    run(h, 0, j - low_bit, j)
+        size *= 2
+    for h in slots:
+        p_ref[h, 0] = split(eye)
+        s_ref[h, 0] = jnp.zeros((dim, 2 * dim), bf16)
+        for n in range(1, blocks):
+            p_ref[h, n], s_ref[h, n] = span[h, 0, n]
 
 
 def reads_kernel(
@@ -248,7 +273,7 @@
     for n in range(blocks):
         q = conv_taps(q0, cq, n * HALF, HALF)
         query[rows[n]] = q
-        kbs = kb0_ref[slot] if n == 0 else kb_ref[head, n - 1]
+        kbs = kb0_ref[head] if n == 0 else kb_ref[head, n - 1]
         scores[rows[n]] = split(jnp.where(causal, mm(split(q), kbs), 0.0))
     for n in range(blocks):
         pulled[rows[n]] = split(query[rows[n]] - mm(scores[rows[n]], w_ref[slot, n]))
@@ -258,15 +283,15 @@
         pulled_ref[rows[n]] = split(mm(pulled[rows[n]], p_ref[slot, n]))
 
 
-def out_kernel(slot, half, index_ref, mine_ref, other_ref, gain_ref, *rest):
+def out_kernel(kept, start, half, index_ref, gain_ref, *rest):
     out_ref = rest[-1]
-    for i in range(2):
+    for i in range(len(rest) // 3):
+        state_ref, pulled_ref, local_ref = rest[3 * i : 3 * i + 3]
 
         @pl.when(pl.program_id(0) == i)
         def _():
-            h = first_head(index_ref, i == 0, half) + slot
-            state = mine_ref[0] if i == 0 else other_ref[0]
-            raw = mm(rest[2 * i][...], split(state)) + rest[2 * i + 1][...]
+            h = first_head(index_ref, kept, half) + start + i
+            raw = mm(pulled_ref[...], split(state_ref[0])) + local_ref[...]
             mean = jnp.mean(raw * raw, 1, keepdims=True)
             out_ref[0] = raw * lax.rsqrt(mean + 1e-06) * pick_row(gain_ref[...], h)
 
@@ -290,34 +315,40 @@
         total_ref[h] = then(jnp.where(upper, mine, got), earlier)
 
 
-def join_kernel(bit, index_ref, mine_ref, got_ref, *rest):
-    *before_ref, total_ref, after_ref = rest
-    upper = (index_ref[0] & bit) != 0
-    dim = mine_ref.shape[1]
+def join_kernel(bits, index_ref, *refs):
+    size = 1 << len(bits)
+    got_refs, before_ref, (total_ref, after_ref) = refs[:size], refs[size:-2], refs[-2:]
+    ups = [(index_ref[0] & bit) != 0 for bit in bits]
+    dim = got_refs[0].shape[1]
     row = lax.broadcasted_iota(jnp.int32, (dim, 2 * dim), 0)
     col = lax.broadcasted_iota(jnp.int32, (dim, 2 * dim), 1)
-    for h in range(mine_ref.shape[0]):
-        mine = mine_ref[h]
-        got = got_ref[h]
-        earlier = jnp.where(upper, got, mine)
-        if total_ref.shape[2] == dim:
-            earlier = earlier[:, dim:]
-        total_ref[h] = then(jnp.where(upper, mine, got), earlier)
-        if before_ref:
-            before = before_ref[0][h]
-            after_ref[h] = jnp.where(upper, then(before, got), before)
+    for h in range(got_refs[0].shape[0]):
+        maps = [ref[h] for ref in got_refs]
+        for i, up in enumerate(ups):
+            maps = [jnp.where(up, maps[j ^ (1 << i)], maps[j]) for j in range(size)]
+        part = slice(dim, None) if total_ref.shape[2] == dim else slice(None)
+        identity = (row == col).astype(f32)
+        if size == 2:
+            total_ref[h] = then(maps[1], maps[0][:, part])
+            prefix = jnp.where(ups[0], maps[0], identity)
         else:
-            after_ref[h] = jnp.where(upper, got, (row == col).astype(f32))
+            low = then(maps[1], maps[0])
+            total_ref[h] = then(then(maps[3], maps[2]), low[:, part])
+            prefix = jnp.where(
+                ups[1],
+                jnp.where(ups[0], then(maps[2], low), low),
+                jnp.where(ups[0], maps[0], identity),
+            )
+        after_ref[h] = then(before_ref[0][h], prefix) if before_ref else prefix
 
 
 def down_kernel(bit, index_ref, before_ref, got_ref, earlier_ref, mine_ref, other_ref):
     upper = (index_ref[0] & 1) != 0
-    for h in range(before_ref.shape[0]):
-        got = jnp.where((index_ref[0] & bit) != 0, got_ref[h], 0.0)
-        state = then(before_ref[h], got)
-        after = then(earlier_ref[h], state)
-        mine_ref[h] = jnp.where(upper, after, state)
-        other_ref[h] = jnp.where(upper, state, after)
+    got = jnp.where((index_ref[0] & bit) != 0, got_ref[0], 0.0)
+    state = then(before_ref[0], got)
+    after = then(earlier_ref[0], state)
+    mine_ref[0] = jnp.where(upper, after, state)
+    other_ref[0] = jnp.where(upper, state, after)
 
 
 def tails_kernel(index_ref, query_ref, key_ref, value_ref, out_ref):
@@ -390,28 +421,41 @@
             shape(inner + (4 * dim,), bf16),
             shape(inner + (2 * dim,), bf16),
             shape(inner + (BLOCK,), f32),
-            shape((heads, blocks - 1, GROUP, BLOCK), f32),
+            shape((heads, blocks * GROUP, BLOCK), f32),
             shape((heads, blocks, BLOCK), f32),
         ],
-        [pltpu.VMEM((4, tokens + 8, dim), f32), pltpu.VMEM((blocks, BLOCK), f32)],
+        [
+            pltpu.VMEM((4, tokens + 8, dim), f32),
+            pltpu.VMEM((blocks, BLOCK), f32),
+            pltpu.VMEM((heads, blocks * GROUP, BLOCK), f32),
+        ],
         LIMIT,
     )
-    halo = lax.optimization_barrier((halo, front[-1]))[0]
+    *front, rates = front
+    halo = lax.optimization_barrier((halo, rates))[0]
+    opening = resident(
+        first_kernel,
+        in_order(rates),
+        (key_pairs, value_pairs, halo, conv_key, conv_value, rates),
+        [
+            shape((heads, BLOCK, 4 * dim), bf16),
+            shape((heads, BLOCK, 2 * dim), bf16),
+            shape((heads, BLOCK, BLOCK), f32),
+            shape((heads * GROUP, BLOCK), f32),
+        ],
+        [pltpu.VMEM((heads, 4, HALF + 8, dim), f32), pltpu.VMEM((heads * GROUP, BLOCK), f32)],
+        LIMIT,
+    )
 
     def maps(kept, start, size, *after):
         wide = shape((size, blocks, BLOCK, 2 * dim), bf16)
         return resident(
             functools.partial(maps_kernel, kept, start, half),
             in_order(*after),
-            (key_pairs, value_pairs, halo, conv_key, conv_value, *front),
-            [shape((size, BLOCK, 2 * dim), bf16)] + [wide] * 4 + [shape((size, dim, 2 * dim), f32)],
+            (*front, *opening),
+            [wide] * 4 + [shape((size, dim, 2 * dim), f32)],
             [
-                pltpu.VMEM((4, HALF + 8, dim), f32),
-                pltpu.VMEM((size, BLOCK, 4 * dim), bf16),
-                pltpu.VMEM((size, BLOCK, BLOCK), f32),
                 pltpu.VMEM((size, blocks, BLOCK, 2 * BLOCK), bf16),
-                pltpu.VMEM((size, blocks * GROUP, BLOCK), f32),
-                pltpu.VMEM((size, blocks * GROUP, BLOCK), f32),
                 pltpu.VMEM((size, blocks, dim, 2 * dim), bf16),
                 pltpu.VMEM((size, blocks, dim, dim), f32),
             ],
@@ -423,7 +467,7 @@
         return resident(
             functools.partial(reads_kernel, kept, slot, at, half),
             in_order(*after),
-            (queries, halo, conv_query, front[1], *saved),
+            (queries, halo, conv_query, front[1], opening[1], *saved),
             [shape((tokens, 2 * dim), bf16), shape((tokens, dim), f32)],
             [
                 pltpu.VMEM((tokens + 8, dim), f32),
@@ -441,57 +485,71 @@
         bits.append(2 << len(bits))
     chains = {}
 
-    def begin(at, got):
+    def begin(at, got, *after):
         total, earlier = resident(
-            functools.partial(pair_kernel, at), index, (kept_total[at], got), [total_shape] * 2
+            functools.partial(pair_kernel, at),
+            in_order(*after),
+            (kept_total[at], got),
+            [total_shape] * 2,
         )
-        chains[at] = dict(current=total, earlier=earlier, before=None, left=list(bits))
+        chains[at] = dict(current=total, earlier=earlier, before=(), left=[(bit,) for bit in bits[:-1]])
         send(at)
         return total
 
     def send(at):
         chain = chains[at]
-        chain["got"] = swap(chain["current"], chain["left"][0], count)
+        now = chain["left"][0] if chain["left"] else bits[-1:]
+        flips = [sum(b for i, b in enumerate(now) if j >> i & 1) for j in range(1 << len(now))]
+        chain["got"] = [swap(chain["current"], flip, count) for flip in flips[1:]]
 
     def join(at, *after):
         chain = chains[at]
-        bit = chain["left"].pop(0)
+        now = chain["left"].pop(0)
         got = lax.optimization_barrier((chain["got"], after))[0]
-        before = () if chain["before"] is None else (chain["before"],)
-        last = len(chain["left"]) == 1
-        chain["current"], chain["before"] = resident(
-            functools.partial(join_kernel, bit),
+        chain["current"], before = resident(
+            functools.partial(join_kernel, now),
             index,
-            (chain["current"], got) + before,
-            [state_shape if last else total_shape, total_shape],
+            (chain["current"], *got, *chain["before"]),
+            [total_shape if chain["left"] else state_shape, total_shape],
         )
+        chain["before"] = (before,)
         send(at)
         return chain["current"]
 
     def down(at, *after):
         chain = chains[at]
-        got = lax.optimization_barrier((chain["got"], after))[0]
-        mine, other = resident(
-            functools.partial(down_kernel, bits[-1]), index, (chain["before"], got, chain["earlier"]), [state_shape] * 2
+        got = lax.optimization_barrier((chain["got"], after))[0][0]
+        return resident(
+            functools.partial(down_kernel, bits[-1]),
+            index,
+            (*chain["before"], got, chain["earlier"]),
+            [state_shape] * 2,
         )
-        return mine, swap(other, 1, count)
 
     out_shape = shape((heads, tokens, dim), f32)
-
-    def finish(at, mine, other, done, *after):
+    done = ()
+
+    def finish(kept, start, states, *after):
+        nonlocal done
         vmem = pl.BlockSpec(memory_space=pltpu.VMEM)
 
         def out_block(i, index_ref):
             upper = index_ref[0] & 1
-            return (jnp.where(i == 0, upper, 1 - upper) * half + at, 0, 0)
-
-        args = [mine, other, out_gain, *read[True, at], *read[False, at]]
+            return ((upper if kept else 1 - upper) * half + start + i, 0, 0)
+
+        args = [out_gain]
+        for i, state in enumerate(states):
+            args += [state, *read[kept, start + i]]
         args = [pltpu.with_memory_space_constraint(a, pltpu.VMEM) for a in args]
-        return pl.pallas_call(
-            functools.partial(out_kernel, at, half),
+
+        def kernel(index_ref, *refs):
+            out_kernel(kept, start, half, index_ref, *refs[: len(args)], refs[-1])
+
+        out = pl.pallas_call(
+            kernel,
             grid_spec=pltpu.PrefetchScalarGridSpec(
                 num_scalar_prefetch=1,
-                grid=(2,),
+                grid=(len(states),),
                 in_specs=[vmem] * len(args) + [pl.BlockSpec(memory_space=pl.ANY)] * len(done),
                 out_specs=pl.BlockSpec((1, tokens, dim), out_block),
             ),
@@ -499,6 +557,8 @@
             input_output_aliases={len(args) + 1: 0} if done else {},
             compiler_params=pltpu.CompilerParams(vmem_limit_bytes=LIMIT),
         )(in_order(*after), *args, *done)
+        done = (out,)
+        return out
 
     kept_saved, kept_total, read = {}, {}, {}
 
@@ -511,34 +571,31 @@
     step = begin(0, got)
     for at in range(1, half):
         keep(at, step)
-        for other in range(at):
-            if len(chains[other]["left"]) > 1:
-                step = join(other, kept_total[at])
-        step = begin(at, got)
+        step = begin(at, got, kept_total[at])
+    step = (step,)
     todo = [(kept, at) for at in range(half) for kept in (False, True)]
 
-    def read_one(after):
-        if todo:
+    def read_some(pieces, *after):
+        for _ in range(min(pieces, len(todo))):
             kept, at = todo.pop(0)
-            read[kept, at] = reads(kept, at, after)
-            return read[kept, at][1]
+            read[kept, at] = reads(kept, at, *after)
+            after = tuple(read[kept, at])
         return after
 
-    step = read_one(read_one(step))
-    while any(len(chain["left"]) > 1 for chain in chains.values()):
+    while any(chain["left"] for chain in chains.values()):
         for at in range(half):
-            if len(chains[at]["left"]) > 1:
-                step = read_one(join(at, step))
-    while todo:
-        step = read_one(step)
-    done = ()
-    states = [down(0, step)]
+            if chains[at]["left"]:
+                step = read_some(1, join(at, *step))
+    step = read_some(len(todo), *step)
+    mine, other = {}, {}
     for at in range(half):
-        out = finish(at, *states[at], done)
+        mine[at], other[at] = down(at, *(done or step))
         if at + 1 < half:
-            states.append(down(at + 1, out))
-        done = (out,)
-    return done[0]
+            finish(True, at, [mine[at]])
+    others = swap(jnp.concatenate([other[at] for at in range(half)], 0), 1, count)
+    last = finish(True, half - 1, [mine[half - 1]])
+    others = lax.optimization_barrier((others, last))[0]
+    return finish(False, 0, [others[at : at + 1] for at in range(half)])
 
 
 def solution(mesh):

time: 48.1 us -> 42.3 us (0.88)
  waiting for transfers between devices: 8.18 us -> 5.4 us
  Pallas kernels: 27.8 us -> 25.6 us
  starting transfers between devices: 11.6 us -> 10.8 us
    pallas_call x16 -> x17, Pallas kernels: 24.1 us -> 21.2 us  [resident(): pl.pallas_call(kernel, in_specs=[smem] + [vmem] * len(args), out_specs=[v...]
    ppermute x9 -> x8, waiting for transfers between devices: 5.88 us -> 3.85 us  [swap(): return lax.ppermute(x, 'seq', [(i, i ^ bit) for i in range(count)])]
    ppermute x9 -> x8, starting transfers between devices: 11.1 us -> 10.3 us  [swap(): return lax.ppermute(x, 'seq', [(i, i ^ bit) for i in range(count)])]
    ppermute x1, waiting for transfers between devices: 2.3 us -> 1.55 us  [per_device(): lax.ppermute(tails, 'seq', [(i, (i + 1) % count) for i in range(count)])]
    pallas_call x2 -> x3, Pallas kernels: 2.76 us -> 3.46 us  [finish(): pl.pallas_call(kernel, grid_spec=pltpu.PrefetchScalarGridSpec(num_scalar_...]
  transfers between devices with their start and end apart: 10 -> 9, of which waited for: 6 -> 6; matrix products, arithmetic and copies ran while one was open for 0% -> 0% of each run, Pallas kernels for 38% -> 42%
where the time goes in v6:
time: 42.3 us; the launch traced here: 42.2 us
  Pallas kernels  25.6 us (61%)
  starting transfers between devices  10.8 us (26%)
  waiting for transfers between devices  5.4 us (13%)
    pallas_call x17, Pallas kernels, resident(): pl.pallas_call(kernel, in_specs=[smem] + [vmem] * len(args), out_specs=[v...  21.2 us
    ppermute x8, starting transfers between devices, swap(): return lax.ppermute(x, 'seq', [(i, i ^ bit) for i in range(count)])  10.3 us
    ppermute x8, waiting for transfers between devices, swap(): return lax.ppermute(x, 'seq', [(i, i ^ bit) for i in range(count)])  3.85 us
    pallas_call x3, Pallas kernels, finish(): pl.pallas_call(kernel, grid_spec=pltpu.PrefetchScalarGridSpec(num_scalar_...  3.46 us
    ppermute x1, waiting for transfers between devices, per_device(): lax.ppermute(tails, 'seq', [(i, (i + 1) % count) for i in range(count)])  1.55 us
    pallas_call x1, Pallas kernels, per_device(): pl.pallas_call(tails_kernel, grid_spec=pltpu.PrefetchScalarGridSpec(num_s...  0.96 us
  transfers between devices with their start and end apart: 9, of which 6 were waited for; matrix products, arithmetic and copies ran while one was open for 0% of the time, Pallas kernels for 42%

profile of v6, /device:TPU:0, one launch (start us, length us, event | category | flops | bytes accessed | tf_op | source)
XLA Modules:
  0.0 42.2 jit_solution(364499856253922672)
XLA Ops:
  0.0 1.0 %shard_map.82 = bf16[4,3,640]{2,1,0:T(4,128)(2,1)S(1)} custom-call(s32[1]{0:T(128)} %bitcast.index_ref, bf16[4,512,128]{2,1,0:T(8,128)(2,1)} %query_ref.9, bf16[4,512,256]{2,1,0:T(8,128)(2,1)} %key_ref.5, bf16[4,512,256]{2,1,0:T(8,128)(2,1)} %value_ref.5), custom_call_target="tpu_custom_call" | custom-call | tf_op jit(solution)/shard_map/pallas_call | solution.py:399
  1.6 4.8 %shard_map.83 = (bf16[4,7,128,512]{3,2,1,0:T(8,128)(2,1)S(1)}, bf16[4,7,128,256]{3,2,1,0:T(8,128)(2,1)S(1)}, f32[4,7,128,128]{3,2,1,0:T(8,128)S(1)}, f32[4,128,128]{2,1,0:T(8,128)S(1)}, f32[4,8,128]{2,1,0:T(8,128)S(1)}) custom-call(s32[1]{0:T(128)} %bitcast.index_ref, bf16[4,512,256]{2,1,0:T(8,128)(2,1)S(1)} %copy-done.1, ...), custom_call_target="tpu_custom_call" | custom-call | tf_op jit(solution)/shard_map/pallas_call | solution.py:370
  6.4 1.5 %collective-permute-done.halo_ref = bf16[4,3,640]{2,1,0:T(4,128)(2,1)S(1)} collective-permute-done((bf16[4,3,640]{2,1,0:T(4,128)(2,1)S(1)}, bf16[4,3,640]{2,1,0:T(4,128)(2,1)S(1)}, u32[]{:S(2)}, u32[]{:S(2)}) %collective-permute-start) | collective-permute-done | bytes 15392 | tf_op jit(solution)/shard_map/ppermute | solution.py:410
  8.0 0.9 %shard_map.84 = (bf16[4,128,512]{2,1,0:T(8,128)(2,1)S(1)}, bf16[4,128,256]{2,1,0:T(8,128)(2,1)S(1)}, f32[4,128,128]{2,1,0:T(8,128)S(1)}, f32[64,128]{1,0:T(8,128)S(1)}) custom-call(s32[1]{0:T(128)} %bitcast.index_ref, bf16[4,512,256]{2,1,0:T(8,128)(2,1)S(1)} %copy-done.1, bf16[4,512,256]{2,1,0:T(8,128)(2,1)S(1)} %copy-done.2, ...), custom_call_target="tpu_custom_call" | custom-call | tf_op jit(solution)/shard_map/pallas_call | solution.py:370
  8.9 4.1 %shard_map.85 = (bf16[2,8,128,256]{3,2,1,0:T(8,128)(2,1)S(1)}, bf16[2,8,128,256]{3,2,1,0:T(8,128)(2,1)S(1)}, bf16[2,8,128,256]{3,2,1,0:T(8,128)(2,1)S(1)}, bf16[...) custom-call(s32[1]{0:T(128)} %bitcast.index_ref, bf16[4,7,128,512]{3,2,1,0:T(8,128)(2,1)S(1)} %get-tuple-element.71.kv_ref, ...), custom_call_target="tpu_custom_call" | custom-call | tf_op jit(solution)/shard_map/pallas_call | solution.py:370
  13.0 1.1 %collective-permute-start.1 = (f32[2,128,256]{2,1,0:T(8,128)S(1)}, f32[2,128,256]{2,1,0:T(8,128)S(1)}, u32[]{:S(2)}, u32[]{:S(2)}) collective-permute-start(f32[2,128,256]{2,1,0:T(8,128)S(1)} %get-tuple-element.82), channel_id=1, source_target_pairs={{0,1},{1,0},{2,3},{3,2},{4,5},{5,4},{6,7},{7,6},{8,9},{9,8},{10,11... | collective-permute-start | bytes 786440 | tf_op jit(solution)/shard_map/ppermute | solution.py:381
  14.1 2.5 %shard_map.86 = (bf16[1,8,128,256]{3,2,1,0:T(8,128)(2,1)S(1)}, bf16[1,8,128,256]{3,2,1,0:T(8,128)(2,1)S(1)}, bf16[1,8,128,256]{3,2,1,0:T(8,128)(2,1)S(1)}, bf16[...) custom-call(s32[1]{0:T(128)} %bitcast.index_ref, bf16[4,7,128,512]{3,2,1,0:T(8,128)(2,1)S(1)} %get-tuple-element.71.kv_ref, ...), custom_call_target="tpu_custom_call" | custom-call | tf_op jit(solution)/shard_map/pallas_call | solution.py:370
  16.9 1.6 %collective-permute-start.2 = (f32[1,128,256]{2,1,0:T(8,128)S(1)}, f32[1,128,256]{2,1,0:T(8,128)S(1)}, u32[]{:S(2)}, u32[]{:S(2)}) collective-permute-start(f32[1,128,256]{2,1,0:T(8,128)S(1)} %get-tuple-element.85.refs_0_), channel_id=1, source_target_pairs={{0,2},{1,3},{2,0},{3,1},{4,6},{5,7},{6,4},{7,5},{8,10},{9,11},{10,... | collective-permute-start | bytes 393224 | tf_op jit(solution)/shard_map/ppermute | solution.py:381
  18.4 2.5 %shard_map.88 = (bf16[1,8,128,256]{3,2,1,0:T(8,128)(2,1)S(1)}, bf16[1,8,128,256]{3,2,1,0:T(8,128)(2,1)S(1)}, bf16[1,8,128,256]{3,2,1,0:T(8,128)(2,1)S(1)}, bf16[...) custom-call(s32[1]{0:T(128)} %bitcast.index_ref, bf16[4,7,128,512]{3,2,1,0:T(8,128)(2,1)S(1)} %get-tuple-element.71.kv_ref, ...), custom_call_target="tpu_custom_call" | custom-call | tf_op jit(solution)/shard_map/pallas_call | solution.py:370
  21.2 0.6 %collective-permute-start.4 = (f32[1,128,256]{2,1,0:T(8,128)S(1)}, f32[1,128,256]{2,1,0:T(8,128)S(1)}, u32[]{:S(2)}, u32[]{:S(2)}) collective-permute-start(f32[1,128,256]{2,1,0:T(8,128)S(1)} %get-tuple-element.89.refs_0_), channel_id=1, source_target_pairs={{0,2},{1,3},{2,0},{3,1},{4,6},{5,7},{6,4},{7,5},{8,10},{9,11},{10,... | collective-permute-start | bytes 393224 | tf_op jit(solution)/shard_map/ppermute | solution.py:381
  21.7 0.6 %collective-permute-done.2.refs_1_ = f32[1,128,256]{2,1,0:T(8,128)S(1)} collective-permute-done((f32[1,128,256]{2,1,0:T(8,128)S(1)}, f32[1,128,256]{2,1,0:T(8,128)S(1)}, u32[]{:S(2)}, u32[]{:S(2)}) %collective-permute-start.2) | collective-permute-done | bytes 131104 | tf_op jit(solution)/shard_map/ppermute | solution.py:381
  22.6 1.6 %collective-permute-start.3 = (f32[1,128,256]{2,1,0:T(8,128)S(1)}, f32[1,128,256]{2,1,0:T(8,128)S(1)}, u32[]{:S(2)}, u32[]{:S(2)}) collective-permute-start(f32[1,128,256]{2,1,0:T(8,128)S(1)} %get-tuple-element.91.refs_0_), channel_id=1, source_target_pairs={{0,4},{1,5},{2,6},{3,7},{4,0},{5,1},{6,2},{7,3},{8,12},{9,13},{10,... | collective-permute-start | bytes 393224 | tf_op jit(solution)/shard_map/ppermute | solution.py:381
  24.2 1.1 %shard_map.91 = (bf16[512,256]{1,0:T(8,128)(2,1)S(1)}, f32[512,128]{1,0:T(8,128)S(1)}) custom-call(s32[1]{0:T(128)} %bitcast.index_ref, bf16[4,512,128]{2,1,0:T(8,128)(2,1)S(1)} %copy-done, bf16[4,3,640]{2,1,0:T(4,128)(2,1)S(1)} %collective-permute-done.halo_ref, f32[4,4,128]{2,1,0:T(4,128)S(1)} %copy-done.3, ...), custom_call_target="tpu_custom_call" | custom-call | tf_op jit(solution)/shard_map/pallas_call | solution.py:370
  25.3 1.1 %collective-permute-done.4.refs_1_ = f32[1,128,256]{2,1,0:T(8,128)S(1)} collective-permute-done((f32[1,128,256]{2,1,0:T(8,128)S(1)}, f32[1,128,256]{2,1,0:T(8,128)S(1)}, u32[]{:S(2)}, u32[]{:S(2)}) %collective-permute-start.4) | collective-permute-done | bytes 131104 | tf_op jit(solution)/shard_map/ppermute | solution.py:381
  26.6 1.6 %collective-permute-start.6 = (f32[1,128,256]{2,1,0:T(8,128)S(1)}, f32[1,128,256]{2,1,0:T(8,128)S(1)}, u32[]{:S(2)}, u32[]{:S(2)}) collective-permute-start(f32[1,128,256]{2,1,0:T(8,128)S(1)} %get-tuple-element.100.refs_0_), channel_id=1, source_target_pairs={{0,4},{1,5},{2,6},{3,7},{4,0},{5,1},{6,2},{7,3},{8,12},{9,13},{10,... | collective-permute-start | bytes 393224 | tf_op jit(solution)/shard_map/ppermute | solution.py:381
  28.2 1.2 %shard_map.93 = (bf16[512,256]{1,0:T(8,128)(2,1)S(1)}, f32[512,128]{1,0:T(8,128)S(1)}) custom-call(s32[1]{0:T(128)} %bitcast.index_ref, bf16[4,512,128]{2,1,0:T(8,128)(2,1)S(1)} %copy-done, bf16[4,3,640]{2,1,0:T(4,128)(2,1)S(1)} %collective-permute-done.halo_ref, f32[4,4,128]{2,1,0:T(4,128)S(1)} %copy-done.3, ...), custom_call_target="tpu_custom_call" | custom-call | tf_op jit(solution)/shard_map/pallas_call | solution.py:370
  29.7 2.0 %collective-permute-start.5 = (f32[1,128,128]{2,1,0:T(8,128)S(1)}, f32[1,128,128]{2,1,0:T(8,128)S(1)}, u32[]{:S(2)}, u32[]{:S(2)}) collective-permute-start(f32[1,128,128]{2,1,0:T(8,128)S(1)} %get-tuple-element.111), channel_id=1, source_target_pairs={{0,8},{1,9},{2,10},{3,11},{4,12},{5,13},{6,14},{7,15},{8,0},{9,1},... | collective-permute-start | bytes 196616 | tf_op jit(solution)/shard_map/ppermute | solution.py:381
  31.7 1.0 %shard_map.95 = (bf16[512,256]{1,0:T(8,128)(2,1)S(1)}, f32[512,128]{1,0:T(8,128)S(1)}) custom-call(s32[1]{0:T(128)} %bitcast.index_ref, bf16[4,512,128]{2,1,0:T(8,128)(2,1)S(1)} %copy-done, bf16[4,3,640]{2,1,0:T(4,128)(2,1)S(1)} %collective-permute-done.halo_ref, f32[4,4,128]{2,1,0:T(4,128)S(1)} %copy-done.3, ...), custom_call_target="tpu_custom_call" | custom-call | tf_op jit(solution)/shard_map/pallas_call | solution.py:370
  33.0 1.7 %collective-permute-start.7 = (f32[1,128,128]{2,1,0:T(8,128)S(1)}, f32[1,128,128]{2,1,0:T(8,128)S(1)}, u32[]{:S(2)}, u32[]{:S(2)}) collective-permute-start(f32[1,128,128]{2,1,0:T(8,128)S(1)} %get-tuple-element.117), channel_id=1, source_target_pairs={{0,8},{1,9},{2,10},{3,11},{4,12},{5,13},{6,14},{7,15},{8,0},{9,1},... | collective-permute-start | bytes 196616 | tf_op jit(solution)/shard_map/ppermute | solution.py:381
  34.7 1.0 %shard_map.97 = (bf16[512,256]{1,0:T(8,128)(2,1)S(1)}, f32[512,128]{1,0:T(8,128)S(1)}) custom-call(s32[1]{0:T(128)} %bitcast.index_ref, bf16[4,512,128]{2,1,0:T(8,128)(2,1)S(1)} %copy-done, bf16[4,3,640]{2,1,0:T(4,128)(2,1)S(1)} %collective-permute-done.halo_ref, f32[4,4,128]{2,1,0:T(4,128)S(1)} %copy-done.3, ...), custom_call_target="tpu_custom_call" | custom-call | tf_op jit(solution)/shard_map/pallas_call | solution.py:370
  36.7 1.0 %shard_map.99.refs_4_ = f32[4,512,128]{2,1,0:T(8,128)} custom-call(s32[1]{0:T(128)} %bitcast.index_ref, f32[4,128]{1,0:T(4,128)S(1)} %copy-done.6, f32[1,128,128]{2,1,0:T(8,128)S(1)} %get-tuple-element.129.refs_1_, bf16[512,256]{1,0:T(8,128)(2,1)S(1)} %get-tuple-element.106.refs_2_, f32[512,128]{1,0:T(8,128)S(1)} %get-tuple-element.107.refs_3_), custom_call_target="tpu_custom_call" | custom-call | tf_op jit(solution)/shard_map/pallas_call | solution.py:548
  37.7 1.2 %collective-permute-done.7.got_ref = f32[1,128,128]{2,1,0:T(8,128)S(1)} collective-permute-done((f32[1,128,128]{2,1,0:T(8,128)S(1)}, f32[1,128,128]{2,1,0:T(8,128)S(1)}, u32[]{:S(2)}, u32[]{:S(2)}) %collective-permute-start.7) | collective-permute-done | bytes 65568 | tf_op jit(solution)/shard_map/ppermute | solution.py:381
  39.4 1.0 %shard_map.101.refs_7_ = f32[4,512,128]{2,1,0:T(8,128)} custom-call(s32[1]{0:T(128)} %bitcast.index_ref, f32[4,128]{1,0:T(4,128)S(1)} %copy-done.6, f32[1,128,128]{2,1,0:T(8,128)S(1)} %get-tuple-element.133.refs_1_, bf16[512,256]{1,0:T(8,128)(2,1)S(1)} %get-tuple-element.123.refs_2_, ...), custom_call_target="tpu_custom_call", output_to_operand_aliasing={{}: (5, {})} | custom-call | tf_op jit(solution)/shard_map/pallas_call | solution.py:548
  40.8 1.4 %shard_map.102 = f32[4,512,128]{2,1,0:T(8,128)} custom-call(s32[1]{0:T(128)} %bitcast.index_ref, f32[4,128]{1,0:T(4,128)S(1)} %copy-done.6, f32[1,128,128]{2,1,0:T(8,128)S(1)} %get-tuple-element.136.refs_1_, bf16[512,256]{1,0:T(8,128)(2,1)S(1)} %get-tuple-element.97.refs_2_, ...), custom_call_target="tpu_custom_call", output_to_operand_aliasing={{}: (8, {})} | custom-call | tf_op jit(solution)/shard_map/pallas_call | solution.py:548
  (33 shorter events, 3.6 us)
Async XLA Ops:
  0.0 1.5 %copy-start.2 = (bf16[4,512,256]{2,1,0:T(8,128)(2,1)S(1)}, bf16[4,512,256]{2,1,0:T(8,128)(2,1)}, u32[]{:S(2)}) copy-start(bf16[4,512,256]{2,1,0:T(8,128)(2,1)} %value_ref.5) | copy-start | bytes 3145732
  0.0 1.6 %copy-start.1 = (bf16[4,512,256]{2,1,0:T(8,128)(2,1)S(1)}, bf16[4,512,256]{2,1,0:T(8,128)(2,1)}, u32[]{:S(2)}) copy-start(bf16[4,512,256]{2,1,0:T(8,128)(2,1)} %key_ref.5) | copy-start | bytes 3145732
  0.0 1.6 %copy-start.5 = (f32[4,4,256]{2,1,0:T(4,128)S(1)}, f32[4,4,256]{2,1,0:T(4,128)}, u32[]{:S(2)}) copy-start(f32[4,4,256]{2,1,0:T(4,128)} %cv_ref.3) | copy-start | bytes 49156
  0.0 1.6 %copy-start.4 = (f32[4,4,256]{2,1,0:T(4,128)S(1)}, f32[4,4,256]{2,1,0:T(4,128)}, u32[]{:S(2)}) copy-start(f32[4,4,256]{2,1,0:T(4,128)} %ck_ref.3) | copy-start | bytes 49156
  0.0 1.6 %copy-start.7 = (f32[4,1024]{1,0:T(4,128)S(1)}, f32[4,1024]{1,0:T(4,128)}, u32[]{:S(2)}) copy-start(f32[4,1024]{1,0:T(4,128)} %rate_ref.1) | copy-start | bytes 49156
  1.0 7.0 %collective-permute-start = (bf16[4,3,640]{2,1,0:T(4,128)(2,1)S(1)}, bf16[4,3,640]{2,1,0:T(4,128)(2,1)S(1)}, u32[]{:S(2)}, u32[]{:S(2)}) collective-permute-start(bf16[4,3,640]{2,1,0:T(4,128)(2,1)S(1)} %shard_map.82), channel_id=1, source_target_pairs={{0,1},{1,2},{2,3},{3,4},{4,5},{5,6},{6,7},{7,8},{8,9},{9,10},{10,1... | collective-permute-start | bytes 46088 | tf_op jit(solution)/shard_map/ppermute | solution.py:410
  13.0 3.6 %collective-permute-start.1 = (f32[2,128,256]{2,1,0:T(8,128)S(1)}, f32[2,128,256]{2,1,0:T(8,128)S(1)}, u32[]{:S(2)}, u32[]{:S(2)}) collective-permute-start(f32[2,128,256]{2,1,0:T(8,128)S(1)} %get-tuple-element.82), channel_id=1, source_target_pairs={{0,1},{1,0},{2,3},{3,2},{4,5},{5,4},{6,7},{7,6},{8,9},{9,8},{10,11... | collective-permute-start | bytes 786440 | tf_op jit(solution)/shard_map/ppermute | solution.py:381
  16.8 7.4 %copy-start = (bf16[4,512,128]{2,1,0:T(8,128)(2,1)S(1)}, bf16[4,512,128]{2,1,0:T(8,128)(2,1)}, u32[]{:S(2)}) copy-start(bf16[4,512,128]{2,1,0:T(8,128)(2,1)} %query_ref.9) | copy-start | bytes 1572868
  16.9 7.3 %copy-start.3 = (f32[4,4,128]{2,1,0:T(4,128)S(1)}, f32[4,4,128]{2,1,0:T(4,128)}, u32[]{:S(2)}) copy-start(f32[4,4,128]{2,1,0:T(4,128)} %cq_ref.7) | copy-start | bytes 24580
  16.9 5.5 %collective-permute-start.2 = (f32[1,128,256]{2,1,0:T(8,128)S(1)}, f32[1,128,256]{2,1,0:T(8,128)S(1)}, u32[]{:S(2)}, u32[]{:S(2)}) collective-permute-start(f32[1,128,256]{2,1,0:T(8,128)S(1)} %get-tuple-element.85.refs_0_), channel_id=1, source_target_pairs={{0,2},{1,3},{2,0},{3,1},{4,6},{5,7},{6,4},{7,5},{8,10},{9,11},{10,... | collective-permute-start | bytes 393224 | tf_op jit(solution)/shard_map/ppermute | solution.py:381
  21.2 5.2 %collective-permute-start.4 = (f32[1,128,256]{2,1,0:T(8,128)S(1)}, f32[1,128,256]{2,1,0:T(8,128)S(1)}, u32[]{:S(2)}, u32[]{:S(2)}) collective-permute-start(f32[1,128,256]{2,1,0:T(8,128)S(1)} %get-tuple-element.89.refs_0_), channel_id=1, source_target_pairs={{0,2},{1,3},{2,0},{3,1},{4,6},{5,7},{6,4},{7,5},{8,10},{9,11},{10,... | collective-permute-start | bytes 393224 | tf_op jit(solution)/shard_map/ppermute | solution.py:381
  22.6 6.9 %collective-permute-start.3 = (f32[1,128,256]{2,1,0:T(8,128)S(1)}, f32[1,128,256]{2,1,0:T(8,128)S(1)}, u32[]{:S(2)}, u32[]{:S(2)}) collective-permute-start(f32[1,128,256]{2,1,0:T(8,128)S(1)} %get-tuple-element.91.refs_0_), channel_id=1, source_target_pairs={{0,4},{1,5},{2,6},{3,7},{4,0},{5,1},{6,2},{7,3},{8,12},{9,13},{10,... | collective-permute-start | bytes 393224 | tf_op jit(solution)/shard_map/ppermute | solution.py:381
  26.6 6.2 %collective-permute-start.6 = (f32[1,128,256]{2,1,0:T(8,128)S(1)}, f32[1,128,256]{2,1,0:T(8,128)S(1)}, u32[]{:S(2)}, u32[]{:S(2)}) collective-permute-start(f32[1,128,256]{2,1,0:T(8,128)S(1)} %get-tuple-element.100.refs_0_), channel_id=1, source_target_pairs={{0,4},{1,5},{2,6},{3,7},{4,0},{5,1},{6,2},{7,3},{8,12},{9,13},{10,... | collective-permute-start | bytes 393224 | tf_op jit(solution)/shard_map/ppermute | solution.py:381
  29.7 6.6 %collective-permute-start.5 = (f32[1,128,128]{2,1,0:T(8,128)S(1)}, f32[1,128,128]{2,1,0:T(8,128)S(1)}, u32[]{:S(2)}, u32[]{:S(2)}) collective-permute-start(f32[1,128,128]{2,1,0:T(8,128)S(1)} %get-tuple-element.111), channel_id=1, source_target_pairs={{0,8},{1,9},{2,10},{3,11},{4,12},{5,13},{6,14},{7,15},{8,0},{9,1},... | collective-permute-start | bytes 196616 | tf_op jit(solution)/shard_map/ppermute | solution.py:381
  33.0 5.9 %collective-permute-start.7 = (f32[1,128,128]{2,1,0:T(8,128)S(1)}, f32[1,128,128]{2,1,0:T(8,128)S(1)}, u32[]{:S(2)}, u32[]{:S(2)}) collective-permute-start(f32[1,128,128]{2,1,0:T(8,128)S(1)} %get-tuple-element.117), channel_id=1, source_target_pairs={{0,8},{1,9},{2,10},{3,11},{4,12},{5,13},{6,14},{7,15},{8,0},{9,1},... | collective-permute-start | bytes 196616 | tf_op jit(solution)/shard_map/ppermute | solution.py:381
  34.7 2.0 %copy-start.6 = (f32[4,128]{1,0:T(4,128)S(1)}, f32[4,128]{1,0:T(4,128)}, u32[]{:S(2)}) copy-start(f32[4,128]{1,0:T(4,128)} %refs_0_.5) | copy-start | bytes 6148
  39.3 1.4 %collective-permute-start.8 = (f32[2,128,128]{2,1,0:T(8,128)S(1)}, f32[2,128,128]{2,1,0:T(8,128)S(1)}, u32[]{:S(2)}, u32[]{:S(2)}) collective-permute-start(f32[2,128,128]{2,1,0:T(8,128)S(1)} %pad_maximum_fusion), channel_id=1, source_target_pairs={{0,1},{1,0},{2,3},{3,2},{4,5},{5,4},{6,7},{7,6},{8,9},{9,8},{10,11... | collective-permute-start | bytes 393224 | tf_op jit(solution)/shard_map/ppermute | solution.py:381

commit v7 on v6

--- a/solution.py
+++ b/solution.py
@@ -74,21 +74,27 @@
     return row, col, lane
 
 
-def block_inputs(key_rows, value_rows, ck, cv, t0, rates):
+def block_inputs(units, keys):
     row, col, lane = block_masks()
-    dim = key_rows[0].shape[1]
-    ka, kb = [conv_taps(r, ck[:, j * dim : (j + 1) * dim], t0, HALF) for j, r in enumerate(key_rows)]
-    keys = interleave(ka, kb)
-    keys = keys * lax.rsqrt(jnp.sum(keys * keys, 1, keepdims=True) + 1e-06)
-    va, vb = [conv_taps(r, cv[:, j * dim : (j + 1) * dim], t0, HALF) for j, r in enumerate(value_rows)]
-    ks = split(keys)
-    kv = jnp.concatenate([ks, split(interleave(va, vb))], 1)
-    kbs = split(keys.T * rates)
-    lower = jnp.where(step_time(col) < step_time(row), mm(ks, kbs), 0.0)
-    diag = jnp.zeros((GROUP, BLOCK), f32)
-    for g in range(BLOCK // GROUP):
-        diag = jnp.where(lane // GROUP == g, lower[g * GROUP : (g + 1) * GROUP], diag)
-    return kv, kbs, lower, diag
+    strict = step_time(col) < step_time(row)
+    for i, (rows, ck, cv, t0, rates, kv, kb, low, diag) in enumerate(units):
+        dim = rows[0].shape[1]
+        taps = [w[:, j * dim : (j + 1) * dim] for w in (ck, cv) for j in range(2)]
+        ka, kb_, va, vb = [conv_taps(r, w, t0, HALF) for r, w in zip(rows, taps)]
+        k = interleave(ka, kb_)
+        k = k * lax.rsqrt(jnp.sum(k * k, 1, keepdims=True) + 1e-06)
+        keys[i] = k
+        kv[:, : 2 * dim] = split(k)
+        kv[:, 2 * dim :] = split(interleave(va, vb))
+    for i, (rows, ck, cv, t0, rates, kv, kb, low, diag) in enumerate(units):
+        kb[...] = split(keys[i].T * rates)
+    for i, (rows, ck, cv, t0, rates, kv, kb, low, diag) in enumerate(units):
+        lower = jnp.where(strict, mm(kv[:, : kb.shape[1]], kb[...]), 0.0)
+        low[...] = lower
+        groups = jnp.zeros((GROUP, BLOCK), f32)
+        for g in range(BLOCK // GROUP):
+            groups = jnp.where(lane // GROUP == g, lower[g * GROUP : (g + 1) * GROUP], groups)
+        diag[...] = groups
 
 
 def invert_groups(diag, out, blocks):
@@ -106,7 +112,7 @@
 
 def front_kernel(
     index_ref, key_ref, value_ref, rate_ref, ck_ref, cv_ref,
-    kv_ref, kb_ref, low_ref, sol_ref, rates_ref, rows, brow, diag,
+    kv_ref, kb_ref, low_ref, sol_ref, rates_ref, rows, brow, diag, keys,
 ):
     dim = rows.shape[2]
     blocks = rates_ref.shape[1]
@@ -123,12 +129,18 @@
             brow[...], order, precision=lax.Precision.HIGHEST, preferred_element_type=f32
         )
         rates_ref[h] = rates
-        for n in range(1, blocks):
-            kv_ref[h, n - 1], kb_ref[h, n - 1], low_ref[h, n - 1], groups = block_inputs(
-                [rows.at[0], rows.at[1]], [rows.at[2], rows.at[3]],
-                ck_ref[h], cv_ref[h], n * HALF, rates[n : n + 1],
-            )
-            diag[h, n * GROUP : (n + 1) * GROUP] = groups
+        ck, cv = ck_ref[h], cv_ref[h]
+        block_inputs(
+            [
+                (
+                    [rows.at[i] for i in range(4)], ck, cv, n * HALF, rates[n : n + 1],
+                    kv_ref.at[h, n - 1], kb_ref.at[h, n - 1], low_ref.at[h, n - 1],
+                    diag.at[h, n * GROUP : (n + 1) * GROUP],
+                )
+                for n in range(1, blocks)
+            ],
+            keys,
+        )
         diag[h, 0:GROUP] = jnp.zeros((GROUP, BLOCK), f32)
         return carry
 
@@ -139,7 +151,7 @@
 
 def first_kernel(
     index_ref, key_ref, value_ref, halo_ref, ck_ref, cv_ref, rates_ref,
-    kv_ref, kb_ref, low_ref, sol_ref, rows, diag,
+    kv_ref, kb_ref, low_ref, sol_ref, rows, diag, keys,
 ):
     heads = key_ref.shape[0]
     dim = rows.shape[3]
@@ -153,12 +165,16 @@
                     halo[:, at : at + dim],
                     ref[h, :HALF, j * dim : (j + 1) * dim],
                 )
-    for h in range(heads):
-        kv_ref[h], kb_ref[h], low_ref[h], groups = block_inputs(
-            [rows.at[h, 0], rows.at[h, 1]], [rows.at[h, 2], rows.at[h, 3]],
-            ck_ref[h], cv_ref[h], 0, rates_ref[h][0:1],
-        )
-        diag[h * GROUP : (h + 1) * GROUP] = groups
+    block_inputs(
+        [
+            (
+                [rows.at[h, i] for i in range(4)], ck_ref[h], cv_ref[h], 0, rates_ref[h][0:1],
+                kv_ref.at[h], kb_ref.at[h], low_ref.at[h], diag.at[h * GROUP : (h + 1) * GROUP],
+            )
+            for h in range(heads)
+        ],
+        keys,
+    )
     invert_groups(diag, sol_ref, heads)
 
 
@@ -169,10 +185,9 @@
 def maps_kernel(
     kept, start, half, index_ref, kv_ref, kb_ref, low_ref, sol_ref,
     kv0_ref, kb0_ref, low0_ref, sol0_ref,
-    w_ref, u_ref, p_ref, s_ref, total_ref,
-    dref, move, written,
+    inv_ref, p_ref, s_ref, total_ref, move, written,
 ):
-    count, blocks = w_ref.shape[:2]
+    count, blocks = inv_ref.shape[:2]
     dim = total_ref.shape[1]
     slots = range(count)
     first = first_head(index_ref, kept, half) + start
@@ -188,7 +203,7 @@
                 base = sol0_ref[pl.ds((first + h) * GROUP, GROUP), :]
             else:
                 base = sol_ref[first + h, n * GROUP : (n + 1) * GROUP, :]
-            dref[h, n] = split(
+            inv_ref[h, n] = split(
                 jnp.concatenate(
                     [jnp.where(lane // GROUP == g, base, 0.0) for g in range(BLOCK // GROUP)], 0
                 )
@@ -202,7 +217,7 @@
         starts = range(size, BLOCK, 2 * size)
         for h in slots:
             for n in range(blocks):
-                inv = dref[h, n]
+                inv = inv_ref[h, n]
                 lower = at(low_ref, low0_ref, h, n)
                 low = jnp.concatenate([lower[a : a + size] for a in starts], 0)
                 z = split(mm(split(jnp.where(keep, low, 0.0)), inv))
@@ -213,22 +228,20 @@
                 new = mm(odd, jnp.concatenate(twice, 0))
                 new = split(odd[:, :BLOCK].astype(f32) + odd[:, BLOCK:].astype(f32) - new)
                 for i, a in enumerate(starts):
-                    dref[h, n, a : a + size] = new[i * size : (i + 1) * size]
+                    inv_ref[h, n, a : a + size] = new[i * size : (i + 1) * size]
         size *= 2
 
     for h in slots:
         for n in range(blocks):
-            inv = dref[h, n]
-            both = at(kv_ref, kv0_ref, h, n)
-            w_ref[h, n] = split(mm(inv, both[:, : 2 * dim]))
-            u_ref[h, n] = split(mm(inv, both[:, 2 * dim :]))
+            move[h, n] = split(mm(at(kb_ref, kb0_ref, h, n), inv_ref[h, n]))
     for h in slots:
         for n in range(blocks):
-            kbs = at(kb_ref, kb0_ref, h, n)
-            move[h, n] = split(eye - mm(kbs, w_ref[h, n]))
-            written[h, n] = mm(kbs, u_ref[h, n])
-
-    span = {(h, n, n + 1): (move[h, n], split(written[h, n])) for h in slots for n in range(blocks)}
+            both = at(kv_ref, kv0_ref, h, n)
+            solved = move[h, n]
+            written[h, n] = split(mm(solved, both[:, 2 * dim :]))
+            move[h, n] = split(eye - mm(solved, both[:, : 2 * dim]))
+
+    span = {(h, n, n + 1): (move[h, n], written[h, n]) for h in slots for n in range(blocks)}
 
     def run(h, i, mid, j):
         later, earlier = span[h, mid, j], span[h, i, mid]
@@ -258,12 +271,12 @@
 
 
 def reads_kernel(
-    kept, slot, at, half, index_ref, query_ref, halo_ref, cq_ref, kb_ref, kb0_ref, w_ref, u_ref, p_ref, s_ref,
-    pulled_ref, local_ref, q0, query, scores, pulled,
+    kept, slot, at, half, index_ref, query_ref, halo_ref, cq_ref, kv_ref, kb_ref, kv0_ref, kb0_ref,
+    inv_ref, p_ref, s_ref, pulled_ref, local_ref, q0, query, scores, pulled,
 ):
     head = first_head(index_ref, kept, half) + at
     dim = q0.shape[1]
-    blocks = w_ref.shape[1]
+    blocks = inv_ref.shape[1]
     fill_rows(q0, own_halo(index_ref, halo_ref[head])[:, :dim], query_ref[head])
     cq = cq_ref[head]
     row = lax.broadcasted_iota(jnp.int32, (HALF, BLOCK), 0)
@@ -276,8 +289,11 @@
         kbs = kb0_ref[head] if n == 0 else kb_ref[head, n - 1]
         scores[rows[n]] = split(jnp.where(causal, mm(split(q), kbs), 0.0))
     for n in range(blocks):
-        pulled[rows[n]] = split(query[rows[n]] - mm(scores[rows[n]], w_ref[slot, n]))
-        local_ref[rows[n]] = mm(scores[rows[n]], u_ref[slot, n])
+        scores[rows[n]] = split(mm(scores[rows[n]], inv_ref[slot, n]))
+    for n in range(blocks):
+        both = kv0_ref[head] if n == 0 else kv_ref[head, n - 1]
+        pulled[rows[n]] = split(query[rows[n]] - mm(scores[rows[n]], both[:, : 2 * dim]))
+        local_ref[rows[n]] = mm(scores[rows[n]], both[:, 2 * dim :])
     for n in range(blocks):
         local_ref[rows[n]] += mm(pulled[rows[n]], s_ref[slot, n])
         pulled_ref[rows[n]] = split(mm(pulled[rows[n]], p_ref[slot, n]))
@@ -291,9 +307,13 @@
         @pl.when(pl.program_id(0) == i)
         def _():
             h = first_head(index_ref, kept, half) + start + i
-            raw = mm(pulled_ref[...], split(state_ref[0])) + local_ref[...]
-            mean = jnp.mean(raw * raw, 1, keepdims=True)
-            out_ref[0] = raw * lax.rsqrt(mean + 1e-06) * pick_row(gain_ref[...], h)
+            state = split(state_ref[0])
+            gain = pick_row(gain_ref[...], h)
+            for at in range(0, pulled_ref.shape[0], BLOCK):
+                rows = slice(at, at + BLOCK)
+                raw = mm(pulled_ref[rows], state) + local_ref[rows]
+                mean = jnp.mean(raw * raw, 1, keepdims=True)
+                out_ref[0, rows] = raw * lax.rsqrt(mean + 1e-06) * gain
 
 
 def then(later, earlier):
@@ -428,6 +448,7 @@
             pltpu.VMEM((4, tokens + 8, dim), f32),
             pltpu.VMEM((blocks, BLOCK), f32),
             pltpu.VMEM((heads, blocks * GROUP, BLOCK), f32),
+            pltpu.VMEM((blocks - 1, BLOCK, dim), f32),
         ],
         LIMIT,
     )
@@ -443,7 +464,11 @@
             shape((heads, BLOCK, BLOCK), f32),
             shape((heads * GROUP, BLOCK), f32),
         ],
-        [pltpu.VMEM((heads, 4, HALF + 8, dim), f32), pltpu.VMEM((heads * GROUP, BLOCK), f32)],
+        [
+            pltpu.VMEM((heads, 4, HALF + 8, dim), f32),
+            pltpu.VMEM((heads * GROUP, BLOCK), f32),
+            pltpu.VMEM((heads, BLOCK, dim), f32),
+        ],
         LIMIT,
     )
 
@@ -453,12 +478,8 @@
             functools.partial(maps_kernel, kept, start, half),
             in_order(*after),
             (*front, *opening),
-            [wide] * 4 + [shape((size, dim, 2 * dim), f32)],
-            [
-                pltpu.VMEM((size, blocks, BLOCK, 2 * BLOCK), bf16),
-                pltpu.VMEM((size, blocks, dim, 2 * dim), bf16),
-                pltpu.VMEM((size, blocks, dim, dim), f32),
-            ],
+            [wide] * 3 + [shape((size, dim, 2 * dim), f32)],
+            [pltpu.VMEM((size, blocks, dim, 2 * dim), bf16)] * 2,
             LIMIT,
         )
 
@@ -467,7 +488,7 @@
         return resident(
             functools.partial(reads_kernel, kept, slot, at, half),
             in_order(*after),
-            (queries, halo, conv_query, front[1], opening[1], *saved),
+            (queries, halo, conv_query, *front[:2], *opening[:2], *saved),
             [shape((tokens, 2 * dim), bf16), shape((tokens, dim), f32)],
             [
                 pltpu.VMEM((tokens + 8, dim), f32),
@@ -585,15 +606,16 @@
     while any(chain["left"] for chain in chains.values()):
         for at in range(half):
             if chains[at]["left"]:
-                step = read_some(1, join(at, *step))
+                step = (join(at, *step),)
+                if at == 0 or len(todo) > 1 + half:
+                    step = read_some(1, *step)
     step = read_some(len(todo), *step)
     mine, other = {}, {}
     for at in range(half):
-        mine[at], other[at] = down(at, *(done or step))
-        if at + 1 < half:
-            finish(True, at, [mine[at]])
+        mine[at], other[at] = down(at, *step)
+        step = (mine[at],)
     others = swap(jnp.concatenate([other[at] for at in range(half)], 0), 1, count)
-    last = finish(True, half - 1, [mine[half - 1]])
+    last = finish(True, 0, [mine[at] for at in range(half)])
     others = lax.optimization_barrier((others, last))[0]
     return finish(False, 0, [others[at : at + 1] for at in range(half)])
 

time: 42.3 us -> 41 us (0.969)
  waiting for transfers between devices: 5.4 us -> 3.78 us
    ppermute x8, waiting for transfers between devices: 3.85 us -> 2.31 us  [swap(): return lax.ppermute(x, 'seq', [(i, i ^ bit) for i in range(count)])]
    pallas_call x3 -> x2, Pallas kernels: 3.46 us -> 2.85 us  [finish(): pl.pallas_call(kernel, grid_spec=pltpu.PrefetchScalarGridSpec(num_scalar_...]
    pallas_call x17, Pallas kernels: 21.2 us -> 21.7 us  [resident(): pl.pallas_call(kernel, in_specs=[smem] + [vmem] * len(args), out_specs=[v...]
    ppermute x8, starting transfers between devices: 10.3 us -> 10.7 us  [swap(): return lax.ppermute(x, 'seq', [(i, i ^ bit) for i in range(count)])]
  transfers between devices with their start and end apart: 9 -> 9, of which waited for: 6 -> 5; matrix products, arithmetic and copies ran while one was open for 0% -> 0% of each run, Pallas kernels for 42% -> 43%
where the time goes in v7:
time: 41 us; the launch traced here: 40.8 us
  Pallas kernels  25.5 us (62%)
  starting transfers between devices  11.2 us (27%)
  waiting for transfers between devices  3.78 us (9%)
    pallas_call x17, Pallas kernels, resident(): pl.pallas_call(kernel, in_specs=[smem] + [vmem] * len(args), out_specs=[v...  21.7 us
    ppermute x8, starting transfers between devices, swap(): return lax.ppermute(x, 'seq', [(i, i ^ bit) for i in range(count)])  10.7 us
    pallas_call x2, Pallas kernels, finish(): pl.pallas_call(kernel, grid_spec=pltpu.PrefetchScalarGridSpec(num_scalar_...  2.85 us
    ppermute x8, waiting for transfers between devices, swap(): return lax.ppermute(x, 'seq', [(i, i ^ bit) for i in range(count)])  2.31 us
    ppermute x1, waiting for transfers between devices, per_device(): lax.ppermute(tails, 'seq', [(i, (i + 1) % count) for i in range(count)])  1.47 us
    pallas_call x1, Pallas kernels, per_device(): pl.pallas_call(tails_kernel, grid_spec=pltpu.PrefetchScalarGridSpec(num_s...  0.96 us
  transfers between devices with their start and end apart: 9, of which 5 were waited for; matrix products, arithmetic and copies ran while one was open for 0% of the time, Pallas kernels for 43%

profile of v7, /device:TPU:0, one launch (start us, length us, event | category | flops | bytes accessed | tf_op | source)
XLA Modules:
  0.0 40.8 jit_solution(16637990821563456215)
XLA Ops:
  0.0 1.0 %shard_map.82 = bf16[4,3,640]{2,1,0:T(4,128)(2,1)S(1)} custom-call(s32[1]{0:T(128)} %bitcast.index_ref, bf16[4,512,128]{2,1,0:T(8,128)(2,1)} %query_ref.9, bf16[4,512,256]{2,1,0:T(8,128)(2,1)} %key_ref.5, bf16[4,512,256]{2,1,0:T(8,128)(2,1)} %value_ref.5), custom_call_target="tpu_custom_call" | custom-call | tf_op jit(solution)/shard_map/pallas_call | solution.py:419
  1.0 0.5 %collective-permute-start = (bf16[4,3,640]{2,1,0:T(4,128)(2,1)S(1)}, bf16[4,3,640]{2,1,0:T(4,128)(2,1)S(1)}, u32[]{:S(2)}, u32[]{:S(2)}) collective-permute-start(bf16[4,3,640]{2,1,0:T(4,128)(2,1)S(1)} %shard_map.82), channel_id=1, source_target_pairs={{0,1},{1,2},{2,3},{3,4},{4,5},{5,6},{6,7},{7,8},{8,9},{9,10},{10,1... | collective-permute-start | bytes 46088 | tf_op jit(solution)/shard_map/ppermute | solution.py:430
  1.6 4.9 %shard_map.83 = (bf16[4,7,128,512]{3,2,1,0:T(8,128)(2,1)S(1)}, bf16[4,7,128,256]{3,2,1,0:T(8,128)(2,1)S(1)}, f32[4,7,128,128]{3,2,1,0:T(8,128)S(1)}, f32[4,128,128]{2,1,0:T(8,128)S(1)}, f32[4,8,128]{2,1,0:T(8,128)S(1)}) custom-call(s32[1]{0:T(128)} %bitcast.index_ref, bf16[4,512,256]{2,1,0:T(8,128)(2,1)S(1)} %copy-done.1, ...), custom_call_target="tpu_custom_call" | custom-call | tf_op jit(solution)/shard_map/pallas_call | solution.py:390
  6.5 1.5 %collective-permute-done.halo_ref = bf16[4,3,640]{2,1,0:T(4,128)(2,1)S(1)} collective-permute-done((bf16[4,3,640]{2,1,0:T(4,128)(2,1)S(1)}, bf16[4,3,640]{2,1,0:T(4,128)(2,1)S(1)}, u32[]{:S(2)}, u32[]{:S(2)}) %collective-permute-start) | collective-permute-done | bytes 15392 | tf_op jit(solution)/shard_map/ppermute | solution.py:430
  8.0 1.0 %shard_map.84 = (bf16[4,128,512]{2,1,0:T(8,128)(2,1)S(1)}, bf16[4,128,256]{2,1,0:T(8,128)(2,1)S(1)}, f32[4,128,128]{2,1,0:T(8,128)S(1)}, f32[64,128]{1,0:T(8,128)S(1)}) custom-call(s32[1]{0:T(128)} %bitcast.index_ref, bf16[4,512,256]{2,1,0:T(8,128)(2,1)S(1)} %copy-done.1, bf16[4,512,256]{2,1,0:T(8,128)(2,1)S(1)} %copy-done.2, ...), custom_call_target="tpu_custom_call" | custom-call | tf_op jit(solution)/shard_map/pallas_call | solution.py:390
  8.9 3.9 %shard_map.85 = (bf16[2,8,128,256]{3,2,1,0:T(8,128)(2,1)S(1)}, bf16[2,8,128,256]{3,2,1,0:T(8,128)(2,1)S(1)}, bf16[2,8,128,256]{3,2,1,0:T(8,128)(2,1)S(1)}, f32[2,128,256]{2,1,0:T(8,128)S(1)}) custom-call(s32[1]{0:T(128)} %bitcast.index_ref, bf16[4,7,128,512]{3,2,1,0:T(8,128)(2,1)S(1)} %get-tuple-element.68.kv_ref, ...), custom_call_target="tpu_custom_call" | custom-call | tf_op jit(solution)/shard_map/pallas_call | solution.py:390
  12.8 1.2 %collective-permute-start.1 = (f32[2,128,256]{2,1,0:T(8,128)S(1)}, f32[2,128,256]{2,1,0:T(8,128)S(1)}, u32[]{:S(2)}, u32[]{:S(2)}) collective-permute-start(f32[2,128,256]{2,1,0:T(8,128)S(1)} %get-tuple-element.79), channel_id=1, source_target_pairs={{0,1},{1,0},{2,3},{3,2},{4,5},{5,4},{6,7},{7,6},{8,9},{9,8},{10,11... | collective-permute-start | bytes 786440 | tf_op jit(solution)/shard_map/ppermute | solution.py:401
  14.0 2.4 %shard_map.86 = (bf16[1,8,128,256]{3,2,1,0:T(8,128)(2,1)S(1)}, bf16[1,8,128,256]{3,2,1,0:T(8,128)(2,1)S(1)}, bf16[1,8,128,256]{3,2,1,0:T(8,128)(2,1)S(1)}, f32[1,128,256]{2,1,0:T(8,128)S(1)}) custom-call(s32[1]{0:T(128)} %bitcast.index_ref, bf16[4,7,128,512]{3,2,1,0:T(8,128)(2,1)S(1)} %get-tuple-element.68.kv_ref, ...), custom_call_target="tpu_custom_call" | custom-call | tf_op jit(solution)/shard_map/pallas_call | solution.py:390
  16.7 1.6 %collective-permute-start.2 = (f32[1,128,256]{2,1,0:T(8,128)S(1)}, f32[1,128,256]{2,1,0:T(8,128)S(1)}, u32[]{:S(2)}, u32[]{:S(2)}) collective-permute-start(f32[1,128,256]{2,1,0:T(8,128)S(1)} %get-tuple-element.82.refs_0_), channel_id=1, source_target_pairs={{0,2},{1,3},{2,0},{3,1},{4,6},{5,7},{6,4},{7,5},{8,10},{9,11},{10,... | collective-permute-start | bytes 393224 | tf_op jit(solution)/shard_map/ppermute | solution.py:401
  18.2 2.4 %shard_map.88 = (bf16[1,8,128,256]{3,2,1,0:T(8,128)(2,1)S(1)}, bf16[1,8,128,256]{3,2,1,0:T(8,128)(2,1)S(1)}, bf16[1,8,128,256]{3,2,1,0:T(8,128)(2,1)S(1)}, f32[1,128,256]{2,1,0:T(8,128)S(1)}) custom-call(s32[1]{0:T(128)} %bitcast.index_ref, bf16[4,7,128,512]{3,2,1,0:T(8,128)(2,1)S(1)} %get-tuple-element.68.kv_ref, ...), custom_call_target="tpu_custom_call" | custom-call | tf_op jit(solution)/shard_map/pallas_call | solution.py:390
  20.9 0.6 %collective-permute-start.4 = (f32[1,128,256]{2,1,0:T(8,128)S(1)}, f32[1,128,256]{2,1,0:T(8,128)S(1)}, u32[]{:S(2)}, u32[]{:S(2)}) collective-permute-start(f32[1,128,256]{2,1,0:T(8,128)S(1)} %get-tuple-element.86.refs_0_), channel_id=1, source_target_pairs={{0,2},{1,3},{2,0},{3,1},{4,6},{5,7},{6,4},{7,5},{8,10},{9,11},{10,... | collective-permute-start | bytes 393224 | tf_op jit(solution)/shard_map/ppermute | solution.py:401
  21.5 0.7 %collective-permute-done.2.refs_1_ = f32[1,128,256]{2,1,0:T(8,128)S(1)} collective-permute-done((f32[1,128,256]{2,1,0:T(8,128)S(1)}, f32[1,128,256]{2,1,0:T(8,128)S(1)}, u32[]{:S(2)}, u32[]{:S(2)}) %collective-permute-start.2) | collective-permute-done | bytes 131104 | tf_op jit(solution)/shard_map/ppermute | solution.py:401
  22.4 1.6 %collective-permute-start.3 = (f32[1,128,256]{2,1,0:T(8,128)S(1)}, f32[1,128,256]{2,1,0:T(8,128)S(1)}, u32[]{:S(2)}, u32[]{:S(2)}) collective-permute-start(f32[1,128,256]{2,1,0:T(8,128)S(1)} %get-tuple-element.88.refs_0_), channel_id=1, source_target_pairs={{0,4},{1,5},{2,6},{3,7},{4,0},{5,1},{6,2},{7,3},{8,12},{9,13},{10,... | collective-permute-start | bytes 393224 | tf_op jit(solution)/shard_map/ppermute | solution.py:401
  24.0 1.2 %shard_map.91 = (bf16[512,256]{1,0:T(8,128)(2,1)S(1)}, f32[512,128]{1,0:T(8,128)S(1)}) custom-call(s32[1]{0:T(128)} %bitcast.index_ref, bf16[4,512,128]{2,1,0:T(8,128)(2,1)S(1)} %copy-done, bf16[4,3,640]{2,1,0:T(4,128)(2,1)S(1)} %collective-permute-done.halo_ref, f32[4,4,128]{2,1,0:T(4,128)S(1)} %copy-done.3, ...), custom_call_target="tpu_custom_call" | custom-call | tf_op jit(solution)/shard_map/pallas_call | solution.py:390
  25.2 0.9 %collective-permute-done.4.refs_1_ = f32[1,128,256]{2,1,0:T(8,128)S(1)} collective-permute-done((f32[1,128,256]{2,1,0:T(8,128)S(1)}, f32[1,128,256]{2,1,0:T(8,128)S(1)}, u32[]{:S(2)}, u32[]{:S(2)}) %collective-permute-start.4) | collective-permute-done | bytes 131104 | tf_op jit(solution)/shard_map/ppermute | solution.py:401
  26.3 1.6 %collective-permute-start.6 = (f32[1,128,256]{2,1,0:T(8,128)S(1)}, f32[1,128,256]{2,1,0:T(8,128)S(1)}, u32[]{:S(2)}, u32[]{:S(2)}) collective-permute-start(f32[1,128,256]{2,1,0:T(8,128)S(1)} %get-tuple-element.96.refs_0_), channel_id=1, source_target_pairs={{0,4},{1,5},{2,6},{3,7},{4,0},{5,1},{6,2},{7,3},{8,12},{9,13},{10,... | collective-permute-start | bytes 393224 | tf_op jit(solution)/shard_map/ppermute | solution.py:401
  28.2 2.1 %collective-permute-start.5 = (f32[1,128,128]{2,1,0:T(8,128)S(1)}, f32[1,128,128]{2,1,0:T(8,128)S(1)}, u32[]{:S(2)}, u32[]{:S(2)}) collective-permute-start(f32[1,128,128]{2,1,0:T(8,128)S(1)} %get-tuple-element.100), channel_id=1, source_target_pairs={{0,8},{1,9},{2,10},{3,11},{4,12},{5,13},{6,14},{7,15},{8,0},{9,1},... | collective-permute-start | bytes 196616 | tf_op jit(solution)/shard_map/ppermute | solution.py:401
  30.3 1.4 %shard_map.94 = (bf16[512,256]{1,0:T(8,128)(2,1)S(1)}, f32[512,128]{1,0:T(8,128)S(1)}) custom-call(s32[1]{0:T(128)} %bitcast.index_ref, bf16[4,512,128]{2,1,0:T(8,128)(2,1)S(1)} %copy-done, bf16[4,3,640]{2,1,0:T(4,128)(2,1)S(1)} %collective-permute-done.halo_ref, f32[4,4,128]{2,1,0:T(4,128)S(1)} %copy-done.3, ...), custom_call_target="tpu_custom_call" | custom-call | tf_op jit(solution)/shard_map/pallas_call | solution.py:390
  32.3 2.0 %collective-permute-start.7 = (f32[1,128,128]{2,1,0:T(8,128)S(1)}, f32[1,128,128]{2,1,0:T(8,128)S(1)}, u32[]{:S(2)}, u32[]{:S(2)}) collective-permute-start(f32[1,128,128]{2,1,0:T(8,128)S(1)} %get-tuple-element.109), channel_id=1, source_target_pairs={{0,8},{1,9},{2,10},{3,11},{4,12},{5,13},{6,14},{7,15},{8,0},{9,1},... | collective-permute-start | bytes 196616 | tf_op jit(solution)/shard_map/ppermute | solution.py:401
  34.2 1.2 %shard_map.96 = (bf16[512,256]{1,0:T(8,128)(2,1)S(1)}, f32[512,128]{1,0:T(8,128)S(1)}) custom-call(s32[1]{0:T(128)} %bitcast.index_ref, bf16[4,512,128]{2,1,0:T(8,128)(2,1)S(1)} %copy-done, bf16[4,3,640]{2,1,0:T(4,128)(2,1)S(1)} %collective-permute-done.halo_ref, f32[4,4,128]{2,1,0:T(4,128)S(1)} %copy-done.3, ...), custom_call_target="tpu_custom_call" | custom-call | tf_op jit(solution)/shard_map/pallas_call | solution.py:390
  35.5 1.2 %shard_map.97 = (bf16[512,256]{1,0:T(8,128)(2,1)S(1)}, f32[512,128]{1,0:T(8,128)S(1)}) custom-call(s32[1]{0:T(128)} %bitcast.index_ref, bf16[4,512,128]{2,1,0:T(8,128)(2,1)S(1)} %copy-done, bf16[4,3,640]{2,1,0:T(4,128)(2,1)S(1)} %collective-permute-done.halo_ref, f32[4,4,128]{2,1,0:T(4,128)S(1)} %copy-done.3, ...), custom_call_target="tpu_custom_call" | custom-call | tf_op jit(solution)/shard_map/pallas_call | solution.py:390
  37.1 0.4 %collective-permute-done.7.got_ref = f32[1,128,128]{2,1,0:T(8,128)S(1)} collective-permute-done((f32[1,128,128]{2,1,0:T(8,128)S(1)}, f32[1,128,128]{2,1,0:T(8,128)S(1)}, u32[]{:S(2)}, u32[]{:S(2)}) %collective-permute-start.7) | collective-permute-done | bytes 65568 | tf_op jit(solution)/shard_map/ppermute | solution.py:401
  38.0 1.4 %shard_map.100.refs_7_ = f32[4,512,128]{2,1,0:T(8,128)} custom-call(s32[1]{0:T(128)} %bitcast.index_ref, f32[4,128]{1,0:T(4,128)S(1)} %copy-done.7, f32[1,128,128]{2,1,0:T(8,128)S(1)} %get-tuple-element.123.refs_1_, bf16[512,256]{1,0:T(8,128)(2,1)S(1)} %get-tuple-element.105.refs_2_, f32[512,128]{1,0:T(8,128)S(1)} %get-tuple-element.106.refs_3_, ...), custom_call_target="tpu_custom_call" | custom-call | tf_op jit(solution)/shard_map/pallas_call | solution.py:569
  39.4 1.4 %shard_map.101 = f32[4,512,128]{2,1,0:T(8,128)} custom-call(s32[1]{0:T(128)} %bitcast.index_ref, f32[4,128]{1,0:T(4,128)S(1)} %copy-done.7, f32[1,128,128]{2,1,0:T(8,128)S(1)} %get-tuple-element.130.refs_1_, bf16[512,256]{1,0:T(8,128)(2,1)S(1)} %get-tuple-element.93.refs_2_, ...), custom_call_target="tpu_custom_call", output_to_operand_aliasing={{}: (8, {})} | custom-call | tf_op jit(solution)/shard_map/pallas_call | solution.py:569
  (32 shorter events, 2.6 us)
Async XLA Ops:
  0.0 1.5 %copy-start.2 = (bf16[4,512,256]{2,1,0:T(8,128)(2,1)S(1)}, bf16[4,512,256]{2,1,0:T(8,128)(2,1)}, u32[]{:S(2)}) copy-start(bf16[4,512,256]{2,1,0:T(8,128)(2,1)} %value_ref.5) | copy-start | bytes 3145732
  0.0 1.6 %copy-start.1 = (bf16[4,512,256]{2,1,0:T(8,128)(2,1)S(1)}, bf16[4,512,256]{2,1,0:T(8,128)(2,1)}, u32[]{:S(2)}) copy-start(bf16[4,512,256]{2,1,0:T(8,128)(2,1)} %key_ref.5) | copy-start | bytes 3145732
  0.0 1.6 %copy-start.5 = (f32[4,4,256]{2,1,0:T(4,128)S(1)}, f32[4,4,256]{2,1,0:T(4,128)}, u32[]{:S(2)}) copy-start(f32[4,4,256]{2,1,0:T(4,128)} %cv_ref.3) | copy-start | bytes 49156
  0.0 1.6 %copy-start.4 = (f32[4,4,256]{2,1,0:T(4,128)S(1)}, f32[4,4,256]{2,1,0:T(4,128)}, u32[]{:S(2)}) copy-start(f32[4,4,256]{2,1,0:T(4,128)} %ck_ref.3) | copy-start | bytes 49156
  0.0 1.6 %copy-start.6 = (f32[4,1024]{1,0:T(4,128)S(1)}, f32[4,1024]{1,0:T(4,128)}, u32[]{:S(2)}) copy-start(f32[4,1024]{1,0:T(4,128)} %rate_ref.1) | copy-start | bytes 49156
  1.0 7.0 %collective-permute-start = (bf16[4,3,640]{2,1,0:T(4,128)(2,1)S(1)}, bf16[4,3,640]{2,1,0:T(4,128)(2,1)S(1)}, u32[]{:S(2)}, u32[]{:S(2)}) collective-permute-start(bf16[4,3,640]{2,1,0:T(4,128)(2,1)S(1)} %shard_map.82), channel_id=1, source_target_pairs={{0,1},{1,2},{2,3},{3,4},{4,5},{5,6},{6,7},{7,8},{8,9},{9,10},{10,1... | collective-permute-start | bytes 46088 | tf_op jit(solution)/shard_map/ppermute | solution.py:430
  12.8 3.6 %collective-permute-start.1 = (f32[2,128,256]{2,1,0:T(8,128)S(1)}, f32[2,128,256]{2,1,0:T(8,128)S(1)}, u32[]{:S(2)}, u32[]{:S(2)}) collective-permute-start(f32[2,128,256]{2,1,0:T(8,128)S(1)} %get-tuple-element.79), channel_id=1, source_target_pairs={{0,1},{1,0},{2,3},{3,2},{4,5},{5,4},{6,7},{7,6},{8,9},{9,8},{10,11... | collective-permute-start | bytes 786440 | tf_op jit(solution)/shard_map/ppermute | solution.py:401
  16.6 7.4 %copy-start = (bf16[4,512,128]{2,1,0:T(8,128)(2,1)S(1)}, bf16[4,512,128]{2,1,0:T(8,128)(2,1)}, u32[]{:S(2)}) copy-start(bf16[4,512,128]{2,1,0:T(8,128)(2,1)} %query_ref.9) | copy-start | bytes 1572868
  16.6 7.4 %copy-start.3 = (f32[4,4,128]{2,1,0:T(4,128)S(1)}, f32[4,4,128]{2,1,0:T(4,128)}, u32[]{:S(2)}) copy-start(f32[4,4,128]{2,1,0:T(4,128)} %cq_ref.7) | copy-start | bytes 24580
  16.7 5.5 %collective-permute-start.2 = (f32[1,128,256]{2,1,0:T(8,128)S(1)}, f32[1,128,256]{2,1,0:T(8,128)S(1)}, u32[]{:S(2)}, u32[]{:S(2)}) collective-permute-start(f32[1,128,256]{2,1,0:T(8,128)S(1)} %get-tuple-element.82.refs_0_), channel_id=1, source_target_pairs={{0,2},{1,3},{2,0},{3,1},{4,6},{5,7},{6,4},{7,5},{8,10},{9,11},{10,... | collective-permute-start | bytes 393224 | tf_op jit(solution)/shard_map/ppermute | solution.py:401
  20.9 5.2 %collective-permute-start.4 = (f32[1,128,256]{2,1,0:T(8,128)S(1)}, f32[1,128,256]{2,1,0:T(8,128)S(1)}, u32[]{:S(2)}, u32[]{:S(2)}) collective-permute-start(f32[1,128,256]{2,1,0:T(8,128)S(1)} %get-tuple-element.86.refs_0_), channel_id=1, source_target_pairs={{0,2},{1,3},{2,0},{3,1},{4,6},{5,7},{6,4},{7,5},{8,10},{9,11},{10,... | collective-permute-start | bytes 393224 | tf_op jit(solution)/shard_map/ppermute | solution.py:401
  22.4 5.6 %collective-permute-start.3 = (f32[1,128,256]{2,1,0:T(8,128)S(1)}, f32[1,128,256]{2,1,0:T(8,128)S(1)}, u32[]{:S(2)}, u32[]{:S(2)}) collective-permute-start(f32[1,128,256]{2,1,0:T(8,128)S(1)} %get-tuple-element.88.refs_0_), channel_id=1, source_target_pairs={{0,4},{1,5},{2,6},{3,7},{4,0},{5,1},{6,2},{7,3},{8,12},{9,13},{10,... | collective-permute-start | bytes 393224 | tf_op jit(solution)/shard_map/ppermute | solution.py:401
  26.3 5.7 %collective-permute-start.6 = (f32[1,128,256]{2,1,0:T(8,128)S(1)}, f32[1,128,256]{2,1,0:T(8,128)S(1)}, u32[]{:S(2)}, u32[]{:S(2)}) collective-permute-start(f32[1,128,256]{2,1,0:T(8,128)S(1)} %get-tuple-element.96.refs_0_), channel_id=1, source_target_pairs={{0,4},{1,5},{2,6},{3,7},{4,0},{5,1},{6,2},{7,3},{8,12},{9,13},{10,... | collective-permute-start | bytes 393224 | tf_op jit(solution)/shard_map/ppermute | solution.py:401
  28.2 8.5 %collective-permute-start.5 = (f32[1,128,128]{2,1,0:T(8,128)S(1)}, f32[1,128,128]{2,1,0:T(8,128)S(1)}, u32[]{:S(2)}, u32[]{:S(2)}) collective-permute-start(f32[1,128,128]{2,1,0:T(8,128)S(1)} %get-tuple-element.100), channel_id=1, source_target_pairs={{0,8},{1,9},{2,10},{3,11},{4,12},{5,13},{6,14},{7,15},{8,0},{9,1},... | collective-permute-start | bytes 196616 | tf_op jit(solution)/shard_map/ppermute | solution.py:401
  32.3 5.2 %collective-permute-start.7 = (f32[1,128,128]{2,1,0:T(8,128)S(1)}, f32[1,128,128]{2,1,0:T(8,128)S(1)}, u32[]{:S(2)}, u32[]{:S(2)}) collective-permute-start(f32[1,128,128]{2,1,0:T(8,128)S(1)} %get-tuple-element.109), channel_id=1, source_target_pairs={{0,8},{1,9},{2,10},{3,11},{4,12},{5,13},{6,14},{7,15},{8,0},{9,1},... | collective-permute-start | bytes 196616 | tf_op jit(solution)/shard_map/ppermute | solution.py:401
  35.5 2.5 %copy-start.7 = (f32[4,128]{1,0:T(4,128)S(1)}, f32[4,128]{1,0:T(4,128)}, u32[]{:S(2)}) copy-start(f32[4,128]{1,0:T(4,128)} %refs_0_.3) | copy-start | bytes 6148
  37.9 1.5 %collective-permute-start.8 = (f32[2,128,128]{2,1,0:T(8,128)S(1)}, f32[2,128,128]{2,1,0:T(8,128)S(1)}, u32[]{:S(2)}, u32[]{:S(2)}) collective-permute-start(f32[2,128,128]{2,1,0:T(8,128)S(1)} %pad_maximum_fusion), channel_id=1, source_target_pairs={{0,1},{1,0},{2,3},{3,2},{4,5},{5,4},{6,7},{7,6},{8,9},{9,8},{10,11... | collective-permute-start | bytes 393224 | tf_op jit(solution)/shard_map/ppermute | solution.py:401

commit v8 on v7

--- a/solution.py
+++ b/solution.py
@@ -24,6 +24,13 @@
 
 def mm(a, b):
     n = b.shape[1] // 2
+    m, k = a.shape[0], b.shape[0]
+    if m <= HALF:
+        p = jnp.dot(
+            jnp.concatenate([a[:, :k], a[:, k:]], 0), b, preferred_element_type=f32
+        )
+        p = p[:m] + p[m:]
+        return p[:, :n] + p[:, n:]
     p = jnp.dot(a, jnp.concatenate([b, b], 0), preferred_element_type=f32)
     return p[:, :n] + p[:, n:]
 
@@ -254,14 +261,10 @@
 
     size = 2
     while size <= blocks:
-        for h in slots:
-            for i in range(0, blocks, size):
-                run(h, i, i + size // 2, i + size)
-        for j in range(size // 2 + 1, size):
-            low_bit = j & -j
-            if low_bit < size // 2:
+        for i in range(0, blocks, size):
+            for j in range(i + size // 2 + 1, i + size + 1):
                 for h in slots:
-                    run(h, 0, j - low_bit, j)
+                    run(h, i, i + size // 2, j)
         size *= 2
     for h in slots:
         p_ref[h, 0] = split(eye)
@@ -607,7 +610,7 @@
         for at in range(half):
             if chains[at]["left"]:
                 step = (join(at, *step),)
-                if at == 0 or len(todo) > 1 + half:
+                if len(todo) > half:
                     step = read_some(1, *step)
     step = read_some(len(todo), *step)
     mine, other = {}, {}

time: 41 us -> 40.9 us (level)
  Pallas kernels: 25.5 us -> 24.2 us
  starting transfers between devices: 11.2 us -> 11.9 us
  waiting for transfers between devices: 3.78 us -> 4.3 us
    pallas_call x17, Pallas kernels: 21.7 us -> 20.4 us  [resident(): pl.pallas_call(kernel, in_specs=[smem] + [vmem] * len(args), out_specs=[v...]
    ppermute x8, starting transfers between devices: 10.7 us -> 11.4 us  [swap(): return lax.ppermute(x, 'seq', [(i, i ^ bit) for i in range(count)])]
    ppermute x8, waiting for transfers between devices: 2.31 us -> 2.84 us  [swap(): return lax.ppermute(x, 'seq', [(i, i ^ bit) for i in range(count)])]
  transfers between devices with their start and end apart: 9 -> 9, of which waited for: 5 -> 5; matrix products, arithmetic and copies ran while one was open for 0% -> 0% of each run, Pallas kernels for 43% -> 41%
where the time goes in v8:
time: 40.9 us; the launch traced here: 40.8 us
  Pallas kernels  24.2 us (59%)
  starting transfers between devices  11.9 us (29%)
  waiting for transfers between devices  4.3 us (11%)
    pallas_call x17, Pallas kernels, resident(): pl.pallas_call(kernel, in_specs=[smem] + [vmem] * len(args), out_specs=[v...  20.4 us
    ppermute x8, starting transfers between devices, swap(): return lax.ppermute(x, 'seq', [(i, i ^ bit) for i in range(count)])  11.4 us
    pallas_call x2, Pallas kernels, finish(): pl.pallas_call(kernel, grid_spec=pltpu.PrefetchScalarGridSpec(num_scalar_...  2.85 us
    ppermute x8, waiting for transfers between devices, swap(): return lax.ppermute(x, 'seq', [(i, i ^ bit) for i in range(count)])  2.84 us
    ppermute x1, waiting for transfers between devices, per_device(): lax.ppermute(tails, 'seq', [(i, (i + 1) % count) for i in range(count)])  1.47 us
    pallas_call x1, Pallas kernels, per_device(): pl.pallas_call(tails_kernel, grid_spec=pltpu.PrefetchScalarGridSpec(num_s...  0.96 us
  transfers between devices with their start and end apart: 9, of which 5 were waited for; matrix products, arithmetic and copies ran while one was open for 0% of the time, Pallas kernels for 41%

profile of v8, /device:TPU:0, one launch (start us, length us, event | category | flops | bytes accessed | tf_op | source)
XLA Modules:
  0.0 40.8 jit_solution(17009236286292372137)
XLA Ops:
  0.0 1.0 %shard_map.82 = bf16[4,3,640]{2,1,0:T(4,128)(2,1)S(1)} custom-call(s32[1]{0:T(128)} %bitcast.index_ref, bf16[4,512,128]{2,1,0:T(8,128)(2,1)} %query_ref.9, bf16[4,512,256]{2,1,0:T(8,128)(2,1)} %key_ref.5, bf16[4,512,256]{2,1,0:T(8,128)(2,1)} %value_ref.5), custom_call_target="tpu_custom_call" | custom-call | tf_op jit(solution)/shard_map/pallas_call | solution.py:422
  1.0 0.5 %collective-permute-start = (bf16[4,3,640]{2,1,0:T(4,128)(2,1)S(1)}, bf16[4,3,640]{2,1,0:T(4,128)(2,1)S(1)}, u32[]{:S(2)}, u32[]{:S(2)}) collective-permute-start(bf16[4,3,640]{2,1,0:T(4,128)(2,1)S(1)} %shard_map.82), channel_id=1, source_target_pairs={{0,1},{1,2},{2,3},{3,4},{4,5},{5,6},{6,7},{7,8},{8,9},{9,10},{10,1... | collective-permute-start | bytes 46088 | tf_op jit(solution)/shard_map/ppermute | solution.py:433
  1.6 4.9 %shard_map.83 = (bf16[4,7,128,512]{3,2,1,0:T(8,128)(2,1)S(1)}, bf16[4,7,128,256]{3,2,1,0:T(8,128)(2,1)S(1)}, f32[4,7,128,128]{3,2,1,0:T(8,128)S(1)}, f32[4,128,128]{2,1,0:T(8,128)S(1)}, f32[4,8,128]{2,1,0:T(8,128)S(1)}) custom-call(s32[1]{0:T(128)} %bitcast.index_ref, bf16[4,512,256]{2,1,0:T(8,128)(2,1)S(1)} %copy-done.1, ...), custom_call_target="tpu_custom_call" | custom-call | tf_op jit(solution)/shard_map/pallas_call | solution.py:393
  6.5 1.5 %collective-permute-done.halo_ref = bf16[4,3,640]{2,1,0:T(4,128)(2,1)S(1)} collective-permute-done((bf16[4,3,640]{2,1,0:T(4,128)(2,1)S(1)}, bf16[4,3,640]{2,1,0:T(4,128)(2,1)S(1)}, u32[]{:S(2)}, u32[]{:S(2)}) %collective-permute-start) | collective-permute-done | bytes 15392 | tf_op jit(solution)/shard_map/ppermute | solution.py:433
  8.0 1.0 %shard_map.84 = (bf16[4,128,512]{2,1,0:T(8,128)(2,1)S(1)}, bf16[4,128,256]{2,1,0:T(8,128)(2,1)S(1)}, f32[4,128,128]{2,1,0:T(8,128)S(1)}, f32[64,128]{1,0:T(8,128)S(1)}) custom-call(s32[1]{0:T(128)} %bitcast.index_ref, bf16[4,512,256]{2,1,0:T(8,128)(2,1)S(1)} %copy-done.1, bf16[4,512,256]{2,1,0:T(8,128)(2,1)S(1)} %copy-done.2, ...), custom_call_target="tpu_custom_call" | custom-call | tf_op jit(solution)/shard_map/pallas_call | solution.py:393
  8.9 3.7 %shard_map.85 = (bf16[2,8,128,256]{3,2,1,0:T(8,128)(2,1)S(1)}, bf16[2,8,128,256]{3,2,1,0:T(8,128)(2,1)S(1)}, bf16[2,8,128,256]{3,2,1,0:T(8,128)(2,1)S(1)}, f32[2,128,256]{2,1,0:T(8,128)S(1)}) custom-call(s32[1]{0:T(128)} %bitcast.index_ref, bf16[4,7,128,512]{3,2,1,0:T(8,128)(2,1)S(1)} %get-tuple-element.68.kv_ref, ...), custom_call_target="tpu_custom_call" | custom-call | tf_op jit(solution)/shard_map/pallas_call | solution.py:393
  12.6 1.2 %collective-permute-start.1 = (f32[2,128,256]{2,1,0:T(8,128)S(1)}, f32[2,128,256]{2,1,0:T(8,128)S(1)}, u32[]{:S(2)}, u32[]{:S(2)}) collective-permute-start(f32[2,128,256]{2,1,0:T(8,128)S(1)} %get-tuple-element.79), channel_id=1, source_target_pairs={{0,1},{1,0},{2,3},{3,2},{4,5},{5,4},{6,7},{7,6},{8,9},{9,8},{10,11... | collective-permute-start | bytes 786440 | tf_op jit(solution)/shard_map/ppermute | solution.py:404
  13.8 2.2 %shard_map.86 = (bf16[1,8,128,256]{3,2,1,0:T(8,128)(2,1)S(1)}, bf16[1,8,128,256]{3,2,1,0:T(8,128)(2,1)S(1)}, bf16[1,8,128,256]{3,2,1,0:T(8,128)(2,1)S(1)}, f32[1,128,256]{2,1,0:T(8,128)S(1)}) custom-call(s32[1]{0:T(128)} %bitcast.index_ref, bf16[4,7,128,512]{3,2,1,0:T(8,128)(2,1)S(1)} %get-tuple-element.68.kv_ref, ...), custom_call_target="tpu_custom_call" | custom-call | tf_op jit(solution)/shard_map/pallas_call | solution.py:393
  16.3 1.6 %collective-permute-start.2 = (f32[1,128,256]{2,1,0:T(8,128)S(1)}, f32[1,128,256]{2,1,0:T(8,128)S(1)}, u32[]{:S(2)}, u32[]{:S(2)}) collective-permute-start(f32[1,128,256]{2,1,0:T(8,128)S(1)} %get-tuple-element.82.refs_0_), channel_id=1, source_target_pairs={{0,2},{1,3},{2,0},{3,1},{4,6},{5,7},{6,4},{7,5},{8,10},{9,11},{10,... | collective-permute-start | bytes 393224 | tf_op jit(solution)/shard_map/ppermute | solution.py:404
  17.9 2.2 %shard_map.88 = (bf16[1,8,128,256]{3,2,1,0:T(8,128)(2,1)S(1)}, bf16[1,8,128,256]{3,2,1,0:T(8,128)(2,1)S(1)}, bf16[1,8,128,256]{3,2,1,0:T(8,128)(2,1)S(1)}, f32[1,128,256]{2,1,0:T(8,128)S(1)}) custom-call(s32[1]{0:T(128)} %bitcast.index_ref, bf16[4,7,128,512]{3,2,1,0:T(8,128)(2,1)S(1)} %get-tuple-element.68.kv_ref, ...), custom_call_target="tpu_custom_call" | custom-call | tf_op jit(solution)/shard_map/pallas_call | solution.py:393
  20.3 0.6 %collective-permute-start.4 = (f32[1,128,256]{2,1,0:T(8,128)S(1)}, f32[1,128,256]{2,1,0:T(8,128)S(1)}, u32[]{:S(2)}, u32[]{:S(2)}) collective-permute-start(f32[1,128,256]{2,1,0:T(8,128)S(1)} %get-tuple-element.86.refs_0_), channel_id=1, source_target_pairs={{0,2},{1,3},{2,0},{3,1},{4,6},{5,7},{6,4},{7,5},{8,10},{9,11},{10,... | collective-permute-start | bytes 393224 | tf_op jit(solution)/shard_map/ppermute | solution.py:404
  20.9 0.9 %collective-permute-done.2.refs_1_ = f32[1,128,256]{2,1,0:T(8,128)S(1)} collective-permute-done((f32[1,128,256]{2,1,0:T(8,128)S(1)}, f32[1,128,256]{2,1,0:T(8,128)S(1)}, u32[]{:S(2)}, u32[]{:S(2)}) %collective-permute-start.2) | collective-permute-done | bytes 131104 | tf_op jit(solution)/shard_map/ppermute | solution.py:404
  22.0 1.6 %collective-permute-start.3 = (f32[1,128,256]{2,1,0:T(8,128)S(1)}, f32[1,128,256]{2,1,0:T(8,128)S(1)}, u32[]{:S(2)}, u32[]{:S(2)}) collective-permute-start(f32[1,128,256]{2,1,0:T(8,128)S(1)} %get-tuple-element.88.refs_0_), channel_id=1, source_target_pairs={{0,4},{1,5},{2,6},{3,7},{4,0},{5,1},{6,2},{7,3},{8,12},{9,13},{10,... | collective-permute-start | bytes 393224 | tf_op jit(solution)/shard_map/ppermute | solution.py:404
  23.6 1.1 %shard_map.91 = (bf16[512,256]{1,0:T(8,128)(2,1)S(1)}, f32[512,128]{1,0:T(8,128)S(1)}) custom-call(s32[1]{0:T(128)} %bitcast.index_ref, bf16[4,512,128]{2,1,0:T(8,128)(2,1)S(1)} %copy-done, bf16[4,3,640]{2,1,0:T(4,128)(2,1)S(1)} %collective-permute-done.halo_ref, f32[4,4,128]{2,1,0:T(4,128)S(1)} %copy-done.3, ...), custom_call_target="tpu_custom_call" | custom-call | tf_op jit(solution)/shard_map/pallas_call | solution.py:393
  24.7 0.8 %collective-permute-done.4.refs_1_ = f32[1,128,256]{2,1,0:T(8,128)S(1)} collective-permute-done((f32[1,128,256]{2,1,0:T(8,128)S(1)}, f32[1,128,256]{2,1,0:T(8,128)S(1)}, u32[]{:S(2)}, u32[]{:S(2)}) %collective-permute-start.4) | collective-permute-done | bytes 131104 | tf_op jit(solution)/shard_map/ppermute | solution.py:404
  25.7 1.6 %collective-permute-start.6 = (f32[1,128,256]{2,1,0:T(8,128)S(1)}, f32[1,128,256]{2,1,0:T(8,128)S(1)}, u32[]{:S(2)}, u32[]{:S(2)}) collective-permute-start(f32[1,128,256]{2,1,0:T(8,128)S(1)} %get-tuple-element.96.refs_0_), channel_id=1, source_target_pairs={{0,4},{1,5},{2,6},{3,7},{4,0},{5,1},{6,2},{7,3},{8,12},{9,13},{10,... | collective-permute-start | bytes 393224 | tf_op jit(solution)/shard_map/ppermute | solution.py:404
  27.4 1.2 %shard_map.93 = (bf16[512,256]{1,0:T(8,128)(2,1)S(1)}, f32[512,128]{1,0:T(8,128)S(1)}) custom-call(s32[1]{0:T(128)} %bitcast.index_ref, bf16[4,512,128]{2,1,0:T(8,128)(2,1)S(1)} %copy-done, bf16[4,3,640]{2,1,0:T(4,128)(2,1)S(1)} %collective-permute-done.halo_ref, f32[4,4,128]{2,1,0:T(4,128)S(1)} %copy-done.3, ...), custom_call_target="tpu_custom_call" | custom-call | tf_op jit(solution)/shard_map/pallas_call | solution.py:393
  28.8 2.0 %collective-permute-start.5 = (f32[1,128,128]{2,1,0:T(8,128)S(1)}, f32[1,128,128]{2,1,0:T(8,128)S(1)}, u32[]{:S(2)}, u32[]{:S(2)}) collective-permute-start(f32[1,128,128]{2,1,0:T(8,128)S(1)} %get-tuple-element.106), channel_id=1, source_target_pairs={{0,8},{1,9},{2,10},{3,11},{4,12},{5,13},{6,14},{7,15},{8,0},{9,1},... | collective-permute-start | bytes 196616 | tf_op jit(solution)/shard_map/ppermute | solution.py:404
  31.1 2.7 %collective-permute-start.7 = (f32[1,128,128]{2,1,0:T(8,128)S(1)}, f32[1,128,128]{2,1,0:T(8,128)S(1)}, u32[]{:S(2)}, u32[]{:S(2)}) collective-permute-start(f32[1,128,128]{2,1,0:T(8,128)S(1)} %get-tuple-element.109), channel_id=1, source_target_pairs={{0,8},{1,9},{2,10},{3,11},{4,12},{5,13},{6,14},{7,15},{8,0},{9,1},... | collective-permute-start | bytes 196616 | tf_op jit(solution)/shard_map/ppermute | solution.py:404
  33.8 1.1 %shard_map.96 = (bf16[512,256]{1,0:T(8,128)(2,1)S(1)}, f32[512,128]{1,0:T(8,128)S(1)}) custom-call(s32[1]{0:T(128)} %bitcast.index_ref, bf16[4,512,128]{2,1,0:T(8,128)(2,1)S(1)} %copy-done, bf16[4,3,640]{2,1,0:T(4,128)(2,1)S(1)} %collective-permute-done.halo_ref, f32[4,4,128]{2,1,0:T(4,128)S(1)} %copy-done.3, ...), custom_call_target="tpu_custom_call" | custom-call | tf_op jit(solution)/shard_map/pallas_call | solution.py:393
  34.9 1.1 %shard_map.97 = (bf16[512,256]{1,0:T(8,128)(2,1)S(1)}, f32[512,128]{1,0:T(8,128)S(1)}) custom-call(s32[1]{0:T(128)} %bitcast.index_ref, bf16[4,512,128]{2,1,0:T(8,128)(2,1)S(1)} %copy-done, bf16[4,3,640]{2,1,0:T(4,128)(2,1)S(1)} %collective-permute-done.halo_ref, f32[4,4,128]{2,1,0:T(4,128)S(1)} %copy-done.3, ...), custom_call_target="tpu_custom_call" | custom-call | tf_op jit(solution)/shard_map/pallas_call | solution.py:393
  36.4 1.0 %collective-permute-done.7.got_ref = f32[1,128,128]{2,1,0:T(8,128)S(1)} collective-permute-done((f32[1,128,128]{2,1,0:T(8,128)S(1)}, f32[1,128,128]{2,1,0:T(8,128)S(1)}, u32[]{:S(2)}, u32[]{:S(2)}) %collective-permute-start.7) | collective-permute-done | bytes 65568 | tf_op jit(solution)/shard_map/ppermute | solution.py:404
  37.9 1.4 %shard_map.100.refs_7_ = f32[4,512,128]{2,1,0:T(8,128)} custom-call(s32[1]{0:T(128)} %bitcast.index_ref, f32[4,128]{1,0:T(4,128)S(1)} %copy-done.7, f32[1,128,128]{2,1,0:T(8,128)S(1)} %get-tuple-element.123.refs_1_, bf16[512,256]{1,0:T(8,128)(2,1)S(1)} %get-tuple-element.101.refs_2_, f32[512,128]{1,0:T(8,128)S(1)} %get-tuple-element.102.refs_3_, ...), custom_call_target="tpu_custom_call" | custom-call | tf_op jit(solution)/shard_map/pallas_call | solution.py:572
  39.4 1.4 %shard_map.101 = f32[4,512,128]{2,1,0:T(8,128)} custom-call(s32[1]{0:T(128)} %bitcast.index_ref, f32[4,128]{1,0:T(4,128)S(1)} %copy-done.7, f32[1,128,128]{2,1,0:T(8,128)S(1)} %get-tuple-element.130.refs_1_, bf16[512,256]{1,0:T(8,128)(2,1)S(1)} %get-tuple-element.93.refs_2_, ...), custom_call_target="tpu_custom_call", output_to_operand_aliasing={{}: (8, {})} | custom-call | tf_op jit(solution)/shard_map/pallas_call | solution.py:572
  (32 shorter events, 2.3 us)
Async XLA Ops:
  0.0 1.5 %copy-start.2 = (bf16[4,512,256]{2,1,0:T(8,128)(2,1)S(1)}, bf16[4,512,256]{2,1,0:T(8,128)(2,1)}, u32[]{:S(2)}) copy-start(bf16[4,512,256]{2,1,0:T(8,128)(2,1)} %value_ref.5) | copy-start | bytes 3145732
  0.0 1.6 %copy-start.1 = (bf16[4,512,256]{2,1,0:T(8,128)(2,1)S(1)}, bf16[4,512,256]{2,1,0:T(8,128)(2,1)}, u32[]{:S(2)}) copy-start(bf16[4,512,256]{2,1,0:T(8,128)(2,1)} %key_ref.5) | copy-start | bytes 3145732
  0.0 1.6 %copy-start.5 = (f32[4,4,256]{2,1,0:T(4,128)S(1)}, f32[4,4,256]{2,1,0:T(4,128)}, u32[]{:S(2)}) copy-start(f32[4,4,256]{2,1,0:T(4,128)} %cv_ref.3) | copy-start | bytes 49156
  0.0 1.6 %copy-start.4 = (f32[4,4,256]{2,1,0:T(4,128)S(1)}, f32[4,4,256]{2,1,0:T(4,128)}, u32[]{:S(2)}) copy-start(f32[4,4,256]{2,1,0:T(4,128)} %ck_ref.3) | copy-start | bytes 49156
  0.0 1.6 %copy-start.6 = (f32[4,1024]{1,0:T(4,128)S(1)}, f32[4,1024]{1,0:T(4,128)}, u32[]{:S(2)}) copy-start(f32[4,1024]{1,0:T(4,128)} %rate_ref.1) | copy-start | bytes 49156
  1.0 7.0 %collective-permute-start = (bf16[4,3,640]{2,1,0:T(4,128)(2,1)S(1)}, bf16[4,3,640]{2,1,0:T(4,128)(2,1)S(1)}, u32[]{:S(2)}, u32[]{:S(2)}) collective-permute-start(bf16[4,3,640]{2,1,0:T(4,128)(2,1)S(1)} %shard_map.82), channel_id=1, source_target_pairs={{0,1},{1,2},{2,3},{3,4},{4,5},{5,6},{6,7},{7,8},{8,9},{9,10},{10,1... | collective-permute-start | bytes 46088 | tf_op jit(solution)/shard_map/ppermute | solution.py:433
  12.6 3.4 %collective-permute-start.1 = (f32[2,128,256]{2,1,0:T(8,128)S(1)}, f32[2,128,256]{2,1,0:T(8,128)S(1)}, u32[]{:S(2)}, u32[]{:S(2)}) collective-permute-start(f32[2,128,256]{2,1,0:T(8,128)S(1)} %get-tuple-element.79), channel_id=1, source_target_pairs={{0,1},{1,0},{2,3},{3,2},{4,5},{5,4},{6,7},{7,6},{8,9},{9,8},{10,11... | collective-permute-start | bytes 786440 | tf_op jit(solution)/shard_map/ppermute | solution.py:404
  16.2 7.4 %copy-start = (bf16[4,512,128]{2,1,0:T(8,128)(2,1)S(1)}, bf16[4,512,128]{2,1,0:T(8,128)(2,1)}, u32[]{:S(2)}) copy-start(bf16[4,512,128]{2,1,0:T(8,128)(2,1)} %query_ref.9) | copy-start | bytes 1572868
  16.3 7.4 %copy-start.3 = (f32[4,4,128]{2,1,0:T(4,128)S(1)}, f32[4,4,128]{2,1,0:T(4,128)}, u32[]{:S(2)}) copy-start(f32[4,4,128]{2,1,0:T(4,128)} %cq_ref.7) | copy-start | bytes 24580
  16.3 5.5 %collective-permute-start.2 = (f32[1,128,256]{2,1,0:T(8,128)S(1)}, f32[1,128,256]{2,1,0:T(8,128)S(1)}, u32[]{:S(2)}, u32[]{:S(2)}) collective-permute-start(f32[1,128,256]{2,1,0:T(8,128)S(1)} %get-tuple-element.82.refs_0_), channel_id=1, source_target_pairs={{0,2},{1,3},{2,0},{3,1},{4,6},{5,7},{6,4},{7,5},{8,10},{9,11},{10,... | collective-permute-start | bytes 393224 | tf_op jit(solution)/shard_map/ppermute | solution.py:404
  20.3 5.2 %collective-permute-start.4 = (f32[1,128,256]{2,1,0:T(8,128)S(1)}, f32[1,128,256]{2,1,0:T(8,128)S(1)}, u32[]{:S(2)}, u32[]{:S(2)}) collective-permute-start(f32[1,128,256]{2,1,0:T(8,128)S(1)} %get-tuple-element.86.refs_0_), channel_id=1, source_target_pairs={{0,2},{1,3},{2,0},{3,1},{4,6},{5,7},{6,4},{7,5},{8,10},{9,11},{10,... | collective-permute-start | bytes 393224 | tf_op jit(solution)/shard_map/ppermute | solution.py:404
  22.0 6.6 %collective-permute-start.3 = (f32[1,128,256]{2,1,0:T(8,128)S(1)}, f32[1,128,256]{2,1,0:T(8,128)S(1)}, u32[]{:S(2)}, u32[]{:S(2)}) collective-permute-start(f32[1,128,256]{2,1,0:T(8,128)S(1)} %get-tuple-element.88.refs_0_), channel_id=1, source_target_pairs={{0,4},{1,5},{2,6},{3,7},{4,0},{5,1},{6,2},{7,3},{8,12},{9,13},{10,... | collective-permute-start | bytes 393224 | tf_op jit(solution)/shard_map/ppermute | solution.py:404
  25.7 5.1 %collective-permute-start.6 = (f32[1,128,256]{2,1,0:T(8,128)S(1)}, f32[1,128,256]{2,1,0:T(8,128)S(1)}, u32[]{:S(2)}, u32[]{:S(2)}) collective-permute-start(f32[1,128,256]{2,1,0:T(8,128)S(1)} %get-tuple-element.96.refs_0_), channel_id=1, source_target_pairs={{0,4},{1,5},{2,6},{3,7},{4,0},{5,1},{6,2},{7,3},{8,12},{9,13},{10,... | collective-permute-start | bytes 393224 | tf_op jit(solution)/shard_map/ppermute | solution.py:404
  28.8 7.2 %collective-permute-start.5 = (f32[1,128,128]{2,1,0:T(8,128)S(1)}, f32[1,128,128]{2,1,0:T(8,128)S(1)}, u32[]{:S(2)}, u32[]{:S(2)}) collective-permute-start(f32[1,128,128]{2,1,0:T(8,128)S(1)} %get-tuple-element.106), channel_id=1, source_target_pairs={{0,8},{1,9},{2,10},{3,11},{4,12},{5,13},{6,14},{7,15},{8,0},{9,1},... | collective-permute-start | bytes 196616 | tf_op jit(solution)/shard_map/ppermute | solution.py:404
  31.1 6.3 %collective-permute-start.7 = (f32[1,128,128]{2,1,0:T(8,128)S(1)}, f32[1,128,128]{2,1,0:T(8,128)S(1)}, u32[]{:S(2)}, u32[]{:S(2)}) collective-permute-start(f32[1,128,128]{2,1,0:T(8,128)S(1)} %get-tuple-element.109), channel_id=1, source_target_pairs={{0,8},{1,9},{2,10},{3,11},{4,12},{5,13},{6,14},{7,15},{8,0},{9,1},... | collective-permute-start | bytes 196616 | tf_op jit(solution)/shard_map/ppermute | solution.py:404
  34.9 3.0 %copy-start.7 = (f32[4,128]{1,0:T(4,128)S(1)}, f32[4,128]{1,0:T(4,128)}, u32[]{:S(2)}) copy-start(f32[4,128]{1,0:T(4,128)} %refs_0_.3) | copy-start | bytes 6148
  37.8 1.5 %collective-permute-start.8 = (f32[2,128,128]{2,1,0:T(8,128)S(1)}, f32[2,128,128]{2,1,0:T(8,128)S(1)}, u32[]{:S(2)}, u32[]{:S(2)}) collective-permute-start(f32[2,128,128]{2,1,0:T(8,128)S(1)} %pad_maximum_fusion), channel_id=1, source_target_pairs={{0,1},{1,0},{2,3},{3,2},{4,5},{5,4},{6,7},{7,6},{8,9},{9,8},{10,11... | collective-permute-start | bytes 393224 | tf_op jit(solution)/shard_map/ppermute | solution.py:404

commit v9 on v8

--- a/solution.py
+++ b/solution.py
@@ -118,9 +118,13 @@
 
 
 def front_kernel(
-    index_ref, key_ref, value_ref, rate_ref, ck_ref, cv_ref,
-    kv_ref, kb_ref, low_ref, sol_ref, rates_ref, rows, brow, diag, keys,
+    early, index_ref, key_ref, value_ref, rate_ref, ck_ref, cv_ref, *refs
 ):
+    if early:
+        kv_ref, kb_ref, low_ref, diag, rates_ref, rows, brow, keys = refs
+    else:
+        kv_ref, kb_ref, low_ref, diag, rates_ref, sol_ref, rows, brow, keys = refs[5:]
+    upper = index_ref[0] & 1
     dim = rows.shape[2]
     blocks = rates_ref.shape[1]
     row, col, _ = block_masks()
@@ -151,7 +155,10 @@
         diag[h, 0:GROUP] = jnp.zeros((GROUP, BLOCK), f32)
         return carry
 
-    lax.fori_loop(0, key_ref.shape[0], one, 0)
+    if early:
+        lax.fori_loop(0, upper, one, 0)
+        return
+    lax.fori_loop(upper, key_ref.shape[0], one, 0)
     for h in range(key_ref.shape[0]):
         invert_groups(diag.at[h], sol_ref.at[h], blocks)
 
@@ -302,21 +309,18 @@
         pulled_ref[rows[n]] = split(mm(pulled[rows[n]], p_ref[slot, n]))
 
 
-def out_kernel(kept, start, half, index_ref, gain_ref, *rest):
+def out_kernel(kept, half, index_ref, gain_ref, *rest):
     out_ref = rest[-1]
-    for i in range(len(rest) // 3):
+    first = first_head(index_ref, kept, half)
+    for i in range(half):
         state_ref, pulled_ref, local_ref = rest[3 * i : 3 * i + 3]
-
-        @pl.when(pl.program_id(0) == i)
-        def _():
-            h = first_head(index_ref, kept, half) + start + i
-            state = split(state_ref[0])
-            gain = pick_row(gain_ref[...], h)
-            for at in range(0, pulled_ref.shape[0], BLOCK):
-                rows = slice(at, at + BLOCK)
-                raw = mm(pulled_ref[rows], state) + local_ref[rows]
-                mean = jnp.mean(raw * raw, 1, keepdims=True)
-                out_ref[0, rows] = raw * lax.rsqrt(mean + 1e-06) * gain
+        state = split(state_ref[0])
+        gain = pick_row(gain_ref[...], first + i)
+        for at in range(0, pulled_ref.shape[0], BLOCK):
+            rows = slice(at, at + BLOCK)
+            raw = mm(pulled_ref[rows], state) + local_ref[rows]
+            mean = jnp.mean(raw * raw, 1, keepdims=True)
+            out_ref[i, rows] = raw * lax.rsqrt(mean + 1e-06) * gain
 
 
 def then(later, earlier):
@@ -387,7 +391,7 @@
     return jax.ShapeDtypeStruct(dims, dtype)
 
 
-def resident(kernel, index, args, outs, scratch=(), limit=4 << 20):
+def resident(kernel, index, args, outs, scratch=(), limit=4 << 20, aliases={}):
     smem = pl.BlockSpec(memory_space=pltpu.SMEM)
     vmem = pl.BlockSpec(memory_space=pltpu.VMEM)
     return pl.pallas_call(
@@ -396,6 +400,7 @@
         out_specs=[vmem] * len(outs),
         out_shape=[pltpu.VMEM(o.shape, o.dtype) for o in outs],
         scratch_shapes=list(scratch),
+        input_output_aliases=aliases,
         compiler_params=pltpu.CompilerParams(vmem_limit_bytes=limit),
     )(index, *[pltpu.with_memory_space_constraint(a, pltpu.VMEM) for a in args])
 
@@ -430,32 +435,43 @@
         out_shape=shape((heads, rim, 5 * dim), bf16),
         compiler_params=pltpu.CompilerParams(vmem_limit_bytes=4 << 20),
     )(index, *[pltpu.with_memory_space_constraint(x, pltpu.HBM) for x in parts])
-    halo = lax.ppermute(tails, "seq", [(i, (i + 1) % count) for i in range(count)])
-
     def in_order(*after):
         return lax.optimization_barrier((index, after))[0]
 
     inner = (heads, blocks - 1, BLOCK)
+    front_args = (key_pairs, value_pairs, write_rates, conv_key, conv_value)
+    front_outs = [
+        shape(inner + (4 * dim,), bf16),
+        shape(inner + (2 * dim,), bf16),
+        shape(inner + (BLOCK,), f32),
+        shape((heads, blocks * GROUP, BLOCK), f32),
+        shape((heads, blocks, BLOCK), f32),
+    ]
+    front_scratch = [
+        pltpu.VMEM((4, tokens + 8, dim), f32),
+        pltpu.VMEM((blocks, BLOCK), f32),
+        pltpu.VMEM((blocks - 1, BLOCK, dim), f32),
+    ]
     front = resident(
-        front_kernel,
+        functools.partial(front_kernel, True),
         in_order(tails),
-        (key_pairs, value_pairs, write_rates, conv_key, conv_value),
-        [
-            shape(inner + (4 * dim,), bf16),
-            shape(inner + (2 * dim,), bf16),
-            shape(inner + (BLOCK,), f32),
-            shape((heads, blocks * GROUP, BLOCK), f32),
-            shape((heads, blocks, BLOCK), f32),
-        ],
-        [
-            pltpu.VMEM((4, tokens + 8, dim), f32),
-            pltpu.VMEM((blocks, BLOCK), f32),
-            pltpu.VMEM((heads, blocks * GROUP, BLOCK), f32),
-            pltpu.VMEM((blocks - 1, BLOCK, dim), f32),
-        ],
+        front_args,
+        front_outs,
+        front_scratch,
         LIMIT,
     )
-    *front, rates = front
+    tails = lax.optimization_barrier((tails, front[-1]))[0]
+    halo = lax.ppermute(tails, "seq", [(i, (i + 1) % count) for i in range(count)])
+    kv, kb, low, _, rates, sol = resident(
+        functools.partial(front_kernel, False),
+        in_order(tails),
+        (*front_args, *front),
+        front_outs + front_outs[3:4],
+        front_scratch,
+        LIMIT,
+        {1 + len(front_args) + i: i for i in range(5)},
+    )
+    front = (kv, kb, low, sol)
     halo = lax.optimization_barrier((halo, rates))[0]
     opening = resident(
         first_kernel,
@@ -553,29 +569,29 @@
     out_shape = shape((heads, tokens, dim), f32)
     done = ()
 
-    def finish(kept, start, states, *after):
+    def finish(kept, states, *after):
         nonlocal done
         vmem = pl.BlockSpec(memory_space=pltpu.VMEM)
 
         def out_block(i, index_ref):
             upper = index_ref[0] & 1
-            return ((upper if kept else 1 - upper) * half + start + i, 0, 0)
+            return (upper if kept else 1 - upper, 0, 0)
 
         args = [out_gain]
         for i, state in enumerate(states):
-            args += [state, *read[kept, start + i]]
+            args += [state, *read[kept, i]]
         args = [pltpu.with_memory_space_constraint(a, pltpu.VMEM) for a in args]
 
         def kernel(index_ref, *refs):
-            out_kernel(kept, start, half, index_ref, *refs[: len(args)], refs[-1])
+            out_kernel(kept, half, index_ref, *refs[: len(args)], refs[-1])
 
         out = pl.pallas_call(
             kernel,
             grid_spec=pltpu.PrefetchScalarGridSpec(
                 num_scalar_prefetch=1,
-                grid=(len(states),),
+                grid=(1,),
                 in_specs=[vmem] * len(args) + [pl.BlockSpec(memory_space=pl.ANY)] * len(done),
-                out_specs=pl.BlockSpec((1, tokens, dim), out_block),
+                out_specs=pl.BlockSpec((half, tokens, dim), out_block),
             ),
             out_shape=out_shape,
             input_output_aliases={len(args) + 1: 0} if done else {},
@@ -618,9 +634,9 @@
         mine[at], other[at] = down(at, *step)
         step = (mine[at],)
     others = swap(jnp.concatenate([other[at] for at in range(half)], 0), 1, count)
-    last = finish(True, 0, [mine[at] for at in range(half)])
+    last = finish(True, [mine[at] for at in range(half)])
     others = lax.optimization_barrier((others, last))[0]
-    return finish(False, 0, [others[at : at + 1] for at in range(half)])
+    return finish(False, [others[at : at + 1] for at in range(half)])
 
 
 def solution(mesh):

time: 40.9 us -> 40.4 us (0.988)
  local copies, waits for them, and re-layouts: 0.13 us -> 0.65 us
    ppermute x8, starting transfers between devices: 11.4 us -> 10.1 us  [swap(): return lax.ppermute(x, 'seq', [(i, i ^ bit) for i in range(count)])]
    ppermute x1, starting transfers between devices: 0.52 us -> 1.52 us  [per_device(): lax.ppermute(tails, 'seq', [(i, (i + 1) % count) for i in range(count)])]
    unnamed x16, local copies, waits for them, and re-layouts: 0.12 us -> 0.64 us
    ppermute x8, waiting for transfers between devices: 2.84 us -> 2.37 us  [swap(): return lax.ppermute(x, 'seq', [(i, i ^ bit) for i in range(count)])]
    pallas_call x2, Pallas kernels: 2.85 us -> 2.43 us  [finish(): pl.pallas_call(kernel, grid_spec=pltpu.PrefetchScalarGridSpec(num_scalar_...]
    pallas_call x17 -> x18, Pallas kernels: 20.4 us -> 20.4 us  [resident(): pl.pallas_call(kernel, in_specs=[smem] + [vmem] * len(args), out_specs=[v...]
where the time goes in v9:
time: 40.4 us; the launch traced here: 40.3 us
  Pallas kernels  23.8 us (59%)
  starting transfers between devices  11.6 us (29%)
  waiting for transfers between devices  3.96 us (10%)
  local copies, waits for them, and re-layouts  0.65 us (2%)
    pallas_call x18, Pallas kernels, resident(): pl.pallas_call(kernel, in_specs=[smem] + [vmem] * len(args), out_specs=[v...  20.4 us
    ppermute x8, starting transfers between devices, swap(): return lax.ppermute(x, 'seq', [(i, i ^ bit) for i in range(count)])  10.1 us
    pallas_call x2, Pallas kernels, finish(): pl.pallas_call(kernel, grid_spec=pltpu.PrefetchScalarGridSpec(num_scalar_...  2.43 us
    ppermute x8, waiting for transfers between devices, swap(): return lax.ppermute(x, 'seq', [(i, i ^ bit) for i in range(count)])  2.37 us
    ppermute x1, waiting for transfers between devices, per_device(): lax.ppermute(tails, 'seq', [(i, (i + 1) % count) for i in range(count)])  1.59 us
    ppermute x1, starting transfers between devices, per_device(): lax.ppermute(tails, 'seq', [(i, (i + 1) % count) for i in range(count)])  1.52 us
    pallas_call x1, Pallas kernels, per_device(): pl.pallas_call(tails_kernel, grid_spec=pltpu.PrefetchScalarGridSpec(num_s...  0.96 us
  transfers between devices with their start and end apart: 9, of which 5 were waited for; matrix products, arithmetic and copies ran while one was open for 0% of the time, Pallas kernels for 41%

profile of v9, /device:TPU:0, one launch (start us, length us, event | category | flops | bytes accessed | tf_op | source)
XLA Modules:
  0.0 40.3 jit_solution(9024214078874172541)
XLA Ops:
  0.0 1.0 %shard_map.82 = bf16[4,3,640]{2,1,0:T(4,128)(2,1)S(1)} custom-call(s32[1]{0:T(128)} %bitcast.index_ref, bf16[4,512,128]{2,1,0:T(8,128)(2,1)} %query_ref.9, bf16[4,512,256]{2,1,0:T(8,128)(2,1)} %key_ref.7, bf16[4,512,256]{2,1,0:T(8,128)(2,1)} %value_ref.7), custom_call_target="tpu_custom_call" | custom-call | tf_op jit(solution)/shard_map/pallas_call | solution.py:427
  1.6 1.5 %collective-permute-start = (bf16[4,3,640]{2,1,0:T(4,128)(2,1)S(1)}, bf16[4,3,640]{2,1,0:T(4,128)(2,1)S(1)}, u32[]{:S(2)}, u32[]{:S(2)}) collective-permute-start(bf16[4,3,640]{2,1,0:T(4,128)(2,1)S(1)} %shard_map.82), channel_id=1, source_target_pairs={{0,1},{1,2},{2,3},{3,4},{4,5},{5,6},{6,7},{7,8},{8,9},{9,10},{10,1... | collective-permute-start | bytes 46088 | tf_op jit(solution)/shard_map/ppermute | solution.py:464
  3.1 4.9 %shard_map.84 = (bf16[4,7,128,512]{3,2,1,0:T(8,128)(2,1)S(1)}, bf16[4,7,128,256]{3,2,1,0:T(8,128)(2,1)S(1)}, f32[4,7,128,128]{3,2,1,0:T(8,128)S(1)}, f32[4,128,1...) custom-call(s32[1]{0:T(128)} %bitcast.index_ref, ...), custom_call_target="tpu_custom_call", output_to_operand_aliasing={{0}: (6, {}), {1}: (7, {}), {2}: (8, {}), {3}: (9, {}), {4}... | custom-call | tf_op jit(solution)/shard_map/pallas_call | solution.py:397
  8.0 1.6 %collective-permute-done.halo_ref = bf16[4,3,640]{2,1,0:T(4,128)(2,1)S(1)} collective-permute-done((bf16[4,3,640]{2,1,0:T(4,128)(2,1)S(1)}, bf16[4,3,640]{2,1,0:T(4,128)(2,1)S(1)}, u32[]{:S(2)}, u32[]{:S(2)}) %collective-permute-start) | collective-permute-done | bytes 15392 | tf_op jit(solution)/shard_map/ppermute | solution.py:464
  9.6 1.0 %shard_map.85 = (bf16[4,128,512]{2,1,0:T(8,128)(2,1)S(1)}, bf16[4,128,256]{2,1,0:T(8,128)(2,1)S(1)}, f32[4,128,128]{2,1,0:T(8,128)S(1)}, f32[64,128]{1,0:T(8,128)S(1)}) custom-call(s32[1]{0:T(128)} %bitcast.index_ref, bf16[4,512,256]{2,1,0:T(8,128)(2,1)S(1)} %copy-done, bf16[4,512,256]{2,1,0:T(8,128)(2,1)S(1)} %copy-done.1, ...), custom_call_target="tpu_custom_call" | custom-call | tf_op jit(solution)/shard_map/pallas_call | solution.py:397
  10.6 3.7 %shard_map.86 = (bf16[2,8,128,256]{3,2,1,0:T(8,128)(2,1)S(1)}, bf16[2,8,128,256]{3,2,1,0:T(8,128)(2,1)S(1)}, bf16[2,8,128,256]{3,2,1,0:T(8,128)(2,1)S(1)}, f32[2,128,256]{2,1,0:T(8,128)S(1)}) custom-call(s32[1]{0:T(128)} %bitcast.index_ref, bf16[4,7,128,512]{3,2,1,0:T(8,128)(2,1)S(1)} %get-tuple-element.82.kv_ref, ...), custom_call_target="tpu_custom_call" | custom-call | tf_op jit(solution)/shard_map/pallas_call | solution.py:397
  14.3 2.2 %shard_map.87 = (bf16[1,8,128,256]{3,2,1,0:T(8,128)(2,1)S(1)}, bf16[1,8,128,256]{3,2,1,0:T(8,128)(2,1)S(1)}, bf16[1,8,128,256]{3,2,1,0:T(8,128)(2,1)S(1)}, f32[1,128,256]{2,1,0:T(8,128)S(1)}) custom-call(s32[1]{0:T(128)} %bitcast.index_ref, bf16[4,7,128,512]{3,2,1,0:T(8,128)(2,1)S(1)} %get-tuple-element.82.kv_ref, ...), custom_call_target="tpu_custom_call" | custom-call | tf_op jit(solution)/shard_map/pallas_call | solution.py:397
  16.8 0.8 %collective-permute-start.2 = (f32[1,128,256]{2,1,0:T(8,128)S(1)}, f32[1,128,256]{2,1,0:T(8,128)S(1)}, u32[]{:S(2)}, u32[]{:S(2)}) collective-permute-start(f32[1,128,256]{2,1,0:T(8,128)S(1)} %get-tuple-element.96.refs_0_), channel_id=1, source_target_pairs={{0,2},{1,3},{2,0},{3,1},{4,6},{5,7},{6,4},{7,5},{8,10},{9,11},{10,... | collective-permute-start | bytes 393224 | tf_op jit(solution)/shard_map/ppermute | solution.py:409
  17.7 2.2 %shard_map.89 = (bf16[1,8,128,256]{3,2,1,0:T(8,128)(2,1)S(1)}, bf16[1,8,128,256]{3,2,1,0:T(8,128)(2,1)S(1)}, bf16[1,8,128,256]{3,2,1,0:T(8,128)(2,1)S(1)}, f32[1,128,256]{2,1,0:T(8,128)S(1)}) custom-call(s32[1]{0:T(128)} %bitcast.index_ref, bf16[4,7,128,512]{3,2,1,0:T(8,128)(2,1)S(1)} %get-tuple-element.82.kv_ref, ...), custom_call_target="tpu_custom_call" | custom-call | tf_op jit(solution)/shard_map/pallas_call | solution.py:397
  20.1 1.3 %collective-permute-start.4 = (f32[1,128,256]{2,1,0:T(8,128)S(1)}, f32[1,128,256]{2,1,0:T(8,128)S(1)}, u32[]{:S(2)}, u32[]{:S(2)}) collective-permute-start(f32[1,128,256]{2,1,0:T(8,128)S(1)} %get-tuple-element.100.refs_0_), channel_id=1, source_target_pairs={{0,2},{1,3},{2,0},{3,1},{4,6},{5,7},{6,4},{7,5},{8,10},{9,11},{10,... | collective-permute-start | bytes 393224 | tf_op jit(solution)/shard_map/ppermute | solution.py:409
  21.4 1.4 %collective-permute-done.2.refs_1_ = f32[1,128,256]{2,1,0:T(8,128)S(1)} collective-permute-done((f32[1,128,256]{2,1,0:T(8,128)S(1)}, f32[1,128,256]{2,1,0:T(8,128)S(1)}, u32[]{:S(2)}, u32[]{:S(2)}) %collective-permute-start.2) | collective-permute-done | bytes 131104 | tf_op jit(solution)/shard_map/ppermute | solution.py:409
  23.0 0.9 %collective-permute-start.3 = (f32[1,128,256]{2,1,0:T(8,128)S(1)}, f32[1,128,256]{2,1,0:T(8,128)S(1)}, u32[]{:S(2)}, u32[]{:S(2)}) collective-permute-start(f32[1,128,256]{2,1,0:T(8,128)S(1)} %get-tuple-element.102.refs_0_), channel_id=1, source_target_pairs={{0,4},{1,5},{2,6},{3,7},{4,0},{5,1},{6,2},{7,3},{8,12},{9,13},{10,... | collective-permute-start | bytes 393224 | tf_op jit(solution)/shard_map/ppermute | solution.py:409
  23.9 1.1 %shard_map.92 = (bf16[512,256]{1,0:T(8,128)(2,1)S(1)}, f32[512,128]{1,0:T(8,128)S(1)}) custom-call(s32[1]{0:T(128)} %bitcast.index_ref, bf16[4,512,128]{2,1,0:T(8,128)(2,1)S(1)} %copy-done.2, bf16[4,3,640]{2,1,0:T(4,128)(2,1)S(1)} %collective-permute-done.halo_ref, f32[4,4,128]{2,1,0:T(4,128)S(1)} %copy-done.5, ...), custom_call_target="tpu_custom_call" | custom-call | tf_op jit(solution)/shard_map/pallas_call | solution.py:397
  25.0 0.8 %collective-permute-done.4.refs_1_ = f32[1,128,256]{2,1,0:T(8,128)S(1)} collective-permute-done((f32[1,128,256]{2,1,0:T(8,128)S(1)}, f32[1,128,256]{2,1,0:T(8,128)S(1)}, u32[]{:S(2)}, u32[]{:S(2)}) %collective-permute-start.4) | collective-permute-done | bytes 131104 | tf_op jit(solution)/shard_map/ppermute | solution.py:409
  26.0 1.6 %collective-permute-start.6 = (f32[1,128,256]{2,1,0:T(8,128)S(1)}, f32[1,128,256]{2,1,0:T(8,128)S(1)}, u32[]{:S(2)}, u32[]{:S(2)}) collective-permute-start(f32[1,128,256]{2,1,0:T(8,128)S(1)} %get-tuple-element.110.refs_0_), channel_id=1, source_target_pairs={{0,4},{1,5},{2,6},{3,7},{4,0},{5,1},{6,2},{7,3},{8,12},{9,13},{10,... | collective-permute-start | bytes 393224 | tf_op jit(solution)/shard_map/ppermute | solution.py:409
  27.7 1.2 %shard_map.94 = (bf16[512,256]{1,0:T(8,128)(2,1)S(1)}, f32[512,128]{1,0:T(8,128)S(1)}) custom-call(s32[1]{0:T(128)} %bitcast.index_ref, bf16[4,512,128]{2,1,0:T(8,128)(2,1)S(1)} %copy-done.2, bf16[4,3,640]{2,1,0:T(4,128)(2,1)S(1)} %collective-permute-done.halo_ref, f32[4,4,128]{2,1,0:T(4,128)S(1)} %copy-done.5, ...), custom_call_target="tpu_custom_call" | custom-call | tf_op jit(solution)/shard_map/pallas_call | solution.py:397
  29.1 2.7 %collective-permute-start.5 = (f32[1,128,128]{2,1,0:T(8,128)S(1)}, f32[1,128,128]{2,1,0:T(8,128)S(1)}, u32[]{:S(2)}, u32[]{:S(2)}) collective-permute-start(f32[1,128,128]{2,1,0:T(8,128)S(1)} %get-tuple-element.120), channel_id=1, source_target_pairs={{0,8},{1,9},{2,10},{3,11},{4,12},{5,13},{6,14},{7,15},{8,0},{9,1},... | collective-permute-start | bytes 196616 | tf_op jit(solution)/shard_map/ppermute | solution.py:409
  32.0 2.6 %collective-permute-start.7 = (f32[1,128,128]{2,1,0:T(8,128)S(1)}, f32[1,128,128]{2,1,0:T(8,128)S(1)}, u32[]{:S(2)}, u32[]{:S(2)}) collective-permute-start(f32[1,128,128]{2,1,0:T(8,128)S(1)} %get-tuple-element.123), channel_id=1, source_target_pairs={{0,8},{1,9},{2,10},{3,11},{4,12},{5,13},{6,14},{7,15},{8,0},{9,1},... | collective-permute-start | bytes 196616 | tf_op jit(solution)/shard_map/ppermute | solution.py:409
  34.6 1.1 %shard_map.97 = (bf16[512,256]{1,0:T(8,128)(2,1)S(1)}, f32[512,128]{1,0:T(8,128)S(1)}) custom-call(s32[1]{0:T(128)} %bitcast.index_ref, bf16[4,512,128]{2,1,0:T(8,128)(2,1)S(1)} %copy-done.2, bf16[4,3,640]{2,1,0:T(4,128)(2,1)S(1)} %collective-permute-done.halo_ref, f32[4,4,128]{2,1,0:T(4,128)S(1)} %copy-done.5, ...), custom_call_target="tpu_custom_call" | custom-call | tf_op jit(solution)/shard_map/pallas_call | solution.py:397
  35.7 1.1 %shard_map.98 = (bf16[512,256]{1,0:T(8,128)(2,1)S(1)}, f32[512,128]{1,0:T(8,128)S(1)}) custom-call(s32[1]{0:T(128)} %bitcast.index_ref, bf16[4,512,128]{2,1,0:T(8,128)(2,1)S(1)} %copy-done.2, bf16[4,3,640]{2,1,0:T(4,128)(2,1)S(1)} %collective-permute-done.halo_ref, f32[4,4,128]{2,1,0:T(4,128)S(1)} %copy-done.5, ...), custom_call_target="tpu_custom_call" | custom-call | tf_op jit(solution)/shard_map/pallas_call | solution.py:397
  36.8 0.4 shard_map.99
  37.3 0.4 shard_map.100
  37.7 1.2 %shard_map.101.refs_7_ = f32[4,512,128]{2,1,0:T(8,128)} custom-call(s32[1]{0:T(128)} %bitcast.index_ref, f32[4,128]{1,0:T(4,128)S(1)} %copy-done.7, f32[1,128,128]{2,1,0:T(8,128)S(1)} %get-tuple-element.137.refs_1_, bf16[512,256]{1,0:T(8,128)(2,1)S(1)} %get-tuple-element.115.refs_2_, f32[512,128]{1,0:T(8,128)S(1)} %get-tuple-element.116.refs_3_, ...), custom_call_target="tpu_custom_call" | custom-call | tf_op jit(solution)/shard_map/pallas_call | solution.py:588
  39.1 1.2 %shard_map.102 = f32[4,512,128]{2,1,0:T(8,128)} custom-call(s32[1]{0:T(128)} %bitcast.index_ref, f32[4,128]{1,0:T(4,128)S(1)} %copy-done.7, f32[1,128,128]{2,1,0:T(8,128)S(1)} %get-tuple-element.144.refs_1_, bf16[512,256]{1,0:T(8,128)(2,1)S(1)} %get-tuple-element.107.refs_2_, ...), custom_call_target="tpu_custom_call", output_to_operand_aliasing={{}: (8, {})} | custom-call | tf_op jit(solution)/shard_map/pallas_call | solution.py:588
  (33 shorter events, 2.3 us)
Async XLA Ops:
  0.0 1.3 %copy-start.1 = (bf16[4,512,256]{2,1,0:T(8,128)(2,1)S(1)}, bf16[4,512,256]{2,1,0:T(8,128)(2,1)}, u32[]{:S(2)}) copy-start(bf16[4,512,256]{2,1,0:T(8,128)(2,1)} %value_ref.7) | copy-start | bytes 3145732
  0.0 1.6 %copy-start = (bf16[4,512,256]{2,1,0:T(8,128)(2,1)S(1)}, bf16[4,512,256]{2,1,0:T(8,128)(2,1)}, u32[]{:S(2)}) copy-start(bf16[4,512,256]{2,1,0:T(8,128)(2,1)} %key_ref.7) | copy-start | bytes 3145732
  0.0 1.6 %copy-start.4 = (f32[4,4,256]{2,1,0:T(4,128)S(1)}, f32[4,4,256]{2,1,0:T(4,128)}, u32[]{:S(2)}) copy-start(f32[4,4,256]{2,1,0:T(4,128)} %cv_ref.5) | copy-start | bytes 49156
  0.0 1.6 %copy-start.3 = (f32[4,4,256]{2,1,0:T(4,128)S(1)}, f32[4,4,256]{2,1,0:T(4,128)}, u32[]{:S(2)}) copy-start(f32[4,4,256]{2,1,0:T(4,128)} %ck_ref.5) | copy-start | bytes 49156
  0.0 1.6 %copy-start.6 = (f32[4,1024]{1,0:T(4,128)S(1)}, f32[4,1024]{1,0:T(4,128)}, u32[]{:S(2)}) copy-start(f32[4,1024]{1,0:T(4,128)} %rate_ref.3) | copy-start | bytes 49156
  1.6 8.0 %collective-permute-start = (bf16[4,3,640]{2,1,0:T(4,128)(2,1)S(1)}, bf16[4,3,640]{2,1,0:T(4,128)(2,1)S(1)}, u32[]{:S(2)}, u32[]{:S(2)}) collective-permute-start(bf16[4,3,640]{2,1,0:T(4,128)(2,1)S(1)} %shard_map.82), channel_id=1, source_target_pairs={{0,1},{1,2},{2,3},{3,4},{4,5},{5,6},{6,7},{7,8},{8,9},{9,10},{10,1... | collective-permute-start | bytes 46088 | tf_op jit(solution)/shard_map/ppermute | solution.py:464
  14.3 2.3 %collective-permute-start.1 = (f32[2,128,256]{2,1,0:T(8,128)S(1)}, f32[2,128,256]{2,1,0:T(8,128)S(1)}, u32[]{:S(2)}, u32[]{:S(2)}) collective-permute-start(f32[2,128,256]{2,1,0:T(8,128)S(1)} %get-tuple-element.93), channel_id=1, source_target_pairs={{0,1},{1,0},{2,3},{3,2},{4,5},{5,4},{6,7},{7,6},{8,9},{9,8},{10,11... | collective-permute-start | bytes 786440 | tf_op jit(solution)/shard_map/ppermute | solution.py:409
  16.8 7.1 %copy-start.2 = (bf16[4,512,128]{2,1,0:T(8,128)(2,1)S(1)}, bf16[4,512,128]{2,1,0:T(8,128)(2,1)}, u32[]{:S(2)}) copy-start(bf16[4,512,128]{2,1,0:T(8,128)(2,1)} %query_ref.9) | copy-start | bytes 1572868
  16.8 7.1 %copy-start.5 = (f32[4,4,128]{2,1,0:T(4,128)S(1)}, f32[4,4,128]{2,1,0:T(4,128)}, u32[]{:S(2)}) copy-start(f32[4,4,128]{2,1,0:T(4,128)} %cq_ref.7) | copy-start | bytes 24580
  16.8 6.0 %collective-permute-start.2 = (f32[1,128,256]{2,1,0:T(8,128)S(1)}, f32[1,128,256]{2,1,0:T(8,128)S(1)}, u32[]{:S(2)}, u32[]{:S(2)}) collective-permute-start(f32[1,128,256]{2,1,0:T(8,128)S(1)} %get-tuple-element.96.refs_0_), channel_id=1, source_target_pairs={{0,2},{1,3},{2,0},{3,1},{4,6},{5,7},{6,4},{7,5},{8,10},{9,11},{10,... | collective-permute-start | bytes 393224 | tf_op jit(solution)/shard_map/ppermute | solution.py:409
  20.1 5.7 %collective-permute-start.4 = (f32[1,128,256]{2,1,0:T(8,128)S(1)}, f32[1,128,256]{2,1,0:T(8,128)S(1)}, u32[]{:S(2)}, u32[]{:S(2)}) collective-permute-start(f32[1,128,256]{2,1,0:T(8,128)S(1)} %get-tuple-element.100.refs_0_), channel_id=1, source_target_pairs={{0,2},{1,3},{2,0},{3,1},{4,6},{5,7},{6,4},{7,5},{8,10},{9,11},{10,... | collective-permute-start | bytes 393224 | tf_op jit(solution)/shard_map/ppermute | solution.py:409
  23.0 5.9 %collective-permute-start.3 = (f32[1,128,256]{2,1,0:T(8,128)S(1)}, f32[1,128,256]{2,1,0:T(8,128)S(1)}, u32[]{:S(2)}, u32[]{:S(2)}) collective-permute-start(f32[1,128,256]{2,1,0:T(8,128)S(1)} %get-tuple-element.102.refs_0_), channel_id=1, source_target_pairs={{0,4},{1,5},{2,6},{3,7},{4,0},{5,1},{6,2},{7,3},{8,12},{9,13},{10,... | collective-permute-start | bytes 393224 | tf_op jit(solution)/shard_map/ppermute | solution.py:409
  26.0 5.8 %collective-permute-start.6 = (f32[1,128,256]{2,1,0:T(8,128)S(1)}, f32[1,128,256]{2,1,0:T(8,128)S(1)}, u32[]{:S(2)}, u32[]{:S(2)}) collective-permute-start(f32[1,128,256]{2,1,0:T(8,128)S(1)} %get-tuple-element.110.refs_0_), channel_id=1, source_target_pairs={{0,4},{1,5},{2,6},{3,7},{4,0},{5,1},{6,2},{7,3},{8,12},{9,13},{10,... | collective-permute-start | bytes 393224 | tf_op jit(solution)/shard_map/ppermute | solution.py:409
  29.1 7.7 %collective-permute-start.5 = (f32[1,128,128]{2,1,0:T(8,128)S(1)}, f32[1,128,128]{2,1,0:T(8,128)S(1)}, u32[]{:S(2)}, u32[]{:S(2)}) collective-permute-start(f32[1,128,128]{2,1,0:T(8,128)S(1)} %get-tuple-element.120), channel_id=1, source_target_pairs={{0,8},{1,9},{2,10},{3,11},{4,12},{5,13},{6,14},{7,15},{8,0},{9,1},... | collective-permute-start | bytes 196616 | tf_op jit(solution)/shard_map/ppermute | solution.py:409
  32.0 5.2 %collective-permute-start.7 = (f32[1,128,128]{2,1,0:T(8,128)S(1)}, f32[1,128,128]{2,1,0:T(8,128)S(1)}, u32[]{:S(2)}, u32[]{:S(2)}) collective-permute-start(f32[1,128,128]{2,1,0:T(8,128)S(1)} %get-tuple-element.123), channel_id=1, source_target_pairs={{0,8},{1,9},{2,10},{3,11},{4,12},{5,13},{6,14},{7,15},{8,0},{9,1},... | collective-permute-start | bytes 196616 | tf_op jit(solution)/shard_map/ppermute | solution.py:409
  35.7 2.0 %copy-start.7 = (f32[4,128]{1,0:T(4,128)S(1)}, f32[4,128]{1,0:T(4,128)}, u32[]{:S(2)}) copy-start(f32[4,128]{1,0:T(4,128)} %refs_0_.3) | copy-start | bytes 6148
  37.6 1.4 %collective-permute-start.8 = (f32[2,128,128]{2,1,0:T(8,128)S(1)}, f32[2,128,128]{2,1,0:T(8,128)S(1)}, u32[]{:S(2)}, u32[]{:S(2)}) collective-permute-start(f32[2,128,128]{2,1,0:T(8,128)S(1)} %pad_maximum_fusion), channel_id=1, source_target_pairs={{0,1},{1,0},{2,3},{3,2},{4,5},{5,4},{6,7},{7,6},{8,9},{9,8},{10,11... | collective-permute-start | bytes 393224 | tf_op jit(solution)/shard_map/ppermute | solution.py:409

commit v10 on v9

--- a/solution.py
+++ b/solution.py
@@ -622,11 +622,12 @@
             after = tuple(read[kept, at])
         return after
 
+    step = read_some(1, *step)
     while any(chain["left"] for chain in chains.values()):
         for at in range(half):
             if chains[at]["left"]:
                 step = (join(at, *step),)
-                if len(todo) > half:
+                if len(todo) > 1:
                     step = read_some(1, *step)
     step = read_some(len(todo), *step)
     mine, other = {}, {}

time: 40.4 us -> 40.4 us (level)
  transfers between devices with their start and end apart: 9 -> 9, of which waited for: 5 -> 6; matrix products, arithmetic and copies ran while one was open for 0% -> 0% of each run, Pallas kernels for 41% -> 40%
where the time goes in v10:
time: 40.4 us; the launch traced here: 40.3 us
  Pallas kernels  23.6 us (58%)
  starting transfers between devices  11.8 us (29%)
  waiting for transfers between devices  4 us (10%)
  local copies, waits for them, and re-layouts  0.65 us (2%)
    pallas_call x18, Pallas kernels, resident(): pl.pallas_call(kernel, in_specs=[smem] + [vmem] * len(args), out_specs=[v...  20.2 us
    ppermute x8, starting transfers between devices, swap(): return lax.ppermute(x, 'seq', [(i, i ^ bit) for i in range(count)])  10.3 us
    pallas_call x2, Pallas kernels, finish(): pl.pallas_call(kernel, grid_spec=pltpu.PrefetchScalarGridSpec(num_scalar_...  2.42 us
    ppermute x8, waiting for transfers between devices, swap(): return lax.ppermute(x, 'seq', [(i, i ^ bit) for i in range(count)])  2.41 us
    ppermute x1, waiting for transfers between devices, per_device(): lax.ppermute(tails, 'seq', [(i, (i + 1) % count) for i in range(count)])  1.59 us
    ppermute x1, starting transfers between devices, per_device(): lax.ppermute(tails, 'seq', [(i, (i + 1) % count) for i in range(count)])  1.52 us
    pallas_call x1, Pallas kernels, per_device(): pl.pallas_call(tails_kernel, grid_spec=pltpu.PrefetchScalarGridSpec(num_s...  0.96 us
  transfers between devices with their start and end apart: 9, of which 6 were waited for; matrix products, arithmetic and copies ran while one was open for 0% of the time, Pallas kernels for 40%

profile of v10, /device:TPU:0, one launch (start us, length us, event | category | flops | bytes accessed | tf_op | source)
XLA Modules:
  0.0 40.3 jit_solution(18311951594900477067)
XLA Ops:
  0.0 1.0 %shard_map.82 = bf16[4,3,640]{2,1,0:T(4,128)(2,1)S(1)} custom-call(s32[1]{0:T(128)} %bitcast.index_ref, bf16[4,512,128]{2,1,0:T(8,128)(2,1)} %query_ref.9, bf16[4,512,256]{2,1,0:T(8,128)(2,1)} %key_ref.7, bf16[4,512,256]{2,1,0:T(8,128)(2,1)} %value_ref.7), custom_call_target="tpu_custom_call" | custom-call | tf_op jit(solution)/shard_map/pallas_call | solution.py:427
  1.6 1.5 %collective-permute-start = (bf16[4,3,640]{2,1,0:T(4,128)(2,1)S(1)}, bf16[4,3,640]{2,1,0:T(4,128)(2,1)S(1)}, u32[]{:S(2)}, u32[]{:S(2)}) collective-permute-start(bf16[4,3,640]{2,1,0:T(4,128)(2,1)S(1)} %shard_map.82), channel_id=1, source_target_pairs={{0,1},{1,2},{2,3},{3,4},{4,5},{5,6},{6,7},{7,8},{8,9},{9,10},{10,1... | collective-permute-start | bytes 46088 | tf_op jit(solution)/shard_map/ppermute | solution.py:464
  3.1 4.9 %shard_map.84 = (bf16[4,7,128,512]{3,2,1,0:T(8,128)(2,1)S(1)}, bf16[4,7,128,256]{3,2,1,0:T(8,128)(2,1)S(1)}, f32[4,7,128,128]{3,2,1,0:T(8,128)S(1)}, f32[4,128,1...) custom-call(s32[1]{0:T(128)} %bitcast.index_ref, ...), custom_call_target="tpu_custom_call", output_to_operand_aliasing={{0}: (6, {}), {1}: (7, {}), {2}: (8, {}), {3}: (9, {}), {4}... | custom-call | tf_op jit(solution)/shard_map/pallas_call | solution.py:397
  8.0 1.6 %collective-permute-done.halo_ref = bf16[4,3,640]{2,1,0:T(4,128)(2,1)S(1)} collective-permute-done((bf16[4,3,640]{2,1,0:T(4,128)(2,1)S(1)}, bf16[4,3,640]{2,1,0:T(4,128)(2,1)S(1)}, u32[]{:S(2)}, u32[]{:S(2)}) %collective-permute-start) | collective-permute-done | bytes 15392 | tf_op jit(solution)/shard_map/ppermute | solution.py:464
  9.6 1.0 %shard_map.85 = (bf16[4,128,512]{2,1,0:T(8,128)(2,1)S(1)}, bf16[4,128,256]{2,1,0:T(8,128)(2,1)S(1)}, f32[4,128,128]{2,1,0:T(8,128)S(1)}, f32[64,128]{1,0:T(8,128)S(1)}) custom-call(s32[1]{0:T(128)} %bitcast.index_ref, bf16[4,512,256]{2,1,0:T(8,128)(2,1)S(1)} %copy-done, bf16[4,512,256]{2,1,0:T(8,128)(2,1)S(1)} %copy-done.1, ...), custom_call_target="tpu_custom_call" | custom-call | tf_op jit(solution)/shard_map/pallas_call | solution.py:397
  10.6 3.7 %shard_map.86 = (bf16[2,8,128,256]{3,2,1,0:T(8,128)(2,1)S(1)}, bf16[2,8,128,256]{3,2,1,0:T(8,128)(2,1)S(1)}, bf16[2,8,128,256]{3,2,1,0:T(8,128)(2,1)S(1)}, f32[2,128,256]{2,1,0:T(8,128)S(1)}) custom-call(s32[1]{0:T(128)} %bitcast.index_ref, bf16[4,7,128,512]{3,2,1,0:T(8,128)(2,1)S(1)} %get-tuple-element.82.kv_ref, ...), custom_call_target="tpu_custom_call" | custom-call | tf_op jit(solution)/shard_map/pallas_call | solution.py:397
  14.3 2.2 %shard_map.87 = (bf16[1,8,128,256]{3,2,1,0:T(8,128)(2,1)S(1)}, bf16[1,8,128,256]{3,2,1,0:T(8,128)(2,1)S(1)}, bf16[1,8,128,256]{3,2,1,0:T(8,128)(2,1)S(1)}, f32[1,128,256]{2,1,0:T(8,128)S(1)}) custom-call(s32[1]{0:T(128)} %bitcast.index_ref, bf16[4,7,128,512]{3,2,1,0:T(8,128)(2,1)S(1)} %get-tuple-element.82.kv_ref, ...), custom_call_target="tpu_custom_call" | custom-call | tf_op jit(solution)/shard_map/pallas_call | solution.py:397
  16.8 0.8 %collective-permute-start.2 = (f32[1,128,256]{2,1,0:T(8,128)S(1)}, f32[1,128,256]{2,1,0:T(8,128)S(1)}, u32[]{:S(2)}, u32[]{:S(2)}) collective-permute-start(f32[1,128,256]{2,1,0:T(8,128)S(1)} %get-tuple-element.96.refs_0_), channel_id=1, source_target_pairs={{0,2},{1,3},{2,0},{3,1},{4,6},{5,7},{6,4},{7,5},{8,10},{9,11},{10,... | collective-permute-start | bytes 393224 | tf_op jit(solution)/shard_map/ppermute | solution.py:409
  17.7 2.2 %shard_map.89 = (bf16[1,8,128,256]{3,2,1,0:T(8,128)(2,1)S(1)}, bf16[1,8,128,256]{3,2,1,0:T(8,128)(2,1)S(1)}, bf16[1,8,128,256]{3,2,1,0:T(8,128)(2,1)S(1)}, f32[1,128,256]{2,1,0:T(8,128)S(1)}) custom-call(s32[1]{0:T(128)} %bitcast.index_ref, bf16[4,7,128,512]{3,2,1,0:T(8,128)(2,1)S(1)} %get-tuple-element.82.kv_ref, ...), custom_call_target="tpu_custom_call" | custom-call | tf_op jit(solution)/shard_map/pallas_call | solution.py:397
  20.1 1.3 %collective-permute-start.4 = (f32[1,128,256]{2,1,0:T(8,128)S(1)}, f32[1,128,256]{2,1,0:T(8,128)S(1)}, u32[]{:S(2)}, u32[]{:S(2)}) collective-permute-start(f32[1,128,256]{2,1,0:T(8,128)S(1)} %get-tuple-element.100.refs_0_), channel_id=1, source_target_pairs={{0,2},{1,3},{2,0},{3,1},{4,6},{5,7},{6,4},{7,5},{8,10},{9,11},{10,... | collective-permute-start | bytes 393224 | tf_op jit(solution)/shard_map/ppermute | solution.py:409
  21.4 1.1 %shard_map.91 = (bf16[512,256]{1,0:T(8,128)(2,1)S(1)}, f32[512,128]{1,0:T(8,128)S(1)}) custom-call(s32[1]{0:T(128)} %bitcast.index_ref, bf16[4,512,128]{2,1,0:T(8,128)(2,1)S(1)} %copy-done.2, bf16[4,3,640]{2,1,0:T(4,128)(2,1)S(1)} %collective-permute-done.halo_ref, f32[4,4,128]{2,1,0:T(4,128)S(1)} %copy-done.5, ...), custom_call_target="tpu_custom_call" | custom-call | tf_op jit(solution)/shard_map/pallas_call | solution.py:397
  23.0 0.9 %collective-permute-start.3 = (f32[1,128,256]{2,1,0:T(8,128)S(1)}, f32[1,128,256]{2,1,0:T(8,128)S(1)}, u32[]{:S(2)}, u32[]{:S(2)}) collective-permute-start(f32[1,128,256]{2,1,0:T(8,128)S(1)} %get-tuple-element.108.refs_0_), channel_id=1, source_target_pairs={{0,4},{1,5},{2,6},{3,7},{4,0},{5,1},{6,2},{7,3},{8,12},{9,13},{10,... | collective-permute-start | bytes 393224 | tf_op jit(solution)/shard_map/ppermute | solution.py:409
  23.9 1.0 %shard_map.93 = (bf16[512,256]{1,0:T(8,128)(2,1)S(1)}, f32[512,128]{1,0:T(8,128)S(1)}) custom-call(s32[1]{0:T(128)} %bitcast.index_ref, bf16[4,512,128]{2,1,0:T(8,128)(2,1)S(1)} %copy-done.2, bf16[4,3,640]{2,1,0:T(4,128)(2,1)S(1)} %collective-permute-done.halo_ref, f32[4,4,128]{2,1,0:T(4,128)S(1)} %copy-done.5, ...), custom_call_target="tpu_custom_call" | custom-call | tf_op jit(solution)/shard_map/pallas_call | solution.py:397
  25.0 0.8 %collective-permute-done.4.refs_1_ = f32[1,128,256]{2,1,0:T(8,128)S(1)} collective-permute-done((f32[1,128,256]{2,1,0:T(8,128)S(1)}, f32[1,128,256]{2,1,0:T(8,128)S(1)}, u32[]{:S(2)}, u32[]{:S(2)}) %collective-permute-start.4) | collective-permute-done | bytes 131104 | tf_op jit(solution)/shard_map/ppermute | solution.py:409
  26.0 1.8 %collective-permute-start.6 = (f32[1,128,256]{2,1,0:T(8,128)S(1)}, f32[1,128,256]{2,1,0:T(8,128)S(1)}, u32[]{:S(2)}, u32[]{:S(2)}) collective-permute-start(f32[1,128,256]{2,1,0:T(8,128)S(1)} %get-tuple-element.116.refs_0_), channel_id=1, source_target_pairs={{0,4},{1,5},{2,6},{3,7},{4,0},{5,1},{6,2},{7,3},{8,12},{9,13},{10,... | collective-permute-start | bytes 393224 | tf_op jit(solution)/shard_map/ppermute | solution.py:409
  27.8 1.1 %shard_map.95 = (bf16[512,256]{1,0:T(8,128)(2,1)S(1)}, f32[512,128]{1,0:T(8,128)S(1)}) custom-call(s32[1]{0:T(128)} %bitcast.index_ref, bf16[4,512,128]{2,1,0:T(8,128)(2,1)S(1)} %copy-done.2, bf16[4,3,640]{2,1,0:T(4,128)(2,1)S(1)} %collective-permute-done.halo_ref, f32[4,4,128]{2,1,0:T(4,128)S(1)} %copy-done.5, ...), custom_call_target="tpu_custom_call" | custom-call | tf_op jit(solution)/shard_map/pallas_call | solution.py:397
  29.1 2.7 %collective-permute-start.5 = (f32[1,128,128]{2,1,0:T(8,128)S(1)}, f32[1,128,128]{2,1,0:T(8,128)S(1)}, u32[]{:S(2)}, u32[]{:S(2)}) collective-permute-start(f32[1,128,128]{2,1,0:T(8,128)S(1)} %get-tuple-element.123), channel_id=1, source_target_pairs={{0,8},{1,9},{2,10},{3,11},{4,12},{5,13},{6,14},{7,15},{8,0},{9,1},... | collective-permute-start | bytes 196616 | tf_op jit(solution)/shard_map/ppermute | solution.py:409
  32.0 2.6 %collective-permute-start.7 = (f32[1,128,128]{2,1,0:T(8,128)S(1)}, f32[1,128,128]{2,1,0:T(8,128)S(1)}, u32[]{:S(2)}, u32[]{:S(2)}) collective-permute-start(f32[1,128,128]{2,1,0:T(8,128)S(1)} %get-tuple-element.126), channel_id=1, source_target_pairs={{0,8},{1,9},{2,10},{3,11},{4,12},{5,13},{6,14},{7,15},{8,0},{9,1},... | collective-permute-start | bytes 196616 | tf_op jit(solution)/shard_map/ppermute | solution.py:409
  34.7 1.1 %shard_map.98 = (bf16[512,256]{1,0:T(8,128)(2,1)S(1)}, f32[512,128]{1,0:T(8,128)S(1)}) custom-call(s32[1]{0:T(128)} %bitcast.index_ref, bf16[4,512,128]{2,1,0:T(8,128)(2,1)S(1)} %copy-done.2, bf16[4,3,640]{2,1,0:T(4,128)(2,1)S(1)} %collective-permute-done.halo_ref, f32[4,4,128]{2,1,0:T(4,128)S(1)} %copy-done.5, ...), custom_call_target="tpu_custom_call" | custom-call | tf_op jit(solution)/shard_map/pallas_call | solution.py:397
  35.7 0.5 %collective-permute-done.5.got_ref = f32[1,128,128]{2,1,0:T(8,128)S(1)} collective-permute-done((f32[1,128,128]{2,1,0:T(8,128)S(1)}, f32[1,128,128]{2,1,0:T(8,128)S(1)}, u32[]{:S(2)}, u32[]{:S(2)}) %collective-permute-start.5) | collective-permute-done | bytes 65568 | tf_op jit(solution)/shard_map/ppermute | solution.py:409
  36.3 0.4 shard_map.99
  36.6 0.7 %collective-permute-done.7.got_ref = f32[1,128,128]{2,1,0:T(8,128)S(1)} collective-permute-done((f32[1,128,128]{2,1,0:T(8,128)S(1)}, f32[1,128,128]{2,1,0:T(8,128)S(1)}, u32[]{:S(2)}, u32[]{:S(2)}) %collective-permute-start.7) | collective-permute-done | bytes 65568 | tf_op jit(solution)/shard_map/ppermute | solution.py:409
  37.7 1.2 %shard_map.101.refs_7_ = f32[4,512,128]{2,1,0:T(8,128)} custom-call(s32[1]{0:T(128)} %bitcast.index_ref, f32[4,128]{1,0:T(4,128)S(1)} %copy-done.7, f32[1,128,128]{2,1,0:T(8,128)S(1)} %get-tuple-element.137.refs_1_, bf16[512,256]{1,0:T(8,128)(2,1)S(1)} %get-tuple-element.113.refs_2_, f32[512,128]{1,0:T(8,128)S(1)} %get-tuple-element.114.refs_3_, ...), custom_call_target="tpu_custom_call" | custom-call | tf_op jit(solution)/shard_map/pallas_call | solution.py:588
  39.1 1.2 %shard_map.102 = f32[4,512,128]{2,1,0:T(8,128)} custom-call(s32[1]{0:T(128)} %bitcast.index_ref, f32[4,128]{1,0:T(4,128)S(1)} %copy-done.7, f32[1,128,128]{2,1,0:T(8,128)S(1)} %get-tuple-element.144.refs_1_, bf16[512,256]{1,0:T(8,128)(2,1)S(1)} %get-tuple-element.105.refs_2_, ...), custom_call_target="tpu_custom_call", output_to_operand_aliasing={{}: (8, {})} | custom-call | tf_op jit(solution)/shard_map/pallas_call | solution.py:588
  (33 shorter events, 2.9 us)
Async XLA Ops:
  0.0 1.3 %copy-start.1 = (bf16[4,512,256]{2,1,0:T(8,128)(2,1)S(1)}, bf16[4,512,256]{2,1,0:T(8,128)(2,1)}, u32[]{:S(2)}) copy-start(bf16[4,512,256]{2,1,0:T(8,128)(2,1)} %value_ref.7) | copy-start | bytes 3145732
  0.0 1.6 %copy-start = (bf16[4,512,256]{2,1,0:T(8,128)(2,1)S(1)}, bf16[4,512,256]{2,1,0:T(8,128)(2,1)}, u32[]{:S(2)}) copy-start(bf16[4,512,256]{2,1,0:T(8,128)(2,1)} %key_ref.7) | copy-start | bytes 3145732
  0.0 1.6 %copy-start.4 = (f32[4,4,256]{2,1,0:T(4,128)S(1)}, f32[4,4,256]{2,1,0:T(4,128)}, u32[]{:S(2)}) copy-start(f32[4,4,256]{2,1,0:T(4,128)} %cv_ref.5) | copy-start | bytes 49156
  0.0 1.6 %copy-start.3 = (f32[4,4,256]{2,1,0:T(4,128)S(1)}, f32[4,4,256]{2,1,0:T(4,128)}, u32[]{:S(2)}) copy-start(f32[4,4,256]{2,1,0:T(4,128)} %ck_ref.5) | copy-start | bytes 49156
  0.0 1.6 %copy-start.6 = (f32[4,1024]{1,0:T(4,128)S(1)}, f32[4,1024]{1,0:T(4,128)}, u32[]{:S(2)}) copy-start(f32[4,1024]{1,0:T(4,128)} %rate_ref.3) | copy-start | bytes 49156
  1.6 8.0 %collective-permute-start = (bf16[4,3,640]{2,1,0:T(4,128)(2,1)S(1)}, bf16[4,3,640]{2,1,0:T(4,128)(2,1)S(1)}, u32[]{:S(2)}, u32[]{:S(2)}) collective-permute-start(bf16[4,3,640]{2,1,0:T(4,128)(2,1)S(1)} %shard_map.82), channel_id=1, source_target_pairs={{0,1},{1,2},{2,3},{3,4},{4,5},{5,6},{6,7},{7,8},{8,9},{9,10},{10,1... | collective-permute-start | bytes 46088 | tf_op jit(solution)/shard_map/ppermute | solution.py:464
  14.3 2.3 %collective-permute-start.1 = (f32[2,128,256]{2,1,0:T(8,128)S(1)}, f32[2,128,256]{2,1,0:T(8,128)S(1)}, u32[]{:S(2)}, u32[]{:S(2)}) collective-permute-start(f32[2,128,256]{2,1,0:T(8,128)S(1)} %get-tuple-element.93), channel_id=1, source_target_pairs={{0,1},{1,0},{2,3},{3,2},{4,5},{5,4},{6,7},{7,6},{8,9},{9,8},{10,11... | collective-permute-start | bytes 786440 | tf_op jit(solution)/shard_map/ppermute | solution.py:409
  16.8 4.6 %copy-start.2 = (bf16[4,512,128]{2,1,0:T(8,128)(2,1)S(1)}, bf16[4,512,128]{2,1,0:T(8,128)(2,1)}, u32[]{:S(2)}) copy-start(bf16[4,512,128]{2,1,0:T(8,128)(2,1)} %query_ref.9) | copy-start | bytes 1572868
  16.8 4.6 %copy-start.5 = (f32[4,4,128]{2,1,0:T(4,128)S(1)}, f32[4,4,128]{2,1,0:T(4,128)}, u32[]{:S(2)}) copy-start(f32[4,4,128]{2,1,0:T(4,128)} %cq_ref.7) | copy-start | bytes 24580
  16.8 6.0 %collective-permute-start.2 = (f32[1,128,256]{2,1,0:T(8,128)S(1)}, f32[1,128,256]{2,1,0:T(8,128)S(1)}, u32[]{:S(2)}, u32[]{:S(2)}) collective-permute-start(f32[1,128,256]{2,1,0:T(8,128)S(1)} %get-tuple-element.96.refs_0_), channel_id=1, source_target_pairs={{0,2},{1,3},{2,0},{3,1},{4,6},{5,7},{6,4},{7,5},{8,10},{9,11},{10,... | collective-permute-start | bytes 393224 | tf_op jit(solution)/shard_map/ppermute | solution.py:409
  20.1 5.7 %collective-permute-start.4 = (f32[1,128,256]{2,1,0:T(8,128)S(1)}, f32[1,128,256]{2,1,0:T(8,128)S(1)}, u32[]{:S(2)}, u32[]{:S(2)}) collective-permute-start(f32[1,128,256]{2,1,0:T(8,128)S(1)} %get-tuple-element.100.refs_0_), channel_id=1, source_target_pairs={{0,2},{1,3},{2,0},{3,1},{4,6},{5,7},{6,4},{7,5},{8,10},{9,11},{10,... | collective-permute-start | bytes 393224 | tf_op jit(solution)/shard_map/ppermute | solution.py:409
  23.0 5.9 %collective-permute-start.3 = (f32[1,128,256]{2,1,0:T(8,128)S(1)}, f32[1,128,256]{2,1,0:T(8,128)S(1)}, u32[]{:S(2)}, u32[]{:S(2)}) collective-permute-start(f32[1,128,256]{2,1,0:T(8,128)S(1)} %get-tuple-element.108.refs_0_), channel_id=1, source_target_pairs={{0,4},{1,5},{2,6},{3,7},{4,0},{5,1},{6,2},{7,3},{8,12},{9,13},{10,... | collective-permute-start | bytes 393224 | tf_op jit(solution)/shard_map/ppermute | solution.py:409
  26.0 5.8 %collective-permute-start.6 = (f32[1,128,256]{2,1,0:T(8,128)S(1)}, f32[1,128,256]{2,1,0:T(8,128)S(1)}, u32[]{:S(2)}, u32[]{:S(2)}) collective-permute-start(f32[1,128,256]{2,1,0:T(8,128)S(1)} %get-tuple-element.116.refs_0_), channel_id=1, source_target_pairs={{0,4},{1,5},{2,6},{3,7},{4,0},{5,1},{6,2},{7,3},{8,12},{9,13},{10,... | collective-permute-start | bytes 393224 | tf_op jit(solution)/shard_map/ppermute | solution.py:409
  29.1 7.1 %collective-permute-start.5 = (f32[1,128,128]{2,1,0:T(8,128)S(1)}, f32[1,128,128]{2,1,0:T(8,128)S(1)}, u32[]{:S(2)}, u32[]{:S(2)}) collective-permute-start(f32[1,128,128]{2,1,0:T(8,128)S(1)} %get-tuple-element.123), channel_id=1, source_target_pairs={{0,8},{1,9},{2,10},{3,11},{4,12},{5,13},{6,14},{7,15},{8,0},{9,1},... | collective-permute-start | bytes 196616 | tf_op jit(solution)/shard_map/ppermute | solution.py:409
  32.0 5.2 %collective-permute-start.7 = (f32[1,128,128]{2,1,0:T(8,128)S(1)}, f32[1,128,128]{2,1,0:T(8,128)S(1)}, u32[]{:S(2)}, u32[]{:S(2)}) collective-permute-start(f32[1,128,128]{2,1,0:T(8,128)S(1)} %get-tuple-element.126), channel_id=1, source_target_pairs={{0,8},{1,9},{2,10},{3,11},{4,12},{5,13},{6,14},{7,15},{8,0},{9,1},... | collective-permute-start | bytes 196616 | tf_op jit(solution)/shard_map/ppermute | solution.py:409
  34.7 3.1 %copy-start.7 = (f32[4,128]{1,0:T(4,128)S(1)}, f32[4,128]{1,0:T(4,128)}, u32[]{:S(2)}) copy-start(f32[4,128]{1,0:T(4,128)} %refs_0_.3) | copy-start | bytes 6148
  37.7 1.4 %collective-permute-start.8 = (f32[2,128,128]{2,1,0:T(8,128)S(1)}, f32[2,128,128]{2,1,0:T(8,128)S(1)}, u32[]{:S(2)}, u32[]{:S(2)}) collective-permute-start(f32[2,128,128]{2,1,0:T(8,128)S(1)} %pad_maximum_fusion), channel_id=1, source_target_pairs={{0,1},{1,0},{2,3},{3,2},{4,5},{5,4},{6,7},{7,6},{8,9},{9,8},{10,11... | collective-permute-start | bytes 393224 | tf_op jit(solution)/shard_map/ppermute | solution.py:409

commit v11 on v8

--- a/solution.py
+++ b/solution.py
@@ -302,21 +302,18 @@
         pulled_ref[rows[n]] = split(mm(pulled[rows[n]], p_ref[slot, n]))
 
 
-def out_kernel(kept, start, half, index_ref, gain_ref, *rest):
+def out_kernel(kept, half, index_ref, gain_ref, *rest):
     out_ref = rest[-1]
-    for i in range(len(rest) // 3):
+    first = first_head(index_ref, kept, half)
+    for i in range(half):
         state_ref, pulled_ref, local_ref = rest[3 * i : 3 * i + 3]
-
-        @pl.when(pl.program_id(0) == i)
-        def _():
-            h = first_head(index_ref, kept, half) + start + i
-            state = split(state_ref[0])
-            gain = pick_row(gain_ref[...], h)
-            for at in range(0, pulled_ref.shape[0], BLOCK):
-                rows = slice(at, at + BLOCK)
-                raw = mm(pulled_ref[rows], state) + local_ref[rows]
-                mean = jnp.mean(raw * raw, 1, keepdims=True)
-                out_ref[0, rows] = raw * lax.rsqrt(mean + 1e-06) * gain
+        state = split(state_ref[0])
+        gain = pick_row(gain_ref[...], first + i)
+        for at in range(0, pulled_ref.shape[0], BLOCK):
+            rows = slice(at, at + BLOCK)
+            raw = mm(pulled_ref[rows], state) + local_ref[rows]
+            mean = jnp.mean(raw * raw, 1, keepdims=True)
+            out_ref[i, rows] = raw * lax.rsqrt(mean + 1e-06) * gain
 
 
 def then(later, earlier):
@@ -553,29 +550,29 @@
     out_shape = shape((heads, tokens, dim), f32)
     done = ()
 
-    def finish(kept, start, states, *after):
+    def finish(kept, states, *after):
         nonlocal done
         vmem = pl.BlockSpec(memory_space=pltpu.VMEM)
 
         def out_block(i, index_ref):
             upper = index_ref[0] & 1
-            return ((upper if kept else 1 - upper) * half + start + i, 0, 0)
+            return (upper if kept else 1 - upper, 0, 0)
 
         args = [out_gain]
         for i, state in enumerate(states):
-            args += [state, *read[kept, start + i]]
+            args += [state, *read[kept, i]]
         args = [pltpu.with_memory_space_constraint(a, pltpu.VMEM) for a in args]
 
         def kernel(index_ref, *refs):
-            out_kernel(kept, start, half, index_ref, *refs[: len(args)], refs[-1])
+            out_kernel(kept, half, index_ref, *refs[: len(args)], refs[-1])
 
         out = pl.pallas_call(
             kernel,
             grid_spec=pltpu.PrefetchScalarGridSpec(
                 num_scalar_prefetch=1,
-                grid=(len(states),),
+                grid=(1,),
                 in_specs=[vmem] * len(args) + [pl.BlockSpec(memory_space=pl.ANY)] * len(done),
-                out_specs=pl.BlockSpec((1, tokens, dim), out_block),
+                out_specs=pl.BlockSpec((half, tokens, dim), out_block),
             ),
             out_shape=out_shape,
             input_output_aliases={len(args) + 1: 0} if done else {},
@@ -606,11 +603,12 @@
             after = tuple(read[kept, at])
         return after
 
+    step = read_some(1, *step)
     while any(chain["left"] for chain in chains.values()):
         for at in range(half):
             if chains[at]["left"]:
                 step = (join(at, *step),)
-                if len(todo) > half:
+                if len(todo) > 1:
                     step = read_some(1, *step)
     step = read_some(len(todo), *step)
     mine, other = {}, {}
@@ -618,9 +616,9 @@
         mine[at], other[at] = down(at, *step)
         step = (mine[at],)
     others = swap(jnp.concatenate([other[at] for at in range(half)], 0), 1, count)
-    last = finish(True, 0, [mine[at] for at in range(half)])
+    last = finish(True, [mine[at] for at in range(half)])
     others = lax.optimization_barrier((others, last))[0]
-    return finish(False, 0, [others[at : at + 1] for at in range(half)])
+    return finish(False, [others[at : at + 1] for at in range(half)])
 
 
 def solution(mesh):

time: 40.9 us -> 40 us (0.978)
  Pallas kernels: 24.2 us -> 23.6 us
  waiting for transfers between devices: 4.3 us -> 3.79 us
    ppermute x8, waiting for transfers between devices: 2.84 us -> 2.32 us  [swap(): return lax.ppermute(x, 'seq', [(i, i ^ bit) for i in range(count)])]
    pallas_call x2, Pallas kernels: 2.85 us -> 2.43 us  [finish(): pl.pallas_call(kernel, grid_spec=pltpu.PrefetchScalarGridSpec(num_scalar_...]
where the time goes in v11:
time: 40 us; the launch traced here: 39.8 us
  Pallas kernels  23.6 us (59%)
  starting transfers between devices  12.1 us (30%)
  waiting for transfers between devices  3.79 us (9%)
    pallas_call x17, Pallas kernels, resident(): pl.pallas_call(kernel, in_specs=[smem] + [vmem] * len(args), out_specs=[v...  20.2 us
    ppermute x8, starting transfers between devices, swap(): return lax.ppermute(x, 'seq', [(i, i ^ bit) for i in range(count)])  11.6 us
    pallas_call x2, Pallas kernels, finish(): pl.pallas_call(kernel, grid_spec=pltpu.PrefetchScalarGridSpec(num_scalar_...  2.43 us
    ppermute x8, waiting for transfers between devices, swap(): return lax.ppermute(x, 'seq', [(i, i ^ bit) for i in range(count)])  2.32 us
    ppermute x1, waiting for transfers between devices, per_device(): lax.ppermute(tails, 'seq', [(i, (i + 1) % count) for i in range(count)])  1.47 us
    pallas_call x1, Pallas kernels, per_device(): pl.pallas_call(tails_kernel, grid_spec=pltpu.PrefetchScalarGridSpec(num_s...  0.96 us
  transfers between devices with their start and end apart: 9, of which 5 were waited for; matrix products, arithmetic and copies ran while one was open for 0% of the time, Pallas kernels for 41%

profile of v11, /device:TPU:0, one launch (start us, length us, event | category | flops | bytes accessed | tf_op | source)
XLA Modules:
  0.0 39.8 jit_solution(18036939479760305145)
XLA Ops:
  0.0 1.0 %shard_map.82 = bf16[4,3,640]{2,1,0:T(4,128)(2,1)S(1)} custom-call(s32[1]{0:T(128)} %bitcast.index_ref, bf16[4,512,128]{2,1,0:T(8,128)(2,1)} %query_ref.9, bf16[4,512,256]{2,1,0:T(8,128)(2,1)} %key_ref.5, bf16[4,512,256]{2,1,0:T(8,128)(2,1)} %value_ref.5), custom_call_target="tpu_custom_call" | custom-call | tf_op jit(solution)/shard_map/pallas_call | solution.py:419
  1.0 0.5 %collective-permute-start = (bf16[4,3,640]{2,1,0:T(4,128)(2,1)S(1)}, bf16[4,3,640]{2,1,0:T(4,128)(2,1)S(1)}, u32[]{:S(2)}, u32[]{:S(2)}) collective-permute-start(bf16[4,3,640]{2,1,0:T(4,128)(2,1)S(1)} %shard_map.82), channel_id=1, source_target_pairs={{0,1},{1,2},{2,3},{3,4},{4,5},{5,6},{6,7},{7,8},{8,9},{9,10},{10,1... | collective-permute-start | bytes 46088 | tf_op jit(solution)/shard_map/ppermute | solution.py:430
  1.6 4.9 %shard_map.83 = (bf16[4,7,128,512]{3,2,1,0:T(8,128)(2,1)S(1)}, bf16[4,7,128,256]{3,2,1,0:T(8,128)(2,1)S(1)}, f32[4,7,128,128]{3,2,1,0:T(8,128)S(1)}, f32[4,128,128]{2,1,0:T(8,128)S(1)}, f32[4,8,128]{2,1,0:T(8,128)S(1)}) custom-call(s32[1]{0:T(128)} %bitcast.index_ref, bf16[4,512,256]{2,1,0:T(8,128)(2,1)S(1)} %copy-done.1, ...), custom_call_target="tpu_custom_call" | custom-call | tf_op jit(solution)/shard_map/pallas_call | solution.py:390
  6.5 1.5 %collective-permute-done.halo_ref = bf16[4,3,640]{2,1,0:T(4,128)(2,1)S(1)} collective-permute-done((bf16[4,3,640]{2,1,0:T(4,128)(2,1)S(1)}, bf16[4,3,640]{2,1,0:T(4,128)(2,1)S(1)}, u32[]{:S(2)}, u32[]{:S(2)}) %collective-permute-start) | collective-permute-done | bytes 15392 | tf_op jit(solution)/shard_map/ppermute | solution.py:430
  8.0 1.0 %shard_map.84 = (bf16[4,128,512]{2,1,0:T(8,128)(2,1)S(1)}, bf16[4,128,256]{2,1,0:T(8,128)(2,1)S(1)}, f32[4,128,128]{2,1,0:T(8,128)S(1)}, f32[64,128]{1,0:T(8,128)S(1)}) custom-call(s32[1]{0:T(128)} %bitcast.index_ref, bf16[4,512,256]{2,1,0:T(8,128)(2,1)S(1)} %copy-done.1, bf16[4,512,256]{2,1,0:T(8,128)(2,1)S(1)} %copy-done.2, ...), custom_call_target="tpu_custom_call" | custom-call | tf_op jit(solution)/shard_map/pallas_call | solution.py:390
  8.9 3.7 %shard_map.85 = (bf16[2,8,128,256]{3,2,1,0:T(8,128)(2,1)S(1)}, bf16[2,8,128,256]{3,2,1,0:T(8,128)(2,1)S(1)}, bf16[2,8,128,256]{3,2,1,0:T(8,128)(2,1)S(1)}, f32[2,128,256]{2,1,0:T(8,128)S(1)}) custom-call(s32[1]{0:T(128)} %bitcast.index_ref, bf16[4,7,128,512]{3,2,1,0:T(8,128)(2,1)S(1)} %get-tuple-element.68.kv_ref, ...), custom_call_target="tpu_custom_call" | custom-call | tf_op jit(solution)/shard_map/pallas_call | solution.py:390
  12.6 1.2 %collective-permute-start.1 = (f32[2,128,256]{2,1,0:T(8,128)S(1)}, f32[2,128,256]{2,1,0:T(8,128)S(1)}, u32[]{:S(2)}, u32[]{:S(2)}) collective-permute-start(f32[2,128,256]{2,1,0:T(8,128)S(1)} %get-tuple-element.79), channel_id=1, source_target_pairs={{0,1},{1,0},{2,3},{3,2},{4,5},{5,4},{6,7},{7,6},{8,9},{9,8},{10,11... | collective-permute-start | bytes 786440 | tf_op jit(solution)/shard_map/ppermute | solution.py:401
  13.8 2.2 %shard_map.86 = (bf16[1,8,128,256]{3,2,1,0:T(8,128)(2,1)S(1)}, bf16[1,8,128,256]{3,2,1,0:T(8,128)(2,1)S(1)}, bf16[1,8,128,256]{3,2,1,0:T(8,128)(2,1)S(1)}, f32[1,128,256]{2,1,0:T(8,128)S(1)}) custom-call(s32[1]{0:T(128)} %bitcast.index_ref, bf16[4,7,128,512]{3,2,1,0:T(8,128)(2,1)S(1)} %get-tuple-element.68.kv_ref, ...), custom_call_target="tpu_custom_call" | custom-call | tf_op jit(solution)/shard_map/pallas_call | solution.py:390
  16.3 1.6 %collective-permute-start.2 = (f32[1,128,256]{2,1,0:T(8,128)S(1)}, f32[1,128,256]{2,1,0:T(8,128)S(1)}, u32[]{:S(2)}, u32[]{:S(2)}) collective-permute-start(f32[1,128,256]{2,1,0:T(8,128)S(1)} %get-tuple-element.82.refs_0_), channel_id=1, source_target_pairs={{0,2},{1,3},{2,0},{3,1},{4,6},{5,7},{6,4},{7,5},{8,10},{9,11},{10,... | collective-permute-start | bytes 393224 | tf_op jit(solution)/shard_map/ppermute | solution.py:401
  17.9 2.2 %shard_map.88 = (bf16[1,8,128,256]{3,2,1,0:T(8,128)(2,1)S(1)}, bf16[1,8,128,256]{3,2,1,0:T(8,128)(2,1)S(1)}, bf16[1,8,128,256]{3,2,1,0:T(8,128)(2,1)S(1)}, f32[1,128,256]{2,1,0:T(8,128)S(1)}) custom-call(s32[1]{0:T(128)} %bitcast.index_ref, bf16[4,7,128,512]{3,2,1,0:T(8,128)(2,1)S(1)} %get-tuple-element.68.kv_ref, ...), custom_call_target="tpu_custom_call" | custom-call | tf_op jit(solution)/shard_map/pallas_call | solution.py:390
  20.3 0.6 %collective-permute-start.4 = (f32[1,128,256]{2,1,0:T(8,128)S(1)}, f32[1,128,256]{2,1,0:T(8,128)S(1)}, u32[]{:S(2)}, u32[]{:S(2)}) collective-permute-start(f32[1,128,256]{2,1,0:T(8,128)S(1)} %get-tuple-element.86.refs_0_), channel_id=1, source_target_pairs={{0,2},{1,3},{2,0},{3,1},{4,6},{5,7},{6,4},{7,5},{8,10},{9,11},{10,... | collective-permute-start | bytes 393224 | tf_op jit(solution)/shard_map/ppermute | solution.py:401
  20.9 1.1 %shard_map.90 = (bf16[512,256]{1,0:T(8,128)(2,1)S(1)}, f32[512,128]{1,0:T(8,128)S(1)}) custom-call(s32[1]{0:T(128)} %bitcast.index_ref, bf16[4,512,128]{2,1,0:T(8,128)(2,1)S(1)} %copy-done, bf16[4,3,640]{2,1,0:T(4,128)(2,1)S(1)} %collective-permute-done.halo_ref, f32[4,4,128]{2,1,0:T(4,128)S(1)} %copy-done.3, ...), custom_call_target="tpu_custom_call" | custom-call | tf_op jit(solution)/shard_map/pallas_call | solution.py:390
  22.2 1.6 %collective-permute-start.3 = (f32[1,128,256]{2,1,0:T(8,128)S(1)}, f32[1,128,256]{2,1,0:T(8,128)S(1)}, u32[]{:S(2)}, u32[]{:S(2)}) collective-permute-start(f32[1,128,256]{2,1,0:T(8,128)S(1)} %get-tuple-element.94.refs_0_), channel_id=1, source_target_pairs={{0,4},{1,5},{2,6},{3,7},{4,0},{5,1},{6,2},{7,3},{8,12},{9,13},{10,... | collective-permute-start | bytes 393224 | tf_op jit(solution)/shard_map/ppermute | solution.py:401
  23.8 1.0 %shard_map.92 = (bf16[512,256]{1,0:T(8,128)(2,1)S(1)}, f32[512,128]{1,0:T(8,128)S(1)}) custom-call(s32[1]{0:T(128)} %bitcast.index_ref, bf16[4,512,128]{2,1,0:T(8,128)(2,1)S(1)} %copy-done, bf16[4,3,640]{2,1,0:T(4,128)(2,1)S(1)} %collective-permute-done.halo_ref, f32[4,4,128]{2,1,0:T(4,128)S(1)} %copy-done.3, ...), custom_call_target="tpu_custom_call" | custom-call | tf_op jit(solution)/shard_map/pallas_call | solution.py:390
  24.9 0.6 %collective-permute-done.4.refs_1_ = f32[1,128,256]{2,1,0:T(8,128)S(1)} collective-permute-done((f32[1,128,256]{2,1,0:T(8,128)S(1)}, f32[1,128,256]{2,1,0:T(8,128)S(1)}, u32[]{:S(2)}, u32[]{:S(2)}) %collective-permute-start.4) | collective-permute-done | bytes 131104 | tf_op jit(solution)/shard_map/ppermute | solution.py:401
  25.7 1.8 %collective-permute-start.6 = (f32[1,128,256]{2,1,0:T(8,128)S(1)}, f32[1,128,256]{2,1,0:T(8,128)S(1)}, u32[]{:S(2)}, u32[]{:S(2)}) collective-permute-start(f32[1,128,256]{2,1,0:T(8,128)S(1)} %get-tuple-element.102.refs_0_), channel_id=1, source_target_pairs={{0,4},{1,5},{2,6},{3,7},{4,0},{5,1},{6,2},{7,3},{8,12},{9,13},{10,... | collective-permute-start | bytes 393224 | tf_op jit(solution)/shard_map/ppermute | solution.py:401
  27.5 1.1 %shard_map.94 = (bf16[512,256]{1,0:T(8,128)(2,1)S(1)}, f32[512,128]{1,0:T(8,128)S(1)}) custom-call(s32[1]{0:T(128)} %bitcast.index_ref, bf16[4,512,128]{2,1,0:T(8,128)(2,1)S(1)} %copy-done, bf16[4,3,640]{2,1,0:T(4,128)(2,1)S(1)} %collective-permute-done.halo_ref, f32[4,4,128]{2,1,0:T(4,128)S(1)} %copy-done.3, ...), custom_call_target="tpu_custom_call" | custom-call | tf_op jit(solution)/shard_map/pallas_call | solution.py:390
  28.9 2.0 %collective-permute-start.5 = (f32[1,128,128]{2,1,0:T(8,128)S(1)}, f32[1,128,128]{2,1,0:T(8,128)S(1)}, u32[]{:S(2)}, u32[]{:S(2)}) collective-permute-start(f32[1,128,128]{2,1,0:T(8,128)S(1)} %get-tuple-element.109), channel_id=1, source_target_pairs={{0,8},{1,9},{2,10},{3,11},{4,12},{5,13},{6,14},{7,15},{8,0},{9,1},... | collective-permute-start | bytes 196616 | tf_op jit(solution)/shard_map/ppermute | solution.py:401
  31.2 2.7 %collective-permute-start.7 = (f32[1,128,128]{2,1,0:T(8,128)S(1)}, f32[1,128,128]{2,1,0:T(8,128)S(1)}, u32[]{:S(2)}, u32[]{:S(2)}) collective-permute-start(f32[1,128,128]{2,1,0:T(8,128)S(1)} %get-tuple-element.112), channel_id=1, source_target_pairs={{0,8},{1,9},{2,10},{3,11},{4,12},{5,13},{6,14},{7,15},{8,0},{9,1},... | collective-permute-start | bytes 196616 | tf_op jit(solution)/shard_map/ppermute | solution.py:401
  33.8 1.1 %shard_map.97 = (bf16[512,256]{1,0:T(8,128)(2,1)S(1)}, f32[512,128]{1,0:T(8,128)S(1)}) custom-call(s32[1]{0:T(128)} %bitcast.index_ref, bf16[4,512,128]{2,1,0:T(8,128)(2,1)S(1)} %copy-done, bf16[4,3,640]{2,1,0:T(4,128)(2,1)S(1)} %collective-permute-done.halo_ref, f32[4,4,128]{2,1,0:T(4,128)S(1)} %copy-done.3, ...), custom_call_target="tpu_custom_call" | custom-call | tf_op jit(solution)/shard_map/pallas_call | solution.py:390
  34.9 1.2 %collective-permute-done.5.got_ref = f32[1,128,128]{2,1,0:T(8,128)S(1)} collective-permute-done((f32[1,128,128]{2,1,0:T(8,128)S(1)}, f32[1,128,128]{2,1,0:T(8,128)S(1)}, u32[]{:S(2)}, u32[]{:S(2)}) %collective-permute-start.5) | collective-permute-done | bytes 65568 | tf_op jit(solution)/shard_map/ppermute | solution.py:401
  36.1 0.4 shard_map.98
  37.3 1.2 %shard_map.100.refs_7_ = f32[4,512,128]{2,1,0:T(8,128)} custom-call(s32[1]{0:T(128)} %bitcast.index_ref, f32[4,128]{1,0:T(4,128)S(1)} %copy-done.7, f32[1,128,128]{2,1,0:T(8,128)S(1)} %get-tuple-element.123.refs_1_, bf16[512,256]{1,0:T(8,128)(2,1)S(1)} %get-tuple-element.99.refs_2_, f32[512,128]{1,0:T(8,128)S(1)} %get-tuple-element.100.refs_3_, ...), custom_call_target="tpu_custom_call" | custom-call | tf_op jit(solution)/shard_map/pallas_call | solution.py:569
  38.6 1.2 %shard_map.101 = f32[4,512,128]{2,1,0:T(8,128)} custom-call(s32[1]{0:T(128)} %bitcast.index_ref, f32[4,128]{1,0:T(4,128)S(1)} %copy-done.7, f32[1,128,128]{2,1,0:T(8,128)S(1)} %get-tuple-element.130.refs_1_, bf16[512,256]{1,0:T(8,128)(2,1)S(1)} %get-tuple-element.91.refs_2_, ...), custom_call_target="tpu_custom_call", output_to_operand_aliasing={{}: (8, {})} | custom-call | tf_op jit(solution)/shard_map/pallas_call | solution.py:569
  (32 shorter events, 2.3 us)
Async XLA Ops:
  0.0 1.5 %copy-start.2 = (bf16[4,512,256]{2,1,0:T(8,128)(2,1)S(1)}, bf16[4,512,256]{2,1,0:T(8,128)(2,1)}, u32[]{:S(2)}) copy-start(bf16[4,512,256]{2,1,0:T(8,128)(2,1)} %value_ref.5) | copy-start | bytes 3145732
  0.0 1.6 %copy-start.1 = (bf16[4,512,256]{2,1,0:T(8,128)(2,1)S(1)}, bf16[4,512,256]{2,1,0:T(8,128)(2,1)}, u32[]{:S(2)}) copy-start(bf16[4,512,256]{2,1,0:T(8,128)(2,1)} %key_ref.5) | copy-start | bytes 3145732
  0.0 1.6 %copy-start.5 = (f32[4,4,256]{2,1,0:T(4,128)S(1)}, f32[4,4,256]{2,1,0:T(4,128)}, u32[]{:S(2)}) copy-start(f32[4,4,256]{2,1,0:T(4,128)} %cv_ref.3) | copy-start | bytes 49156
  0.0 1.6 %copy-start.4 = (f32[4,4,256]{2,1,0:T(4,128)S(1)}, f32[4,4,256]{2,1,0:T(4,128)}, u32[]{:S(2)}) copy-start(f32[4,4,256]{2,1,0:T(4,128)} %ck_ref.3) | copy-start | bytes 49156
  0.0 1.6 %copy-start.6 = (f32[4,1024]{1,0:T(4,128)S(1)}, f32[4,1024]{1,0:T(4,128)}, u32[]{:S(2)}) copy-start(f32[4,1024]{1,0:T(4,128)} %rate_ref.1) | copy-start | bytes 49156
  1.0 7.0 %collective-permute-start = (bf16[4,3,640]{2,1,0:T(4,128)(2,1)S(1)}, bf16[4,3,640]{2,1,0:T(4,128)(2,1)S(1)}, u32[]{:S(2)}, u32[]{:S(2)}) collective-permute-start(bf16[4,3,640]{2,1,0:T(4,128)(2,1)S(1)} %shard_map.82), channel_id=1, source_target_pairs={{0,1},{1,2},{2,3},{3,4},{4,5},{5,6},{6,7},{7,8},{8,9},{9,10},{10,1... | collective-permute-start | bytes 46088 | tf_op jit(solution)/shard_map/ppermute | solution.py:430
  12.6 3.4 %collective-permute-start.1 = (f32[2,128,256]{2,1,0:T(8,128)S(1)}, f32[2,128,256]{2,1,0:T(8,128)S(1)}, u32[]{:S(2)}, u32[]{:S(2)}) collective-permute-start(f32[2,128,256]{2,1,0:T(8,128)S(1)} %get-tuple-element.79), channel_id=1, source_target_pairs={{0,1},{1,0},{2,3},{3,2},{4,5},{5,4},{6,7},{7,6},{8,9},{9,8},{10,11... | collective-permute-start | bytes 786440 | tf_op jit(solution)/shard_map/ppermute | solution.py:401
  16.2 4.6 %copy-start = (bf16[4,512,128]{2,1,0:T(8,128)(2,1)S(1)}, bf16[4,512,128]{2,1,0:T(8,128)(2,1)}, u32[]{:S(2)}) copy-start(bf16[4,512,128]{2,1,0:T(8,128)(2,1)} %query_ref.9) | copy-start | bytes 1572868
  16.3 4.6 %copy-start.3 = (f32[4,4,128]{2,1,0:T(4,128)S(1)}, f32[4,4,128]{2,1,0:T(4,128)}, u32[]{:S(2)}) copy-start(f32[4,4,128]{2,1,0:T(4,128)} %cq_ref.7) | copy-start | bytes 24580
  16.3 5.7 %collective-permute-start.2 = (f32[1,128,256]{2,1,0:T(8,128)S(1)}, f32[1,128,256]{2,1,0:T(8,128)S(1)}, u32[]{:S(2)}, u32[]{:S(2)}) collective-permute-start(f32[1,128,256]{2,1,0:T(8,128)S(1)} %get-tuple-element.82.refs_0_), channel_id=1, source_target_pairs={{0,2},{1,3},{2,0},{3,1},{4,6},{5,7},{6,4},{7,5},{8,10},{9,11},{10,... | collective-permute-start | bytes 393224 | tf_op jit(solution)/shard_map/ppermute | solution.py:401
  20.3 5.2 %collective-permute-start.4 = (f32[1,128,256]{2,1,0:T(8,128)S(1)}, f32[1,128,256]{2,1,0:T(8,128)S(1)}, u32[]{:S(2)}, u32[]{:S(2)}) collective-permute-start(f32[1,128,256]{2,1,0:T(8,128)S(1)} %get-tuple-element.86.refs_0_), channel_id=1, source_target_pairs={{0,2},{1,3},{2,0},{3,1},{4,6},{5,7},{6,4},{7,5},{8,10},{9,11},{10,... | collective-permute-start | bytes 393224 | tf_op jit(solution)/shard_map/ppermute | solution.py:401
  22.2 6.4 %collective-permute-start.3 = (f32[1,128,256]{2,1,0:T(8,128)S(1)}, f32[1,128,256]{2,1,0:T(8,128)S(1)}, u32[]{:S(2)}, u32[]{:S(2)}) collective-permute-start(f32[1,128,256]{2,1,0:T(8,128)S(1)} %get-tuple-element.94.refs_0_), channel_id=1, source_target_pairs={{0,4},{1,5},{2,6},{3,7},{4,0},{5,1},{6,2},{7,3},{8,12},{9,13},{10,... | collective-permute-start | bytes 393224 | tf_op jit(solution)/shard_map/ppermute | solution.py:401
  25.7 5.2 %collective-permute-start.6 = (f32[1,128,256]{2,1,0:T(8,128)S(1)}, f32[1,128,256]{2,1,0:T(8,128)S(1)}, u32[]{:S(2)}, u32[]{:S(2)}) collective-permute-start(f32[1,128,256]{2,1,0:T(8,128)S(1)} %get-tuple-element.102.refs_0_), channel_id=1, source_target_pairs={{0,4},{1,5},{2,6},{3,7},{4,0},{5,1},{6,2},{7,3},{8,12},{9,13},{10,... | collective-permute-start | bytes 393224 | tf_op jit(solution)/shard_map/ppermute | solution.py:401
  28.9 7.2 %collective-permute-start.5 = (f32[1,128,128]{2,1,0:T(8,128)S(1)}, f32[1,128,128]{2,1,0:T(8,128)S(1)}, u32[]{:S(2)}, u32[]{:S(2)}) collective-permute-start(f32[1,128,128]{2,1,0:T(8,128)S(1)} %get-tuple-element.109), channel_id=1, source_target_pairs={{0,8},{1,9},{2,10},{3,11},{4,12},{5,13},{6,14},{7,15},{8,0},{9,1},... | collective-permute-start | bytes 196616 | tf_op jit(solution)/shard_map/ppermute | solution.py:401
  31.2 5.6 %collective-permute-start.7 = (f32[1,128,128]{2,1,0:T(8,128)S(1)}, f32[1,128,128]{2,1,0:T(8,128)S(1)}, u32[]{:S(2)}, u32[]{:S(2)}) collective-permute-start(f32[1,128,128]{2,1,0:T(8,128)S(1)} %get-tuple-element.112), channel_id=1, source_target_pairs={{0,8},{1,9},{2,10},{3,11},{4,12},{5,13},{6,14},{7,15},{8,0},{9,1},... | collective-permute-start | bytes 196616 | tf_op jit(solution)/shard_map/ppermute | solution.py:401
  33.8 3.4 %copy-start.7 = (f32[4,128]{1,0:T(4,128)S(1)}, f32[4,128]{1,0:T(4,128)}, u32[]{:S(2)}) copy-start(f32[4,128]{1,0:T(4,128)} %refs_0_.3) | copy-start | bytes 6148
  37.2 1.4 %collective-permute-start.8 = (f32[2,128,128]{2,1,0:T(8,128)S(1)}, f32[2,128,128]{2,1,0:T(8,128)S(1)}, u32[]{:S(2)}, u32[]{:S(2)}) collective-permute-start(f32[2,128,128]{2,1,0:T(8,128)S(1)} %pad_maximum_fusion), channel_id=1, source_target_pairs={{0,1},{1,0},{2,3},{3,2},{4,5},{5,4},{6,7},{7,6},{8,9},{9,8},{10,11... | collective-permute-start | bytes 393224 | tf_op jit(solution)/shard_map/ppermute | solution.py:401
